TPU v7x, 32 devices: a whole 2x2x4 slice. The times are simulated.
32 devices in a mesh: dp: 8 (over z, core), fsdp: 4 (over y, x).
Axes of the slice: x: 2, y: 2, z: 4, core: 2. Of those that a mesh axis runs over, the one named last changes fastest.
Arguments:
- inputs: bfloat16 [4, 800, 48, 256], P('fsdp', None, 'dp'), may hold values from -20 to 20, as said below
- out_grad: bfloat16 [4, 800, 48, 256], P('fsdp', None, 'dp'), may hold values from -6 to 6
- ocean_mask: int32 [48, 256], P('dp'), may hold values from 0 to 1, as said below
- rollout_lengths: int32 [4], replicated, may hold values from 1 to 8
- conv_weight: float32 [800, 49], P('fsdp'), may hold values from -0.875 to 0.875
- norm_gain: float32 [800], P('fsdp'), may hold values from 0.25 to 1.75
- norm_bias: float32 [800], P('fsdp'), may hold values from -3 to 3
- expand_weight: bfloat16 [800, 3200], P('fsdp'), may hold values from -0.21875 to 0.21875
- expand_bias: bfloat16 [3200], P('fsdp'), may hold values from -3 to 3
- project_weight: bfloat16 [800, 3200], P('fsdp'), may hold values from -0.21875 to 0.21875
- project_bias: bfloat16 [800], P('fsdp'), may hold values from -3 to 3
Outputs:
- block_out: bfloat16 [4, 800, 48, 256], P('fsdp', None, 'dp')
- input_grad: float32 [4, 800, 48, 256], P('fsdp', None, 'dp')
- conv_weight_grad: float32 [800, 49], P('fsdp')
- norm_gain_grad: float32 [800], P('fsdp')
- norm_bias_grad: float32 [800], P('fsdp')
- expand_weight_grad: float32 [800, 3200], P('fsdp')
- expand_bias_grad: float32 [3200], P('fsdp')
- project_weight_grad: float32 [800, 3200], P('fsdp')
- project_bias_grad: float32 [800], P('fsdp')
- chan_mean: float32 [800], replicated
- chan_std: float32 [800], replicated
Inputs may be any that keep to these rules, and one draw needn't show every extreme that they name: `inputs`: fields whose spread and per-channel offset change with the row. `ocean_mask`: 1 marks ocean, 0 land; the first column of every row is ocean.
All inputs are finite; a program needn't handle non-finite values.
Results may differ from a plain program's by a relative error of at most 0.0058.
Values may be sent and summed in bfloat16 or wider, within the bound.
No kernel may reach another device: no remote copies, remote signals or barrier semaphores. Data moves between devices by JAX's collectives and lax.ppermute only.
A program may use at most 192 MiB of HBM per device.

v0:
```python
import jax
import jax.numpy as jnp
from jax import lax
from jax.sharding import PartitionSpec as P

KS = 7
ROLLOUT = 8


EPS = 1e-05


def padded_2(shard, sides, width):
    for axis, dim in sides:
        size, length = (lax.axis_size(axis), shard.shape[dim])
        up = [(i, (i + 1) % size) for i in range(size - 1)]
        down = [(j, i) for i, j in up]
        last = lax.slice_in_dim(shard, length - width, length, axis=dim)
        first = lax.slice_in_dim(shard, 0, width, axis=dim)
        before = lax.ppermute(last, axis, up)
        after = lax.ppermute(first, axis, down)
        shard = jnp.concatenate([before, shard, after], axis=dim)
    return shard


def wrap_columns(field, reach):
    return jnp.concatenate([field[..., -reach:], field, field[..., :reach]], axis=-1)


def per_device(
    inputs,
    out_grad,
    ocean_mask,
    rollout_lengths,
    conv_weight,
    norm_gain,
    norm_bias,
    expand_weight,
    expand_bias,
    project_weight,
    project_bias,
):
    reach = KS // 2
    samples_dev, channels, rows_dev, columns = inputs.shape
    pixels = rows_dev * columns
    first_sample = lax.axis_index("fsdp") * samples_dev
    sample_ids = first_sample + jnp.arange(samples_dev, dtype=jnp.int32)
    own_lengths = lax.dynamic_slice_in_dim(rollout_lengths, first_sample, samples_dev)
    live_flag = jnp.where(sample_ids % ROLLOUT < own_lengths, 1.0, 0.0).astype(jnp.float32)
    weight = live_flag[:, None, None] * ocean_mask.astype(jnp.float32)[None]
    weight_c = weight[:, None]
    conv_full, gain_full, bias_full = (
        lax.all_gather(conv_weight, "fsdp", axis=0, tiled=True),
        lax.all_gather(norm_gain, "fsdp", axis=0, tiled=True),
        lax.all_gather(norm_bias, "fsdp", axis=0, tiled=True),
    )
    padded = padded_2(inputs, (("dp", 2),), reach)
    widened = wrap_columns(padded.astype(jnp.float32), reach)
    conv_out = jnp.zeros(inputs.shape, jnp.float32)
    for row_step in range(KS):
        for col_step in range(KS):
            tap_weight = conv_full[:, KS * row_step + col_step][None, :, None, None]
            conv_out = (
                conv_out
                + tap_weight
                * widened[:, :, row_step : row_step + rows_dev, col_step : col_step + columns]
            )
    ocean_count, chan_sums = lax.psum(
        (jnp.sum(weight), jnp.sum(weight_c * conv_out, axis=(0, 2, 3))), ("dp", "fsdp")
    )
    chan_mean = chan_sums / ocean_count
    centered = conv_out - chan_mean[None, :, None, None]
    squared = lax.psum(jnp.sum(weight_c * centered * centered, axis=(0, 2, 3)), ("dp", "fsdp"))
    variance = squared / ocean_count
    inv_std = lax.rsqrt(variance + EPS)
    normalized = centered * inv_std[None, :, None, None]
    activation = (
        normalized * gain_full[None, :, None, None] + bias_full[None, :, None, None]
    ).astype(jnp.bfloat16)
    activation = activation.reshape(samples_dev, channels, pixels)
    expand_full, expand_bias_full, project_full, project_bias_full = (
        lax.all_gather(expand_weight, "fsdp", axis=0, tiled=True),
        lax.all_gather(expand_bias, "fsdp", axis=0, tiled=True),
        lax.all_gather(project_weight, "fsdp", axis=0, tiled=True),
        lax.all_gather(project_bias, "fsdp", axis=0, tiled=True),
    )
    hidden_pre = jnp.einsum(
        "ck,scp->skp", expand_full, activation, preferred_element_type=jnp.float32
    )
    hidden_pre = hidden_pre + expand_bias_full.astype(jnp.float32)[None, :, None]
    gelu_value, gelu_pull = jax.vjp(jax.nn.gelu, hidden_pre)
    hidden = gelu_value.astype(jnp.bfloat16)
    branch = jnp.einsum("ck,skp->scp", project_full, hidden, preferred_element_type=jnp.float32)
    branch = branch + project_bias_full.astype(jnp.float32)[None, :, None]
    block_out = ((inputs.astype(jnp.float32) + branch.reshape(inputs.shape)) * weight_c).astype(
        jnp.bfloat16
    )
    masked_grad = out_grad.astype(jnp.float32) * weight_c
    branch_grad = masked_grad.astype(jnp.bfloat16).reshape(samples_dev, channels, pixels)
    expand_back, project_back = (
        lax.all_gather(expand_weight, "fsdp", axis=0, tiled=True),
        lax.all_gather(project_weight, "fsdp", axis=0, tiled=True),
    )
    hidden_pull = jnp.einsum(
        "ck,scp->skp", project_back, branch_grad, preferred_element_type=jnp.float32
    )
    hidden_grad = gelu_pull(hidden_pull)[0].astype(jnp.bfloat16)
    project_weight_local = jnp.einsum(
        "scp,skp->ck", branch_grad, hidden, preferred_element_type=jnp.float32
    )
    project_bias_local = jnp.sum(branch_grad.astype(jnp.float32), axis=(0, 2))
    expand_weight_local = jnp.einsum(
        "scp,skp->ck", activation, hidden_grad, preferred_element_type=jnp.float32
    )
    expand_bias_local = jnp.sum(hidden_grad.astype(jnp.float32), axis=(0, 2))
    activation_grad = jnp.einsum(
        "ck,skp->scp", expand_back, hidden_grad, preferred_element_type=jnp.float32
    )
    activation_grad = activation_grad.reshape(inputs.shape)
    bias_total, gain_total = lax.psum(
        (
            jnp.sum(activation_grad, axis=(0, 2, 3)),
            jnp.sum(activation_grad * normalized, axis=(0, 2, 3)),
        ),
        ("dp", "fsdp"),
    )
    factor = (gain_full * inv_std)[None, :, None, None]
    correction = (
        weight_c
        / ocean_count
        * (bias_total[None, :, None, None] + normalized * gain_total[None, :, None, None])
    )
    conv_grad = (factor * (activation_grad - correction)).astype(jnp.bfloat16)
    conv_grad_wide = conv_grad.astype(jnp.float32)
    conv_taps = []
    for row_step in range(KS):
        for col_step in range(KS):
            window = widened[:, :, row_step : row_step + rows_dev, col_step : col_step + columns]
            conv_taps.append(jnp.sum(conv_grad_wide * window, axis=(0, 2, 3)))
    conv_weight_local = jnp.stack(conv_taps, axis=1)
    grad_padded = padded_2(conv_grad, (("dp", 2),), reach)
    grad_widened = wrap_columns(grad_padded.astype(jnp.float32), reach)
    input_grad = masked_grad
    for row_step in range(KS):
        for col_step in range(KS):
            tap_weight = conv_full[:, KS * row_step + col_step][None, :, None, None]
            row_start = KS - 1 - row_step
            col_start = KS - 1 - col_step
            input_grad = (
                input_grad
                + tap_weight
                * grad_widened[
                    :, :, row_start : row_start + rows_dev, col_start : col_start + columns
                ]
            )
    local_grads = (
        conv_weight_local,
        expand_weight_local,
        expand_bias_local,
        project_weight_local,
        project_bias_local,
    )
    summed = lax.psum(
        (local_grads[0], local_grads[1], local_grads[2], local_grads[3], local_grads[4]), "dp"
    )
    shares = (
        lax.psum_scatter(summed[0], "fsdp", scatter_dimension=0, tiled=True),
        lax.psum_scatter(summed[1], "fsdp", scatter_dimension=0, tiled=True),
        lax.psum_scatter(summed[2], "fsdp", scatter_dimension=0, tiled=True),
        lax.psum_scatter(summed[3], "fsdp", scatter_dimension=0, tiled=True),
        lax.psum_scatter(summed[4], "fsdp", scatter_dimension=0, tiled=True),
    )
    share_len = norm_gain.shape[0]
    share_start = lax.axis_index("fsdp") * share_len
    gain_share = lax.dynamic_slice_in_dim(gain_total, share_start, share_len)
    bias_share = lax.dynamic_slice_in_dim(bias_total, share_start, share_len)
    chan_std = jnp.sqrt(variance + EPS)
    return (
        block_out,
        input_grad,
        shares[0],
        gain_share,
        bias_share,
        shares[1],
        shares[2],
        shares[3],
        shares[4],
        chan_mean,
        chan_std,
    )


def solution(mesh):
    return jax.shard_map(
        per_device,
        mesh=mesh,
        in_specs=(
            P("fsdp", None, "dp", None),
            P("fsdp", None, "dp", None),
            P("dp", None),
            P(),
            P("fsdp", None),
            P("fsdp"),
            P("fsdp"),
            P("fsdp", None),
            P("fsdp"),
            P("fsdp", None),
            P("fsdp"),
        ),
        out_specs=(
            P("fsdp", None, "dp", None),
            P("fsdp", None, "dp", None),
            P("fsdp", None),
            P("fsdp"),
            P("fsdp"),
            P("fsdp", None),
            P("fsdp"),
            P("fsdp", None),
            P("fsdp"),
            P(),
            P(),
        ),
        check_vma=False,
    )
```

profile of v0, /device:TPU:0, one launch (start us, length us, event | category | flops | bytes accessed | tf_op | source)
XLA Modules:
  0.0 870.9 jit_solution(2975729160768379454)
XLA Ops:
  8.0 3.3 fusion.263
  11.3 3.4 collective-permute-start
  16.1 2.9 copy.35
  19.0 12.2 %all-gather = f32[4,200,49]{1,2,0:T(8,128)S(1)} all-gather(f32[1,200,49]{1,2,0:T(8,128)S(1)} %bitcast.107), channel_id=1, replica_groups=mesh['dp'=8,'fsdp'=4] {'fsdp'}, dimensions={0}, use_global_device_ids=true | all-gather | bytes 196000 | tf_op jit(solution)/shard_map/all_gather | solution.py:53
  33.9 15.1 %all-reduce.15 = (bf16[800]{0:T(1024)(128)(2,1)S(1)}, bf16[3200]{0:T(1024)(128)(2,1)S(1)}) all-reduce(bf16[800]{0:T(1024)(128)(2,1)S(1)} %dynamic-update-slice.3, bf16[3200]{0:T(1024)(128)(2,1)S(1)} %dynamic-update-slice.2), channel_id=1, replica_groups=mesh['dp'=8,'fsdp'=4] {'fsdp'}, use_global_device_ids=true, to_apply=%add.3 | all-reduce | flops 4000 | bytes 16000
  49.1 4.4 copy.41
  55.2 8.5 all-reduce.14
  65.8 1.8 copy.37
  67.6 2.5 copy.39
  70.1 3.4 maximum_convert_fusion
  73.9 51.2 %multiply_reduce_fusion.1 = (f32[800]{0:T(1024)S(1)}, f32[1,800,6,256]{1,3,2,0:T(8,128)}) fusion(f32[6,256]{1,0:T(8,128)S(1)} %get-tuple-element.155, f32[1,800,12,3]{1,3,2,0:T(4,128)S(1)} %get-tuple-element.161, f32[1,800,12,256]{1,3,2,0:T(8,128)S(1)} %maximum_convert_fusion, f32[800]{0:T(1024)S(1)} %get-tuple-element.85, f32[800]{0:T(1024)S(1)} %get-tuple-element.86, ...), kind=kLoop, calls=%fused_computation.433 | loop fusion | flops 173260000 | bytes 55006720 | tf_op jit(solution)/shard_map/reduce_sum | solution.py:69
  125.1 41.4 %all-reduce.10 = (f32[800]{0:T(1024)S(1)}, f32[]{:T(128)}) all-reduce(f32[800]{0:T(1024)S(1)} %get-tuple-element.156, f32[]{:T(128)} %get-tuple-element.154), channel_id=1, replica_groups=mesh['dp'=8,'fsdp'=4] {'dp','fsdp'}, use_global_device_ids=true, to_apply=%region_1.2 | all-reduce | flops 801 | bytes 6408 | tf_op jit(solution)/shard_map/psum | solution.py:68
  167.2 3.4 fusion.19
  170.6 40.8 %psum.72 = f32[800]{0:T(1024)S(1)} all-reduce(f32[800]{0:T(1024)S(1)} %fusion.19), channel_id=1, replica_groups=mesh['dp'=8,'fsdp'=4] {'dp','fsdp'}, use_global_device_ids=true, to_apply=%region_5.6 | all-reduce | flops 800 | bytes 6400 | tf_op jit(solution)/shard_map/psum | solution.py:73
  213.3 3.5 add_convert_fusion
  216.8 17.1 %fusion.266 = f32[1536,3200]{1,0:T(8,128)} fusion(bf16[800,1536]{0,1:T(8,128)(2,1)S(1)} %bitcast.103, bf16[800,3200]{1,0:T(8,128)(2,1)} %all-gather.4.cloned.1.call-done), kind=kOutput, calls=%fused_computation.510 | convolution fusion | flops 7864320000 | bytes 27238400 | tf_op jit(solution)/shard_map/ck,scp->skp/dot_general | solution.py:87
  234.0 15.7 %fusion.241 = f32[1,800,1536]{2,1,0:T(8,128)} fusion(bf16[800,3200]{1,0:T(8,128)(2,1)} %all-gather.6.cloned.1.call-done, f32[800]{0:T(1024)S(1)} %convert_element_type.73, f32[1536,3200]{1,0:T(8,128)} %fusion.266, f32[3200]{0:T(1024)S(1)} %convert_element_type.71), kind=kOutput, calls=%fused_computation.437 | convolution fusion | flops 7914700800 | bytes 29712000 | tf_op jit(solution)/shard_map/ck,skp->scp/dot_general | solution.py:93
  249.7 6.1 copy.40
  255.8 5.3 convert_reduce_fusion.1
  261.1 22.4 %convert_reduce_fusion = (f32[3200]{0:T(1024)S(1)}, bf16[1,3200,1536]{1,2,0:T(8,128)(2,1)S(1)}) fusion(f32[3200]{0:T(1024)S(1)} %convert_element_type.71, f32[1536,3200]{1,0:T(8,128)} %fusion.266, bf16[800,1536]{0,1:T(8,128)(2,1)S(1)} %bitcast.105, bf16[800,3200]{1,0:T(8,128)(2,1)} %all-gather.6.cloned.1.call-done), kind=kOutput, calls=%fused_computation.146 | convolution fusion | flops 7977366528 | bytes 37094400 | tf_op jit(solution)/shard_map/ck,scp->skp/dot_general | solution.py:104
  283.5 10.3 %fusion.265 = (f32[800]{0:T(1024)S(1)}, f32[1536,800]{0,1:T(8,128)}) fusion(bf16[800,3200]{1,0:T(8,128)(2,1)S(1)} %bitcast.109, bf16[1,3200,1536]{1,2,0:T(8,128)(2,1)S(1)} %get-tuple-element.173), kind=kOutput, calls=%fused_computation.509 | convolution fusion | flops 7865547776 | bytes 19868800 | tf_op jit(solution)/shard_map/ck,skp->scp/dot_general | solution.py:116
  293.8 6.0 copy.42
  299.7 5.0 multiply_reduce_fusion
  304.8 40.0 %all-reduce.9 = (f32[800]{0:T(1024)S(1)}, f32[800]{0:T(1024)S(1)}) all-reduce(f32[800]{0:T(1024)S(1)} %multiply_reduce_fusion, f32[800]{0:T(1024)S(1)} %get-tuple-element.170), channel_id=1, replica_groups=mesh['dp'=8,'fsdp'=4] {'dp','fsdp'}, use_global_device_ids=true, to_apply=%region_9.10 | all-reduce | flops 1600 | bytes 12800 | tf_op jit(solution)/shard_map/psum | solution.py:120
  344.8 6.9 fusion.65
  351.7 21.4 %fusion.63 = (f32[800]{0:T(1024)S(1)}, f32[800]{0:T(1024)S(1)}, f32[800]{0:T(1024)S(1)}, f32[800]{0:T(1024)S(1)}, f32[800]{0:T(1024)S(1)}, /*index=5*/f32[800]{0...) fusion(bf16[1,800,6,256]{1,3,2,0:T(8,128)(2,1)S(1)} %get-tuple-element.151, ...), kind=kLoop, calls=%fused_computation.200 | loop fusion | flops 34399200 | bytes 12432000 | tf_op jit(solution)/shard_map/reduce_sum | solution.py:139
  373.2 15.9 %fusion.67 = (f32[800]{0:T(1024)S(1)}, f32[800]{0:T(1024)S(1)}, f32[800]{0:T(1024)S(1)}, f32[800]{0:T(1024)S(1)}, f32[800]{0:T(1024)S(1)}, /*index=5*/f32[800]{0...) fusion(bf16[1,800,6,256]{1,3,2,0:T(8,128)(2,1)S(1)} %get-tuple-element.151, ...), kind=kLoop, calls=%fused_computation.204 | loop fusion | flops 34399200 | bytes 12432000 | tf_op jit(solution)/shard_map/reduce_sum | solution.py:139
  389.1 15.2 %fusion.68 = (f32[800]{0:T(1024)S(1)}, f32[800]{0:T(1024)S(1)}, f32[800]{0:T(1024)S(1)}, f32[800]{0:T(1024)S(1)}, f32[800]{0:T(1024)S(1)}, /*index=5*/f32[800]{0...) fusion(bf16[1,800,6,256]{1,3,2,0:T(8,128)(2,1)S(1)} %get-tuple-element.151, ...), kind=kLoop, calls=%fused_computation.205 | loop fusion | flops 34399200 | bytes 12432000 | tf_op jit(solution)/shard_map/reduce_sum | solution.py:139
  404.3 8.2 fusion.64
  412.5 27.2 %fusion.66 = (f32[800]{0:T(1024)S(1)}, f32[800]{0:T(1024)S(1)}, f32[800]{0:T(1024)S(1)}, f32[800]{0:T(1024)S(1)}, f32[800]{0:T(1024)S(1)}, /*index=5*/f32[800]{0...) fusion(bf16[1,800,6,256]{1,3,2,0:T(8,128)(2,1)S(1)} %get-tuple-, ...), kind=kLoop, calls=%fused_computation.203 | loop fusion | flops 38083200 | bytes 46766592 | tf_op jit(solution)/shard_map/reduce_sum | solution.py:139
  440.2 4.5 stack.199
  444.8 16.9 %fusion.15 = f32[800,3200]{1,0:T(8,128)} fusion(bf16[800,1536]{0,1:T(8,128)(2,1)} %bitcast.106, f32[1536,3200]{1,0:T(8,128)} %fusion.266, f32[3200]{0:T(1024)S(1)} %convert_element_type.71), kind=kOutput, calls=%fused_computation.151 | convolution fusion | flops 7913472000 | bytes 32371200 | tf_op jit(solution)/shard_map/scp,skp->ck/dot_general | solution.py:108
  461.8 14.9 %fusion.11 = f32[800,3200]{1,0:T(8,128)} fusion(bf16[800,1536]{0,1:T(8,128)(2,1)} %bitcast.104, bf16[1,3200,1536]{1,2,0:T(8,128)(2,1)} %copy-done.95), kind=kOutput, calls=%fused_computation.147 | convolution fusion | flops 7864320000 | bytes 22528000 | tf_op jit(solution)/shard_map/scp,skp->ck/dot_general | solution.py:112
  478.5 2.6 copy.43
  481.2 2.3 collective-permute-start.2
  483.5 2.4 copy.44
  489.8 2.6 copy.47
  492.3 16.9 %all-reduce.13 = (f32[3200]{0:T(1024)S(1)}, f32[800]{0:T(1024)S(1)}) all-reduce(f32[3200]{0:T(1024)S(1)} %get-tuple-element.172, f32[800]{0:T(1024)S(1)} %get-tuple-element.148), channel_id=4, replica_groups=mesh['dp'=8,'fsdp'=4] {'fsdp'}, use_global_device_ids=true, to_apply=%region_65.66.clone | all-reduce | flops 4000 | bytes 32000
  510.3 28.1 %all-reduce.11 = (f32[200,49]{0,1:T(8,128)}, f32[800]{0:T(1024)}, f32[200]{0:T(256)}) all-reduce(f32[200,49]{0,1:T(8,128)S(1)} %constant_dynamic-slice_fusion, f32[800]{0:T(1024)S(1)} %dynamic-slice.9, f32[200]{0:T(256)S(1)} %dynamic-slice.13), channel_id=1, replica_groups=mesh['dp'=8,'fsdp'=4] {'dp'}, use_global_device_ids=true, to_apply=%region_59.60 | all-reduce | flops 10800 | bytes 86400 | tf_op jit(solution)/shard_map/psum | solution.py:163
  538.4 1.8 copy.45
  540.2 2.5 copy.46
  542.7 3.4 maximum_convert_fusion.1
  546.1 4.2 copy-done.1
  550.7 62.5 %reduce-scatter.10.cloned.1.call-done = f32[200,3200]{1,0:T(8,128)} async-done(((f32[800,3200]{1,0:T(8,128)}), f32[200,3200]{1,0:T(8,128)}) %reduce-scatter.10.cloned.1.call-update) | async-done | bytes 2560016
  613.1 124.7 %reduce-scatter.8.cloned.1.call-done = f32[200,3200]{1,0:T(8,128)} async-done(((f32[800,3200]{1,0:T(8,128)}), f32[200,3200]{1,0:T(8,128)}) %reduce-scatter.8.cloned.1.call-update) | async-done | bytes 2560016
  738.3 114.5 %fusion.72 = f32[1,800,6,256]{1,3,2,0:T(8,128)} fusion(f32[1,800,12,3]{1,3,2,0:T(4,128)S(1)} %get-tuple-element.159, f32[1,800,12,256]{1,3,2,0:T(8,128)} %copy-done.1, f32[1,800,12,3]{1,3,2,0:T(4,128)S(1)} %get-tuple-element.158, bf16[1,800,6,256]{1,3,2,0:T(8,128)(2,1)S(1)} %copy-done.4, f32[6,256]{1,0:T(8,128)S(1)} %get-tuple-element.155, ...), kind=kLoop, calls=%fused_computation.209 | loop fusion | flops 174489600 | bytes 57321216 | tf_op jit(solution)/shard_map/add | solution.py:150
  852.8 5.9 copy.48
  858.7 3.5 copy.58
  (304 shorter events, 16.6 us)
Async XLA Ops:
  7.2 209.6 %all-gather.4.cloned.1.call-start = ((), (), s32[]{:S(2)}) async-start(), calls=%async_computation.2 | async-start | bytes 6400000 | tf_op jit(solution)/shard_map/all_gather | solution.py:82
  8.0 226.0 %all-gather.6.cloned.1.call-start = ((), (), s32[]{:S(2)}) async-start(), calls=%async_computation.3 | async-start | bytes 6400000 | tf_op jit(solution)/shard_map/all_gather | solution.py:84
  11.3 54.6 %collective-permute-start = (bf16[1,800,3,256]{3,1,2,0:T(8,128)(2,1)}, bf16[1,800,3,256]{3,1,2,0:T(8,128)(2,1)}, u32[]{:S(2)}, u32[]{:S(2)}) collective-permute-start(bf16[1,800,3,256]{3,1,2,0:T(8,128)(2,1)} %get-tuple-element.164), channel_id=1, source_target_pairs={{0,4},{4,8},{8,12},{12,16},{16,20},{20,24},{24,28},{1,5},{5,9},{9,... | collective-permute-start | bytes 3686408 | tf_op jit(solution)/shard_map/ppermute | solution.py:20
  14.7 52.9 %collective-permute-start.1 = (bf16[1,800,3,256]{3,1,2,0:T(8,128)(2,1)}, bf16[1,800,3,256]{3,1,2,0:T(8,128)(2,1)}, u32[]{:S(2)}, u32[]{:S(2)}) collective-permute-start(bf16[1,800,3,256]{3,1,2,0:T(8,128)(2,1)} %get-tuple-element.165), channel_id=1, source_target_pairs={{4,0},{8,4},{12,8},{16,12},{20,16},{24,20},{28,24},{5,1},{9,5},{13... | collective-permute-start | bytes 3686408 | tf_op jit(solution)/shard_map/ppermute | solution.py:21
  16.0 493.4 %all-reduce.19.cloned.1.call-start = ((), (), s32[]{:S(2)}) async-start(), calls=%async_computation.4 | async-start | bytes 401408
  444.8 168.3 %reduce-scatter.10.cloned.1.call-start = ((), (), s32[]{:S(2)}) async-start(), calls=%async_computation.6 | async-start | bytes 12800000
  461.7 276.2 %reduce-scatter.8.cloned.1.call-start = ((), (), s32[]{:S(2)}) async-start(), calls=%async_computation.5 | async-start | bytes 12800000
  476.7 382.0 %all-reduce.21.cloned.1.call-start = ((), (), s32[]{:S(2)}) async-start(), calls=%async_computation.7 | async-start | bytes 10240000 | tf_op jit(solution)/shard_map/psum | solution.py:163
  481.2 57.2 %collective-permute-start.2 = (bf16[1,800,3,256]{3,1,2,0:T(8,128)(2,1)}, bf16[1,800,3,256]{3,1,2,0:T(8,128)(2,1)}, u32[]{:S(2)}, u32[]{:S(2)}) collective-permute-start(bf16[1,800,3,256]{3,1,2,0:T(8,128)(2,1)} %copy.43), channel_id=1, source_target_pairs={{0,4},{4,8},{8,12},{12,16},{16,20},{20,24},{24,28},{1,5},{5,9},{9,... | collective-permute-start | bytes 3686408 | tf_op jit(solution)/shard_map/ppermute | solution.py:20
  485.9 54.3 %collective-permute-start.3 = (bf16[1,800,3,256]{3,1,2,0:T(8,128)(2,1)}, bf16[1,800,3,256]{3,1,2,0:T(8,128)(2,1)}, u32[]{:S(2)}, u32[]{:S(2)}) collective-permute-start(bf16[1,800,3,256]{3,1,2,0:T(8,128)(2,1)} %copy.44), channel_id=1, source_target_pairs={{4,0},{8,4},{12,8},{16,12},{20,16},{24,20},{28,24},{5,1},{9,5},{13... | collective-permute-start | bytes 3686408 | tf_op jit(solution)/shard_map/ppermute | solution.py:21
  550.2 187.7 %copy-start.13 = (f32[800]{0:T(1024)S(1)}, f32[800]{0:T(1024)}, u32[]{:S(2)}) copy-start(f32[800]{0:T(1024)} %copy-done.12) | copy-start | bytes 9604
  550.2 187.7 %copy-start.15 = (f32[800]{0:T(1024)S(1)}, f32[800]{0:T(1024)}, u32[]{:S(2)}) copy-start(f32[800]{0:T(1024)} %copy-done.14) | copy-start | bytes 9604
  550.2 187.7 %copy-start.17 = (f32[800]{0:T(1024)S(1)}, f32[800]{0:T(1024)}, u32[]{:S(2)}) copy-start(f32[800]{0:T(1024)} %copy-done.16) | copy-start | bytes 9604
  550.2 187.7 %copy-start.19 = (f32[800]{0:T(1024)S(1)}, f32[800]{0:T(1024)}, u32[]{:S(2)}) copy-start(f32[800]{0:T(1024)} %copy-done.18) | copy-start | bytes 9604
  550.2 187.7 %copy-start.21 = (f32[800]{0:T(1024)S(1)}, f32[800]{0:T(1024)}, u32[]{:S(2)}) copy-start(f32[800]{0:T(1024)} %copy-done.20) | copy-start | bytes 9604
  550.3 187.7 %copy-start.23 = (f32[800]{0:T(1024)S(1)}, f32[800]{0:T(1024)}, u32[]{:S(2)}) copy-start(f32[800]{0:T(1024)} %copy-done.22) | copy-start | bytes 9604
  550.3 187.7 %copy-start.25 = (f32[800]{0:T(1024)S(1)}, f32[800]{0:T(1024)}, u32[]{:S(2)}) copy-start(f32[800]{0:T(1024)} %copy-done.24) | copy-start | bytes 9604
  550.3 187.7 %copy-start.27 = (f32[800]{0:T(1024)S(1)}, f32[800]{0:T(1024)}, u32[]{:S(2)}) copy-start(f32[800]{0:T(1024)} %copy-done.26) | copy-start | bytes 9604
  550.3 187.7 %copy-start.29 = (f32[800]{0:T(1024)S(1)}, f32[800]{0:T(1024)}, u32[]{:S(2)}) copy-start(f32[800]{0:T(1024)} %copy-done.28) | copy-start | bytes 9604
  550.3 187.7 %copy-start.31 = (f32[800]{0:T(1024)S(1)}, f32[800]{0:T(1024)}, u32[]{:S(2)}) copy-start(f32[800]{0:T(1024)} %copy-done.30) | copy-start | bytes 9604
  550.3 187.7 %copy-start.33 = (f32[800]{0:T(1024)S(1)}, f32[800]{0:T(1024)}, u32[]{:S(2)}) copy-start(f32[800]{0:T(1024)} %copy-done.32) | copy-start | bytes 9604
  550.3 187.7 %copy-start.35 = (f32[800]{0:T(1024)S(1)}, f32[800]{0:T(1024)}, u32[]{:S(2)}) copy-start(f32[800]{0:T(1024)} %copy-done.34) | copy-start | bytes 9604
  550.3 187.7 %copy-start.37 = (f32[800]{0:T(1024)S(1)}, f32[800]{0:T(1024)}, u32[]{:S(2)}) copy-start(f32[800]{0:T(1024)} %copy-done.36) | copy-start | bytes 9604
  550.3 187.7 %copy-start.39 = (f32[800]{0:T(1024)S(1)}, f32[800]{0:T(1024)}, u32[]{:S(2)}) copy-start(f32[800]{0:T(1024)} %copy-done.38) | copy-start | bytes 9604
  550.3 187.7 %copy-start.41 = (f32[800]{0:T(1024)S(1)}, f32[800]{0:T(1024)}, u32[]{:S(2)}) copy-start(f32[800]{0:T(1024)} %copy-done.40) | copy-start | bytes 9604
  550.4 187.7 %copy-start.43 = (f32[800]{0:T(1024)S(1)}, f32[800]{0:T(1024)}, u32[]{:S(2)}) copy-start(f32[800]{0:T(1024)} %copy-done.42) | copy-start | bytes 9604
  550.4 187.7 %copy-start.45 = (f32[800]{0:T(1024)S(1)}, f32[800]{0:T(1024)}, u32[]{:S(2)}) copy-start(f32[800]{0:T(1024)} %copy-done.44) | copy-start | bytes 9604
  550.4 187.7 %copy-start.47 = (f32[800]{0:T(1024)S(1)}, f32[800]{0:T(1024)}, u32[]{:S(2)}) copy-start(f32[800]{0:T(1024)} %copy-done.46) | copy-start | bytes 9604
  550.4 187.7 %copy-start.49 = (f32[800]{0:T(1024)S(1)}, f32[800]{0:T(1024)}, u32[]{:S(2)}) copy-start(f32[800]{0:T(1024)} %copy-done.48) | copy-start | bytes 9604
  550.4 187.7 %copy-start.51 = (f32[800]{0:T(1024)S(1)}, f32[800]{0:T(1024)}, u32[]{:S(2)}) copy-start(f32[800]{0:T(1024)} %copy-done.50) | copy-start | bytes 9604
  550.4 187.7 %copy-start.53 = (f32[800]{0:T(1024)S(1)}, f32[800]{0:T(1024)}, u32[]{:S(2)}) copy-start(f32[800]{0:T(1024)} %copy-done.52) | copy-start | bytes 9604
  550.4 187.7 %copy-start.55 = (f32[800]{0:T(1024)S(1)}, f32[800]{0:T(1024)}, u32[]{:S(2)}) copy-start(f32[800]{0:T(1024)} %copy-done.54) | copy-start | bytes 9604
  550.4 187.7 %copy-start.57 = (f32[800]{0:T(1024)S(1)}, f32[800]{0:T(1024)}, u32[]{:S(2)}) copy-start(f32[800]{0:T(1024)} %copy-done.56) | copy-start | bytes 9604
  550.4 187.7 %copy-start.59 = (f32[800]{0:T(1024)S(1)}, f32[800]{0:T(1024)}, u32[]{:S(2)}) copy-start(f32[800]{0:T(1024)} %copy-done.58) | copy-start | bytes 9604
  550.4 187.7 %copy-start.61 = (f32[800]{0:T(1024)S(1)}, f32[800]{0:T(1024)}, u32[]{:S(2)}) copy-start(f32[800]{0:T(1024)} %copy-done.60) | copy-start | bytes 9604
  550.5 187.7 %copy-start.63 = (f32[800]{0:T(1024)S(1)}, f32[800]{0:T(1024)}, u32[]{:S(2)}) copy-start(f32[800]{0:T(1024)} %copy-done.62) | copy-start | bytes 9604
  550.5 187.7 %copy-start.65 = (f32[800]{0:T(1024)S(1)}, f32[800]{0:T(1024)}, u32[]{:S(2)}) copy-start(f32[800]{0:T(1024)} %copy-done.64) | copy-start | bytes 9604
  550.5 187.7 %copy-start.67 = (f32[800]{0:T(1024)S(1)}, f32[800]{0:T(1024)}, u32[]{:S(2)}) copy-start(f32[800]{0:T(1024)} %copy-done.66) | copy-start | bytes 9604
  550.5 187.7 %copy-start.69 = (f32[800]{0:T(1024)S(1)}, f32[800]{0:T(1024)}, u32[]{:S(2)}) copy-start(f32[800]{0:T(1024)} %copy-done.68) | copy-start | bytes 9604
  550.5 187.7 %copy-start.71 = (f32[800]{0:T(1024)S(1)}, f32[800]{0:T(1024)}, u32[]{:S(2)}) copy-start(f32[800]{0:T(1024)} %copy-done.70) | copy-start | bytes 9604
  550.5 187.7 %copy-start.73 = (f32[800]{0:T(1024)S(1)}, f32[800]{0:T(1024)}, u32[]{:S(2)}) copy-start(f32[800]{0:T(1024)} %copy-done.72) | copy-start | bytes 9604
  550.5 187.7 %copy-start.75 = (f32[800]{0:T(1024)S(1)}, f32[800]{0:T(1024)}, u32[]{:S(2)}) copy-start(f32[800]{0:T(1024)} %copy-done.74) | copy-start | bytes 9604
  550.5 187.7 %copy-start.77 = (f32[800]{0:T(1024)S(1)}, f32[800]{0:T(1024)}, u32[]{:S(2)}) copy-start(f32[800]{0:T(1024)} %copy-done.76) | copy-start | bytes 9604
  550.5 187.7 %copy-start.79 = (f32[800]{0:T(1024)S(1)}, f32[800]{0:T(1024)}, u32[]{:S(2)}) copy-start(f32[800]{0:T(1024)} %copy-done.78) | copy-start | bytes 9604
  550.5 187.7 %copy-start.81 = (f32[800]{0:T(1024)S(1)}, f32[800]{0:T(1024)}, u32[]{:S(2)}) copy-start(f32[800]{0:T(1024)} %copy-done.80) | copy-start | bytes 9604
  550.6 187.7 %copy-start.83 = (f32[800]{0:T(1024)S(1)}, f32[800]{0:T(1024)}, u32[]{:S(2)}) copy-start(f32[800]{0:T(1024)} %copy-done.82) | copy-start | bytes 9604
  550.6 187.7 %copy-start.85 = (f32[800]{0:T(1024)S(1)}, f32[800]{0:T(1024)}, u32[]{:S(2)}) copy-start(f32[800]{0:T(1024)} %copy-done.84) | copy-start | bytes 9604
  550.6 187.7 %copy-start.87 = (f32[800]{0:T(1024)S(1)}, f32[800]{0:T(1024)}, u32[]{:S(2)}) copy-start(f32[800]{0:T(1024)} %copy-done.86) | copy-start | bytes 9604
  (63 other events, 1340.0 us)
Sparse Core Ops, SparseCore 0:
  9.9 65.5 all-gather.3
  77.3 60.9 all-gather.5
  444.9 42.1 all-reduce.18
  490.3 122.8 reduce-scatter.9
  616.3 121.4 reduce-scatter.7
  740.4 115.0 all-reduce.20
where the time goes:
time: 879 us; the launch traced here: 871 us
  other arithmetic  288 us (33%)
  blocking collectives  203 us (23%)
  waiting for transfers between devices  188 us (21%)
  matrix products  97.2 us (11%)
  local copies, waits for them, and re-layouts  66.7 us (8%)
  between operations  19.9 us (2%)
    unnamed x9, waiting for transfers between devices  188 us
    add x1, other arithmetic, per_device(): input_grad + tap_weight * grad_widened[:, :, row_start:row_start + rows_d...  114 us
    reduce_sum x6, other arithmetic, per_device(): conv_taps.append(jnp.sum(conv_grad_wide * window, axis=(0, 2, 3)))  94.8 us
    reduce_sum x1, other arithmetic, per_device(): jnp.sum(weight_c * conv_out, axis=(0, 2, 3))  51.2 us
    psum x1, blocking collectives, per_device(): lax.psum((jnp.sum(weight), jnp.sum(weight_c * conv_out, axis=(0, 2, 3))),...  41.4 us
    psum x1, blocking collectives, per_device(): lax.psum(jnp.sum(weight_c * centered * centered, axis=(0, 2, 3)), ('dp',...  40.8 us
    unnamed x3, blocking collectives  40.5 us
    psum x1, blocking collectives, per_device(): lax.psum((jnp.sum(activation_grad, axis=(0, 2, 3)), jnp.sum(activation_gr...  40 us
  transfers between devices with their start and end apart: 10, of which 2 were waited for; matrix products, arithmetic and copies ran while one was open for 31% of the time, Pallas kernels for 0%

commit v1 on v0

v1 whole, which is shorter than its diff:
```python
import functools

import jax
import jax.numpy as jnp
from jax import lax
from jax.experimental import pallas as pl
from jax.experimental.pallas import tpu as pltpu
from jax.sharding import PartitionSpec as P

KS = 7
REACH = KS // 2
TAPS = KS * KS
ROLLOUT = 8
EPS = 1e-05
F32, BF16 = jnp.float32, jnp.bfloat16
GRP = 16
TILE = 256
MIB = 2**20
GELU_A = 0.7978845608028654
GELU_B = 0.044715
NT = (((1,), (1,)), ((), ()))


def params(limit):
    return pltpu.CompilerParams(vmem_limit_bytes=limit * MIB)


def cost(flops, nbytes, trans=0):
    return pl.CostEstimate(flops=int(flops), bytes_accessed=int(nbytes), transcendentals=int(trans))


def whole(shape):
    zeros = (0,) * len(shape)
    return pl.BlockSpec(shape, lambda *g: zeros, pipeline_mode=pl.Buffered(1))


def roll_lanes(v, shift):
    shift %= v.shape[-1]
    return v if shift == 0 else pltpu.roll(v, shift, v.ndim - 1)


def columns_of(rows_ref):
    pieces = []
    for k in range(0, rows_ref.shape[1], 128):
        block = jnp.concatenate([rows_ref[:, k : k + 128], jnp.zeros((120, 128), F32)], axis=0)
        pieces.append(block.T)
    return jnp.concatenate(pieces, axis=0)


def rows_of(cols_ref, out_ref):
    for k in range(0, cols_ref.shape[0], 128):
        out_ref[:, k : k + 128] = cols_ref[k : k + 128, :].T[0:8]


def spread_taps(taps):
    channels = taps.shape[0]
    by_col = taps.reshape(channels, KS, KS).transpose(2, 0, 1)
    own = jnp.arange(channels)[:, None] % GRP == jnp.arange(GRP)[None, :]
    spread = jnp.where(own[None, :, None, :], by_col[..., None], 0.0)
    spread = spread.reshape(KS, channels, KS * GRP)
    spread = jnp.pad(spread, ((0, 0), (0, 0), (0, 128 - KS * GRP)))
    high = lax.reduce_precision(spread, 8, 7)
    return jnp.stack([high.astype(BF16), (spread - high).astype(BF16)])


def conv_rows(field_ref, taps_ref, s, rows, flip):
    x = field_ref[:, s, :].reshape((rows + 2 * REACH) * GRP, field_ref.shape[-1])
    parts = [taps_ref[h, :, s, :].reshape(KS * GRP, 128)[:, : KS * GRP] for h in range(2)]
    taps = jnp.concatenate(parts, axis=1)
    out = []
    for r in range(rows):
        src = rows - 1 - r if flip else r
        window = x[src * GRP : (src + KS) * GRP]
        sums = jnp.dot(taps, jnp.concatenate([window, window], axis=0), preferred_element_type=F32)
        acc = None
        for j in range(KS):
            moved = roll_lanes(sums[j * GRP : (j + 1) * GRP], j - REACH if flip else REACH - j)
            acc = moved if acc is None else acc + moved
        out.append(acc)
    return out


def conv_kernel(n_ref, x_ref, up_ref, dn_ref, e_ref, m_ref, out_ref, st_ref, field_ref, cols_ref):
    rows, block = x_ref.shape[0], x_ref.shape[1]
    step = pl.program_id(0)
    count = n_ref[0]
    inv_n = n_ref[1]
    field_ref[0:REACH] = up_ref[...]
    field_ref[REACH : REACH + rows] = x_ref[...]
    field_ref[REACH + rows :] = dn_ref[...]

    @pl.when(step == 0)
    def _():
        cols_ref[...] = jnp.full(cols_ref.shape, count, F32)

    lane = lax.broadcasted_iota(jnp.int32, (GRP, 128), 1)
    for g in range(block // GRP):
        s = pl.ds(g * GRP, GRP)
        acc = conv_rows(field_ref, e_ref, s, rows, False)
        total = None
        for r in range(rows):
            out_ref[r, s, :] = acc[r]
            v = acc[r] * m_ref[r]
            total = v if total is None else total + v
        mean = jnp.sum(total, axis=-1, keepdims=True) * inv_n
        total = None
        for r in range(rows):
            d = acc[r] - mean
            v = d * d * m_ref[r]
            total = v if total is None else total + v
        dev = jnp.sum(total, axis=-1, keepdims=True)
        at = pl.multiple_of(step * block + g * GRP, GRP)
        cols_ref[pl.ds(at, GRP), :] = jnp.where(lane == 0, mean, dev)

    @pl.when(step == pl.num_programs(0) - 1)
    def _():
        rows_of(cols_ref, st_ref)


def conv_forward(x, up, dn, spread, m16, counts, padded, block):
    rows, channels, width = x.shape
    return pl.pallas_call(
        conv_kernel,
        grid=(channels // block,),
        in_specs=[
            pl.BlockSpec(memory_space=pltpu.SMEM),
            pl.BlockSpec((rows, block, width), lambda g: (0, g, 0)),
            pl.BlockSpec((REACH, block, width), lambda g: (0, g, 0)),
            pl.BlockSpec((REACH, block, width), lambda g: (0, g, 0)),
            pl.BlockSpec((2, KS, block, 128), lambda g: (0, 0, g, 0)),
            whole((rows, GRP, width)),
        ],
        out_specs=[
            pl.BlockSpec((rows, block, width), lambda g: (0, g, 0)),
            pl.BlockSpec((8, padded), lambda g: (0, 0)),
        ],
        out_shape=[
            jax.ShapeDtypeStruct((rows, channels, width), F32),
            jax.ShapeDtypeStruct((8, padded), F32),
        ],
        scratch_shapes=[
            pltpu.VMEM((rows + 2 * REACH, block, width), BF16),
            pltpu.VMEM((padded, 128), F32),
        ],
        compiler_params=params(24),
        cost_estimate=cost(20e9, 12e6),
        name="conv_forward",
    )(counts, x, up, dn, spread, m16)


def input_grad_kernel(g_ref, up_ref, dn_ref, e_ref, og_ref, m_ref, out_ref, field_ref):
    rows, block = g_ref.shape[0], g_ref.shape[1]
    last = rows + 2 * REACH - 1
    for q in range(REACH):
        field_ref[last - q] = up_ref[q]
        field_ref[REACH - 1 - q] = dn_ref[q]
    for q in range(rows):
        field_ref[last - REACH - q] = g_ref[q]
    for g in range(block // GRP):
        s = pl.ds(g * GRP, GRP)
        acc = conv_rows(field_ref, e_ref, s, rows, True)
        for r in range(rows):
            out_ref[r, s, :] = og_ref[r, s, :].astype(F32) * m_ref[r] + acc[r]


def input_gradient(grad, up, dn, spread, og, m16, block):
    rows, channels, width = grad.shape
    return pl.pallas_call(
        input_grad_kernel,
        grid=(channels // block,),
        in_specs=[
            pl.BlockSpec((rows, block, width), lambda g: (0, g, 0)),
            pl.BlockSpec((REACH, block, width), lambda g: (0, g, 0)),
            pl.BlockSpec((REACH, block, width), lambda g: (0, g, 0)),
            pl.BlockSpec((2, KS, block, 128), lambda g: (0, 0, g, 0)),
            pl.BlockSpec((rows, block, width), lambda g: (0, g, 0)),
            whole((rows, GRP, width)),
        ],
        out_specs=pl.BlockSpec((rows, block, width), lambda g: (0, g, 0)),
        out_shape=jax.ShapeDtypeStruct((rows, channels, width), F32),
        scratch_shapes=[pltpu.VMEM((rows + 2 * REACH, block, width), BF16)],
        compiler_params=params(24),
        cost_estimate=cost(18e9, 15e6),
        name="input_gradient",
    )(grad, up, dn, spread, og, m16)


def tap_grad_kernel(x_ref, up_ref, dn_ref, g_ref, out_ref, field_ref):
    rows, block, width = x_ref.shape
    field_ref[0:REACH] = up_ref[...]
    field_ref[REACH : REACH + rows] = x_ref[...]
    field_ref[REACH + rows :] = dn_ref[...]
    lane = lax.broadcasted_iota(jnp.int32, (GRP, 128), 1)
    own = lax.broadcasted_iota(jnp.int32, (GRP, 128), 0) == lane % GRP
    for g in range(block // GRP):
        s = pl.ds(g * GRP, GRP)
        x = field_ref[:, s, :].reshape((rows + 2 * REACH) * GRP, width)
        fields = jnp.concatenate([x[r * GRP : (r + KS) * GRP] for r in range(rows)], axis=1)
        grads = []
        for j in range(KS):
            moved = [roll_lanes(g_ref[r, s, :], j - REACH) for r in range(rows)]
            grads.append(jnp.concatenate(moved, axis=1))
        grads = jnp.concatenate(grads, axis=0)
        sums = lax.dot_general(grads, fields, NT, preferred_element_type=F32)
        sums = jnp.concatenate([sums, jnp.zeros((KS * GRP, 128 - KS * GRP), F32)], axis=1)
        out = None
        for j in range(KS):
            acc = jnp.where(own, sums[j * GRP : (j + 1) * GRP], 0.0)
            for k in (8, 4, 2, 1):
                acc = acc + pltpu.roll(acc, 128 - k, 1)
            acc = roll_lanes(acc, j)
            out = acc if out is None else jnp.where(lane % GRP == j, acc, out)
        out_ref[s, :] = out


def tap_gradient(x, up, dn, grad, block):
    rows, channels, width = x.shape
    out = pl.pallas_call(
        tap_grad_kernel,
        grid=(channels // block,),
        in_specs=[
            pl.BlockSpec((rows, block, width), lambda g: (0, g, 0)),
            pl.BlockSpec((REACH, block, width), lambda g: (0, g, 0)),
            pl.BlockSpec((REACH, block, width), lambda g: (0, g, 0)),
            pl.BlockSpec((rows, block, width), lambda g: (0, g, 0)),
        ],
        out_specs=pl.BlockSpec((block, 128), lambda g: (g, 0)),
        out_shape=jax.ShapeDtypeStruct((channels, 128), F32),
        scratch_shapes=[pltpu.VMEM((rows + 2 * REACH, block, width), BF16)],
        compiler_params=params(24),
        cost_estimate=cost(18e9, 8e6),
        name="tap_gradient",
    )(x, up, dn, grad)
    return out.reshape(channels, 8, GRP)[:, :KS, :KS].reshape(channels, TAPS)


def mask_grad_kernel(og_ref, m_ref, by_chan_ref, by_pixel_ref, sum_ref, cols_ref):
    row = pl.program_id(0)
    channels = og_ref.shape[1]
    v = og_ref[0].astype(F32) * m_ref[0, 0:1]
    by_chan_ref[...] = v.astype(BF16)
    by_pixel_ref[...] = v.T.astype(BF16)
    part = v[:, 0:128]
    for k in range(128, v.shape[1], 128):
        part = part + v[:, k : k + 128]

    @pl.when(row == 0)
    def _():
        cols_ref[...] = jnp.zeros(cols_ref.shape, F32)

    cols_ref[0:channels, :] += part

    @pl.when(row == pl.num_programs(0) - 1)
    def _():
        cols_ref[...] = jnp.broadcast_to(
            jnp.sum(cols_ref[...], axis=1, keepdims=True), cols_ref.shape
        )
        rows_of(cols_ref, sum_ref)


def mask_gradient(og, m16, padded):
    rows, channels, width = og.shape
    pixels = rows * width
    return pl.pallas_call(
        mask_grad_kernel,
        grid=(rows,),
        in_specs=[
            pl.BlockSpec((1, channels, width), lambda r: (r, 0, 0)),
            pl.BlockSpec((1, GRP, width), lambda r: (r, 0, 0)),
        ],
        out_specs=[
            pl.BlockSpec((channels, width), lambda r: (0, r)),
            pl.BlockSpec((width, channels), lambda r: (r, 0)),
            pl.BlockSpec((8, padded), lambda r: (0, 0)),
        ],
        out_shape=[
            jax.ShapeDtypeStruct((channels, pixels), BF16),
            jax.ShapeDtypeStruct((pixels, channels), BF16),
            jax.ShapeDtypeStruct((8, padded), F32),
        ],
        scratch_shapes=[pltpu.VMEM((padded, 128), F32)],
        compiler_params=params(24),
        cost_estimate=cost(1e9, 8e6),
        name="mask_gradient",
    )(og, m16)


def activate_kernel(conv_ref, par_ref, by_chan_ref, by_pixel_ref, cols_ref):
    channels = conv_ref.shape[1]

    @pl.when(pl.program_id(0) == 0)
    def _():
        cols_ref[...] = columns_of(par_ref)

    c = cols_ref[0:channels, :]
    v = (conv_ref[0] - c[:, 0:1]) * c[:, 1:2] + c[:, 2:3]
    by_chan_ref[...] = v.astype(BF16)
    by_pixel_ref[...] = v.T.astype(BF16)


def activate(conv, par):
    rows, channels, width = conv.shape
    pixels = rows * width
    padded = par.shape[1]
    return pl.pallas_call(
        activate_kernel,
        grid=(rows,),
        in_specs=[pl.BlockSpec((1, channels, width), lambda r: (r, 0, 0)), whole((8, padded))],
        out_specs=[
            pl.BlockSpec((channels, width), lambda r: (0, r)),
            pl.BlockSpec((width, channels), lambda r: (r, 0)),
        ],
        out_shape=[
            jax.ShapeDtypeStruct((channels, pixels), BF16),
            jax.ShapeDtypeStruct((pixels, channels), BF16),
        ],
        scratch_shapes=[pltpu.VMEM((padded, 128), F32)],
        compiler_params=params(24),
        cost_estimate=cost(1e9, 10e6),
        name="activate",
    )(conv, par)


def gelu_parts(v):
    v2 = v * v
    t = jnp.tanh(v * (GELU_A + (GELU_A * GELU_B) * v2))
    s = 0.5 * t + 0.5
    h = v * s
    return h, s + h * (1.0 - s) * (2 * GELU_A + (6 * GELU_A * GELU_B) * v2)


def hidden_kernel(
    act_p, act_c, bg_p, bg_c, we_ref, wp_ref, eb_ref, h_ref, g_ref, dwp_ref, dwe_ref, ebg_ref, *, step
):
    we, wp, bias = we_ref[...], wp_ref[...], eb_ref[...]
    total = None
    for p in range(0, act_p.shape[0], step):
        pre = jnp.dot(act_p[p : p + step, :], we, preferred_element_type=F32) + bias
        pull = jnp.dot(bg_p[p : p + step, :], wp, preferred_element_type=F32)
        h, slope = gelu_parts(pre)
        grad = (pull * slope).astype(BF16)
        h_ref[p : p + step, :] = h.astype(BF16)
        g_ref[p : p + step, :] = grad
        part = jnp.sum(grad.astype(F32), axis=0, keepdims=True)
        total = part if total is None else total + part
    ebg_ref[...] = total
    dwp_ref[...] = jnp.dot(bg_c[...], h_ref[...], preferred_element_type=F32).astype(dwp_ref.dtype)
    dwe_ref[...] = jnp.dot(act_c[...], g_ref[...], preferred_element_type=F32).astype(dwe_ref.dtype)


def hidden_layer(act_p, act_c, bg_p, bg_c, we, wp, eb, first, units, dtype):
    pixels, channels = act_p.shape
    steps = pl.cdiv(units, TILE)
    off = first // TILE
    weight = pl.BlockSpec((channels, TILE), lambda g: (0, g + off))
    return pl.pallas_call(
        functools.partial(hidden_kernel, step=pixels // 3),
        grid=(steps,),
        in_specs=[
            whole((pixels, channels)),
            whole((channels, pixels)),
            whole((pixels, channels)),
            whole((channels, pixels)),
            weight,
            weight,
            pl.BlockSpec((1, TILE), lambda g: (0, g + off)),
        ],
        out_specs=[
            pl.BlockSpec((pixels, TILE), lambda g: (0, g)),
            pl.BlockSpec((pixels, TILE), lambda g: (0, g)),
            pl.BlockSpec((channels, TILE), lambda g: (0, g)),
            pl.BlockSpec((channels, TILE), lambda g: (0, g)),
            pl.BlockSpec((1, TILE), lambda g: (0, g)),
        ],
        out_shape=[
            jax.ShapeDtypeStruct((pixels, units), BF16),
            jax.ShapeDtypeStruct((pixels, units), BF16),
            jax.ShapeDtypeStruct((channels, units), dtype),
            jax.ShapeDtypeStruct((channels, units), dtype),
            jax.ShapeDtypeStruct((1, units), F32),
        ],
        compiler_params=params(40),
        cost_estimate=cost(8 * pixels * channels * units, 20e6, pixels * units),
        name="hidden_layer",
    )(act_p, act_c, bg_p, bg_c, we, wp, eb)


def contract(weights, hiddens):
    total = None
    for (w_ref, first, units), h_ref in zip(weights, hiddens, strict=True):
        part = lax.dot_general(
            w_ref[:, first : first + units], h_ref[...], NT, preferred_element_type=F32
        )
        total = part if total is None else total + part
    return total


def act_grad_kernel(*refs, cuts):
    n = len(cuts)
    w_refs, h_refs = refs[0:2], refs[2 : 2 + n]
    conv_ref, par_ref, out_ref, sum_ref, cols_ref, acc_ref = refs[2 + n :]
    channels = conv_ref.shape[1]
    row = pl.program_id(0)

    @pl.when(row == 0)
    def _():
        cols_ref[...] = columns_of(par_ref)
        acc_ref[...] = jnp.zeros(acc_ref.shape, F32)

    grad = contract([(w_refs[w], first, units) for w, first, units in cuts], h_refs)
    out_ref[0] = grad
    c = cols_ref[0:channels, :]
    scaled = grad * ((conv_ref[0] - c[:, 0:1]) * c[:, 3:4])
    plain, weighted = grad[:, 0:128], scaled[:, 0:128]
    for k in range(128, grad.shape[1], 128):
        plain = plain + grad[:, k : k + 128]
        weighted = weighted + scaled[:, k : k + 128]
    acc_ref[0, 0:channels, :] += plain
    acc_ref[1, 0:channels, :] += weighted

    @pl.when(row == pl.num_programs(0) - 1)
    def _():
        lane = lax.broadcasted_iota(jnp.int32, cols_ref.shape, 1)
        plain = jnp.sum(acc_ref[0], axis=1, keepdims=True)
        weighted = jnp.sum(acc_ref[1], axis=1, keepdims=True)
        cols_ref[...] = jnp.where(lane == 0, plain, weighted)
        rows_of(cols_ref, sum_ref)


def activation_gradient(weights, hiddens, cuts, conv, par):
    rows, channels, width = conv.shape
    padded = par.shape[1]
    return pl.pallas_call(
        functools.partial(act_grad_kernel, cuts=cuts),
        grid=(rows,),
        in_specs=[whole(w.shape) for w in weights]
        + [pl.BlockSpec((width, h.shape[1]), lambda r: (r, 0)) for h in hiddens]
        + [pl.BlockSpec((1, channels, width), lambda r: (r, 0, 0)), whole((8, padded))],
        out_specs=[
            pl.BlockSpec((1, channels, width), lambda r: (r, 0, 0)),
            pl.BlockSpec((8, padded), lambda r: (0, 0)),
        ],
        out_shape=[
            jax.ShapeDtypeStruct((rows, channels, width), F32),
            jax.ShapeDtypeStruct((8, padded), F32),
        ],
        scratch_shapes=[pltpu.VMEM((padded, 128), F32), pltpu.VMEM((2, padded, 128), F32)],
        compiler_params=params(40),
        cost_estimate=cost(8e9, 25e6),
        name="activation_gradient",
    )(*weights, *hiddens, conv, par)


def block_out_kernel(*refs, cuts):
    n = len(cuts)
    w_refs, h_refs = refs[0:2], refs[2 : 2 + n]
    x_ref, m_ref, par_ref, out_ref, cols_ref = refs[2 + n :]
    channels = x_ref.shape[1]

    @pl.when(pl.program_id(0) == 0)
    def _():
        cols_ref[...] = columns_of(par_ref)

    branch = contract([(w_refs[w], first, units) for w, first, units in cuts], h_refs)
    branch = branch + cols_ref[0:channels, 4:5]
    out_ref[0] = ((x_ref[0].astype(F32) + branch) * m_ref[0, 0:1]).astype(BF16)


def block_output(weights, hiddens, cuts, x, m16, par):
    rows, channels, width = x.shape
    padded = par.shape[1]
    return pl.pallas_call(
        functools.partial(block_out_kernel, cuts=cuts),
        grid=(rows,),
        in_specs=[whole(w.shape) for w in weights]
        + [pl.BlockSpec((width, h.shape[1]), lambda r: (r, 0)) for h in hiddens]
        + [
            pl.BlockSpec((1, channels, width), lambda r: (r, 0, 0)),
            pl.BlockSpec((1, GRP, width), lambda r: (r, 0, 0)),
            whole((8, padded)),
        ],
        out_specs=pl.BlockSpec((1, channels, width), lambda r: (r, 0, 0)),
        out_shape=jax.ShapeDtypeStruct((rows, channels, width), BF16),
        scratch_shapes=[pltpu.VMEM((padded, 128), F32)],
        compiler_params=params(40),
        cost_estimate=cost(8e9, 22e6),
        name="block_output",
    )(*weights, *hiddens, x, m16, par)


def conv_grad_kernel(da_ref, conv_ref, m_ref, par_ref, out_ref, cols_ref):
    channels = conv_ref.shape[1]

    @pl.when(pl.program_id(0) == 0)
    def _():
        cols_ref[...] = columns_of(par_ref)

    c = cols_ref[0:channels, :]
    normalized = (conv_ref[0] - c[:, 0:1]) * c[:, 1:2]
    correction = m_ref[0, 0:1] * (c[:, 3:4] + normalized * c[:, 4:5])
    out_ref[0] = (c[:, 2:3] * (da_ref[0] - correction)).astype(BF16)


def conv_gradient(da, conv, m16, par):
    rows, channels, width = conv.shape
    padded = par.shape[1]
    return pl.pallas_call(
        conv_grad_kernel,
        grid=(rows,),
        in_specs=[
            pl.BlockSpec((1, channels, width), lambda r: (r, 0, 0)),
            pl.BlockSpec((1, channels, width), lambda r: (r, 0, 0)),
            pl.BlockSpec((1, GRP, width), lambda r: (r, 0, 0)),
            whole((8, padded)),
        ],
        out_specs=pl.BlockSpec((1, channels, width), lambda r: (r, 0, 0)),
        out_shape=jax.ShapeDtypeStruct((rows, channels, width), BF16),
        scratch_shapes=[pltpu.VMEM((padded, 128), F32)],
        compiler_params=params(24),
        cost_estimate=cost(1e9, 12e6),
        name="conv_gradient",
    )(da, conv, m16, par)


def halo(field):
    size = lax.axis_size("dp")
    up = [(i, i + 1) for i in range(size - 1)]
    down = [(j, i) for i, j in up]
    return (
        lax.ppermute(field[-REACH:], "dp", up),
        lax.ppermute(field[:REACH], "dp", down),
    )


def from_all(values, axes):
    size = 1
    for axis in axes:
        size *= lax.axis_size(axis)
    copies = jnp.broadcast_to(values[None], (size,) + values.shape)
    return lax.all_to_all(copies, axes, 0, 0)


def flip_bit(values, axis, bit):
    size = lax.axis_size(axis)
    return lax.ppermute(values, axis, [(i, i ^ (1 << bit)) for i in range(size)])


def bit_of(axis, bit):
    return (lax.axis_index(axis) >> bit) & 1


def gather_rows(shard, order):
    bits = lax.axis_size("fsdp").bit_length() - 1
    rows, cols = shard.shape
    have = shard.reshape((1,) * bits + (rows, cols))
    for bit in order:
        other = flip_bit(have, "fsdp", bit)
        mine = bit_of("fsdp", bit) == 0
        dim = bits - 1 - bit
        first, second = jnp.where(mine, have, other), jnp.where(mine, other, have)
        have = jnp.concatenate([first, second], axis=dim)
    return have.reshape(-1, cols)


def scatter_rows(full, order):
    bits = lax.axis_size("fsdp").bit_length() - 1
    cols = full.shape[1]
    have = full.reshape((2,) * bits + (-1, cols))
    for bit in order:
        dim = bits - 1 - bit
        mine = bit_of("fsdp", bit)
        send = lax.dynamic_slice_in_dim(have, 1 - mine, 1, axis=dim).astype(BF16)
        keep = lax.dynamic_slice_in_dim(have, mine, 1, axis=dim)
        have = keep + flip_bit(send, "fsdp", bit).astype(F32)
    return have.reshape(-1, cols)


def per_device(
    inputs,
    out_grad,
    ocean_mask,
    rollout_lengths,
    conv_weight,
    norm_gain,
    norm_bias,
    expand_weight,
    expand_bias,
    project_weight,
    project_bias,
):
    channels, rows, width = inputs.shape[1:]
    n_fs, n_dp = lax.axis_size("fsdp"), lax.axis_size("dp")
    share = conv_weight.shape[0]
    units = expand_weight.shape[1]
    half = pl.cdiv(units // 128, 2) * 128
    padded = pl.cdiv(channels, 128) * 128
    bits = list(range(n_fs.bit_length() - 1))
    core = bit_of("dp", 0)
    x = inputs[0].transpose(1, 0, 2)
    og = out_grad[0].transpose(1, 0, 2)
    block = 5 * GRP

    ratio = expand_bias.shape[0] // share
    small = jnp.concatenate(
        [
            conv_weight,
            norm_gain[:, None],
            norm_bias[:, None],
            project_bias.astype(F32)[:, None],
            expand_bias.astype(F32).reshape(share, ratio),
        ],
        axis=1,
    )
    small = from_all(small, ("fsdp",)).reshape(channels, -1)
    taps, gain, bias = small[:, :TAPS], small[:, TAPS], small[:, TAPS + 1]
    p_bias = small[:, TAPS + 2]
    e_bias = jnp.pad(small[:, TAPS + 3 :].reshape(1, units), ((0, 0), (0, 2 * half - units)))
    spread = spread_taps(taps)
    x_up, x_dn = halo(x)

    def columns(weight):
        wide = jnp.pad(weight, ((0, 0), (0, 2 * half - units)))
        return lax.dynamic_slice_in_dim(wide, core * half, half, axis=1)

    we_own = gather_rows(columns(expand_weight), bits)
    wp_own = gather_rows(columns(project_weight), bits[::-1])
    we_peer = flip_bit(we_own, "dp", 0)
    wp_peer = flip_bit(wp_own, "dp", 0)
    eb_own = lax.dynamic_slice_in_dim(e_bias, core * half, half, axis=1)
    eb_peer = lax.dynamic_slice_in_dim(e_bias, (1 - core) * half, half, axis=1)

    sample = lax.axis_index("fsdp")
    length = lax.dynamic_index_in_dim(rollout_lengths, sample, keepdims=False)
    live = jnp.where(sample % ROLLOUT < length, 1.0, 0.0).astype(F32)
    weight = live * ocean_mask.astype(F32)
    m16 = jnp.broadcast_to(weight[:, None, :], (rows, GRP, width))
    count_here = jnp.sum(weight)
    counts = jnp.stack([count_here, 1.0 / jnp.maximum(count_here, 1.0)])

    bg_c, bg_p, bg_sum = mask_gradient(og, m16, padded)

    conv, stats = conv_forward(x, x_up, x_dn, spread, m16, counts, padded, block)
    stats = from_all(stats[:2], ("dp", "fsdp"))
    counts_all = stats[:, 0, padded - 1]
    count = jnp.sum(counts_all)
    mean = jnp.sum(counts_all[:, None] * stats[:, 0], axis=0) / count
    apart = stats[:, 0] - mean[None]
    squares = jnp.sum(stats[:, 1] + counts_all[:, None] * apart * apart, axis=0)
    variance = squares / count
    inv_std = lax.rsqrt(variance + EPS)
    pad_c = lambda v: jnp.pad(v, (0, padded - channels))
    gain_p = pad_c(gain)
    nothing = jnp.zeros_like(mean)
    par = jnp.stack(
        [mean, inv_std * gain_p, pad_c(bias), inv_std, pad_c(p_bias), nothing, nothing, nothing]
    )
    act_c, act_p = activate(conv, par)

    first = half // (2 * TILE) * TILE
    second = half - first
    common = (act_p, act_c, bg_p, bg_c)
    q1 = hidden_layer(*common, we_peer, wp_peer, eb_peer, 0, first, BF16)
    o1 = hidden_layer(*common, we_own, wp_own, eb_own, 0, first, F32)
    q2 = hidden_layer(*common, we_peer, wp_peer, eb_peer, first, second, BF16)
    o2 = hidden_layer(*common, we_own, wp_own, eb_own, first, second, F32)
    cuts = ((1, 0, first), (0, 0, first), (1, first, second), (0, first, second))
    parts = (q1, o1, q2, o2)
    da, sums = activation_gradient(
        (we_own, we_peer), [p[1] for p in parts], cuts, conv, par
    )
    sums = jnp.sum(from_all(sums[:2], ("dp", "fsdp")), axis=0)
    block_out = block_output(
        (wp_own, wp_peer), [p[0] for p in parts], cuts, x, m16, par
    )
    bias_total, gain_total = sums[0], sums[1]
    par_b = jnp.stack(
        [mean, inv_std, gain_p * inv_std, bias_total / count, gain_total / count]
        + [nothing] * 3
    )
    conv_grad = conv_gradient(da, conv, m16, par_b)
    g_up, g_dn = halo(conv_grad)
    tap_local = tap_gradient(x, x_up, x_dn, conv_grad, block)
    input_grad = input_gradient(conv_grad, g_up, g_dn, spread, og, m16, block)

    groups = [[i for i in range(n_dp) if i % 2 == c] for c in range(2)]

    def reduced(peer, own, order):
        total = own + flip_bit(peer, "dp", 0).astype(F32)
        mine = scatter_rows(total, order).astype(BF16)
        return lax.psum(mine, "dp", axis_index_groups=groups)

    def joined(which, order):
        mine = jnp.concatenate(
            [reduced(q1[which], o1[which], order), reduced(q2[which], o2[which], order)], axis=1
        )
        other = flip_bit(mine, "dp", 0)
        low, high = jnp.where(core == 0, mine, other), jnp.where(core == 0, other, mine)
        return jnp.concatenate([low, high], axis=1)[:, :units].astype(F32)

    project_grad = joined(2, bits[::-1])
    expand_grad = joined(3, bits)

    eb_o = jnp.concatenate([o1[4], o2[4]], axis=1)
    eb_q = jnp.concatenate([q1[4], q2[4]], axis=1)
    eb_all = jnp.concatenate(
        [jnp.where(core == 0, eb_o, eb_q), jnp.where(core == 0, eb_q, eb_o)], axis=1
    )[0, :units]
    local = jnp.concatenate(
        [
            tap_local.reshape(n_fs, share * TAPS),
            eb_all.reshape(n_fs, share * ratio),
            bg_sum[0, :channels].reshape(n_fs, share),
        ],
        axis=1,
    )
    local = jnp.sum(lax.all_to_all(local, "fsdp", 0, 0), axis=0)
    local = lax.psum(local, "dp")
    tap_grad = local[: share * TAPS].reshape(share, TAPS)
    eb_grad = local[share * TAPS : share * (TAPS + ratio)]
    pb_grad = local[share * (TAPS + ratio) :]

    start = lax.axis_index("fsdp") * share
    gain_grad = lax.dynamic_slice_in_dim(gain_total, start, share)
    bias_grad = lax.dynamic_slice_in_dim(bias_total, start, share)
    return (
        block_out.transpose(1, 0, 2)[None],
        input_grad.transpose(1, 0, 2)[None],
        tap_grad,
        gain_grad,
        bias_grad,
        expand_grad,
        eb_grad,
        project_grad,
        pb_grad,
        mean[:channels],
        jnp.sqrt(variance + EPS)[:channels],
    )


def solution(mesh):
    rows = P("fsdp", None, "dp", None)
    return jax.shard_map(
        per_device,
        mesh=mesh,
        in_specs=(
            rows,
            rows,
            P("dp", None),
            P(),
            P("fsdp", None),
            P("fsdp"),
            P("fsdp"),
            P("fsdp", None),
            P("fsdp"),
            P("fsdp", None),
            P("fsdp"),
        ),
        out_specs=(
            rows,
            rows,
            P("fsdp", None),
            P("fsdp"),
            P("fsdp"),
            P("fsdp", None),
            P("fsdp"),
            P("fsdp", None),
            P("fsdp"),
            P(),
            P(),
        ),
        check_vma=False,
    )
```

time: 879 us -> 394 us (0.45)
  other arithmetic: 288 us -> 31.1 us
  blocking collectives: 203 us -> 26.7 us
  Pallas kernels: 0 us -> 159 us
  waiting for transfers between devices: 188 us -> 52.3 us
  matrix products: 97.2 us -> 0 us
  starting transfers between devices: 8.52 us -> 40.8 us
    unnamed x9 -> x1, waiting for transfers between devices: 188 us -> 0.02 us
    pallas_call x0 -> x12, Pallas kernels: none -> 159 us  [the longest x4 66.8 us: hidden_layer(): pl.pallas_call(functools.partial(hidden_kernel, step=pixels // 3), grid=(...]
    reduce_sum x11 -> x6, other arithmetic: 160 us -> 2.05 us  [the longest x1 1.01 us: per_device(): count = jnp.sum(counts_all)]
    psum x4 -> x1, blocking collectives: 150 us -> 26.7 us  [per_device(): local = lax.psum(local, 'dp')]
    add x1 -> x6, other arithmetic: 114 us -> 5.26 us  [the longest x2 4.75 us: reduced(): total = own + flip_bit(peer, 'dp', 0).astype(F32)]
    dot_general x6 -> x0, matrix products: 97.2 us -> none  [the longest x1 22.4 us: per_device(): jnp.einsum('ck,scp->skp', project_back, branch_grad, preferred_element_ty...]
    unnamed x3 -> x0, blocking collectives: 40.5 us -> none
    ppermute x4 -> x24, waiting for transfers between devices: 0.01 us -> 38 us  [the longest x20 38 us: flip_bit(): return lax.ppermute(values, axis, [(i, i ^ 1 << bit) for i in range(size)])]
  transfers between devices with their start and end apart: 10 -> 29, of which waited for: 2 -> 9; matrix products, arithmetic and copies ran while one was open for 31% -> 14% of each run, Pallas kernels for 0% -> 36%
where the time goes in v1:
time: 394 us; the launch traced here: 393 us
  Pallas kernels  159 us (40%)
  local copies, waits for them, and re-layouts  66.1 us (17%)
  waiting for transfers between devices  52.3 us (13%)
  starting transfers between devices  40.8 us (10%)
  other arithmetic  31.1 us (8%)
  blocking collectives  26.7 us (7%)
  between operations  16.3 us (4%)
    pallas_call x4, Pallas kernels, hidden_layer(): pl.pallas_call(functools.partial(hidden_kernel, step=pixels // 3), grid=(...  66.8 us
    ppermute x20, waiting for transfers between devices, flip_bit(): return lax.ppermute(values, axis, [(i, i ^ 1 << bit) for i in range(size)])  38 us
    unnamed x83, local copies, waits for them, and re-layouts  36.6 us
    psum x1, blocking collectives, per_device(): local = lax.psum(local, 'dp')  26.7 us
    pallas_call x1, Pallas kernels, conv_forward(): pl.pallas_call(conv_kernel, grid=(channels // block,), in_specs=[pl.Block...  21.4 us
    pallas_call x1, Pallas kernels, tap_gradient(): pl.pallas_call(tap_grad_kernel, grid=(channels // block,), in_specs=[pl.B...  16.7 us
    pallas_call x1, Pallas kernels, input_gradient(): pl.pallas_call(input_grad_kernel, grid=(channels // block,), in_specs=[pl...  15.9 us
    all_to_all x3, starting transfers between devices, from_all(): return lax.all_to_all(copies, axes, 0, 0)  15.2 us
  transfers between devices with their start and end apart: 29, of which 9 were waited for; matrix products, arithmetic and copies ran while one was open for 14% of the time, Pallas kernels for 36%

profile of v1, /device:TPU:0, one launch (start us, length us, event | category | flops | bytes accessed | tf_op | source)
XLA Modules:
  0.0 392.7 jit_solution(6386303570865225560)
XLA Ops:
  11.0 5.2 %all-to-all-start = ((f32[4,200,56]{1,2,0:T(8,128)}), f32[4,200,56]{1,2,0:T(8,128)S(1)}, u32[]{:S(2)}, u32[]{:S(2)}) async-start(f32[4,200,56]{1,2,0:T(8,128)} %broadcast_in_dim.80), calls=%async_computation | async-start | bytes 458752 | tf_op jit(solution)/shard_map/all_to_all | solution.py:540
  16.1 3.2 fusion.22
  19.4 2.5 collective-permute-start.3
  23.2 2.1 fusion.6
  25.3 1.9 collective-permute-start.5
  27.2 2.0 fusion.5
  32.6 2.1 mask_gradient.1
  39.9 2.8 copy.69
  42.8 2.0 broadcast_select_fusion
  54.0 21.4 %conv_forward.1 = (f32[6,800,256]{2,1,0:T(8,128)S(1)}, f32[8,896]{1,0:T(8,128)S(1)}) custom-call(f32[2]{0:T(128)S(1)} %pad_maximum_fusion.8.n_ref, bf16[6,800,256]{2,1,0:T(8,128)(2,1)S(1)} %bitcast.71, bf16[3,800,256]{2,1,0:T(8,128)(2,1)} %collective-permute-done.3.up_ref, bf16[3,800,256]{2,1,0:T(8,128)(2,1)} %collective-permute-done.4.dn_ref, ...), custom_call_target="tpu_custom_call" | custom-call | flops 20000000000 | bytes 12000000 | tf_op jit(solution)/shard_map/conv_forward/pallas_call | solution.py:122
  75.4 2.2 copy-done
  78.4 7.5 %all-to-all-start.1 = ((f32[32,2,896]{2,1,0:T(2,128)}), f32[32,2,896]{2,1,0:T(2,128)S(1)}, u32[]{:S(2)}, u32[]{:S(2)}) async-start(f32[32,2,896]{2,1,0:T(2,128)} %broadcast_in_dim.85), calls=%async_computation.1 | async-start | bytes 458752 | tf_op jit(solution)/shard_map/all_to_all | solution.py:540
  87.6 1.8 pad_maximum_fusion.2
  91.8 4.2 %all-to-all-done.1 = f32[32,2,896]{2,1,0:T(2,128)S(1)} async-done(((f32[32,2,896]{2,1,0:T(2,128)}), f32[32,2,896]{2,1,0:T(2,128)S(1)}, u32[]{:S(2)}, u32[]{:S(2)}) %all-to-all-start.1) | async-done | bytes 229408 | tf_op jit(solution)/shard_map/all_to_all | solution.py:540
  99.5 2.4 copy-done.1
  101.8 3.6 activate.1
  107.1 14.2 %hidden_layer.5 = (bf16[1536,768]{1,0:T(8,128)(2,1)S(1)}, bf16[1536,768]{1,0:T(8,128)(2,1)S(1)}, f32[800,768]{1,0:T(8,128)S(1)}, f32[800,768]{1,0:T(8,128)S(1)}, f32[1,768]{1,0:T(1,128)S(1)}) custom-call(bf16[1536,800]{1,0:T(8,128)(2,1)} %copy-done.16, bf16[800,1536]{1,0:T(8,128)(2,1)S(1)} %get-tuple-element.43.act_c, bf16[1536,800]{1,0:T(8,128)(2,1)} %copy-done.19, ...), custom_call_target="tpu_custom_call" | custom-call | flops 7549747200 | bytes 20000000 | tf_op jit(solution)/shard_map/hidden_layer/pallas_call | solution.py:356
  125.6 19.3 %hidden_layer.7 = (bf16[1536,896]{1,0:T(8,128)(2,1)S(1)}, bf16[1536,896]{1,0:T(8,128)(2,1)}, f32[800,896]{1,0:T(8,128)}, f32[800,896]{1,0:T(8,128)}, f32[1,896]{1,0:T(1,128)S(1)}) custom-call(bf16[1536,800]{1,0:T(8,128)(2,1)} %copy-done.16, bf16[800,1536]{1,0:T(8,128)(2,1)S(1)} %get-tuple-element.43.act_c, bf16[1536,800]{1,0:T(8,128)(2,1)} %copy-done.19, ...), custom_call_target="tpu_custom_call" | custom-call | flops 8808038400 | bytes 20000000 | tf_op jit(solution)/shard_map/hidden_layer/pallas_call | solution.py:356
  146.5 18.3 %hidden_layer.6 = (bf16[1536,896]{1,0:T(8,128)(2,1)}, bf16[1536,896]{1,0:T(8,128)(2,1)}, bf16[800,896]{1,0:T(8,128)(2,1)}, bf16[800,896]{1,0:T(8,128)(2,1)}, f32[1,896]{1,0:T(1,128)S(1)}) custom-call(bf16[1536,800]{1,0:T(8,128)(2,1)} %copy-done.16, bf16[800,1536]{1,0:T(8,128)(2,1)S(1)} %get-tuple-element.43.act_c, bf16[1536,800]{1,0:T(8,128)(2,1)} %copy-done.19, ...), custom_call_target="tpu_custom_call" | custom-call | flops 8808038400 | bytes 20000000 | tf_op jit(solution)/shard_map/hidden_layer/pallas_call | solution.py:356
  165.3 14.9 %hidden_layer.4 = (bf16[1536,768]{1,0:T(8,128)(2,1)S(1)}, bf16[1536,768]{1,0:T(8,128)(2,1)S(1)}, bf16[800,768]{1,0:T(8,128)(2,1)}, bf16[800,768]{1,0:T(8,128)(2,1)}, f32[1,768]{1,0:T(1,128)S(1)}) custom-call(bf16[1536,800]{1,0:T(8,128)(2,1)} %copy-done.16, bf16[800,1536]{1,0:T(8,128)(2,1)S(1)} %get-tuple-element.43.act_c, bf16[1536,800]{1,0:T(8,128)(2,1)} %copy-done.19, ...), custom_call_target="tpu_custom_call" | custom-call | flops 7549747200 | bytes 20000000 | tf_op jit(solution)/shard_map/hidden_layer/pallas_call | solution.py:356
  182.1 14.8 %activation_gradient.1 = (f32[6,800,256]{2,1,0:T(8,128)}, f32[8,896]{1,0:T(8,128)S(1)}) custom-call(bf16[800,1664]{1,0:T(8,128)(2,1)} %bitcast.20.we_ref.refs_0_, bf16[800,1664]{1,0:T(8,128)(2,1)} %collective-permute-done.7.we_ref.refs_1_, bf16[1536,768]{1,0:T(8,128)(2,1)S(1)} %get-tuple-element.50.refs_2_, bf16[1536,768]{1,0:T(8,128)(2,1)S(1)} %copy-done.29, ...), custom_call_target="tpu_custom_call" | custom-call | flops 8000000000 | bytes 25000000 | tf_op jit(solution)/shard_map/activation_gradient/pallas_call | solution.py:433
  197.7 2.6 all-to-all-start.2
  200.5 10.1 %all-to-all-done.2 = f32[32,2,896]{2,1,0:T(2,128)S(1)} async-done(((f32[32,2,896]{2,1,0:T(2,128)}), f32[32,2,896]{2,1,0:T(2,128)S(1)}, u32[]{:S(2)}, u32[]{:S(2)}) %all-to-all-start.2) | async-done | bytes 229408 | tf_op jit(solution)/shard_map/all_to_all | solution.py:540
  211.4 2.4 copy-done.2
  213.8 2.4 copy-done.3
  216.2 4.8 %conv_gradient.1.g_ref = bf16[6,800,256]{2,1,0:T(8,128)(2,1)S(1)} custom-call(f32[6,800,256]{2,1,0:T(8,128)S(1)} %copy-done.3, f32[6,800,256]{2,1,0:T(8,128)S(1)} %copy-done.2, f32[6,16,256]{2,1,0:T(8,128)S(1)} %broadcast_in_dim.84.m_ref.refs_7_, f32[8,896]{1,0:T(8,128)S(1)} %stack.50.par_ref), custom_call_target="tpu_custom_call" | custom-call | flops 1000000000 | bytes 12000000 | tf_op jit(solution)/shard_map/conv_gradient/pallas_call | solution.py:507
  222.6 2.5 collective-permute-start.8
  226.5 2.5 convert_add_fusion.2
  231.1 2.3 convert_add_fusion
  234.6 11.0 %collective-permute-done.18 = bf16[1,2,200,768]{3,2,1,0:T(8,128)(2,1)S(1)} collective-permute-done((bf16[1,2,200,768]{3,2,1,0:T(8,128)(2,1)S(1)}, bf16[1,2,200,768]{3,2,1,0:T(8,128)(2,1)S(1)}, u32[]{:S(2)}, u32[]{:S(2)}) %collective-permute-start.18) | collective-permute-done | bytes 614432 | tf_op jit(solution)/shard_map/ppermute | solution.py:545
  248.1 12.9 %collective-permute-done.21 = bf16[1,2,200,896]{3,2,1,0:T(8,128)(2,1)S(1)} collective-permute-done((bf16[1,2,200,896]{3,2,1,0:T(8,128)(2,1)S(1)}, bf16[1,2,200,896]{3,2,1,0:T(8,128)(2,1)S(1)}, u32[]{:S(2)}, u32[]{:S(2)}) %collective-permute-start.21) | collective-permute-done | bytes 716832 | tf_op jit(solution)/shard_map/ppermute | solution.py:545
  262.3 2.2 collective-permute-done.14
  265.6 5.5 %collective-permute-done.19 = bf16[1,1,200,768]{3,2,1,0:T(8,128)(2,1)S(1)} collective-permute-done((bf16[1,1,200,768]{3,2,1,0:T(8,128)(2,1)S(1)}, bf16[1,1,200,768]{3,2,1,0:T(8,128)(2,1)S(1)}, u32[]{:S(2)}, u32[]{:S(2)}) %collective-permute-start.19) | collective-permute-done | bytes 307232 | tf_op jit(solution)/shard_map/ppermute | solution.py:545
  273.8 4.5 %collective-permute-done.22 = bf16[1,1,200,896]{3,2,1,0:T(8,128)(2,1)S(1)} collective-permute-done((bf16[1,1,200,896]{3,2,1,0:T(8,128)(2,1)S(1)}, bf16[1,1,200,896]{3,2,1,0:T(8,128)(2,1)S(1)}, u32[]{:S(2)}, u32[]{:S(2)}) %collective-permute-start.22) | collective-permute-done | bytes 358432 | tf_op jit(solution)/shard_map/ppermute | solution.py:545
  281.4 1.7 copy-done.10
  283.1 16.7 %tap_gradient.1 = f32[800,128]{1,0:T(8,128)S(1)} custom-call(bf16[6,800,256]{2,1,0:T(8,128)(2,1)S(1)} %bitcast.72, bf16[3,800,256]{2,1,0:T(8,128)(2,1)} %collective-permute-done.3.up_ref, bf16[3,800,256]{2,1,0:T(8,128)(2,1)} %collective-permute-done.4.dn_ref, bf16[6,800,256]{2,1,0:T(8,128)(2,1)S(1)} %conv_gradient.1.g_ref), custom_call_target="tpu_custom_call" | custom-call | flops 17999998976 | bytes 8000000 | tf_op jit(solution)/shard_map/tap_gradient/pallas_call | solution.py:218
  300.0 2.5 copy.74
  302.5 3.2 reshape_reshape.3
  306.7 3.4 all-to-all-start.3
  310.1 1.7 copy-done.8
  311.8 1.7 copy-done.11
  313.5 1.7 copy-done.25
  315.2 1.8 copy-done.27
  317.0 13.4 %block_output.1 = bf16[6,800,256]{2,1,0:T(8,128)(2,1)} custom-call(bf16[800,1664]{1,0:T(8,128)(2,1)S(1)} %bitcast.69, bf16[800,1664]{1,0:T(8,128)(2,1)} %collective-permute-done.2.wp_ref.refs_1_, bf16[1536,768]{1,0:T(8,128)(2,1)S(1)} %copy-done.27, bf16[1536,768]{1,0:T(8,128)(2,1)S(1)} %copy-done.25, bf16[1536,896]{1,0:T(8,128)(2,1)} %get-tuple-element.48.refs_4_, ...), custom_call_target="tpu_custom_call" | custom-call | flops 8000000000 | bytes 22000000 | tf_op jit(solution)/shard_map/block_output/pallas_call | solution.py:472
  331.2 26.7 %psum.35 = f32[10800]{0:T(1024)S(1)} all-reduce(f32[10800]{0:T(1024)S(1)} %reduce_sum.59), channel_id=1, replica_groups=mesh['dp'=8,'fsdp'=4] {'dp'}, use_global_device_ids=true, to_apply=%region_6.7 | all-reduce | flops 10800 | bytes 86400 | tf_op jit(solution)/shard_map/psum | solution.py:717
  362.3 1.8 copy-done.5
  364.1 1.7 copy-done.18
  365.8 15.9 %input_gradient.1 = f32[6,800,256]{2,1,0:T(8,128)} custom-call(bf16[6,800,256]{2,1,0:T(8,128)(2,1)S(1)} %conv_gradient.1.g_ref, bf16[3,800,256]{2,1,0:T(8,128)(2,1)} %collective-permute-done.8.up_ref, bf16[3,800,256]{2,1,0:T(8,128)(2,1)} %collective-permute-done.9.dn_ref, bf16[2,7,800,128]{3,2,1,0:T(8,128)(2,1)S(1)} %copy-done.5, ...), custom_call_target="tpu_custom_call" | custom-call | flops 17999998976 | bytes 15000000 | tf_op jit(solution)/shard_map/input_gradient/pallas_call | solution.py:168
  (212 shorter events, 68.4 us)
Async XLA Ops:
  11.0 28.4 %all-to-all-start = ((f32[4,200,56]{1,2,0:T(8,128)}), f32[4,200,56]{1,2,0:T(8,128)S(1)}, u32[]{:S(2)}, u32[]{:S(2)}) async-start(f32[4,200,56]{1,2,0:T(8,128)} %broadcast_in_dim.80), calls=%async_computation | async-start | bytes 458752 | tf_op jit(solution)/shard_map/all_to_all | solution.py:540
  19.4 34.3 %collective-permute-start.3 = (bf16[3,800,256]{2,1,0:T(8,128)(2,1)}, bf16[3,800,256]{2,1,0:T(8,128)(2,1)}, u32[]{:S(2)}, u32[]{:S(2)}) collective-permute-start(bf16[3,800,256]{2,1,0:T(8,128)(2,1)} %get-tuple-element.146), channel_id=1, source_target_pairs={{0,4},{4,8},{8,12},{12,16},{16,20},{20,24},{24,28},{1,5},{5,9},{9,... | collective-permute-start | bytes 3686408 | tf_op jit(solution)/shard_map/ppermute | solution.py:530
  21.9 31.8 %collective-permute-start.4 = (bf16[3,800,256]{2,1,0:T(8,128)(2,1)}, bf16[3,800,256]{2,1,0:T(8,128)(2,1)}, u32[]{:S(2)}, u32[]{:S(2)}) collective-permute-start(bf16[3,800,256]{2,1,0:T(8,128)(2,1)} %get-tuple-element.145), channel_id=1, source_target_pairs={{4,0},{8,4},{12,8},{16,12},{20,16},{24,20},{28,24},{5,1},{9,5},{13... | collective-permute-start | bytes 3686408 | tf_op jit(solution)/shard_map/ppermute | solution.py:531
  23.2 9.4 %copy-start.17 = (bf16[1,800,6,256]{3,1,2,0:T(8,128)(2,1)S(1)}, bf16[1,800,6,256]{3,1,2,0:T(8,128)(2,1)}, u32[]{:S(2)}) copy-start(bf16[1,800,6,256]{3,1,2,0:T(8,128)(2,1)} %param.12) | copy-start | bytes 7372804
  25.3 5.3 %copy-start.38 = (s32[4]{0:T(128)S(1)}, s32[4]{0:T(128)}, u32[]{:S(2)}) copy-start(s32[4]{0:T(128)} %param.14) | copy-start | bytes 52
  25.3 6.6 %copy-start.37 = (s32[6,256]{1,0:T(8,128)S(1)}, s32[6,256]{1,0:T(8,128)}, u32[]{:S(2)}) copy-start(s32[6,256]{1,0:T(8,128)} %param.13) | copy-start | bytes 18436
  25.3 20.8 %collective-permute-start.5 = (bf16[1,1,200,1664]{3,2,1,0:T(8,128)(2,1)}, bf16[1,1,200,1664]{3,2,1,0:T(8,128)(2,1)}, u32[]{:S(2)}, u32[]{:S(2)}) collective-permute-start(bf16[1,1,200,1664]{3,2,1,0:T(8,128)(2,1)} %fusion.6), channel_id=1, source_target_pairs={{0,1},{1,0},{2,3},{3,2},{4,5},{5,4},{6,7},{7,6},{8,9},{9,8},{10,11... | collective-permute-start | bytes 1996808 | tf_op jit(solution)/shard_map/ppermute | solution.py:545
  29.2 21.3 %collective-permute-start = (bf16[1,1,200,1664]{3,2,1,0:T(8,128)(2,1)}, bf16[1,1,200,1664]{3,2,1,0:T(8,128)(2,1)}, u32[]{:S(2)}, u32[]{:S(2)}) collective-permute-start(bf16[1,1,200,1664]{3,2,1,0:T(8,128)(2,1)} %fusion.5), channel_id=1, source_target_pairs={{0,2},{1,3},{2,0},{3,1},{4,6},{5,7},{6,4},{7,5},{8,10},{9,11},{10,... | collective-permute-start | bytes 1996808 | tf_op jit(solution)/shard_map/ppermute | solution.py:545
  46.1 7.5 %copy-start.4 = (bf16[2,7,800,128]{3,2,1,0:T(8,128)(2,1)}, bf16[2,7,800,128]{3,2,1,0:T(8,128)(2,1)S(1)}, u32[]{:S(2)}) copy-start(bf16[2,7,800,128]{3,2,1,0:T(8,128)(2,1)S(1)} %pad_maximum_fusion.e_ref) | copy-start | bytes 8601604
  49.9 36.0 %collective-permute-start.6 = (bf16[1,2,200,1664]{3,2,1,0:T(8,128)(2,1)}, bf16[1,2,200,1664]{3,2,1,0:T(8,128)(2,1)}, u32[]{:S(2)}, u32[]{:S(2)}) collective-permute-start(bf16[1,2,200,1664]{3,2,1,0:T(8,128)(2,1)} %pad_maximum_fusion.4), channel_id=1, source_target_pairs={{0,2},{1,3},{2,0},{3,1},{4,6},{5,7},{6,4},{7,5},{8,10},{9,11},{10,... | collective-permute-start | bytes 3993608 | tf_op jit(solution)/shard_map/ppermute | solution.py:545
  53.1 36.3 %collective-permute-start.1 = (bf16[2,1,200,1664]{3,2,1,0:T(8,128)(2,1)}, bf16[2,1,200,1664]{3,2,1,0:T(8,128)(2,1)}, u32[]{:S(2)}, u32[]{:S(2)}) collective-permute-start(bf16[2,1,200,1664]{3,2,1,0:T(8,128)(2,1)} %pad_maximum_fusion.3), channel_id=1, source_target_pairs={{0,1},{1,0},{2,3},{3,2},{4,5},{5,4},{6,7},{7,6},{8,9},{9,8},{10,11... | collective-permute-start | bytes 3993608 | tf_op jit(solution)/shard_map/ppermute | solution.py:545
  78.4 17.6 %all-to-all-start.1 = ((f32[32,2,896]{2,1,0:T(2,128)}), f32[32,2,896]{2,1,0:T(2,128)S(1)}, u32[]{:S(2)}, u32[]{:S(2)}) async-start(f32[32,2,896]{2,1,0:T(2,128)} %broadcast_in_dim.85), calls=%async_computation.1 | async-start | bytes 458752 | tf_op jit(solution)/shard_map/all_to_all | solution.py:540
  89.3 57.1 %collective-permute-start.7 = (bf16[800,1664]{1,0:T(8,128)(2,1)}, bf16[800,1664]{1,0:T(8,128)(2,1)}, u32[]{:S(2)}, u32[]{:S(2)}) collective-permute-start(bf16[800,1664]{1,0:T(8,128)(2,1)} %bitcast.20.we_ref.refs_0_), channel_id=1, source_target_pairs={{0,4},{4,0},{8,12},{12,8},{16,20},{20,16},{24,28},{28,24},{1,5},{5... | collective-permute-start | bytes 7987208 | tf_op jit(solution)/shard_map/ppermute | solution.py:545
  91.3 14.1 %copy-start.6 = (bf16[2,2,200,1664]{3,2,1,0:T(8,128)(2,1)}, bf16[2,2,200,1664]{3,2,1,0:T(8,128)(2,1)S(1)}, u32[]{:S(2)}) copy-start(bf16[2,2,200,1664]{3,2,1,0:T(8,128)(2,1)S(1)} %pad_maximum_fusion.1) | copy-start | bytes 7987204
  91.3 55.1 %collective-permute-start.2 = (bf16[800,1664]{1,0:T(8,128)(2,1)S(1)}, bf16[800,1664]{1,0:T(8,128)(2,1)}, u32[]{:S(2)}, u32[]{:S(2)}) collective-permute-start(bf16[800,1664]{1,0:T(8,128)(2,1)S(1)} %bitcast.66), channel_id=1, source_target_pairs={{0,4},{4,0},{8,12},{12,8},{16,20},{20,16},{24,28},{28,24},{1,5},{5... | collective-permute-start | bytes 7987208 | tf_op jit(solution)/shard_map/ppermute | solution.py:545
  98.0 7.5 %copy-start.36 = (f32[896]{0:T(1024)}, f32[896]{0:T(1024)S(1)}, u32[]{:S(2)}) copy-start(f32[896]{0:T(1024)S(1)} %broadcast_divide_fusion) | copy-start | bytes 10756
  99.4 2.4 copy-start.1
  101.8 5.2 %copy-start.21 = (bf16[800,1536]{1,0:T(8,128)(2,1)S(1)}, bf16[800,1536]{1,0:T(8,128)(2,1)}, u32[]{:S(2)}) copy-start(bf16[800,1536]{1,0:T(8,128)(2,1)} %copy-done.20) | copy-start | bytes 7372804
  107.1 18.5 %copy-start.7 = (bf16[2,2,200,1664]{3,2,1,0:T(8,128)(2,1)S(1)}, bf16[2,2,200,1664]{3,2,1,0:T(8,128)(2,1)}, u32[]{:S(2)}) copy-start(bf16[2,2,200,1664]{3,2,1,0:T(8,128)(2,1)} %copy-done.6) | copy-start | bytes 7987204
  125.6 19.3 %copy-start.24 = (bf16[1536,768]{1,0:T(8,128)(2,1)}, bf16[1536,768]{1,0:T(8,128)(2,1)S(1)}, u32[]{:S(2)}) copy-start(bf16[1536,768]{1,0:T(8,128)(2,1)S(1)} %get-tuple-element.47.refs_3_) | copy-start | bytes 7077892
  164.8 65.5 %collective-permute-start.13 = (bf16[800,896]{1,0:T(8,128)(2,1)}, bf16[800,896]{1,0:T(8,128)(2,1)}, u32[]{:S(2)}, u32[]{:S(2)}) collective-permute-start(bf16[800,896]{1,0:T(8,128)(2,1)} %get-tuple-element.64), channel_id=1, source_target_pairs={{0,4},{4,0},{8,12},{12,8},{16,20},{20,16},{24,28},{28,24},{1,5},{5... | collective-permute-start | bytes 4300808 | tf_op jit(solution)/shard_map/ppermute | solution.py:545
  164.8 17.3 %copy-start.23 = (bf16[1536,896]{1,0:T(8,128)(2,1)S(1)}, bf16[1536,896]{1,0:T(8,128)(2,1)}, u32[]{:S(2)}) copy-start(bf16[1536,896]{1,0:T(8,128)(2,1)} %get-tuple-element.52.refs_4_) | copy-start | bytes 8257540
  164.8 17.3 %copy-start.29 = (bf16[1536,768]{1,0:T(8,128)(2,1)S(1)}, bf16[1536,768]{1,0:T(8,128)(2,1)}, u32[]{:S(2)}) copy-start(bf16[1536,768]{1,0:T(8,128)(2,1)} %copy-done.28) | copy-start | bytes 7077892
  164.8 66.3 %collective-permute-start.20 = (bf16[800,896]{1,0:T(8,128)(2,1)}, bf16[800,896]{1,0:T(8,128)(2,1)}, u32[]{:S(2)}, u32[]{:S(2)}) collective-permute-start(bf16[800,896]{1,0:T(8,128)(2,1)} %get-tuple-element.68), channel_id=1, source_target_pairs={{0,4},{4,0},{8,12},{12,8},{16,20},{20,16},{24,28},{28,24},{1,5},{5... | collective-permute-start | bytes 4300808 | tf_op jit(solution)/shard_map/ppermute | solution.py:545
  181.6 43.5 %collective-permute-start.10 = (bf16[800,768]{1,0:T(8,128)(2,1)}, bf16[800,768]{1,0:T(8,128)(2,1)}, u32[]{:S(2)}, u32[]{:S(2)}) collective-permute-start(bf16[800,768]{1,0:T(8,128)(2,1)} %get-tuple-element.62), channel_id=1, source_target_pairs={{0,4},{4,0},{8,12},{12,8},{16,20},{20,16},{24,28},{28,24},{1,5},{5... | collective-permute-start | bytes 3686408 | tf_op jit(solution)/shard_map/ppermute | solution.py:545
  181.7 44.7 %collective-permute-start.17 = (bf16[800,768]{1,0:T(8,128)(2,1)}, bf16[800,768]{1,0:T(8,128)(2,1)}, u32[]{:S(2)}, u32[]{:S(2)}) collective-permute-start(bf16[800,768]{1,0:T(8,128)(2,1)} %get-tuple-element.66), channel_id=1, source_target_pairs={{0,4},{4,0},{8,12},{12,8},{16,20},{20,16},{24,28},{28,24},{1,5},{5... | collective-permute-start | bytes 3686408 | tf_op jit(solution)/shard_map/ppermute | solution.py:545
  197.7 12.9 %all-to-all-start.2 = ((f32[32,2,896]{2,1,0:T(2,128)}), f32[32,2,896]{2,1,0:T(2,128)S(1)}, u32[]{:S(2)}, u32[]{:S(2)}) async-start(f32[32,2,896]{2,1,0:T(2,128)} %broadcast_in_dim.87), calls=%async_computation.2 | async-start | bytes 458752 | tf_op jit(solution)/shard_map/all_to_all | solution.py:540
  200.3 159.8 %all-reduce.10.cloned.1.call-start = ((), (), s32[]{:S(2)}) async-start(), calls=%async_computation.4 | async-start | bytes 2662400 | tf_op jit(solution)/shard_map/psum | solution.py:690
  211.4 2.4 copy-start.2
  221.0 5.5 %copy-start.13 = (f32[800,768]{1,0:T(8,128)S(1)}, f32[800,768]{1,0:T(8,128)}, u32[]{:S(2)}) copy-start(f32[800,768]{1,0:T(8,128)} %copy-done.12) | copy-start | bytes 7372804
  221.0 5.5 %copy-start.15 = (f32[800,768]{1,0:T(8,128)S(1)}, f32[800,768]{1,0:T(8,128)}, u32[]{:S(2)}) copy-start(f32[800,768]{1,0:T(8,128)} %copy-done.14) | copy-start | bytes 7372804
  222.6 139.7 %collective-permute-start.8 = (bf16[3,800,256]{2,1,0:T(8,128)(2,1)}, bf16[3,800,256]{2,1,0:T(8,128)(2,1)}, u32[]{:S(2)}, u32[]{:S(2)}) collective-permute-start(bf16[3,800,256]{2,1,0:T(8,128)(2,1)} %get-tuple-element.144), channel_id=1, source_target_pairs={{0,4},{4,8},{8,12},{12,16},{16,20},{20,24},{24,28},{1,5},{5,9},{9,... | collective-permute-start | bytes 3686408 | tf_op jit(solution)/shard_map/ppermute | solution.py:530
  225.1 137.2 %collective-permute-start.9 = (bf16[3,800,256]{2,1,0:T(8,128)(2,1)}, bf16[3,800,256]{2,1,0:T(8,128)(2,1)}, u32[]{:S(2)}, u32[]{:S(2)}) collective-permute-start(bf16[3,800,256]{2,1,0:T(8,128)(2,1)} %get-tuple-element.143), channel_id=1, source_target_pairs={{4,0},{8,4},{12,8},{16,12},{20,16},{24,20},{28,24},{5,1},{9,5},{13... | collective-permute-start | bytes 3686408 | tf_op jit(solution)/shard_map/ppermute | solution.py:531
  226.5 4.6 %copy-start.32 = (f32[800,896]{1,0:T(8,128)S(1)}, f32[800,896]{1,0:T(8,128)}, u32[]{:S(2)}) copy-start(f32[800,896]{1,0:T(8,128)} %get-tuple-element.67) | copy-start | bytes 8601604
  226.5 4.6 %copy-start.33 = (f32[800,896]{1,0:T(8,128)S(1)}, f32[800,896]{1,0:T(8,128)}, u32[]{:S(2)}) copy-start(f32[800,896]{1,0:T(8,128)} %get-tuple-element.63) | copy-start | bytes 8601604
  229.0 16.6 %collective-permute-start.18 = (bf16[1,2,200,768]{3,2,1,0:T(8,128)(2,1)S(1)}, bf16[1,2,200,768]{3,2,1,0:T(8,128)(2,1)S(1)}, u32[]{:S(2)}, u32[]{:S(2)}) collective-permute-start(bf16[1,2,200,768]{3,2,1,0:T(8,128)(2,1)S(1)} %dynamic-slice_convert_fusion.2), channel_id=1, source_target_pairs={{0,2},{1,3},{2,0},{3,1},{4,6},{5,7},{6,4},{7,5},{8,10},{9,11},{10,... | collective-permute-start | bytes 1843208 | tf_op jit(solution)/shard_map/ppermute | solution.py:545
  230.3 16.7 %collective-permute-start.11 = (bf16[2,1,200,768]{3,2,1,0:T(8,128)(2,1)S(1)}, bf16[2,1,200,768]{3,2,1,0:T(8,128)(2,1)S(1)}, u32[]{:S(2)}, u32[]{:S(2)}) collective-permute-start(bf16[2,1,200,768]{3,2,1,0:T(8,128)(2,1)S(1)} %dynamic-slice_convert_fusion.3), channel_id=1, source_target_pairs={{0,1},{1,0},{2,3},{3,2},{4,5},{5,4},{6,7},{7,6},{8,9},{9,8},{10,11... | collective-permute-start | bytes 1843208 | tf_op jit(solution)/shard_map/ppermute | solution.py:545
  233.4 27.6 %collective-permute-start.21 = (bf16[1,2,200,896]{3,2,1,0:T(8,128)(2,1)S(1)}, bf16[1,2,200,896]{3,2,1,0:T(8,128)(2,1)S(1)}, u32[]{:S(2)}, u32[]{:S(2)}) collective-permute-start(bf16[1,2,200,896]{3,2,1,0:T(8,128)(2,1)S(1)} %dynamic-slice_convert_fusion), channel_id=1, source_target_pairs={{0,2},{1,3},{2,0},{3,1},{4,6},{5,7},{6,4},{7,5},{8,10},{9,11},{10,... | collective-permute-start | bytes 2150408 | tf_op jit(solution)/shard_map/ppermute | solution.py:545
  245.7 18.9 %collective-permute-start.14 = (bf16[2,1,200,896]{3,2,1,0:T(8,128)(2,1)S(1)}, bf16[2,1,200,896]{3,2,1,0:T(8,128)(2,1)S(1)}, u32[]{:S(2)}, u32[]{:S(2)}) collective-permute-start(bf16[2,1,200,896]{3,2,1,0:T(8,128)(2,1)S(1)} %dynamic-slice_convert_fusion.1), channel_id=1, source_target_pairs={{0,1},{1,0},{2,3},{3,2},{4,5},{5,4},{6,7},{7,6},{8,9},{9,8},{10,11... | collective-permute-start | bytes 2150408 | tf_op jit(solution)/shard_map/ppermute | solution.py:545
  247.0 24.1 %collective-permute-start.19 = (bf16[1,1,200,768]{3,2,1,0:T(8,128)(2,1)S(1)}, bf16[1,1,200,768]{3,2,1,0:T(8,128)(2,1)S(1)}, u32[]{:S(2)}, u32[]{:S(2)}) collective-permute-start(bf16[1,1,200,768]{3,2,1,0:T(8,128)(2,1)S(1)} %dynamic-slice_convert_fusion.6), channel_id=1, source_target_pairs={{0,1},{1,0},{2,3},{3,2},{4,5},{5,4},{6,7},{7,6},{8,9},{9,8},{10,11... | collective-permute-start | bytes 921608 | tf_op jit(solution)/shard_map/ppermute | solution.py:545
  261.0 12.0 %collective-permute-start.12 = (bf16[1,1,200,768]{3,2,1,0:T(8,128)(2,1)S(1)}, bf16[1,1,200,768]{3,2,1,0:T(8,128)(2,1)S(1)}, u32[]{:S(2)}, u32[]{:S(2)}) collective-permute-start(bf16[1,1,200,768]{3,2,1,0:T(8,128)(2,1)S(1)} %dynamic-slice_convert_fusion.7), channel_id=1, source_target_pairs={{0,2},{1,3},{2,0},{3,1},{4,6},{5,7},{6,4},{7,5},{8,10},{9,11},{10,... | collective-permute-start | bytes 921608 | tf_op jit(solution)/shard_map/ppermute | solution.py:545
  264.5 13.8 %collective-permute-start.22 = (bf16[1,1,200,896]{3,2,1,0:T(8,128)(2,1)S(1)}, bf16[1,1,200,896]{3,2,1,0:T(8,128)(2,1)S(1)}, u32[]{:S(2)}, u32[]{:S(2)}) collective-permute-start(bf16[1,1,200,896]{3,2,1,0:T(8,128)(2,1)S(1)} %dynamic-slice_convert_fusion.4), channel_id=1, source_target_pairs={{0,1},{1,0},{2,3},{3,2},{4,5},{5,4},{6,7},{7,6},{8,9},{9,8},{10,11... | collective-permute-start | bytes 1075208 | tf_op jit(solution)/shard_map/ppermute | solution.py:545
  271.1 9.5 %collective-permute-start.15 = (bf16[1,1,200,896]{3,2,1,0:T(8,128)(2,1)S(1)}, bf16[1,1,200,896]{3,2,1,0:T(8,128)(2,1)S(1)}, u32[]{:S(2)}, u32[]{:S(2)}) collective-permute-start(bf16[1,1,200,896]{3,2,1,0:T(8,128)(2,1)S(1)} %dynamic-slice_convert_fusion.5), channel_id=1, source_target_pairs={{0,2},{1,3},{2,0},{3,1},{4,6},{5,7},{6,4},{7,5},{8,10},{9,11},{10,... | collective-permute-start | bytes 1075208 | tf_op jit(solution)/shard_map/ppermute | solution.py:545
  306.7 24.3 %all-to-all-start.3 = ((f32[4,1,10800]{2,1,0:T(1,128)}), f32[4,1,10800]{2,1,0:T(1,128)S(1)}, u32[]{:S(2)}, u32[]{:S(2)}) async-start(f32[4,1,10800]{2,1,0:T(1,128)} %copy.75), calls=%async_computation.3 | async-start | bytes 348160 | tf_op jit(solution)/shard_map/all_to_all | solution.py:716
  361.1 20.6 %copy-start.35 = (bf16[200,768]{1,0:T(8,128)(2,1)S(1)}, bf16[200,768]{1,0:T(8,128)(2,1)}, u32[]{:S(2)}) copy-start(bf16[200,768]{1,0:T(8,128)(2,1)} %get-tuple-element.129) | copy-start | bytes 921604
  361.1 20.6 %copy-start.34 = (bf16[200,896]{1,0:T(8,128)(2,1)S(1)}, bf16[200,896]{1,0:T(8,128)(2,1)}, u32[]{:S(2)}) copy-start(bf16[200,896]{1,0:T(8,128)(2,1)} %get-tuple-element.130) | copy-start | bytes 1075204
  362.2 20.1 %collective-permute-start.23 = (bf16[200,1664]{1,0:T(8,128)(2,1)S(1)}, bf16[200,1664]{1,0:T(8,128)(2,1)S(1)}, u32[]{:S(2)}, u32[]{:S(2)}) collective-permute-start(bf16[200,1664]{1,0:T(8,128)(2,1)S(1)} %constant_dynamic-update-slice_fusion.6), channel_id=1, source_target_pairs={{0,4},{4,0},{8,12},{12,8},{16,20},{20,16},{24,28},{28,24},{1,5},{5... | collective-permute-start | bytes 1996808 | tf_op jit(solution)/shard_map/ppermute | solution.py:545
  381.8 2.3 collective-permute-start.16
  (20 other events, 34.0 us)
Sparse Core Ops, SparseCore 0:
  281.5 60.4 all-reduce.9

commit v2 on v1

v2 whole, which is shorter than its diff:
```python
import functools

import jax
import jax.numpy as jnp
from jax import lax
from jax.experimental import pallas as pl
from jax.experimental.pallas import tpu as pltpu
from jax.sharding import PartitionSpec as P

KS = 7
REACH = KS // 2
TAPS = KS * KS
ROLLOUT = 8
EPS = 1e-05
F32, BF16 = jnp.float32, jnp.bfloat16
GRP = 16
TILE = 256
MIB = 2**20
GELU_A = 0.7978845608028654
GELU_B = 0.044715
NT = (((1,), (1,)), ((), ()))


def params(limit=60):
    return pltpu.CompilerParams(vmem_limit_bytes=limit * MIB)


def cost(flops, nbytes, trans=0):
    return pl.CostEstimate(flops=int(flops), bytes_accessed=int(nbytes), transcendentals=int(trans))


def whole(shape):
    zeros = (0,) * len(shape)
    return pl.BlockSpec(shape, lambda *g: zeros, pipeline_mode=pl.Buffered(1))


def roll_lanes(v, shift):
    shift %= v.shape[-1]
    return v if shift == 0 else pltpu.roll(v, shift, v.ndim - 1)


def columns_of(*rows):
    pieces = []
    for k in range(rows[0].shape[0]):
        used = [v[k : k + 1, :] for v in rows]
        block = jnp.concatenate(used + [jnp.zeros((128 - len(rows), 128), F32)], axis=0)
        pieces.append(block.T)
    return jnp.concatenate(pieces, axis=0)


def copies_of(cols, out_ref):
    copies = out_ref.shape[0]
    for k in range(cols.shape[0] // 128):
        block = cols[k * 128 : (k + 1) * 128, :].T
        for q in range(2):
            row = jnp.broadcast_to(block[q : q + 1, :][None], (copies, 1, 128))
            out_ref[:, 8 * q + k : 8 * q + k + 1, :] = row


def spread_taps(cols, pick_ref, e_ref):
    count = cols.shape[0]
    lane = lax.broadcasted_iota(jnp.int32, (count, 128), 1)
    own = lax.broadcasted_iota(jnp.int32, (count, 128), 0) % GRP == lane % GRP
    high = cols.astype(BF16)
    low = (cols - high.astype(F32)).astype(BF16)
    for h, part in enumerate((high, low)):
        for j in range(KS):
            picked = jnp.dot(part, pick_ref[j], preferred_element_type=F32)
            e_ref[h, j] = jnp.where(own, picked, 0.0).astype(BF16)


def tap_picker():
    col, tap, lane = (lax.broadcasted_iota(jnp.int32, (KS, 128, 128), d) for d in range(3))
    return jnp.where((tap == KS * (lane // GRP) + col) & (lane < KS * GRP), 1.0, 0.0).astype(BF16)


def conv_rows(field_ref, taps_ref, s, rows, flip):
    x = field_ref[:, s, :].reshape((rows + 2 * REACH) * GRP, field_ref.shape[-1])
    parts = [taps_ref[h, :, s, :].reshape(KS * GRP, 128)[:, : KS * GRP] for h in range(2)]
    taps = jnp.concatenate(parts, axis=1)
    out = []
    for r in range(rows):
        src = rows - 1 - r if flip else r
        window = x[src * GRP : (src + KS) * GRP]
        sums = jnp.dot(taps, jnp.concatenate([window, window], axis=0), preferred_element_type=F32)
        acc = None
        for j in range(KS):
            moved = roll_lanes(sums[j * GRP : (j + 1) * GRP], j - REACH if flip else REACH - j)
            acc = moved if acc is None else acc + moved
        out.append(acc)
    return out


def conv_kernel(
    n_ref, x_ref, up_ref, dn_ref, small_ref, pick_ref, m_ref, out_ref, st_ref, par_ref,
    field_ref, cols_ref, e_ref, *, share
):
    rows, block = x_ref.shape[0], x_ref.shape[1]
    step = pl.program_id(0)
    count = n_ref[0]
    inv_n = n_ref[1]

    @pl.when(step == 0)
    def _():
        cols_ref[...] = jnp.full(cols_ref.shape, count, F32)
        given, wide = small_ref.shape[1], pl.cdiv(share, 128) * 128
        for f in range(small_ref.shape[0]):
            v = small_ref[f]
            v = jnp.concatenate([v, jnp.zeros((given, wide - share), F32)], axis=1)
            v = jnp.concatenate([v, jnp.zeros((128 - given, wide), F32)], axis=0)
            par_ref[f * share : (f + 1) * share, :] = v.T[:share]

    field_ref[0:REACH] = up_ref[...]
    field_ref[REACH : REACH + rows] = x_ref[...]
    field_ref[REACH + rows :] = dn_ref[...]
    here = pl.multiple_of(step * block, GRP)
    spread_taps(par_ref[pl.ds(here, block), :], pick_ref, e_ref)
    lane = lax.broadcasted_iota(jnp.int32, (GRP, 128), 1)
    for g in range(block // GRP):
        s = pl.ds(g * GRP, GRP)
        acc = conv_rows(field_ref, e_ref, s, rows, False)
        total = None
        for r in range(rows):
            out_ref[r, s, :] = acc[r]
            v = acc[r] * m_ref[r]
            total = v if total is None else total + v
        mean = jnp.sum(total, axis=-1, keepdims=True) * inv_n
        total = None
        for r in range(rows):
            d = acc[r] - mean
            v = d * d * m_ref[r]
            total = v if total is None else total + v
        dev = jnp.sum(total, axis=-1, keepdims=True)
        at = pl.multiple_of(step * block + g * GRP, GRP)
        cols_ref[pl.ds(at, GRP), :] = jnp.where(lane == 0, mean, dev)

    @pl.when(step == pl.num_programs(0) - 1)
    def _():
        st_ref[...] = jnp.full(st_ref.shape, count, F32)
        copies_of(cols_ref[...], st_ref)


def conv_forward(x, up, dn, small, pick, m16, counts, copies, block):
    rows, channels, width = x.shape
    n_fs, given, share = small.shape
    padded = pl.cdiv(channels, 128) * 128
    return pl.pallas_call(
        functools.partial(conv_kernel, share=share),
        grid=(channels // block,),
        in_specs=[
            pl.BlockSpec(memory_space=pltpu.SMEM),
            pl.BlockSpec((rows, block, width), lambda g: (0, g, 0)),
            pl.BlockSpec((REACH, block, width), lambda g: (0, g, 0)),
            pl.BlockSpec((REACH, block, width), lambda g: (0, g, 0)),
            whole((n_fs, given, share)),
            whole((KS, 128, 128)),
            whole((rows, GRP, width)),
        ],
        out_specs=[
            pl.BlockSpec((rows, block, width), lambda g: (0, g, 0)),
            pl.BlockSpec((copies, 16, 128), lambda g: (0, 0, 0)),
            pl.BlockSpec((channels, 128), lambda g: (0, 0)),
        ],
        out_shape=[
            jax.ShapeDtypeStruct((rows, channels, width), F32),
            jax.ShapeDtypeStruct((copies, 16, 128), F32),
            jax.ShapeDtypeStruct((channels, 128), F32),
        ],
        scratch_shapes=[
            pltpu.VMEM((rows + 2 * REACH, block, width), BF16),
            pltpu.VMEM((padded, 128), F32),
            pltpu.VMEM((2, KS, block, 128), BF16),
        ],
        compiler_params=params(),
        cost_estimate=cost(20e9, 12e6),
        name="conv_forward",
    )(counts, x, up, dn, small, pick, m16)


def input_grad_kernel(
    g_ref, up_ref, dn_ref, par_ref, pick_ref, og_ref, m_ref, out_ref, field_ref, e_ref
):
    rows, block = g_ref.shape[0], g_ref.shape[1]
    last = rows + 2 * REACH - 1
    for q in range(REACH):
        field_ref[last - q] = up_ref[q]
        field_ref[REACH - 1 - q] = dn_ref[q]
    for q in range(rows):
        field_ref[last - REACH - q] = g_ref[q]
    spread_taps(par_ref[...], pick_ref, e_ref)
    for g in range(block // GRP):
        s = pl.ds(g * GRP, GRP)
        acc = conv_rows(field_ref, e_ref, s, rows, True)
        for r in range(rows):
            out_ref[r, s, :] = og_ref[r, s, :].astype(F32) * m_ref[r] + acc[r]


def input_gradient(grad, up, dn, par, pick, og, m16, block):
    rows, channels, width = grad.shape
    return pl.pallas_call(
        input_grad_kernel,
        grid=(channels // block,),
        in_specs=[
            pl.BlockSpec((rows, block, width), lambda g: (0, g, 0)),
            pl.BlockSpec((REACH, block, width), lambda g: (0, g, 0)),
            pl.BlockSpec((REACH, block, width), lambda g: (0, g, 0)),
            pl.BlockSpec((block, 128), lambda g: (g, 0)),
            whole((KS, 128, 128)),
            pl.BlockSpec((rows, block, width), lambda g: (0, g, 0)),
            whole((rows, GRP, width)),
        ],
        out_specs=pl.BlockSpec((rows, block, width), lambda g: (0, g, 0)),
        out_shape=jax.ShapeDtypeStruct((rows, channels, width), F32),
        scratch_shapes=[
            pltpu.VMEM((rows + 2 * REACH, block, width), BF16),
            pltpu.VMEM((2, KS, block, 128), BF16),
        ],
        compiler_params=params(),
        cost_estimate=cost(18e9, 15e6),
        name="input_gradient",
    )(grad, up, dn, par, pick, og, m16)


def tap_grad_kernel(x_ref, up_ref, dn_ref, g_ref, out_ref, field_ref, cols_ref, *, share):
    rows, block, width = x_ref.shape
    field_ref[0:REACH] = up_ref[...]
    field_ref[REACH : REACH + rows] = x_ref[...]
    field_ref[REACH + rows :] = dn_ref[...]
    lane = lax.broadcasted_iota(jnp.int32, (GRP, 128), 1)
    own = lax.broadcasted_iota(jnp.int32, (GRP, 128), 0) == lane % GRP
    for g in range(block // GRP):
        s = pl.ds(g * GRP, GRP)
        x = field_ref[:, s, :].reshape((rows + 2 * REACH) * GRP, width)
        fields = jnp.concatenate([x[r * GRP : (r + KS) * GRP] for r in range(rows)], axis=1)
        grads = []
        for j in range(KS):
            moved = [roll_lanes(g_ref[r, s, :], j - REACH) for r in range(rows)]
            grads.append(jnp.concatenate(moved, axis=1))
        grads = jnp.concatenate(grads, axis=0)
        sums = lax.dot_general(grads, fields, NT, preferred_element_type=F32)
        sums = jnp.concatenate([sums, jnp.zeros((KS * GRP, 128 - KS * GRP), F32)], axis=1)
        out = None
        for j in range(KS):
            acc = jnp.where(own, sums[j * GRP : (j + 1) * GRP], 0.0)
            for k in (8, 4, 2, 1):
                acc = acc + pltpu.roll(acc, 128 - k, 1)
            acc = roll_lanes(acc, j)
            out = acc if out is None else jnp.where(lane % GRP == j, acc, out)
        at = pl.multiple_of(pl.program_id(0) * block + g * GRP, GRP)
        cols_ref[pl.ds(at, GRP), :] = out

    @pl.when(pl.program_id(0) == pl.num_programs(0) - 1)
    def _():
        blocks = [cols_ref[k : k + 128, :].T for k in range(0, cols_ref.shape[0], 128)]
        wide = jnp.concatenate(blocks, axis=1)
        taps = jnp.concatenate([wide[GRP * i : GRP * i + KS] for i in range(KS)], axis=0)
        for f in range(out_ref.shape[0]):
            out_ref[f] = taps[:, f * share : (f + 1) * share]


def tap_gradient(x, up, dn, grad, block, share):
    rows, channels, width = x.shape
    padded = pl.cdiv(channels, 128) * 128
    return pl.pallas_call(
        functools.partial(tap_grad_kernel, share=share),
        grid=(channels // block,),
        in_specs=[
            pl.BlockSpec((rows, block, width), lambda g: (0, g, 0)),
            pl.BlockSpec((REACH, block, width), lambda g: (0, g, 0)),
            pl.BlockSpec((REACH, block, width), lambda g: (0, g, 0)),
            pl.BlockSpec((rows, block, width), lambda g: (0, g, 0)),
        ],
        out_specs=pl.BlockSpec((channels // share, TAPS, share), lambda g: (0, 0, 0)),
        out_shape=jax.ShapeDtypeStruct((channels // share, TAPS, share), F32),
        scratch_shapes=[
            pltpu.VMEM((rows + 2 * REACH, block, width), BF16),
            pltpu.VMEM((padded, 128), F32),
        ],
        compiler_params=params(),
        cost_estimate=cost(18e9, 8e6),
        name="tap_gradient",
    )(x, up, dn, grad)


def mask_grad_kernel(og_ref, m_ref, by_chan_ref, by_pixel_ref, sum_ref, cols_ref):
    row = pl.program_id(0)
    channels = og_ref.shape[1]
    v = og_ref[0].astype(F32) * m_ref[0, 0:1]
    by_chan_ref[...] = v.astype(BF16)
    by_pixel_ref[...] = v.T.astype(BF16)
    part = v[:, 0:128]
    for k in range(128, v.shape[1], 128):
        part = part + v[:, k : k + 128]

    @pl.when(row == 0)
    def _():
        cols_ref[...] = jnp.zeros(cols_ref.shape, F32)

    cols_ref[0:channels, :] += part

    @pl.when(row == pl.num_programs(0) - 1)
    def _():
        sums = jnp.broadcast_to(jnp.sum(cols_ref[...], axis=1, keepdims=True), cols_ref.shape)
        copies_of(sums, sum_ref)


def mask_gradient(og, m16):
    rows, channels, width = og.shape
    padded = pl.cdiv(channels, 128) * 128
    pixels = rows * width
    return pl.pallas_call(
        mask_grad_kernel,
        grid=(rows,),
        in_specs=[
            pl.BlockSpec((1, channels, width), lambda r: (r, 0, 0)),
            pl.BlockSpec((1, GRP, width), lambda r: (r, 0, 0)),
        ],
        out_specs=[
            pl.BlockSpec((channels, width), lambda r: (0, r)),
            pl.BlockSpec((width, channels), lambda r: (r, 0)),
            pl.BlockSpec((1, 16, 128), lambda r: (0, 0, 0)),
        ],
        out_shape=[
            jax.ShapeDtypeStruct((channels, pixels), BF16),
            jax.ShapeDtypeStruct((pixels, channels), BF16),
            jax.ShapeDtypeStruct((1, 16, 128), F32),
        ],
        scratch_shapes=[pltpu.VMEM((padded, 128), F32)],
        compiler_params=params(),
        cost_estimate=cost(1e9, 8e6),
        name="mask_gradient",
    )(og, m16)


def activate_kernel(conv_ref, all_ref, par_ref, by_chan_ref, by_pixel_ref, stat_ref, cols_ref):
    channels = conv_ref.shape[1]

    @pl.when(pl.program_id(0) == 0)
    def _():
        means, squares = all_ref[:, 0:8, :], all_ref[:, 8:16, :]
        counts = all_ref[:, 7:8, :]
        count = jnp.sum(counts, axis=0)
        mean = jnp.sum(counts * means, axis=0) / count
        apart = means - mean[None]
        variance = jnp.sum(squares + counts * apart * apart, axis=0) / count
        inv_std = lax.rsqrt(variance + EPS)
        stat_ref[0:8] = mean
        stat_ref[8:16] = inv_std
        stat_ref[16:24] = jnp.sqrt(variance + EPS)
        stat_ref[24:32] = jnp.broadcast_to(count, (8, 128))
        cols_ref[...] = columns_of(mean[0:7], inv_std[0:7])[: cols_ref.shape[0]]

    c, p = cols_ref[0:channels, :], par_ref[...]
    v = (conv_ref[0] - c[:, 0:1]) * (c[:, 1:2] * p[:, TAPS : TAPS + 1]) + p[:, TAPS + 1 : TAPS + 2]
    by_chan_ref[...] = v.astype(BF16)
    by_pixel_ref[...] = v.T.astype(BF16)


def activate(conv, stats, par):
    rows, channels, width = conv.shape
    pixels = rows * width
    padded = pl.cdiv(channels, 128) * 128
    return pl.pallas_call(
        activate_kernel,
        grid=(rows,),
        in_specs=[
            pl.BlockSpec((1, channels, width), lambda r: (r, 0, 0)),
            whole(stats.shape),
            whole(par.shape),
        ],
        out_specs=[
            pl.BlockSpec((channels, width), lambda r: (0, r)),
            pl.BlockSpec((width, channels), lambda r: (r, 0)),
            pl.BlockSpec((32, 128), lambda r: (0, 0)),
        ],
        out_shape=[
            jax.ShapeDtypeStruct((channels, pixels), BF16),
            jax.ShapeDtypeStruct((pixels, channels), BF16),
            jax.ShapeDtypeStruct((32, 128), F32),
        ],
        scratch_shapes=[pltpu.VMEM((padded, 128), F32)],
        compiler_params=params(),
        cost_estimate=cost(1e9, 10e6),
        name="activate",
    )(conv, stats, par)


def gelu_parts(v):
    v2 = v * v
    t = jnp.tanh(v * (GELU_A + (GELU_A * GELU_B) * v2))
    s = 0.5 * t + 0.5
    h = v * s
    return h, s + h * (1.0 - s) * (2 * GELU_A + (6 * GELU_A * GELU_B) * v2)


def hidden_kernel(
    act_p, act_c, bg_p, bg_c, we_ref, wp_ref, eb_ref, h_ref, g_ref, dwp_ref, dwe_ref, ebg_ref, *, step
):
    we, wp, bias = we_ref[...], wp_ref[...], eb_ref[...]
    total = None
    for p in range(0, act_p.shape[0], step):
        pre = jnp.dot(act_p[p : p + step, :], we, preferred_element_type=F32) + bias
        pull = jnp.dot(bg_p[p : p + step, :], wp, preferred_element_type=F32)
        h, slope = gelu_parts(pre)
        grad = (pull * slope).astype(BF16)
        h_ref[p : p + step, :] = h.astype(BF16)
        g_ref[p : p + step, :] = grad
        part = jnp.sum(grad.astype(F32), axis=0, keepdims=True)
        total = part if total is None else total + part
    ebg_ref[...] = total
    dwp_ref[...] = jnp.dot(bg_c[...], h_ref[...], preferred_element_type=F32).astype(dwp_ref.dtype)
    dwe_ref[...] = jnp.dot(act_c[...], g_ref[...], preferred_element_type=F32).astype(dwe_ref.dtype)


def hidden_layer(act_p, act_c, bg_p, bg_c, we, wp, eb, first, units, dtype):
    pixels, channels = act_p.shape
    steps = pl.cdiv(units, TILE)
    off = first // TILE
    weight = pl.BlockSpec((channels, TILE), lambda g: (0, g + off))
    return pl.pallas_call(
        functools.partial(hidden_kernel, step=pixels // 3),
        grid=(steps,),
        in_specs=[
            whole((pixels, channels)),
            whole((channels, pixels)),
            whole((pixels, channels)),
            whole((channels, pixels)),
            weight,
            weight,
            pl.BlockSpec((1, TILE), lambda g: (0, g + off)),
        ],
        out_specs=[
            pl.BlockSpec((pixels, TILE), lambda g: (0, g)),
            pl.BlockSpec((pixels, TILE), lambda g: (0, g)),
            pl.BlockSpec((channels, TILE), lambda g: (0, g)),
            pl.BlockSpec((channels, TILE), lambda g: (0, g)),
            pl.BlockSpec((1, TILE), lambda g: (0, g)),
        ],
        out_shape=[
            jax.ShapeDtypeStruct((pixels, units), BF16),
            jax.ShapeDtypeStruct((pixels, units), BF16),
            jax.ShapeDtypeStruct((channels, units), dtype),
            jax.ShapeDtypeStruct((channels, units), dtype),
            jax.ShapeDtypeStruct((1, units), F32),
        ],
        compiler_params=params(),
        cost_estimate=cost(8 * pixels * channels * units, 20e6, pixels * units),
        name="hidden_layer",
    )(act_p, act_c, bg_p, bg_c, we, wp, eb)


def contract(weights, hiddens):
    total = None
    for (w_ref, first, units), h_ref in zip(weights, hiddens, strict=True):
        part = lax.dot_general(
            w_ref[:, first : first + units], h_ref[...], NT, preferred_element_type=F32
        )
        total = part if total is None else total + part
    return total


def act_grad_kernel(*refs, cuts):
    n = len(cuts)
    w_refs, h_refs = refs[0:2], refs[2 : 2 + n]
    conv_ref, stat_ref, out_ref, sum_ref, cols_ref, acc_ref = refs[2 + n :]
    channels = conv_ref.shape[1]
    row = pl.program_id(0)

    @pl.when(row == 0)
    def _():
        cols_ref[...] = columns_of(stat_ref[0:7], stat_ref[8:15])[: cols_ref.shape[0]]
        acc_ref[...] = jnp.zeros(acc_ref.shape, F32)

    grad = contract([(w_refs[w], first, units) for w, first, units in cuts], h_refs)
    out_ref[0] = grad
    c = cols_ref[0:channels, :]
    scaled = grad * ((conv_ref[0] - c[:, 0:1]) * c[:, 1:2])
    plain, weighted = grad[:, 0:128], scaled[:, 0:128]
    for k in range(128, grad.shape[1], 128):
        plain = plain + grad[:, k : k + 128]
        weighted = weighted + scaled[:, k : k + 128]
    acc_ref[0, 0:channels, :] += plain
    acc_ref[1, 0:channels, :] += weighted

    @pl.when(row == pl.num_programs(0) - 1)
    def _():
        lane = lax.broadcasted_iota(jnp.int32, cols_ref.shape, 1)
        plain = jnp.sum(acc_ref[0], axis=1, keepdims=True)
        weighted = jnp.sum(acc_ref[1], axis=1, keepdims=True)
        sum_ref[...] = jnp.zeros(sum_ref.shape, F32)
        copies_of(jnp.where(lane == 0, plain, weighted), sum_ref)


def activation_gradient(weights, hiddens, cuts, conv, stat, copies):
    rows, channels, width = conv.shape
    padded = pl.cdiv(channels, 128) * 128
    return pl.pallas_call(
        functools.partial(act_grad_kernel, cuts=cuts),
        grid=(rows,),
        in_specs=[whole(w.shape) for w in weights]
        + [pl.BlockSpec((width, h.shape[1]), lambda r: (r, 0)) for h in hiddens]
        + [pl.BlockSpec((1, channels, width), lambda r: (r, 0, 0)), whole(stat.shape)],
        out_specs=[
            pl.BlockSpec((1, channels, width), lambda r: (r, 0, 0)),
            pl.BlockSpec((copies, 16, 128), lambda r: (0, 0, 0)),
        ],
        out_shape=[
            jax.ShapeDtypeStruct((rows, channels, width), F32),
            jax.ShapeDtypeStruct((copies, 16, 128), F32),
        ],
        scratch_shapes=[pltpu.VMEM((padded, 128), F32), pltpu.VMEM((2, padded, 128), F32)],
        compiler_params=params(),
        cost_estimate=cost(8e9, 25e6),
        name="activation_gradient",
    )(*weights, *hiddens, conv, stat)


def block_out_kernel(*refs, cuts):
    n = len(cuts)
    w_refs, h_refs = refs[0:2], refs[2 : 2 + n]
    x_ref, m_ref, par_ref, out_ref = refs[2 + n :]
    branch = contract([(w_refs[w], first, units) for w, first, units in cuts], h_refs)
    branch = branch + par_ref[:, TAPS + 2 : TAPS + 3]
    out_ref[0] = ((x_ref[0].astype(F32) + branch) * m_ref[0, 0:1]).astype(BF16)


def block_output(weights, hiddens, cuts, x, m16, par):
    rows, channels, width = x.shape
    return pl.pallas_call(
        functools.partial(block_out_kernel, cuts=cuts),
        grid=(rows,),
        in_specs=[whole(w.shape) for w in weights]
        + [pl.BlockSpec((width, h.shape[1]), lambda r: (r, 0)) for h in hiddens]
        + [
            pl.BlockSpec((1, channels, width), lambda r: (r, 0, 0)),
            pl.BlockSpec((1, GRP, width), lambda r: (r, 0, 0)),
            whole(par.shape),
        ],
        out_specs=pl.BlockSpec((1, channels, width), lambda r: (r, 0, 0)),
        out_shape=jax.ShapeDtypeStruct((rows, channels, width), BF16),
        compiler_params=params(),
        cost_estimate=cost(8e9, 22e6),
        name="block_output",
    )(*weights, *hiddens, x, m16, par)


def conv_grad_kernel(da_ref, conv_ref, m_ref, all_ref, stat_ref, par_ref, out_ref, sum_ref, cols_ref):
    channels = conv_ref.shape[1]

    @pl.when(pl.program_id(0) == 0)
    def _():
        sums = jnp.sum(all_ref[...], axis=0)
        sum_ref[...] = sums
        count = stat_ref[24:32]
        cols_ref[...] = columns_of(
            stat_ref[0:7], stat_ref[8:15], (sums[0:8] / count)[0:7], (sums[8:16] / count)[0:7]
        )[: cols_ref.shape[0]]

    c = cols_ref[0:channels, :]
    normalized = (conv_ref[0] - c[:, 0:1]) * c[:, 1:2]
    correction = m_ref[0, 0:1] * (c[:, 2:3] + normalized * c[:, 3:4])
    factor = c[:, 1:2] * par_ref[:, TAPS : TAPS + 1]
    out_ref[0] = (factor * (da_ref[0] - correction)).astype(BF16)


def conv_gradient(da, conv, m16, sums, stat, par):
    rows, channels, width = conv.shape
    padded = pl.cdiv(channels, 128) * 128
    return pl.pallas_call(
        conv_grad_kernel,
        grid=(rows,),
        in_specs=[
            pl.BlockSpec((1, channels, width), lambda r: (r, 0, 0)),
            pl.BlockSpec((1, channels, width), lambda r: (r, 0, 0)),
            pl.BlockSpec((1, GRP, width), lambda r: (r, 0, 0)),
            whole(sums.shape),
            whole(stat.shape),
            whole(par.shape),
        ],
        out_specs=[
            pl.BlockSpec((1, channels, width), lambda r: (r, 0, 0)),
            pl.BlockSpec((16, 128), lambda r: (0, 0)),
        ],
        out_shape=[
            jax.ShapeDtypeStruct((rows, channels, width), BF16),
            jax.ShapeDtypeStruct((16, 128), F32),
        ],
        scratch_shapes=[pltpu.VMEM((padded, 128), F32)],
        compiler_params=params(),
        cost_estimate=cost(1e9, 12e6),
        name="conv_gradient",
    )(da, conv, m16, sums, stat, par)


def halo(field):
    size = lax.axis_size("dp")
    up = [(i, i + 1) for i in range(size - 1)]
    down = [(j, i) for i, j in up]
    return (
        lax.ppermute(field[-REACH:], "dp", up),
        lax.ppermute(field[:REACH], "dp", down),
    )


def after(value, *others):
    return lax.optimization_barrier((value,) + others)[0]


def from_all(values, axis):
    copies = jnp.broadcast_to(values[None], (lax.axis_size(axis),) + values.shape)
    return lax.all_to_all(copies, axis, 0, 0)


def flip_bit(values, axis, bit):
    size = lax.axis_size(axis)
    return lax.ppermute(values, axis, [(i, i ^ (1 << bit)) for i in range(size)])


def bit_of(axis, bit):
    return (lax.axis_index(axis) >> bit) & 1


def gather_step(have, bit, mine):
    other = flip_bit(have, "fsdp", bit)
    dim = lax.axis_size("fsdp").bit_length() - 2 - bit
    first, second = jnp.where(mine, have, other), jnp.where(mine, other, have)
    return jnp.concatenate([first, second], axis=dim)


def scatter_step(have, bit, done):
    bits = lax.axis_size("fsdp").bit_length() - 1
    cols = have.shape[-1]
    if done == 0:
        have = have.reshape((2,) * bits + (-1, cols))
    dim = bits - 1 - bit
    mine = bit_of("fsdp", bit)
    send = lax.dynamic_slice_in_dim(have, 1 - mine, 1, axis=dim).astype(BF16)
    keep = lax.dynamic_slice_in_dim(have, mine, 1, axis=dim)
    have = keep + flip_bit(send, "fsdp", bit).astype(F32)
    return have.reshape(-1, cols) if done == bits - 1 else have


def per_device(
    inputs,
    out_grad,
    ocean_mask,
    rollout_lengths,
    conv_weight,
    norm_gain,
    norm_bias,
    expand_weight,
    expand_bias,
    project_weight,
    project_bias,
):
    channels, rows, width = inputs.shape[1:]
    n_fs, n_dp = lax.axis_size("fsdp"), lax.axis_size("dp")
    devices = ("dp", "fsdp")
    share = conv_weight.shape[0]
    units = expand_weight.shape[1]
    half = pl.cdiv(units // 128, 2) * 128
    bits = list(range(n_fs.bit_length() - 1))
    core = bit_of("dp", 0)
    x = inputs[0].transpose(1, 0, 2)
    og = out_grad[0].transpose(1, 0, 2)
    block = 5 * GRP

    ratio = expand_bias.shape[0] // share
    small = jnp.concatenate(
        [
            conv_weight.T,
            norm_gain[None],
            norm_bias[None],
            project_bias.astype(F32)[None],
            expand_bias.astype(F32).reshape(ratio, share),
        ],
        axis=0,
    )
    small = from_all(small, "fsdp")
    e_bias = jnp.pad(small[:, TAPS + 3 :].reshape(1, units), ((0, 0), (0, 2 * half - units)))
    pick = tap_picker()
    x_up, x_dn = halo(x)

    def columns(weight):
        wide = jnp.pad(weight, ((0, 0), (0, 2 * half - units)))
        mine = lax.dynamic_slice_in_dim(wide, core * half, half, axis=1)
        return mine.reshape((1,) * len(bits) + (share, half))

    we_own, wp_own = columns(expand_weight), columns(project_weight)
    zeros = [bit_of("fsdp", bit) == 0 for bit in bits]
    for n in bits[:-1]:
        we_own = gather_step(we_own, n, zeros[n])
        wp_own = gather_step(wp_own, bits[-1 - n], zeros[-1 - n])
    eb_own = lax.dynamic_slice_in_dim(e_bias, core * half, half, axis=1)
    eb_peer = lax.dynamic_slice_in_dim(e_bias, (1 - core) * half, half, axis=1)

    sample = lax.axis_index("fsdp")
    length = lax.dynamic_index_in_dim(rollout_lengths, sample, keepdims=False)
    live = jnp.where(sample % ROLLOUT < length, 1.0, 0.0).astype(F32)
    weight = live * ocean_mask.astype(F32)
    m16 = jnp.broadcast_to(weight[:, None, :], (rows, GRP, width))
    count_here = jnp.sum(weight)
    counts = jnp.stack([count_here, 1.0 / jnp.maximum(count_here, 1.0)])

    bg_c, bg_p, bg_sum = mask_gradient(og, m16)

    copies = n_fs * n_dp
    ready = after(m16, bg_c, we_own, wp_own)
    conv, stats, par = conv_forward(x, x_up, x_dn, small, pick, ready, counts, copies, block)
    n = bits[-1]
    we_own = gather_step(we_own, n, after(zeros[n], conv)).reshape(channels, half)
    wp_own = gather_step(wp_own, bits[-1 - n], after(zeros[-1 - n], conv)).reshape(channels, half)
    we_peer = flip_bit(we_own, "dp", 0)
    wp_peer = flip_bit(wp_own, "dp", 0)
    stats = lax.all_to_all(stats, devices, 0, 0)
    act_c, act_p, stat = activate(conv, stats, par)

    groups = [[i for i in range(n_dp) if i % 2 == c] for c in range(2)]
    orders = {2: bits[::-1], 3: bits}
    first = half // (2 * TILE) * TILE
    second = half - first
    common = (act_p, act_c, bg_p, bg_c)

    def added(peer, own):
        return {k: own[k] + flip_bit(peer[k], "dp", 0).astype(F32) for k in orders}

    def stage(sums, n):
        return {k: scatter_step(v, orders[k][n], n) for k, v in sums.items()}

    def over_bands(sums):
        return {k: lax.psum(v.astype(BF16), "dp", axis_index_groups=groups) for k, v in sums.items()}

    q1 = hidden_layer(*common, we_peer, wp_peer, eb_peer, 0, first, BF16)
    o1 = hidden_layer(*common, we_own, wp_own, after(eb_own, q1[0]), 0, first, F32)
    s1 = added(q1, o1)
    q2 = hidden_layer(*common, we_peer, wp_peer, after(eb_peer, s1[2], s1[3]), first, second, BF16)
    for n in range(len(bits) - 1):
        s1 = stage(s1, n)
    o2 = hidden_layer(*common, we_own, wp_own, after(eb_own, q2[0], s1[2], s1[3]), first, second, F32)
    s1 = stage(s1, len(bits) - 1)
    s1 = {k: v.astype(BF16) for k, v in s1.items()}

    cuts = ((1, 0, first), (0, 0, first), (1, first, second), (0, first, second))
    parts = (q1, o1, q2, o2)
    s2 = added(q2, o2)
    ready = after(stat, s1[2], s1[3], s2[2], s2[3])
    da, sums = activation_gradient((we_own, we_peer), [p[1] for p in parts], cuts, conv, ready, copies)
    sums = lax.all_to_all(sums, devices, 0, 0)
    s1 = over_bands(s1)
    block_out = block_output(
        (wp_own, wp_peer), [p[0] for p in parts], cuts, x, m16, after(par, da, s2[2], s2[3])
    )
    for n in range(len(bits) - 1):
        s2 = stage(s2, n)
    conv_grad, totals = conv_gradient(da, conv, m16, sums, stat, after(par, block_out, s2[2], s2[3]))
    g_up, g_dn = halo(conv_grad)
    s2 = stage(s2, len(bits) - 1)
    s2 = {k: v.astype(BF16) for k, v in s2.items()}
    tap_local = tap_gradient(x, x_up, x_dn, after(conv_grad, s2[2], s2[3]), block, share)
    s2 = over_bands({k: after(v, s1[2], s1[3]) for k, v in s2.items()})

    eb_o = jnp.concatenate([o1[4], o2[4]], axis=1)
    eb_q = jnp.concatenate([q1[4], q2[4]], axis=1)
    eb_all = jnp.concatenate(
        [jnp.where(core == 0, eb_o, eb_q), jnp.where(core == 0, eb_q, eb_o)], axis=1
    )[0, :units]
    local = jnp.concatenate(
        [
            tap_local,
            bg_sum[0, :8].reshape(-1)[:channels].reshape(n_fs, 1, share),
            eb_all.reshape(n_fs, ratio, share),
        ],
        axis=1,
    )
    local = jnp.sum(lax.all_to_all(local, "fsdp", 0, 0), axis=0)
    input_grad = input_gradient(conv_grad, g_up, g_dn, after(par, tap_local), pick, og, m16, block)
    local = jnp.sum(from_all(local, "dp"), axis=0)

    def joined(which):
        mine = jnp.concatenate([s1[which], after(s2[which], input_grad)], axis=1)
        other = flip_bit(mine, "dp", 0)
        low, high = jnp.where(core == 0, mine, other), jnp.where(core == 0, other, mine)
        return jnp.concatenate([low, high], axis=1)[:, :units].astype(F32)

    project_grad = joined(2)
    expand_grad = joined(3)

    start = lax.axis_index("fsdp") * share
    totals = totals.reshape(2, -1)
    per_channel = lambda v: v.reshape(-1)[:channels]
    return (
        block_out.transpose(1, 0, 2)[None],
        input_grad.transpose(1, 0, 2)[None],
        local[:TAPS].T,
        lax.dynamic_slice_in_dim(totals[1], start, share),
        lax.dynamic_slice_in_dim(totals[0], start, share),
        expand_grad,
        local[TAPS + 1 :].reshape(-1),
        project_grad,
        local[TAPS],
        per_channel(stat[0:8]),
        per_channel(stat[16:24]),
    )


def solution(mesh):
    rows = P("fsdp", None, "dp", None)
    return jax.shard_map(
        per_device,
        mesh=mesh,
        in_specs=(
            rows,
            rows,
            P("dp", None),
            P(),
            P("fsdp", None),
            P("fsdp"),
            P("fsdp"),
            P("fsdp", None),
            P("fsdp"),
            P("fsdp", None),
            P("fsdp"),
        ),
        out_specs=(
            rows,
            rows,
            P("fsdp", None),
            P("fsdp"),
            P("fsdp"),
            P("fsdp", None),
            P("fsdp"),
            P("fsdp", None),
            P("fsdp"),
            P(),
            P(),
        ),
        check_vma=False,
    )
```

time: 394 us -> 362 us (0.919)
  local copies, waits for them, and re-layouts: 66.1 us -> 30.2 us
  blocking collectives: 26.7 us -> 0 us
  Pallas kernels: 159 us -> 180 us
  other arithmetic: 31.1 us -> 35.6 us
    unnamed x83 -> x50, local copies, waits for them, and re-layouts: 36.6 us -> 6.48 us
    psum x1 -> x2, waiting for transfers between devices: 0.01 us -> 29.2 us  [over_bands(): lax.psum(v.astype(BF16), 'dp', axis_index_groups=groups)]
    psum x1 -> x0, blocking collectives: 26.7 us -> none  [per_device(): local = lax.psum(local, 'dp')]
    ppermute x20, waiting for transfers between devices: 38 us -> 11.4 us  [flip_bit(): return lax.ppermute(values, axis, [(i, i ^ 1 << bit) for i in range(size)])]
    add x6 -> x8, other arithmetic: 5.26 us -> 13.5 us  [the longest x4 8.01 us: added(): return {k: own[k] + flip_bit(peer[k], 'dp', 0).astype(F32) for k in orders}]
    all_to_all x3 -> x4, waiting for transfers between devices: 14.3 us -> 9.23 us  [the longest x1 9.22 us: per_device(): stats = lax.all_to_all(stats, devices, 0, 0)]
    pallas_call x4, Pallas kernels: 66.8 us -> 71.6 us  [hidden_layer(): pl.pallas_call(functools.partial(hidden_kernel, step=pixels // 3), grid=(...]
    pallas_call x1, Pallas kernels: 4.82 us -> 9.48 us  [conv_gradient(): pl.pallas_call(conv_grad_kernel, grid=(rows,), in_specs=[pl.BlockSpec((1,...]
  transfers between devices with their start and end apart: 29 -> 31, of which waited for: 9 -> 5; matrix products, arithmetic and copies ran while one was open for 14% -> 16% of each run, Pallas kernels for 36% -> 46%
where the time goes in v2:
time: 362 us; the launch traced here: 360 us
  Pallas kernels  180 us (50%)
  waiting for transfers between devices  53.7 us (15%)
  starting transfers between devices  44.7 us (12%)
  other arithmetic  35.6 us (10%)
  local copies, waits for them, and re-layouts  30.2 us (8%)
  between operations  15.9 us (4%)
    pallas_call x4, Pallas kernels, hidden_layer(): pl.pallas_call(functools.partial(hidden_kernel, step=pixels // 3), grid=(...  71.6 us
    psum x2, waiting for transfers between devices, over_bands(): lax.psum(v.astype(BF16), 'dp', axis_index_groups=groups)  29.2 us
    pallas_call x1, Pallas kernels, conv_forward(): pl.pallas_call(functools.partial(conv_kernel, share=share), grid=(channel...  20 us
    pallas_call x1, Pallas kernels, tap_gradient(): pl.pallas_call(functools.partial(tap_grad_kernel, share=share), grid=(cha...  17.7 us
    pallas_call x1, Pallas kernels, input_gradient(): pl.pallas_call(input_grad_kernel, grid=(channels // block,), in_specs=[pl...  16.3 us
    pallas_call x1, Pallas kernels, activation_gradient(): pl.pallas_call(functools.partial(act_grad_kernel, cuts=cuts), grid=(rows,...  16.1 us
    ppermute x20, starting transfers between devices, flip_bit(): return lax.ppermute(values, axis, [(i, i ^ 1 << bit) for i in range(size)])  14.9 us
    pallas_call x1, Pallas kernels, block_output(): pl.pallas_call(functools.partial(block_out_kernel, cuts=cuts), grid=(rows...  14.7 us
  transfers between devices with their start and end apart: 31, of which 5 were waited for; matrix products, arithmetic and copies ran while one was open for 16% of the time, Pallas kernels for 46%

profile of v2, /device:TPU:0, one launch (start us, length us, event | category | flops | bytes accessed | tf_op | source)
XLA Modules:
  0.0 360.1 jit_solution(3868392950061264421)
XLA Ops:
  8.7 1.5 concatenate.71
  11.0 5.2 %all-to-all-start = ((f32[4,56,200]{2,1,0:T(8,128)}), f32[4,56,200]{2,1,0:T(8,128)}, u32[]{:S(2)}, u32[]{:S(2)}) async-start(f32[4,56,200]{2,1,0:T(8,128)} %broadcast_in_dim.48), calls=%async_computation | async-start | bytes 458752 | tf_op jit(solution)/shard_map/all_to_all | solution.py:611
  17.4 2.1 collective-permute-start.3
  20.4 1.5 collective-permute-start.2
  21.9 1.6 fusion.12
  24.8 4.1 %collective-permute-start = (bf16[3,800,256]{2,1,0:T(8,128)(2,1)}, bf16[3,800,256]{2,1,0:T(8,128)(2,1)}, u32[]{:S(2)}, u32[]{:S(2)}) collective-permute-start(bf16[3,800,256]{2,1,0:T(8,128)(2,1)} %get-tuple-element.120), channel_id=1, source_target_pairs={{0,4},{4,8},{8,12},{12,16},{16,20},{20,24},{24,28},{1,5},{5,9},{9,... | collective-permute-start | bytes 3686408 | tf_op jit(solution)/shard_map/ppermute | solution.py:600
  32.0 6.4 %mask_gradient.1 = (bf16[800,1536]{1,0:T(8,128)(2,1)}, bf16[1536,800]{1,0:T(8,128)(2,1)}, f32[1,16,128]{2,1,0:T(8,128)}) custom-call(bf16[6,800,256]{2,1,0:T(8,128)(2,1)} %bitcast.81, f32[6,16,256]{2,1,0:T(8,128)} %broadcast_in_dim.51.m_ref.refs_7_), custom_call_target="tpu_custom_call" | custom-call | flops 1000000000 | bytes 8000000 | tf_op jit(solution)/shard_map/mask_gradient/pallas_call | solution.py:311
  40.5 1.3 broadcast_select_fusion.9
  45.7 20.0 %conv_forward.1 = (f32[6,800,256]{2,1,0:T(8,128)}, f32[32,16,128]{2,1,0:T(8,128)}, f32[800,128]{1,0:T(8,128)}) custom-call(f32[2]{0:T(128)} %pad_maximum_fusion.8.n_ref, bf16[6,800,256]{2,1,0:T(8,128)(2,1)} %bitcast.69, bf16[3,800,256]{2,1,0:T(8,128)(2,1)} %collective-permute-done.up_ref, bf16[3,800,256]{2,1,0:T(8,128)(2,1)} %collective-permute-done.1.dn_ref, ...), custom_call_target="tpu_custom_call" | custom-call | flops 20000000000 | bytes 12000000 | tf_op jit(solution)/shard_map/conv_forward/pallas_call | solution.py:147
  65.7 9.3 %collective-permute-done.4 = bf16[2,1,200,1664]{3,2,1,0:T(8,128)(2,1)} collective-permute-done((bf16[2,1,200,1664]{3,2,1,0:T(8,128)(2,1)}, bf16[2,1,200,1664]{3,2,1,0:T(8,128)(2,1)}, u32[]{:S(2)}, u32[]{:S(2)}) %collective-permute-start.4) | collective-permute-done | bytes 1331232 | tf_op jit(solution)/shard_map/ppermute | solution.py:616
  75.0 1.6 broadcast_select_fusion.3
  76.6 1.8 pad_maximum_fusion
  78.4 1.6 broadcast_select_fusion.1
  80.9 3.2 all-to-all-start.1
  85.8 9.2 %all-to-all-done.1.all_ref = f32[32,16,128]{2,1,0:T(8,128)S(1)} async-done(((f32[32,16,128]{2,1,0:T(8,128)}), f32[32,16,128]{2,1,0:T(8,128)S(1)}, u32[]{:S(2)}, u32[]{:S(2)}) %all-to-all-start.1) | async-done | bytes 262176 | tf_op jit(solution)/shard_map/all_to_all | solution.py:715
  95.7 7.8 %activate.1 = (bf16[800,1536]{1,0:T(8,128)(2,1)}, bf16[1536,800]{1,0:T(8,128)(2,1)}, f32[32,128]{1,0:T(8,128)}) custom-call(f32[6,800,256]{2,1,0:T(8,128)} %get-tuple-element.61.conv_ref.refs_6_, f32[32,16,128]{2,1,0:T(8,128)} %copy-done.14, f32[800,128]{1,0:T(8,128)} %get-tuple-element.96.par_ref.refs_8_), custom_call_target="tpu_custom_call" | custom-call | flops 1000000000 | bytes 10000000 | tf_op jit(solution)/shard_map/activate/pallas_call | solution.py:363
  103.6 15.9 %hidden_layer.4 = (bf16[1536,768]{1,0:T(8,128)(2,1)}, bf16[1536,768]{1,0:T(8,128)(2,1)}, bf16[800,768]{1,0:T(8,128)(2,1)}, bf16[800,768]{1,0:T(8,128)(2,1)}, f32[1,768]{1,0:T(1,128)}) custom-call(bf16[1536,800]{1,0:T(8,128)(2,1)} %get-tuple-element.65.act_p, bf16[800,1536]{1,0:T(8,128)(2,1)} %get-tuple-element.66.act_c, ...), custom_call_target="tpu_custom_call" | custom-call | flops 7549747200 | bytes 20000000 | tf_op jit(solution)/shard_map/hidden_layer/pallas_call | solution.py:420
  120.8 16.1 %hidden_layer.5 = (bf16[1536,768]{1,0:T(8,128)(2,1)}, bf16[1536,768]{1,0:T(8,128)(2,1)}, f32[800,768]{1,0:T(8,128)}, f32[800,768]{1,0:T(8,128)}, f32[1,768]{1,0:T(1,128)}) custom-call(bf16[1536,800]{1,0:T(8,128)(2,1)} %get-tuple-element.65.act_p, bf16[800,1536]{1,0:T(8,128)(2,1)} %get-tuple-element.66.act_c, bf16[1536,800]{1,0:T(8,128)(2,1)} %get-tuple-element.67.bg_p, ...), custom_call_target="tpu_custom_call" | custom-call | flops 7549747200 | bytes 20000000 | tf_op jit(solution)/shard_map/hidden_layer/pallas_call | solution.py:420
  137.7 2.1 convert_add_fusion.3
  140.1 1.7 convert_add_fusion.2
  141.8 1.4 copy-done.1
  145.3 19.7 %hidden_layer.6 = (bf16[1536,896]{1,0:T(8,128)(2,1)}, bf16[1536,896]{1,0:T(8,128)(2,1)}, bf16[800,896]{1,0:T(8,128)(2,1)}, bf16[800,896]{1,0:T(8,128)(2,1)}, f32[1,896]{1,0:T(1,128)}) custom-call(bf16[1536,800]{1,0:T(8,128)(2,1)} %get-tuple-element.65.act_p, bf16[800,1536]{1,0:T(8,128)(2,1)} %get-tuple-element.66.act_c, ...), custom_call_target="tpu_custom_call" | custom-call | flops 8808038400 | bytes 20000000 | tf_op jit(solution)/shard_map/hidden_layer/pallas_call | solution.py:420
  166.3 1.3 convert_add_fusion.7
  170.5 1.8 collective-permute-start.13
  172.3 19.8 %hidden_layer.7 = (bf16[1536,896]{1,0:T(8,128)(2,1)}, bf16[1536,896]{1,0:T(8,128)(2,1)}, f32[800,896]{1,0:T(8,128)}, f32[800,896]{1,0:T(8,128)}, f32[1,896]{1,0:T(1,128)}) custom-call(bf16[1536,800]{1,0:T(8,128)(2,1)} %get-tuple-element.65.act_p, bf16[800,1536]{1,0:T(8,128)(2,1)} %get-tuple-element.66.act_c, bf16[1536,800]{1,0:T(8,128)(2,1)} %get-tuple-element.67.bg_p, ...), custom_call_target="tpu_custom_call" | custom-call | flops 8808038400 | bytes 20000000 | tf_op jit(solution)/shard_map/hidden_layer/pallas_call | solution.py:420
  194.7 2.6 convert_add_fusion.1
  198.7 1.7 convert_add_fusion
  200.4 16.1 %activation_gradient.1 = (f32[6,800,256]{2,1,0:T(8,128)}, f32[32,16,128]{2,1,0:T(8,128)}) custom-call(bf16[800,1664]{1,0:T(8,128)(2,1)} %bitcast.68, bf16[800,1664]{1,0:T(8,128)(2,1)} %collective-permute-done.7.we_ref.refs_1_, bf16[1536,768]{1,0:T(8,128)(2,1)} %get-tuple-element.80.refs_2_, bf16[1536,768]{1,0:T(8,128)(2,1)} %get-tuple-element.81.refs_3_, ...), custom_call_target="tpu_custom_call" | custom-call | flops 8000000000 | bytes 25000000 | tf_op jit(solution)/shard_map/activation_gradient/pallas_call | solution.py:497
  216.6 3.0 all-to-all-start.2
  220.5 1.8 collective-permute-start.17
  222.3 14.7 %block_output.1 = bf16[6,800,256]{2,1,0:T(8,128)(2,1)} custom-call(bf16[800,1664]{1,0:T(8,128)(2,1)} %bitcast.14.wp_ref.refs_0_, bf16[800,1664]{1,0:T(8,128)(2,1)} %collective-permute-done.5.wp_ref.refs_1_, bf16[1536,768]{1,0:T(8,128)(2,1)} %get-tuple-element.69.refs_2_, bf16[1536,768]{1,0:T(8,128)(2,1)} %get-tuple-element.71.refs_3_, ...), custom_call_target="tpu_custom_call" | custom-call | flops 8000000000 | bytes 22000000 | tf_op jit(solution)/shard_map/block_output/pallas_call | solution.py:529
  237.0 1.7 convert_add_fusion.5
  239.0 2.1 collective-permute-done.17
  243.4 1.6 collective-permute-start.21
  245.7 9.5 %conv_gradient.1 = (bf16[6,800,256]{2,1,0:T(8,128)(2,1)}, f32[16,128]{1,0:T(8,128)}) custom-call(f32[6,800,256]{2,1,0:T(8,128)} %get-tuple-element.90.da_ref, f32[6,800,256]{2,1,0:T(8,128)} %get-tuple-element.61.conv_ref.refs_6_, f32[6,16,256]{2,1,0:T(8,128)} %broadcast_in_dim.51.m_ref.refs_7_, f32[32,16,128]{2,1,0:T(8,128)} %copy-done.15, ...), custom_call_target="tpu_custom_call" | custom-call | flops 1000000000 | bytes 12000000 | tf_op jit(solution)/shard_map/conv_gradient/pallas_call | solution.py:569
  255.2 3.0 fusion.11
  258.1 1.4 collective-permute-start.19
  259.5 4.1 %collective-permute-start.18 = (bf16[3,800,256]{2,1,0:T(8,128)(2,1)S(1)}, bf16[3,800,256]{2,1,0:T(8,128)(2,1)}, u32[]{:S(2)}, u32[]{:S(2)}) collective-permute-start(bf16[3,800,256]{2,1,0:T(8,128)(2,1)S(1)} %get-tuple-element.118), channel_id=1, source_target_pairs={{0,4},{4,8},{8,12},{12,16},{16,20},{20,24},{24,28},{1,5},{5,9},{9,... | collective-permute-start | bytes 3686408 | tf_op jit(solution)/shard_map/ppermute | solution.py:600
  263.6 1.8 fusion.5
  266.2 17.7 %tap_gradient.1 = f32[4,49,200]{2,1,0:T(8,128)} custom-call(bf16[6,800,256]{2,1,0:T(8,128)(2,1)} %bitcast.71, bf16[3,800,256]{2,1,0:T(8,128)(2,1)} %collective-permute-done.up_ref, bf16[3,800,256]{2,1,0:T(8,128)(2,1)} %collective-permute-done.1.dn_ref, bf16[6,800,256]{2,1,0:T(8,128)(2,1)} %get-tuple-element.95.g_ref), custom_call_target="tpu_custom_call" | custom-call | flops 17999998976 | bytes 8000000 | tf_op jit(solution)/shard_map/tap_gradient/pallas_call | solution.py:264
  283.9 1.6 pad_maximum_fusion.6
  285.6 3.4 all-to-all-start.3
  290.6 3.8 %all-to-all-done.3 = f32[4,54,200]{2,1,0:T(8,128)S(1)} async-done(((f32[4,54,200]{2,1,0:T(8,128)}), f32[4,54,200]{2,1,0:T(8,128)S(1)}, u32[]{:S(2)}, u32[]{:S(2)}) %all-to-all-start.3) | async-done | bytes 172832 | tf_op jit(solution)/shard_map/all_to_all | solution.py:775
  295.2 4.0 %all-to-all-start.4 = ((f32[8,54,200]{2,1,0:T(8,128)}), f32[8,54,200]{2,1,0:T(8,128)S(1)}, u32[]{:S(2)}, u32[]{:S(2)}) async-start(f32[8,54,200]{2,1,0:T(8,128)} %broadcast_in_dim.54), calls=%async_computation.4 | async-start | bytes 917504 | tf_op jit(solution)/shard_map/all_to_all | solution.py:611
  299.2 16.3 %input_gradient.1 = f32[6,800,256]{2,1,0:T(8,128)} custom-call(bf16[6,800,256]{2,1,0:T(8,128)(2,1)} %get-tuple-element.95.g_ref, bf16[3,800,256]{2,1,0:T(8,128)(2,1)} %collective-permute-done.18.up_ref, bf16[3,800,256]{2,1,0:T(8,128)(2,1)} %collective-permute-done.19.dn_ref, f32[800,128]{1,0:T(8,128)} %get-tuple-element.96.par_ref.refs_8_, ...), custom_call_target="tpu_custom_call" | custom-call | flops 17999998976 | bytes 15000000 | tf_op jit(solution)/shard_map/input_gradient/pallas_call | solution.py:200
  315.6 29.2 %all-reduce.8.cloned.1.call-done = (bf16[200,896]{1,0:T(8,128)(2,1)}, bf16[200,896]{1,0:T(8,128)(2,1)}) async-done(((bf16[200,896]{1,0:T(8,128)(2,1)}, bf16[200,896]{1,0:T(8,128)(2,1)}), (bf16[200,896]{1,0:T(8,128)(2,1)}, bf16[200,896]{1,0:T(8,128)(2,1)})) %all-reduce.8.cloned.1.call-update) | async-done | bytes 716816 | tf_op jit(solution)/shard_map/psum | solution.py:731
  349.9 1.6 fusion
  351.6 1.6 fusion.1
  (149 shorter events, 41.9 us)
Async XLA Ops:
  7.2 12.3 %copy-start.4 = (bf16[200,3200]{1,0:T(8,128)(2,1)S(1)}, bf16[200,3200]{1,0:T(8,128)(2,1)}, u32[]{:S(2)}) copy-start(bf16[200,3200]{1,0:T(8,128)(2,1)} %param.18) | copy-start | bytes 3840004
  11.0 34.7 %all-to-all-start = ((f32[4,56,200]{2,1,0:T(8,128)}), f32[4,56,200]{2,1,0:T(8,128)}, u32[]{:S(2)}, u32[]{:S(2)}) async-start(f32[4,56,200]{2,1,0:T(8,128)} %broadcast_in_dim.48), calls=%async_computation | async-start | bytes 458752 | tf_op jit(solution)/shard_map/all_to_all | solution.py:611
  16.1 5.7 %copy-start.12 = (bf16[1,800,6,256]{3,1,2,0:T(8,128)(2,1)S(1)}, bf16[1,800,6,256]{3,1,2,0:T(8,128)(2,1)}, u32[]{:S(2)}) copy-start(bf16[1,800,6,256]{3,1,2,0:T(8,128)(2,1)} %param.11) | copy-start | bytes 7372804
  17.4 23.1 %collective-permute-start.3 = (bf16[1,1,200,1664]{3,2,1,0:T(8,128)(2,1)S(1)}, bf16[1,1,200,1664]{3,2,1,0:T(8,128)(2,1)}, u32[]{:S(2)}, u32[]{:S(2)}) collective-permute-start(bf16[1,1,200,1664]{3,2,1,0:T(8,128)(2,1)S(1)} %fusion.3), channel_id=1, source_target_pairs={{0,2},{1,3},{2,0},{3,1},{4,6},{5,7},{6,4},{7,5},{8,10},{9,11},{10,... | collective-permute-start | bytes 1996808 | tf_op jit(solution)/shard_map/ppermute | solution.py:616
  20.4 23.2 %collective-permute-start.2 = (bf16[1,1,200,1664]{3,2,1,0:T(8,128)(2,1)}, bf16[1,1,200,1664]{3,2,1,0:T(8,128)(2,1)S(1)}, u32[]{:S(2)}, u32[]{:S(2)}) collective-permute-start(bf16[1,1,200,1664]{3,2,1,0:T(8,128)(2,1)} %fusion.2), channel_id=1, source_target_pairs={{0,1},{1,0},{2,3},{3,2},{4,5},{5,4},{6,7},{7,6},{8,9},{9,8},{10,11... | collective-permute-start | bytes 1996808 | tf_op jit(solution)/shard_map/ppermute | solution.py:616
  21.9 7.0 %copy-start.22 = (s32[4]{0:T(128)S(1)}, s32[4]{0:T(128)}, u32[]{:S(2)}) copy-start(s32[4]{0:T(128)} %param.14) | copy-start | bytes 52
  21.9 8.2 %copy-start.19 = (s32[6,256]{1,0:T(8,128)S(1)}, s32[6,256]{1,0:T(8,128)}, u32[]{:S(2)}) copy-start(s32[6,256]{1,0:T(8,128)} %param.13) | copy-start | bytes 18436
  23.5 22.2 %collective-permute-start.1 = (bf16[3,800,256]{2,1,0:T(8,128)(2,1)}, bf16[3,800,256]{2,1,0:T(8,128)(2,1)}, u32[]{:S(2)}, u32[]{:S(2)}) collective-permute-start(bf16[3,800,256]{2,1,0:T(8,128)(2,1)} %get-tuple-element.119), channel_id=1, source_target_pairs={{4,0},{8,4},{12,8},{16,12},{20,16},{24,20},{28,24},{5,1},{9,5},{13... | collective-permute-start | bytes 3686408 | tf_op jit(solution)/shard_map/ppermute | solution.py:601
  24.8 20.9 %collective-permute-start = (bf16[3,800,256]{2,1,0:T(8,128)(2,1)}, bf16[3,800,256]{2,1,0:T(8,128)(2,1)}, u32[]{:S(2)}, u32[]{:S(2)}) collective-permute-start(bf16[3,800,256]{2,1,0:T(8,128)(2,1)} %get-tuple-element.120), channel_id=1, source_target_pairs={{0,4},{4,8},{8,12},{12,16},{16,20},{20,24},{24,28},{1,5},{5,9},{9,... | collective-permute-start | bytes 3686408 | tf_op jit(solution)/shard_map/ppermute | solution.py:600
  32.0 8.4 %copy-start.3 = (bf16[200,3200]{1,0:T(8,128)(2,1)S(1)}, bf16[200,3200]{1,0:T(8,128)(2,1)}, u32[]{:S(2)}) copy-start(bf16[200,3200]{1,0:T(8,128)(2,1)} %param.20) | copy-start | bytes 3840004
  43.0 31.9 %collective-permute-start.4 = (bf16[2,1,200,1664]{3,2,1,0:T(8,128)(2,1)}, bf16[2,1,200,1664]{3,2,1,0:T(8,128)(2,1)}, u32[]{:S(2)}, u32[]{:S(2)}) collective-permute-start(bf16[2,1,200,1664]{3,2,1,0:T(8,128)(2,1)} %pad_maximum_fusion.3), channel_id=1, source_target_pairs={{0,1},{1,0},{2,3},{3,2},{4,5},{5,4},{6,7},{7,6},{8,9},{9,8},{10,11... | collective-permute-start | bytes 3993608 | tf_op jit(solution)/shard_map/ppermute | solution.py:616
  45.1 33.3 %collective-permute-start.6 = (bf16[1,2,200,1664]{3,2,1,0:T(8,128)(2,1)}, bf16[1,2,200,1664]{3,2,1,0:T(8,128)(2,1)}, u32[]{:S(2)}, u32[]{:S(2)}) collective-permute-start(bf16[1,2,200,1664]{3,2,1,0:T(8,128)(2,1)} %pad_maximum_fusion.2), channel_id=1, source_target_pairs={{0,2},{1,3},{2,0},{3,1},{4,6},{5,7},{6,4},{7,5},{8,10},{9,11},{10,... | collective-permute-start | bytes 3993608 | tf_op jit(solution)/shard_map/ppermute | solution.py:616
  78.4 25.1 %collective-permute-start.5 = (bf16[800,1664]{1,0:T(8,128)(2,1)}, bf16[800,1664]{1,0:T(8,128)(2,1)}, u32[]{:S(2)}, u32[]{:S(2)}) collective-permute-start(bf16[800,1664]{1,0:T(8,128)(2,1)} %bitcast.14.wp_ref.refs_0_), channel_id=1, source_target_pairs={{0,4},{4,0},{8,12},{12,8},{16,20},{20,16},{24,28},{28,24},{1,5},{5... | collective-permute-start | bytes 7987208 | tf_op jit(solution)/shard_map/ppermute | solution.py:616
  80.3 23.3 %copy-start.11 = (bf16[2,2,200,1664]{3,2,1,0:T(8,128)(2,1)}, bf16[2,2,200,1664]{3,2,1,0:T(8,128)(2,1)S(1)}, u32[]{:S(2)}) copy-start(bf16[2,2,200,1664]{3,2,1,0:T(8,128)(2,1)S(1)} %pad_maximum_fusion.1) | copy-start | bytes 7987204
  80.3 23.2 %collective-permute-start.7 = (bf16[800,1664]{1,0:T(8,128)(2,1)S(1)}, bf16[800,1664]{1,0:T(8,128)(2,1)}, u32[]{:S(2)}, u32[]{:S(2)}) collective-permute-start(bf16[800,1664]{1,0:T(8,128)(2,1)S(1)} %bitcast.65), channel_id=1, source_target_pairs={{0,4},{4,0},{8,12},{12,8},{16,20},{20,16},{24,28},{28,24},{1,5},{5... | collective-permute-start | bytes 7987208 | tf_op jit(solution)/shard_map/ppermute | solution.py:616
  80.9 14.1 %all-to-all-start.1 = ((f32[32,16,128]{2,1,0:T(8,128)}), f32[32,16,128]{2,1,0:T(8,128)S(1)}, u32[]{:S(2)}, u32[]{:S(2)}) async-start(f32[32,16,128]{2,1,0:T(8,128)} %get-tuple-element.63), calls=%async_computation.1 | async-start | bytes 524288 | tf_op jit(solution)/shard_map/all_to_all | solution.py:715
  84.1 205.6 %all-reduce.10.cloned.1.call-start = ((), (), s32[]{:S(2)}) async-start(), calls=%async_computation.6 | async-start | bytes 1228800 | tf_op jit(solution)/shard_map/psum | solution.py:731
  103.5 16.0 %copy-start.21 = (f32[1,16,128]{2,1,0:T(8,128)S(1)}, f32[1,16,128]{2,1,0:T(8,128)}, u32[]{:S(2)}) copy-start(f32[1,16,128]{2,1,0:T(8,128)} %get-tuple-element.97) | copy-start | bytes 24580
  119.5 18.2 %collective-permute-start.8 = (bf16[800,768]{1,0:T(8,128)(2,1)}, bf16[800,768]{1,0:T(8,128)(2,1)S(1)}, u32[]{:S(2)}, u32[]{:S(2)}) collective-permute-start(bf16[800,768]{1,0:T(8,128)(2,1)} %get-tuple-element.73), channel_id=1, source_target_pairs={{0,4},{4,0},{8,12},{12,8},{16,20},{20,16},{24,28},{28,24},{1,5},{5... | collective-permute-start | bytes 3686408 | tf_op jit(solution)/shard_map/ppermute | solution.py:616
  119.6 20.3 %collective-permute-start.9 = (bf16[800,768]{1,0:T(8,128)(2,1)}, bf16[800,768]{1,0:T(8,128)(2,1)}, u32[]{:S(2)}, u32[]{:S(2)}) collective-permute-start(bf16[800,768]{1,0:T(8,128)(2,1)} %get-tuple-element.75), channel_id=1, source_target_pairs={{0,4},{4,0},{8,12},{12,8},{16,20},{20,16},{24,28},{28,24},{1,5},{5... | collective-permute-start | bytes 3686408 | tf_op jit(solution)/shard_map/ppermute | solution.py:616
  137.7 2.4 copy-start.13
  139.8 26.4 %collective-permute-start.10 = (bf16[1,2,200,768]{3,2,1,0:T(8,128)(2,1)S(1)}, bf16[1,2,200,768]{3,2,1,0:T(8,128)(2,1)}, u32[]{:S(2)}, u32[]{:S(2)}) collective-permute-start(bf16[1,2,200,768]{3,2,1,0:T(8,128)(2,1)S(1)} %dynamic-slice_convert_fusion.3), channel_id=1, source_target_pairs={{0,2},{1,3},{2,0},{3,1},{4,6},{5,7},{6,4},{7,5},{8,10},{9,11},{10,... | collective-permute-start | bytes 1843208 | tf_op jit(solution)/shard_map/ppermute | solution.py:616
  144.1 24.4 %collective-permute-start.11 = (bf16[2,1,200,768]{3,2,1,0:T(8,128)(2,1)}, bf16[2,1,200,768]{3,2,1,0:T(8,128)(2,1)}, u32[]{:S(2)}, u32[]{:S(2)}) collective-permute-start(bf16[2,1,200,768]{3,2,1,0:T(8,128)(2,1)} %dynamic-slice_convert_fusion.2), channel_id=1, source_target_pairs={{0,1},{1,0},{2,3},{3,2},{4,5},{5,4},{6,7},{7,6},{8,9},{9,8},{10,11... | collective-permute-start | bytes 1843208 | tf_op jit(solution)/shard_map/ppermute | solution.py:616
  165.0 29.6 %collective-permute-start.14 = (bf16[800,896]{1,0:T(8,128)(2,1)}, bf16[800,896]{1,0:T(8,128)(2,1)}, u32[]{:S(2)}, u32[]{:S(2)}) collective-permute-start(bf16[800,896]{1,0:T(8,128)(2,1)} %get-tuple-element.86), channel_id=1, source_target_pairs={{0,4},{4,0},{8,12},{12,8},{16,20},{20,16},{24,28},{28,24},{1,5},{5... | collective-permute-start | bytes 4300808 | tf_op jit(solution)/shard_map/ppermute | solution.py:616
  165.1 33.6 %collective-permute-start.15 = (bf16[800,896]{1,0:T(8,128)(2,1)}, bf16[800,896]{1,0:T(8,128)(2,1)}, u32[]{:S(2)}, u32[]{:S(2)}) collective-permute-start(bf16[800,896]{1,0:T(8,128)(2,1)} %get-tuple-element.88), channel_id=1, source_target_pairs={{0,4},{4,0},{8,12},{12,8},{16,20},{20,16},{24,28},{28,24},{1,5},{5... | collective-permute-start | bytes 4300808 | tf_op jit(solution)/shard_map/ppermute | solution.py:616
  167.7 25.4 %collective-permute-start.12 = (bf16[1,1,200,768]{3,2,1,0:T(8,128)(2,1)S(1)}, bf16[1,1,200,768]{3,2,1,0:T(8,128)(2,1)S(1)}, u32[]{:S(2)}, u32[]{:S(2)}) collective-permute-start(bf16[1,1,200,768]{3,2,1,0:T(8,128)(2,1)S(1)} %dynamic-slice_convert_fusion.7), channel_id=1, source_target_pairs={{0,1},{1,0},{2,3},{3,2},{4,5},{5,4},{6,7},{7,6},{8,9},{9,8},{10,11... | collective-permute-start | bytes 921608 | tf_op jit(solution)/shard_map/ppermute | solution.py:616
  170.5 23.4 %collective-permute-start.13 = (bf16[1,1,200,768]{3,2,1,0:T(8,128)(2,1)}, bf16[1,1,200,768]{3,2,1,0:T(8,128)(2,1)S(1)}, u32[]{:S(2)}, u32[]{:S(2)}) collective-permute-start(bf16[1,1,200,768]{3,2,1,0:T(8,128)(2,1)} %dynamic-slice_convert_fusion.6), channel_id=1, source_target_pairs={{0,2},{1,3},{2,0},{3,1},{4,6},{5,7},{6,4},{7,5},{8,10},{9,11},{10,... | collective-permute-start | bytes 921608 | tf_op jit(solution)/shard_map/ppermute | solution.py:616
  194.6 4.1 %copy-start.10 = (f32[800,896]{1,0:T(8,128)S(1)}, f32[800,896]{1,0:T(8,128)}, u32[]{:S(2)}) copy-start(f32[800,896]{1,0:T(8,128)} %get-tuple-element.87) | copy-start | bytes 8601604
  197.3 3.1 copy-start
  198.4 38.6 %collective-permute-start.16 = (bf16[1,2,200,896]{3,2,1,0:T(8,128)(2,1)}, bf16[1,2,200,896]{3,2,1,0:T(8,128)(2,1)}, u32[]{:S(2)}, u32[]{:S(2)}) collective-permute-start(bf16[1,2,200,896]{3,2,1,0:T(8,128)(2,1)} %dynamic-slice_convert_fusion.1), channel_id=1, source_target_pairs={{0,2},{1,3},{2,0},{3,1},{4,6},{5,7},{6,4},{7,5},{8,10},{9,11},{10,... | collective-permute-start | bytes 2150408 | tf_op jit(solution)/shard_map/ppermute | solution.py:616
  216.6 28.4 %all-to-all-start.2 = ((f32[32,16,128]{2,1,0:T(8,128)}), f32[32,16,128]{2,1,0:T(8,128)S(1)}, u32[]{:S(2)}, u32[]{:S(2)}) async-start(f32[32,16,128]{2,1,0:T(8,128)} %get-tuple-element.92), calls=%async_computation.2 | async-start | bytes 524288 | tf_op jit(solution)/shard_map/all_to_all | solution.py:748
  220.5 20.5 %collective-permute-start.17 = (bf16[2,1,200,896]{3,2,1,0:T(8,128)(2,1)}, bf16[2,1,200,896]{3,2,1,0:T(8,128)(2,1)}, u32[]{:S(2)}, u32[]{:S(2)}) collective-permute-start(bf16[2,1,200,896]{3,2,1,0:T(8,128)(2,1)} %dynamic-slice_convert_fusion), channel_id=1, source_target_pairs={{0,1},{1,0},{2,3},{3,2},{4,5},{5,4},{6,7},{7,6},{8,9},{9,8},{10,11... | collective-permute-start | bytes 2150408 | tf_op jit(solution)/shard_map/ppermute | solution.py:616
  238.7 3.6 copy-start.6
  238.8 24.9 %collective-permute-start.20 = (bf16[1,1,200,896]{3,2,1,0:T(8,128)(2,1)S(1)}, bf16[1,1,200,896]{3,2,1,0:T(8,128)(2,1)}, u32[]{:S(2)}, u32[]{:S(2)}) collective-permute-start(bf16[1,1,200,896]{3,2,1,0:T(8,128)(2,1)S(1)} %dynamic-slice_convert_fusion.5), channel_id=1, source_target_pairs={{0,1},{1,0},{2,3},{3,2},{4,5},{5,4},{6,7},{7,6},{8,9},{9,8},{10,11... | collective-permute-start | bytes 1075208 | tf_op jit(solution)/shard_map/ppermute | solution.py:616
  243.4 22.0 %collective-permute-start.21 = (bf16[1,1,200,896]{3,2,1,0:T(8,128)(2,1)S(1)}, bf16[1,1,200,896]{3,2,1,0:T(8,128)(2,1)S(1)}, u32[]{:S(2)}, u32[]{:S(2)}) collective-permute-start(bf16[1,1,200,896]{3,2,1,0:T(8,128)(2,1)S(1)} %dynamic-slice_convert_fusion.4), channel_id=1, source_target_pairs={{0,2},{1,3},{2,0},{3,1},{4,6},{5,7},{6,4},{7,5},{8,10},{9,11},{10,... | collective-permute-start | bytes 1075208 | tf_op jit(solution)/shard_map/ppermute | solution.py:616
  255.2 8.5 %copy-start.7 = (f32[1,2,200,896]{3,2,1,0:T(8,128)S(1)}, f32[1,2,200,896]{3,2,1,0:T(8,128)}, u32[]{:S(2)}) copy-start(f32[1,2,200,896]{3,2,1,0:T(8,128)} %copy-done.6) | copy-start | bytes 4300804
  258.1 7.3 %copy-start.9 = (f32[2,1,200,896]{3,2,1,0:T(8,128)S(1)}, f32[2,1,200,896]{3,2,1,0:T(8,128)}, u32[]{:S(2)}) copy-start(f32[2,1,200,896]{3,2,1,0:T(8,128)} %copy-done.8) | copy-start | bytes 4300804
  258.1 41.1 %collective-permute-start.19 = (bf16[3,800,256]{2,1,0:T(8,128)(2,1)}, bf16[3,800,256]{2,1,0:T(8,128)(2,1)}, u32[]{:S(2)}, u32[]{:S(2)}) collective-permute-start(bf16[3,800,256]{2,1,0:T(8,128)(2,1)} %get-tuple-element.117), channel_id=1, source_target_pairs={{4,0},{8,4},{12,8},{16,12},{20,16},{24,20},{28,24},{5,1},{9,5},{13... | collective-permute-start | bytes 3686408 | tf_op jit(solution)/shard_map/ppermute | solution.py:601
  259.5 39.7 %collective-permute-start.18 = (bf16[3,800,256]{2,1,0:T(8,128)(2,1)S(1)}, bf16[3,800,256]{2,1,0:T(8,128)(2,1)}, u32[]{:S(2)}, u32[]{:S(2)}) collective-permute-start(bf16[3,800,256]{2,1,0:T(8,128)(2,1)S(1)} %get-tuple-element.118), channel_id=1, source_target_pairs={{0,4},{4,8},{8,12},{12,16},{16,20},{20,24},{24,28},{1,5},{5,9},{9,... | collective-permute-start | bytes 3686408 | tf_op jit(solution)/shard_map/ppermute | solution.py:600
  266.2 22.8 %copy-start.18 = (f32[32,128]{1,0:T(8,128)S(1)}, f32[32,128]{1,0:T(8,128)}, u32[]{:S(2)}) copy-start(f32[32,128]{1,0:T(8,128)} %get-tuple-element.89.refs_7_.stat_ref) | copy-start | bytes 49156
  285.6 8.9 %all-to-all-start.3 = ((f32[4,54,200]{2,1,0:T(8,128)}), f32[4,54,200]{2,1,0:T(8,128)S(1)}, u32[]{:S(2)}, u32[]{:S(2)}) async-start(f32[4,54,200]{2,1,0:T(8,128)} %pad_maximum_fusion.6), calls=%async_computation.3 | async-start | bytes 458752 | tf_op jit(solution)/shard_map/all_to_all | solution.py:775
  288.9 55.8 %all-reduce.8.cloned.1.call-start = ((), (), s32[]{:S(2)}) async-start(), calls=%async_computation.5 | async-start | bytes 1433600 | tf_op jit(solution)/shard_map/psum | solution.py:731
  295.2 52.0 %all-to-all-start.4 = ((f32[8,54,200]{2,1,0:T(8,128)}), f32[8,54,200]{2,1,0:T(8,128)S(1)}, u32[]{:S(2)}, u32[]{:S(2)}) async-start(f32[8,54,200]{2,1,0:T(8,128)} %broadcast_in_dim.54), calls=%async_computation.4 | async-start | bytes 917504 | tf_op jit(solution)/shard_map/all_to_all | solution.py:611
  299.2 46.7 %copy-start.17 = (bf16[200,768]{1,0:T(8,128)(2,1)S(1)}, bf16[200,768]{1,0:T(8,128)(2,1)}, u32[]{:S(2)}) copy-start(bf16[200,768]{1,0:T(8,128)(2,1)} %get-tuple-element.109) | copy-start | bytes 921604
  299.2 46.7 %copy-start.20 = (f32[16,128]{1,0:T(8,128)S(1)}, f32[16,128]{1,0:T(8,128)}, u32[]{:S(2)}) copy-start(f32[16,128]{1,0:T(8,128)} %get-tuple-element.102) | copy-start | bytes 24580
  344.7 4.4 %copy-start.16 = (bf16[200,896]{1,0:T(8,128)(2,1)S(1)}, bf16[200,896]{1,0:T(8,128)(2,1)}, u32[]{:S(2)}) copy-start(bf16[200,896]{1,0:T(8,128)(2,1)} %get-tuple-element.104) | copy-start | bytes 1075204
  345.8 3.9 %collective-permute-start.23 = (bf16[200,1664]{1,0:T(8,128)(2,1)S(1)}, bf16[200,1664]{1,0:T(8,128)(2,1)S(1)}, u32[]{:S(2)}, u32[]{:S(2)}) collective-permute-start(bf16[200,1664]{1,0:T(8,128)(2,1)S(1)} %constant_dynamic-update-slice_fusion.6), channel_id=1, source_target_pairs={{0,4},{4,0},{8,12},{12,8},{16,20},{20,16},{24,28},{28,24},{1,5},{5... | collective-permute-start | bytes 1996808 | tf_op jit(solution)/shard_map/ppermute | solution.py:616
  349.2 2.3 collective-permute-start.22
  (6 other events, 8.0 us)
Sparse Core Ops, SparseCore 0:
  200.5 39.1 all-reduce.9
  292.2 52.4 all-reduce.7

commit v3 on v2

--- a/solution.py
+++ b/solution.py
@@ -19,14 +19,15 @@
 GELU_A = 0.7978845608028654
 GELU_B = 0.044715
 NT = (((1,), (1,)), ((), ()))
+TN = (((0,), (0,)), ((), ()))
 
 
 def params(limit=60):
     return pltpu.CompilerParams(vmem_limit_bytes=limit * MIB)
 
 
-def cost(flops, nbytes, trans=0):
-    return pl.CostEstimate(flops=int(flops), bytes_accessed=int(nbytes), transcendentals=int(trans))
+def cost(us):
+    return pl.CostEstimate(flops=int(us * 1.15e9), bytes_accessed=10**5, transcendentals=0)
 
 
 def whole(shape):
@@ -46,6 +47,10 @@
         block = jnp.concatenate(used + [jnp.zeros((128 - len(rows), 128), F32)], axis=0)
         pieces.append(block.T)
     return jnp.concatenate(pieces, axis=0)
+
+
+def wide(column):
+    return jnp.broadcast_to(column, (column.shape[0], 128))
 
 
 def copies_of(cols, out_ref):
@@ -70,8 +75,11 @@
 
 
 def tap_picker():
-    col, tap, lane = (lax.broadcasted_iota(jnp.int32, (KS, 128, 128), d) for d in range(3))
-    return jnp.where((tap == KS * (lane // GRP) + col) & (lane < KS * GRP), 1.0, 0.0).astype(BF16)
+    tap = lax.broadcasted_iota(jnp.int32, (128, 128), 0)
+    lane = lax.broadcasted_iota(jnp.int32, (128, 128), 1)
+    inside = lane < KS * GRP
+    first = KS * (lane // GRP)
+    return [jnp.where((tap == first + j) & inside, 1.0, 0.0).astype(BF16) for j in range(KS)]
 
 
 def conv_rows(field_ref, taps_ref, s, rows, flip):
@@ -92,17 +100,19 @@
 
 
 def conv_kernel(
-    n_ref, x_ref, up_ref, dn_ref, small_ref, pick_ref, m_ref, out_ref, st_ref, par_ref,
-    field_ref, cols_ref, e_ref, *, share
+    x_ref, up_ref, dn_ref, small_ref, m_ref, out_ref, st_ref, par_ref,
+    field_ref, cols_ref, e_ref, pick_ref, count_ref, *, share
 ):
     rows, block = x_ref.shape[0], x_ref.shape[1]
     step = pl.program_id(0)
-    count = n_ref[0]
-    inv_n = n_ref[1]
 
     @pl.when(step == 0)
     def _():
-        cols_ref[...] = jnp.full(cols_ref.shape, count, F32)
+        for j, pick in enumerate(tap_picker()):
+            pick_ref[j] = pick
+        count = jnp.sum(jnp.sum(m_ref[...], axis=0), axis=1, keepdims=True)[0:8]
+        count_ref[...] = jnp.broadcast_to(count, (8, 128))
+        cols_ref[...] = jnp.zeros(cols_ref.shape, F32)
         given, wide = small_ref.shape[1], pl.cdiv(share, 128) * 128
         for f in range(small_ref.shape[0]):
             v = small_ref[f]
@@ -116,6 +126,7 @@
     here = pl.multiple_of(step * block, GRP)
     spread_taps(par_ref[pl.ds(here, block), :], pick_ref, e_ref)
     lane = lax.broadcasted_iota(jnp.int32, (GRP, 128), 1)
+    inv_n = 1.0 / jnp.maximum(count_ref[0:1, 0:1], 1.0)
     for g in range(block // GRP):
         s = pl.ds(g * GRP, GRP)
         acc = conv_rows(field_ref, e_ref, s, rows, False)
@@ -136,11 +147,11 @@
 
     @pl.when(step == pl.num_programs(0) - 1)
     def _():
-        st_ref[...] = jnp.full(st_ref.shape, count, F32)
+        st_ref[...] = jnp.broadcast_to(count_ref[0:1, :][None], st_ref.shape)
         copies_of(cols_ref[...], st_ref)
 
 
-def conv_forward(x, up, dn, small, pick, m16, counts, copies, block):
+def conv_forward(x, up, dn, small, m16, copies, block):
     rows, channels, width = x.shape
     n_fs, given, share = small.shape
     padded = pl.cdiv(channels, 128) * 128
@@ -148,12 +159,10 @@
         functools.partial(conv_kernel, share=share),
         grid=(channels // block,),
         in_specs=[
-            pl.BlockSpec(memory_space=pltpu.SMEM),
             pl.BlockSpec((rows, block, width), lambda g: (0, g, 0)),
             pl.BlockSpec((REACH, block, width), lambda g: (0, g, 0)),
             pl.BlockSpec((REACH, block, width), lambda g: (0, g, 0)),
             whole((n_fs, given, share)),
-            whole((KS, 128, 128)),
             whole((rows, GRP, width)),
         ],
         out_specs=[
@@ -170,16 +179,23 @@
             pltpu.VMEM((rows + 2 * REACH, block, width), BF16),
             pltpu.VMEM((padded, 128), F32),
             pltpu.VMEM((2, KS, block, 128), BF16),
-        ],
-        compiler_params=params(),
-        cost_estimate=cost(20e9, 12e6),
+            pltpu.VMEM((KS, 128, 128), BF16),
+            pltpu.VMEM((8, 128), F32),
+        ],
+        compiler_params=params(),
+        cost_estimate=cost(0.4),
         name="conv_forward",
-    )(counts, x, up, dn, small, pick, m16)
+    )(x, up, dn, small, m16)
 
 
 def input_grad_kernel(
-    g_ref, up_ref, dn_ref, par_ref, pick_ref, og_ref, m_ref, out_ref, field_ref, e_ref
+    g_ref, up_ref, dn_ref, par_ref, og_ref, m_ref, out_ref, field_ref, e_ref, pick_ref
 ):
+    @pl.when(pl.program_id(0) == 0)
+    def _():
+        for j, pick in enumerate(tap_picker()):
+            pick_ref[j] = pick
+
     rows, block = g_ref.shape[0], g_ref.shape[1]
     last = rows + 2 * REACH - 1
     for q in range(REACH):
@@ -195,7 +211,7 @@
             out_ref[r, s, :] = og_ref[r, s, :].astype(F32) * m_ref[r] + acc[r]
 
 
-def input_gradient(grad, up, dn, par, pick, og, m16, block):
+def input_gradient(grad, up, dn, par, og, m16, block):
     rows, channels, width = grad.shape
     return pl.pallas_call(
         input_grad_kernel,
@@ -205,7 +221,6 @@
             pl.BlockSpec((REACH, block, width), lambda g: (0, g, 0)),
             pl.BlockSpec((REACH, block, width), lambda g: (0, g, 0)),
             pl.BlockSpec((block, 128), lambda g: (g, 0)),
-            whole((KS, 128, 128)),
             pl.BlockSpec((rows, block, width), lambda g: (0, g, 0)),
             whole((rows, GRP, width)),
         ],
@@ -214,11 +229,12 @@
         scratch_shapes=[
             pltpu.VMEM((rows + 2 * REACH, block, width), BF16),
             pltpu.VMEM((2, KS, block, 128), BF16),
-        ],
-        compiler_params=params(),
-        cost_estimate=cost(18e9, 15e6),
+            pltpu.VMEM((KS, 128, 128), BF16),
+        ],
+        compiler_params=params(),
+        cost_estimate=cost(0.32),
         name="input_gradient",
-    )(grad, up, dn, par, pick, og, m16)
+    )(grad, up, dn, par, og, m16)
 
 
 def tap_grad_kernel(x_ref, up_ref, dn_ref, g_ref, out_ref, field_ref, cols_ref, *, share):
@@ -277,17 +293,16 @@
             pltpu.VMEM((padded, 128), F32),
         ],
         compiler_params=params(),
-        cost_estimate=cost(18e9, 8e6),
+        cost_estimate=cost(0.35),
         name="tap_gradient",
     )(x, up, dn, grad)
 
 
-def mask_grad_kernel(og_ref, m_ref, by_chan_ref, by_pixel_ref, sum_ref, cols_ref):
+def mask_grad_kernel(og_ref, m_ref, out_ref, sum_ref, cols_ref):
     row = pl.program_id(0)
     channels = og_ref.shape[1]
     v = og_ref[0].astype(F32) * m_ref[0, 0:1]
-    by_chan_ref[...] = v.astype(BF16)
-    by_pixel_ref[...] = v.T.astype(BF16)
+    out_ref[...] = v.astype(BF16)
     part = v[:, 0:128]
     for k in range(128, v.shape[1], 128):
         part = part + v[:, k : k + 128]
@@ -317,22 +332,20 @@
         ],
         out_specs=[
             pl.BlockSpec((channels, width), lambda r: (0, r)),
-            pl.BlockSpec((width, channels), lambda r: (r, 0)),
             pl.BlockSpec((1, 16, 128), lambda r: (0, 0, 0)),
         ],
         out_shape=[
             jax.ShapeDtypeStruct((channels, pixels), BF16),
-            jax.ShapeDtypeStruct((pixels, channels), BF16),
             jax.ShapeDtypeStruct((1, 16, 128), F32),
         ],
         scratch_shapes=[pltpu.VMEM((padded, 128), F32)],
         compiler_params=params(),
-        cost_estimate=cost(1e9, 8e6),
+        cost_estimate=cost(0.11),
         name="mask_gradient",
     )(og, m16)
 
 
-def activate_kernel(conv_ref, all_ref, par_ref, by_chan_ref, by_pixel_ref, stat_ref, cols_ref):
+def activate_kernel(conv_ref, all_ref, par_ref, out_ref, stat_ref, cols_ref):
     channels = conv_ref.shape[1]
 
     @pl.when(pl.program_id(0) == 0)
@@ -348,18 +361,19 @@
         stat_ref[8:16] = inv_std
         stat_ref[16:24] = jnp.sqrt(variance + EPS)
         stat_ref[24:32] = jnp.broadcast_to(count, (8, 128))
-        cols_ref[...] = columns_of(mean[0:7], inv_std[0:7])[: cols_ref.shape[0]]
-
-    c, p = cols_ref[0:channels, :], par_ref[...]
-    v = (conv_ref[0] - c[:, 0:1]) * (c[:, 1:2] * p[:, TAPS : TAPS + 1]) + p[:, TAPS + 1 : TAPS + 2]
-    by_chan_ref[...] = v.astype(BF16)
-    by_pixel_ref[...] = v.T.astype(BF16)
+        c, p = columns_of(mean[0:7], inv_std[0:7])[:channels], par_ref[...]
+        cols_ref[0] = wide(c[:, 0:1])
+        cols_ref[1] = wide(c[:, 1:2] * p[:, TAPS : TAPS + 1])
+        cols_ref[2] = wide(p[:, TAPS + 1 : TAPS + 2])
+
+    for k in range(0, out_ref.shape[1], 128):
+        v = (conv_ref[0, :, k : k + 128] - cols_ref[0]) * cols_ref[1] + cols_ref[2]
+        out_ref[:, k : k + 128] = v.astype(BF16)
 
 
 def activate(conv, stats, par):
     rows, channels, width = conv.shape
     pixels = rows * width
-    padded = pl.cdiv(channels, 128) * 128
     return pl.pallas_call(
         activate_kernel,
         grid=(rows,),
@@ -370,17 +384,15 @@
         ],
         out_specs=[
             pl.BlockSpec((channels, width), lambda r: (0, r)),
-            pl.BlockSpec((width, channels), lambda r: (r, 0)),
             pl.BlockSpec((32, 128), lambda r: (0, 0)),
         ],
         out_shape=[
             jax.ShapeDtypeStruct((channels, pixels), BF16),
-            jax.ShapeDtypeStruct((pixels, channels), BF16),
             jax.ShapeDtypeStruct((32, 128), F32),
         ],
-        scratch_shapes=[pltpu.VMEM((padded, 128), F32)],
-        compiler_params=params(),
-        cost_estimate=cost(1e9, 10e6),
+        scratch_shapes=[pltpu.VMEM((3, channels, 128), F32)],
+        compiler_params=params(),
+        cost_estimate=cost(0.13),
         name="activate",
     )(conv, stats, par)
 
@@ -393,14 +405,25 @@
     return h, s + h * (1.0 - s) * (2 * GELU_A + (6 * GELU_A * GELU_B) * v2)
 
 
-def hidden_kernel(
-    act_p, act_c, bg_p, bg_c, we_ref, wp_ref, eb_ref, h_ref, g_ref, dwp_ref, dwe_ref, ebg_ref, *, step
-):
+def halves(v, mine, piece):
+    keep, send = [], []
+    for o in range(0, v.shape[0], 2 * piece):
+        first, second = v[o : o + piece], v[o + piece : o + 2 * piece]
+        keep.append(jnp.where(mine == 0, first, second))
+        send.append(jnp.where(mine == 0, second, first))
+    return jnp.concatenate(keep, axis=0), jnp.concatenate(send, axis=0)
+
+
+def hidden_kernel(bits_ref, act_ref, bg_ref, we_ref, wp_ref, eb_ref, *refs, step, pieces):
+    if pieces is None:
+        h_ref, g_ref, dwp_ref, dwe_ref, ebg_ref = refs
+    else:
+        other_p, other_e, h_ref, g_ref, keep_p, send_p, keep_e, send_e, ebg_ref = refs
     we, wp, bias = we_ref[...], wp_ref[...], eb_ref[...]
     total = None
-    for p in range(0, act_p.shape[0], step):
-        pre = jnp.dot(act_p[p : p + step, :], we, preferred_element_type=F32) + bias
-        pull = jnp.dot(bg_p[p : p + step, :], wp, preferred_element_type=F32)
+    for p in range(0, act_ref.shape[1], step):
+        pre = lax.dot_general(act_ref[:, p : p + step], we, TN, preferred_element_type=F32) + bias
+        pull = lax.dot_general(bg_ref[:, p : p + step], wp, TN, preferred_element_type=F32)
         h, slope = gelu_parts(pre)
         grad = (pull * slope).astype(BF16)
         h_ref[p : p + step, :] = h.astype(BF16)
@@ -408,45 +431,51 @@
         part = jnp.sum(grad.astype(F32), axis=0, keepdims=True)
         total = part if total is None else total + part
     ebg_ref[...] = total
-    dwp_ref[...] = jnp.dot(bg_c[...], h_ref[...], preferred_element_type=F32).astype(dwp_ref.dtype)
-    dwe_ref[...] = jnp.dot(act_c[...], g_ref[...], preferred_element_type=F32).astype(dwe_ref.dtype)
-
-
-def hidden_layer(act_p, act_c, bg_p, bg_c, we, wp, eb, first, units, dtype):
-    pixels, channels = act_p.shape
-    steps = pl.cdiv(units, TILE)
+    dwp = jnp.dot(bg_ref[...], h_ref[...], preferred_element_type=F32)
+    dwe = jnp.dot(act_ref[...], g_ref[...], preferred_element_type=F32)
+    if pieces is None:
+        dwp_ref[...] = dwp.astype(BF16)
+        dwe_ref[...] = dwe.astype(BF16)
+    else:
+        keep, send = halves(dwp + other_p[...].astype(F32), bits_ref[0], pieces[0])
+        keep_p[...] = keep
+        send_p[...] = send.astype(BF16)
+        keep, send = halves(dwe + other_e[...].astype(F32), bits_ref[1], pieces[1])
+        keep_e[...] = keep
+        send_e[...] = send.astype(BF16)
+
+
+def hidden_layer(act, bg, we, wp, eb, first, units, bits, others=None, pieces=None):
+    channels, pixels = act.shape
     off = first // TILE
+    column = lambda rows: pl.BlockSpec((rows, TILE), lambda g: (0, g))
     weight = pl.BlockSpec((channels, TILE), lambda g: (0, g + off))
-    return pl.pallas_call(
-        functools.partial(hidden_kernel, step=pixels // 3),
-        grid=(steps,),
-        in_specs=[
-            whole((pixels, channels)),
-            whole((channels, pixels)),
-            whole((pixels, channels)),
-            whole((channels, pixels)),
-            weight,
-            weight,
-            pl.BlockSpec((1, TILE), lambda g: (0, g + off)),
-        ],
-        out_specs=[
-            pl.BlockSpec((pixels, TILE), lambda g: (0, g)),
-            pl.BlockSpec((pixels, TILE), lambda g: (0, g)),
-            pl.BlockSpec((channels, TILE), lambda g: (0, g)),
-            pl.BlockSpec((channels, TILE), lambda g: (0, g)),
-            pl.BlockSpec((1, TILE), lambda g: (0, g)),
-        ],
-        out_shape=[
-            jax.ShapeDtypeStruct((pixels, units), BF16),
-            jax.ShapeDtypeStruct((pixels, units), BF16),
-            jax.ShapeDtypeStruct((channels, units), dtype),
-            jax.ShapeDtypeStruct((channels, units), dtype),
-            jax.ShapeDtypeStruct((1, units), F32),
-        ],
-        compiler_params=params(),
-        cost_estimate=cost(8 * pixels * channels * units, 20e6, pixels * units),
+    shape = lambda rows, dtype: jax.ShapeDtypeStruct((rows, units), dtype)
+    in_specs = [pl.BlockSpec(memory_space=pltpu.SMEM), whole(act.shape), whole(bg.shape), weight, weight]
+    in_specs.append(pl.BlockSpec((1, TILE), lambda g: (0, g + off)))
+    operands = [bits, act, bg, we, wp, eb]
+    out_specs = [column(pixels), column(pixels)]
+    out_shape = [shape(pixels, BF16), shape(pixels, BF16)]
+    if others is None:
+        out_specs += [column(channels), column(channels)]
+        out_shape += [shape(channels, BF16), shape(channels, BF16)]
+    else:
+        in_specs += [column(channels), column(channels)]
+        operands += list(others)
+        out_specs += [column(channels // 2)] * 4
+        out_shape += [shape(channels // 2, F32), shape(channels // 2, BF16)] * 2
+    out_specs.append(column(1))
+    out_shape.append(shape(1, F32))
+    return pl.pallas_call(
+        functools.partial(hidden_kernel, step=128, pieces=pieces),
+        grid=(pl.cdiv(units, TILE),),
+        in_specs=in_specs,
+        out_specs=out_specs,
+        out_shape=out_shape,
+        compiler_params=params(),
+        cost_estimate=cost(0.3),
         name="hidden_layer",
-    )(act_p, act_c, bg_p, bg_c, we, wp, eb)
+    )(*operands)
 
 
 def contract(weights, hiddens):
@@ -510,7 +539,7 @@
         ],
         scratch_shapes=[pltpu.VMEM((padded, 128), F32), pltpu.VMEM((2, padded, 128), F32)],
         compiler_params=params(),
-        cost_estimate=cost(8e9, 25e6),
+        cost_estimate=cost(0.32),
         name="activation_gradient",
     )(*weights, *hiddens, conv, stat)
 
@@ -518,7 +547,8 @@
 def block_out_kernel(*refs, cuts):
     n = len(cuts)
     w_refs, h_refs = refs[0:2], refs[2 : 2 + n]
-    x_ref, m_ref, par_ref, out_ref = refs[2 + n :]
+    x_ref, m_ref, par_ref = refs[2 + n : 5 + n]
+    out_ref = refs[-1]
     branch = contract([(w_refs[w], first, units) for w, first, units in cuts], h_refs)
     branch = branch + par_ref[:, TAPS + 2 : TAPS + 3]
     out_ref[0] = ((x_ref[0].astype(F32) + branch) * m_ref[0, 0:1]).astype(BF16)
@@ -539,12 +569,15 @@
         out_specs=pl.BlockSpec((1, channels, width), lambda r: (r, 0, 0)),
         out_shape=jax.ShapeDtypeStruct((rows, channels, width), BF16),
         compiler_params=params(),
-        cost_estimate=cost(8e9, 22e6),
+        cost_estimate=cost(0.29),
         name="block_output",
     )(*weights, *hiddens, x, m16, par)
 
 
-def conv_grad_kernel(da_ref, conv_ref, m_ref, all_ref, stat_ref, par_ref, out_ref, sum_ref, cols_ref):
+def conv_grad_kernel(
+    da_ref, conv_ref, m_ref, all_ref, stat_ref, par_ref, out_ref, top_ref, end_ref, sum_ref, cols_ref
+):
+    row = pl.program_id(0)
     channels = conv_ref.shape[1]
 
     @pl.when(pl.program_id(0) == 0)
@@ -552,20 +585,33 @@
         sums = jnp.sum(all_ref[...], axis=0)
         sum_ref[...] = sums
         count = stat_ref[24:32]
-        cols_ref[...] = columns_of(
+        c = columns_of(
             stat_ref[0:7], stat_ref[8:15], (sums[0:8] / count)[0:7], (sums[8:16] / count)[0:7]
-        )[: cols_ref.shape[0]]
-
-    c = cols_ref[0:channels, :]
-    normalized = (conv_ref[0] - c[:, 0:1]) * c[:, 1:2]
-    correction = m_ref[0, 0:1] * (c[:, 2:3] + normalized * c[:, 3:4])
-    factor = c[:, 1:2] * par_ref[:, TAPS : TAPS + 1]
-    out_ref[0] = (factor * (da_ref[0] - correction)).astype(BF16)
+        )[:channels]
+        factor = c[:, 1:2] * par_ref[:, TAPS : TAPS + 1]
+        cols_ref[0] = wide(c[:, 0:1])
+        cols_ref[1] = wide(factor)
+        cols_ref[2] = wide(factor * c[:, 2:3])
+        cols_ref[3] = wide(factor * c[:, 1:2] * c[:, 3:4])
+
+    for k in range(0, out_ref.shape[2], 128):
+        s = slice(k, k + 128)
+        apart = conv_ref[0, :, s] - cols_ref[0]
+        correction = m_ref[0, 0:1, s] * (cols_ref[2] + apart * cols_ref[3])
+        out_ref[0, :, s] = (cols_ref[1] * da_ref[0, :, s] - correction).astype(BF16)
+    grad = out_ref[0]
+
+    @pl.when(row < REACH)
+    def _():
+        top_ref[0] = grad
+
+    @pl.when(row >= pl.num_programs(0) - REACH)
+    def _():
+        end_ref[0] = grad
 
 
 def conv_gradient(da, conv, m16, sums, stat, par):
     rows, channels, width = conv.shape
-    padded = pl.cdiv(channels, 128) * 128
     return pl.pallas_call(
         conv_grad_kernel,
         grid=(rows,),
@@ -579,26 +625,101 @@
         ],
         out_specs=[
             pl.BlockSpec((1, channels, width), lambda r: (r, 0, 0)),
+            pl.BlockSpec((1, channels, width), lambda r: (jnp.minimum(r, REACH - 1), 0, 0)),
+            pl.BlockSpec((1, channels, width), lambda r: (jnp.maximum(r - rows + REACH, 0), 0, 0)),
             pl.BlockSpec((16, 128), lambda r: (0, 0)),
         ],
         out_shape=[
             jax.ShapeDtypeStruct((rows, channels, width), BF16),
+            jax.ShapeDtypeStruct((REACH, channels, width), BF16),
+            jax.ShapeDtypeStruct((REACH, channels, width), BF16),
             jax.ShapeDtypeStruct((16, 128), F32),
         ],
-        scratch_shapes=[pltpu.VMEM((padded, 128), F32)],
-        compiler_params=params(),
-        cost_estimate=cost(1e9, 12e6),
+        scratch_shapes=[pltpu.VMEM((4, channels, 128), F32)],
+        compiler_params=params(),
+        cost_estimate=cost(0.19),
         name="conv_gradient",
     )(da, conv, m16, sums, stat, par)
 
 
-def halo(field):
+def join_kernel(index_ref, *refs, names, share):
+    n = len(names)
+    for index in names:
+
+        @pl.when(index_ref[0] == index)
+        def _(index=index):
+            for w in range(2):
+                for k, name in enumerate(names):
+                    row = (index ^ name) * share
+                    refs[2 * n + w][row : row + share, :] = refs[w * n + k][...]
+
+
+def join_pieces(index, first, second):
+    names = sorted(first)
+    share, cols = first[0].shape
+    channels = share * len(names)
+    if share % 8:
+        out = []
+        for pieces in (first, second):
+            whole_array = jnp.zeros((channels, cols), BF16)
+            for name in names:
+                start = (index ^ name) * share
+                whole_array = lax.dynamic_update_slice_in_dim(whole_array, pieces[name], start, axis=0)
+            out.append(whole_array)
+        return out
+    tile = 2 * TILE
+    column = lambda height: pl.BlockSpec((height, tile), lambda g: (0, g))
+    return pl.pallas_call(
+        functools.partial(join_kernel, names=names, share=share),
+        grid=(pl.cdiv(cols, tile),),
+        in_specs=[pl.BlockSpec(memory_space=pltpu.SMEM)] + [column(share)] * (2 * len(names)),
+        out_specs=[column(channels)] * 2,
+        out_shape=[jax.ShapeDtypeStruct((channels, cols), BF16)] * 2,
+        compiler_params=params(),
+        cost_estimate=cost(0.08),
+        name="join_pieces",
+    )(index[None], *[first[k] for k in names], *[second[k] for k in names])
+
+
+def place_kernel(core_ref, *refs, starts):
+    n = len(starts)
+    for w in range(2):
+        out_ref = refs[4 * n + w]
+        for k, (low, high) in enumerate(starts):
+            mine, other = refs[2 * (w * n + k)][...], refs[2 * (w * n + k) + 1][...]
+            mine, other = mine.astype(F32), other.astype(F32)
+            for at, v in (
+                (low, jnp.where(core_ref[0] == 0, mine, other)),
+                (high, jnp.where(core_ref[0] == 0, other, mine)),
+            ):
+                wide = min(v.shape[1], out_ref.shape[1] - at)
+                out_ref[:, at : at + wide] = v[:, :wide]
+
+
+def place_columns(core, pairs, starts, units):
+    share = pairs[0][0][0].shape[0]
+    tile = share
+    operands = [v for parts in pairs for pair in parts for v in pair]
+    return pl.pallas_call(
+        functools.partial(place_kernel, starts=starts),
+        grid=(share // tile,),
+        in_specs=[pl.BlockSpec(memory_space=pltpu.SMEM)]
+        + [pl.BlockSpec((tile, v.shape[1]), lambda g: (g, 0)) for v in operands],
+        out_specs=[pl.BlockSpec((tile, units), lambda g: (g, 0))] * 2,
+        out_shape=[jax.ShapeDtypeStruct((share, units), F32)] * 2,
+        compiler_params=params(),
+        cost_estimate=cost(0.08),
+        name="place_columns",
+    )(core[None], *operands)
+
+
+def halo(first, last):
     size = lax.axis_size("dp")
     up = [(i, i + 1) for i in range(size - 1)]
     down = [(j, i) for i, j in up]
     return (
-        lax.ppermute(field[-REACH:], "dp", up),
-        lax.ppermute(field[:REACH], "dp", down),
+        lax.ppermute(last, "dp", up),
+        lax.ppermute(first, "dp", down),
     )
 
 
@@ -620,24 +741,17 @@
     return (lax.axis_index(axis) >> bit) & 1
 
 
-def gather_step(have, bit, mine):
-    other = flip_bit(have, "fsdp", bit)
-    dim = lax.axis_size("fsdp").bit_length() - 2 - bit
-    first, second = jnp.where(mine, have, other), jnp.where(mine, other, have)
-    return jnp.concatenate([first, second], axis=dim)
-
-
-def scatter_step(have, bit, done):
-    bits = lax.axis_size("fsdp").bit_length() - 1
-    cols = have.shape[-1]
-    if done == 0:
-        have = have.reshape((2,) * bits + (-1, cols))
-    dim = bits - 1 - bit
-    mine = bit_of("fsdp", bit)
-    send = lax.dynamic_slice_in_dim(have, 1 - mine, 1, axis=dim).astype(BF16)
-    keep = lax.dynamic_slice_in_dim(have, mine, 1, axis=dim)
-    have = keep + flip_bit(send, "fsdp", bit).astype(F32)
-    return have.reshape(-1, cols) if done == bits - 1 else have
+def gather_pieces(own, order):
+    return {0: own} | {1 << bit: flip_bit(own, "fsdp", bit) for bit in order}
+
+
+def gather_others(have, order, *others):
+    reached = {0: have[0]}
+    for bit in order:
+        for name, v in list(reached.items()):
+            far = have.get(name | 1 << bit)
+            reached[name | 1 << bit] = far if far is not None else flip_bit(after(v, *others), "fsdp", bit)
+    return reached
 
 
 def per_device(
@@ -676,21 +790,14 @@
         ],
         axis=0,
     )
-    small = from_all(small, "fsdp")
-    e_bias = jnp.pad(small[:, TAPS + 3 :].reshape(1, units), ((0, 0), (0, 2 * half - units)))
-    pick = tap_picker()
-    x_up, x_dn = halo(x)
+    every = from_all(small, "fsdp")
+    e_bias = jnp.pad(every[:, TAPS + 3 :].reshape(1, units), ((0, 0), (0, 2 * half - units)))
+    x_up, x_dn = halo(x[:REACH], x[-REACH:])
 
     def columns(weight):
         wide = jnp.pad(weight, ((0, 0), (0, 2 * half - units)))
-        mine = lax.dynamic_slice_in_dim(wide, core * half, half, axis=1)
-        return mine.reshape((1,) * len(bits) + (share, half))
-
-    we_own, wp_own = columns(expand_weight), columns(project_weight)
-    zeros = [bit_of("fsdp", bit) == 0 for bit in bits]
-    for n in bits[:-1]:
-        we_own = gather_step(we_own, n, zeros[n])
-        wp_own = gather_step(wp_own, bits[-1 - n], zeros[-1 - n])
+        return lax.dynamic_slice_in_dim(after(wide, every), (1 - core) * half, half, axis=1)
+
     eb_own = lax.dynamic_slice_in_dim(e_bias, core * half, half, axis=1)
     eb_peer = lax.dynamic_slice_in_dim(e_bias, (1 - core) * half, half, axis=1)
 
@@ -699,68 +806,100 @@
     live = jnp.where(sample % ROLLOUT < length, 1.0, 0.0).astype(F32)
     weight = live * ocean_mask.astype(F32)
     m16 = jnp.broadcast_to(weight[:, None, :], (rows, GRP, width))
-    count_here = jnp.sum(weight)
-    counts = jnp.stack([count_here, 1.0 / jnp.maximum(count_here, 1.0)])
-
-    bg_c, bg_p, bg_sum = mask_gradient(og, m16)
+
+    we_pieces = gather_pieces(columns(expand_weight), bits)
+    wp_pieces = gather_pieces(columns(project_weight), bits[::-1])
+    bg, bg_sum = mask_gradient(og, after(m16, small))
+    early = [p[1 << b] for p, b in ((we_pieces, bits[0]), (wp_pieces, bits[-1]))]
+    we_pieces = gather_others(we_pieces, bits, bg)
+    wp_pieces = gather_others(wp_pieces, bits[::-1], bg)
 
     copies = n_fs * n_dp
-    ready = after(m16, bg_c, we_own, wp_own)
-    conv, stats, par = conv_forward(x, x_up, x_dn, small, pick, ready, counts, copies, block)
-    n = bits[-1]
-    we_own = gather_step(we_own, n, after(zeros[n], conv)).reshape(channels, half)
-    wp_own = gather_step(wp_own, bits[-1 - n], after(zeros[-1 - n], conv)).reshape(channels, half)
-    we_peer = flip_bit(we_own, "dp", 0)
-    wp_peer = flip_bit(wp_own, "dp", 0)
+    ready = after(m16, bg, *early)
+    conv, stats, par = conv_forward(x, x_up, x_dn, every, ready, copies, block)
+    index = lax.axis_index("fsdp")
+    far = n_fs - 1
+    we_pieces[far], wp_pieces[far], index, _ = lax.optimization_barrier(
+        (we_pieces[far], wp_pieces[far], index, conv)
+    )
+    we_peer, wp_peer = join_pieces(index, we_pieces, wp_pieces)
+    we_own = flip_bit(we_peer, "dp", 0)
+    wp_own = flip_bit(wp_peer, "dp", 0)
     stats = lax.all_to_all(stats, devices, 0, 0)
-    act_c, act_p, stat = activate(conv, stats, par)
+    act, stat = activate(conv, stats, par)
 
     groups = [[i for i in range(n_dp) if i % 2 == c] for c in range(2)]
-    orders = {2: bits[::-1], 3: bits}
+    orders = (bits[::-1], bits)
+    flags = jnp.stack([bit_of("fsdp", bit) for bit in bits]).astype(jnp.int32)
     first = half // (2 * TILE) * TILE
     second = half - first
-    common = (act_p, act_c, bg_p, bg_c)
-
-    def added(peer, own):
-        return {k: own[k] + flip_bit(peer[k], "dp", 0).astype(F32) for k in orders}
-
-    def stage(sums, n):
-        return {k: scatter_step(v, orders[k][n], n) for k, v in sums.items()}
-
-    def over_bands(sums):
-        return {k: lax.psum(v.astype(BF16), "dp", axis_index_groups=groups) for k, v in sums.items()}
-
-    q1 = hidden_layer(*common, we_peer, wp_peer, eb_peer, 0, first, BF16)
-    o1 = hidden_layer(*common, we_own, wp_own, after(eb_own, q1[0]), 0, first, F32)
-    s1 = added(q1, o1)
-    q2 = hidden_layer(*common, we_peer, wp_peer, after(eb_peer, s1[2], s1[3]), first, second, BF16)
-    for n in range(len(bits) - 1):
-        s1 = stage(s1, n)
-    o2 = hidden_layer(*common, we_own, wp_own, after(eb_own, q2[0], s1[2], s1[3]), first, second, F32)
-    s1 = stage(s1, len(bits) - 1)
-    s1 = {k: v.astype(BF16) for k, v in s1.items()}
+
+    def piece(order, n):
+        return share << len([b for b in order[n + 1 :] if b < order[n]])
+
+    def other_core(grads):
+        return [flip_bit(v, "dp", 0) for v in grads]
+
+    def exchanged(pairs, n):
+        return [(keep, flip_bit(send, "fsdp", o[n])) for (keep, send), o in zip(pairs, orders, strict=True)]
+
+    def arrived(pairs, *cover):
+        came = lax.optimization_barrier((*[came for _, came in pairs], *cover))
+        return [(keep, v) for (keep, _), v in zip(pairs, came)]
+
+    def split(pairs, n):
+        out = []
+        for (kept, came), order in zip(pairs, orders, strict=True):
+            total = kept + came.astype(F32)
+            keep, send = halves(total, flags[order[n]], piece(order, n))
+            out.append((keep, send.astype(BF16)))
+        return out
+
+    def sends(pairs):
+        return [send for _, send in pairs]
+
+    def rounded(pairs):
+        return [(keep + came.astype(F32)).astype(BF16) for keep, came in pairs]
+
+    def over_bands(sums, groups):
+        return [lax.psum(v, "dp", axis_index_groups=groups) for v in sums]
+
+    lead = jnp.stack([flags[o[0]] for o in orders])
+    pieces = tuple(piece(o, 0) for o in orders)
+    q1 = hidden_layer(act, bg, we_peer, wp_peer, eb_peer, 0, first, lead)
+    c1 = other_core(q1[2:4])
+    q2 = hidden_layer(act, bg, we_peer, wp_peer, after(eb_peer, q1[0]), first, second, lead)
+    c2 = other_core(q2[2:4])
+    o1 = hidden_layer(act, bg, we_own, wp_own, after(eb_own, q2[0]), 0, first, lead, c1, pieces)
+    s1 = exchanged([(o1[2], o1[3]), (o1[4], o1[5])], 0)
+    o2 = hidden_layer(act, bg, we_own, wp_own, after(eb_own, o1[0]), first, second, lead, c2, pieces)
+    for n in range(1, len(bits)):
+        s1 = split(arrived(s1, o2[0]), n)
+        last = sends(s1)
+        s1 = exchanged(s1, n)
+    s2 = exchanged([(o2[2], after(o2[3], *last)), (o2[4], after(o2[5], *last))], 0)
 
     cuts = ((1, 0, first), (0, 0, first), (1, first, second), (0, first, second))
     parts = (q1, o1, q2, o2)
-    s2 = added(q2, o2)
-    ready = after(stat, s1[2], s1[3], s2[2], s2[3])
+    hidden = [p[0] for p in parts]
+    block_out = block_output((wp_own, wp_peer), hidden, cuts, x, m16, after(par, *last))
+    s1 = rounded(arrived(s1, block_out))
+    b1 = over_bands(s1, groups)
+    for n in range(1, len(bits)):
+        s2 = split(arrived(s2, block_out, *s1), n)
+        last = sends(s2)
+        s2 = exchanged(s2, n)
+    ready = after(stat, *s1, *last)
     da, sums = activation_gradient((we_own, we_peer), [p[1] for p in parts], cuts, conv, ready, copies)
     sums = lax.all_to_all(sums, devices, 0, 0)
-    s1 = over_bands(s1)
-    block_out = block_output(
-        (wp_own, wp_peer), [p[0] for p in parts], cuts, x, m16, after(par, da, s2[2], s2[3])
-    )
-    for n in range(len(bits) - 1):
-        s2 = stage(s2, n)
-    conv_grad, totals = conv_gradient(da, conv, m16, sums, stat, after(par, block_out, s2[2], s2[3]))
-    g_up, g_dn = halo(conv_grad)
-    s2 = stage(s2, len(bits) - 1)
-    s2 = {k: v.astype(BF16) for k, v in s2.items()}
-    tap_local = tap_gradient(x, x_up, x_dn, after(conv_grad, s2[2], s2[3]), block, share)
-    s2 = over_bands({k: after(v, s1[2], s1[3]) for k, v in s2.items()})
-
-    eb_o = jnp.concatenate([o1[4], o2[4]], axis=1)
-    eb_q = jnp.concatenate([q1[4], q2[4]], axis=1)
+    s2 = rounded(arrived(s2, da))
+    conv_grad, g_first, g_last, totals = conv_gradient(da, conv, m16, sums, stat, after(par, *s2))
+    g_up, g_dn = halo(g_first, g_last)
+    b2 = over_bands(s2, groups[::-1])
+    tap_local = tap_gradient(x, x_up, x_dn, conv_grad, block, share)
+
+    eb_o = jnp.concatenate([o1[-1], o2[-1]], axis=1)
+    eb_q = jnp.concatenate([q1[-1], q2[-1]], axis=1)
     eb_all = jnp.concatenate(
         [jnp.where(core == 0, eb_o, eb_q), jnp.where(core == 0, eb_q, eb_o)], axis=1
     )[0, :units]
@@ -772,18 +911,18 @@
         ],
         axis=1,
     )
-    local = jnp.sum(lax.all_to_all(local, "fsdp", 0, 0), axis=0)
-    input_grad = input_gradient(conv_grad, g_up, g_dn, after(par, tap_local), pick, og, m16, block)
-    local = jnp.sum(from_all(local, "dp"), axis=0)
-
-    def joined(which):
-        mine = jnp.concatenate([s1[which], after(s2[which], input_grad)], axis=1)
-        other = flip_bit(mine, "dp", 0)
-        low, high = jnp.where(core == 0, mine, other), jnp.where(core == 0, other, mine)
-        return jnp.concatenate([low, high], axis=1)[:, :units].astype(F32)
-
-    project_grad = joined(2)
-    expand_grad = joined(3)
+    local = lax.all_to_all(local, "fsdp", 0, 0)
+    local = from_all(jnp.sum(local, axis=0), "dp")
+    g_up, g_dn, ready, _ = lax.optimization_barrier((g_up, g_dn, par, tap_local))
+    input_grad = input_gradient(conv_grad, g_up, g_dn, ready, og, m16, block)
+    local = jnp.sum(after(local, input_grad), axis=0)
+
+    pairs = []
+    for one, two in zip(b1, b2, strict=True):
+        two = after(two, input_grad)
+        pairs.append([(one, flip_bit(one, "dp", 0)), (two, flip_bit(two, "dp", 0))])
+    starts = ((0, half), (first, half + first))
+    project_grad, expand_grad = place_columns(core, pairs, starts, units)
 
     start = lax.axis_index("fsdp") * share
     totals = totals.reshape(2, -1)

time: 362 us -> 331 us (0.914)
  other arithmetic: 35.6 us -> 13.1 us
  waiting for transfers between devices: 53.7 us -> 41.8 us
  blocking collectives: 0 us -> 8.85 us
  local copies, waits for them, and re-layouts: 30.2 us -> 25.5 us
    psum x2, waiting for transfers between devices: 29.2 us -> 5.97 us  [over_bands(): return [lax.psum(v, 'dp', axis_index_groups=groups) for v in sums]]
    add x8 -> x4, other arithmetic: 13.5 us -> 2.89 us  [split(): total = kept + came.astype(F32)]
    all_to_all x1, waiting for transfers between devices: 0.01 us -> 9.23 us  [per_device(): sums = lax.all_to_all(sums, devices, 0, 0)]
    all_to_all x0 -> x1, blocking collectives: none -> 8.85 us  [per_device(): local = lax.all_to_all(local, 'fsdp', 0, 0)]
    ppermute x20 -> x24, waiting for transfers between devices: 11.4 us -> 17.9 us  [flip_bit(): return lax.ppermute(values, axis, [(i, i ^ 1 << bit) for i in range(size)])]
    ppermute x4, starting transfers between devices: 10.9 us -> 5.45 us  [halo(): return (lax.ppermute(last, 'dp', up), lax.ppermute(first, 'dp', down))]
    select_n x6 -> x0, other arithmetic: 5.07 us -> none  [the longest x4 4.83 us: gather_step(): first, second = (jnp.where(mine, have, other), jnp.where(mine, other, have))]
    concatenate x4 -> x0, other arithmetic: 4.47 us -> none  [gather_step(): return jnp.concatenate([first, second], axis=dim)]
  transfers between devices with their start and end apart: 31 -> 34, of which waited for: 5 -> 8; matrix products, arithmetic and copies ran while one was open for 16% -> 6% of each run, Pallas kernels for 46% -> 52%
where the time goes in v3:
time: 331 us; the launch traced here: 329 us
  Pallas kernels  181 us (55%)
  starting transfers between devices  44.2 us (13%)
  waiting for transfers between devices  41.8 us (13%)
  local copies, waits for them, and re-layouts  25.5 us (8%)
  between operations  15.2 us (5%)
  other arithmetic  13.1 us (4%)
  blocking collectives  8.85 us (3%)
    pallas_call x4, Pallas kernels, hidden_layer(): pl.pallas_call(functools.partial(hidden_kernel, step=128, pieces=pieces),...  62.8 us
    pallas_call x1, Pallas kernels, conv_forward(): pl.pallas_call(functools.partial(conv_kernel, share=share), grid=(channel...  20.9 us
    ppermute x24, starting transfers between devices, flip_bit(): return lax.ppermute(values, axis, [(i, i ^ 1 << bit) for i in range(size)])  18.9 us
    ppermute x24, waiting for transfers between devices, flip_bit(): return lax.ppermute(values, axis, [(i, i ^ 1 << bit) for i in range(size)])  17.9 us
    pallas_call x1, Pallas kernels, tap_gradient(): pl.pallas_call(functools.partial(tap_grad_kernel, share=share), grid=(cha...  17.7 us
    pallas_call x1, Pallas kernels, input_gradient(): pl.pallas_call(input_grad_kernel, grid=(channels // block,), in_specs=[pl...  16.3 us
    pallas_call x1, Pallas kernels, activation_gradient(): pl.pallas_call(functools.partial(act_grad_kernel, cuts=cuts), grid=(rows,...  16.2 us
    pallas_call x1, Pallas kernels, block_output(): pl.pallas_call(functools.partial(block_out_kernel, cuts=cuts), grid=(rows...  14.7 us
  transfers between devices with their start and end apart: 34, of which 8 were waited for; matrix products, arithmetic and copies ran while one was open for 6% of the time, Pallas kernels for 52%

profile of v3, /device:TPU:0, one launch (start us, length us, event | category | flops | bytes accessed | tf_op | source)
XLA Modules:
  0.0 329.3 jit_solution(6373507615191101767)
XLA Ops:
  8.6 1.5 concatenate.47
  10.8 5.2 %all-to-all-start = ((f32[4,56,200]{2,1,0:T(8,128)}), f32[4,56,200]{2,1,0:T(8,128)S(1)}, u32[]{:S(2)}, u32[]{:S(2)}) async-start(f32[4,56,200]{2,1,0:T(8,128)} %broadcast_in_dim.46), calls=%async_computation | async-start | bytes 458752 | tf_op jit(solution)/shard_map/all_to_all | solution.py:732
  16.0 3.4 %fusion.1 = (bf16[3,800,256]{2,1,0:T(8,128)(2,1)}, bf16[3,800,256]{2,1,0:T(8,128)(2,1)}) fusion(bf16[6,800,256]{2,1,0:T(8,128)(2,1)} %bitcast.37), kind=kLoop, calls=%fused_computation.33 | loop fusion | bytes 4915200 | tf_op jit(solution)/shard_map/slice | solution.py:795
  19.4 1.5 collective-permute-start.4
  22.8 1.2 constant_dynamic-slice_fusion.refs_4_
  24.1 1.9 collective-permute-start.2
  26.9 1.5 collective-permute-start
  28.4 1.3 collective-permute-start.5
  31.6 5.5 %mask_gradient.1 = (bf16[800,1536]{1,0:T(8,128)(2,1)}, f32[1,16,128]{2,1,0:T(8,128)}) custom-call(bf16[6,800,256]{2,1,0:T(8,128)(2,1)} %bitcast.41, f32[6,16,256]{2,1,0:T(8,128)} %broadcast_in_dim.47.m_ref.refs_7_), custom_call_target="tpu_custom_call" | custom-call | flops 126500000 | bytes 100000 | tf_op jit(solution)/shard_map/mask_gradient/pallas_call | solution.py:326
  37.1 3.5 %collective-permute-done.2.refs_6_ = bf16[200,1664]{1,0:T(8,128)(2,1)} collective-permute-done((bf16[200,1664]{1,0:T(8,128)(2,1)S(1)}, bf16[200,1664]{1,0:T(8,128)(2,1)}, u32[]{:S(2)}, u32[]{:S(2)}) %collective-permute-start.2) | collective-permute-done | bytes 665632 | tf_op jit(solution)/shard_map/ppermute | solution.py:737
  40.7 2.0 collective-permute-start.3
  42.6 1.4 collective-permute-done.refs_1_
  44.1 2.0 collective-permute-start.7
  46.1 1.5 collective-permute-start.6
  48.6 20.9 %conv_forward.1 = (f32[6,800,256]{2,1,0:T(8,128)}, f32[32,16,128]{2,1,0:T(8,128)}, f32[800,128]{1,0:T(8,128)}) custom-call(bf16[6,800,256]{2,1,0:T(8,128)(2,1)} %bitcast.38, bf16[3,800,256]{2,1,0:T(8,128)(2,1)} %copy-done.1, bf16[3,800,256]{2,1,0:T(8,128)(2,1)} %copy-done.2, f32[4,56,200]{2,1,0:T(8,128)} %copy-done.14, ...), custom_call_target="tpu_custom_call" | custom-call | flops 460000000 | bytes 100000 | tf_op jit(solution)/shard_map/conv_forward/pallas_call | solution.py:158
  69.5 3.6 %collective-permute-done.7.refs_5_ = bf16[200,1664]{1,0:T(8,128)(2,1)} collective-permute-done((bf16[200,1664]{1,0:T(8,128)(2,1)S(1)}, bf16[200,1664]{1,0:T(8,128)(2,1)}, u32[]{:S(2)}, u32[]{:S(2)}) %collective-permute-start.7) | collective-permute-done | bytes 665632 | tf_op jit(solution)/shard_map/ppermute | solution.py:737
  73.1 2.8 collective-permute-done.6.refs_2_
  76.0 5.8 %join_pieces.1 = (bf16[800,1664]{1,0:T(8,128)(2,1)}, bf16[800,1664]{1,0:T(8,128)(2,1)}) custom-call(s32[1]{0:T(128)} %bitcast.10.index_ref, bf16[200,1664]{1,0:T(8,128)(2,1)} %constant_dynamic-slice_fusion.1.refs_0_, bf16[200,1664]{1,0:T(8,128)(2,1)} %collective-permute-done.refs_1_, bf16[200,1664]{1,0:T(8,128)(2,1)} %collective-permute-done.6.refs_2_, ...), custom_call_target="tpu_custom_call" | custom-call | flops 92000000 | bytes 100000 | tf_op jit(solution)/shard_map/join_pieces/pallas_call | solution.py:672
  82.3 4.7 %all-to-all-start.1 = ((f32[32,16,128]{2,1,0:T(8,128)}), f32[32,16,128]{2,1,0:T(8,128)S(1)}, u32[]{:S(2)}, u32[]{:S(2)}) async-start(f32[32,16,128]{2,1,0:T(8,128)} %get-tuple-element.95), calls=%async_computation.1 | async-start | bytes 524288 | tf_op jit(solution)/shard_map/all_to_all | solution.py:828
  89.4 8.6 %all-to-all-done.1.all_ref = f32[32,16,128]{2,1,0:T(8,128)S(1)} async-done(((f32[32,16,128]{2,1,0:T(8,128)}), f32[32,16,128]{2,1,0:T(8,128)S(1)}, u32[]{:S(2)}, u32[]{:S(2)}) %all-to-all-start.1) | async-done | bytes 262176 | tf_op jit(solution)/shard_map/all_to_all | solution.py:828
  98.7 6.7 %activate.1 = (bf16[800,1536]{1,0:T(8,128)(2,1)}, f32[32,128]{1,0:T(8,128)}) custom-call(f32[6,800,256]{2,1,0:T(8,128)} %get-tuple-element.90.conv_ref.refs_6_, f32[32,16,128]{2,1,0:T(8,128)} %copy-done.12, f32[800,128]{1,0:T(8,128)} %get-tuple-element.143.par_ref.refs_8_), custom_call_target="tpu_custom_call" | custom-call | flops 149500000 | bytes 100000 | tf_op jit(solution)/shard_map/activate/pallas_call | solution.py:377
  105.4 13.4 %hidden_layer.4 = (bf16[1536,768]{1,0:T(8,128)(2,1)}, bf16[1536,768]{1,0:T(8,128)(2,1)}, bf16[800,768]{1,0:T(8,128)(2,1)}, bf16[800,768]{1,0:T(8,128)(2,1)}, f32[1,768]{1,0:T(1,128)}) custom-call(s32[2]{0:T(128)} %pad_add_fusion.bits_ref, bf16[800,1536]{1,0:T(8,128)(2,1)} %get-tuple-element.97.act_ref, bf16[800,1536]{1,0:T(8,128)(2,1)} %get-tuple-element.85.bg_ref, ...), custom_call_target="tpu_custom_call" | custom-call | flops 345000000 | bytes 100000 | tf_op jit(solution)/shard_map/hidden_layer/pallas_call | solution.py:469
  119.3 17.0 %hidden_layer.5 = (bf16[1536,896]{1,0:T(8,128)(2,1)}, bf16[1536,896]{1,0:T(8,128)(2,1)}, bf16[800,896]{1,0:T(8,128)(2,1)}, bf16[800,896]{1,0:T(8,128)(2,1)}, f32[1,896]{1,0:T(1,128)}) custom-call(s32[2]{0:T(128)} %pad_add_fusion.bits_ref, bf16[800,1536]{1,0:T(8,128)(2,1)} %get-tuple-element.97.act_ref, bf16[800,1536]{1,0:T(8,128)(2,1)} %get-tuple-element.85.bg_ref, ...), custom_call_target="tpu_custom_call" | custom-call | flops 345000000 | bytes 100000 | tf_op jit(solution)/shard_map/hidden_layer/pallas_call | solution.py:469
  137.0 1.6 copy-done
  138.5 14.3 %hidden_layer.6 = (bf16[1536,768]{1,0:T(8,128)(2,1)}, bf16[1536,768]{1,0:T(8,128)(2,1)}, f32[400,768]{1,0:T(8,128)}, bf16[400,768]{1,0:T(8,128)(2,1)}, f32[400,7...) custom-call(s32[2]{0:T(128)} %pad_add_fusion.bits_ref, bf16[800,1536]{1,0:T(8,128)(2,1)} %get-tuple-element.97.act_ref, ...), custom_call_target="tpu_custom_call" | custom-call | flops 345000000 | bytes 100000 | tf_op jit(solution)/shard_map/hidden_layer/pallas_call | solution.py:469
  153.1 1.3 collective-permute-start.15
  154.3 18.0 %hidden_layer.7 = (bf16[1536,896]{1,0:T(8,128)(2,1)}, bf16[1536,896]{1,0:T(8,128)(2,1)}, f32[400,896]{1,0:T(8,128)}, bf16[400,896]{1,0:T(8,128)(2,1)}, f32[400,8...) custom-call(s32[2]{0:T(128)} %pad_add_fusion.bits_ref, bf16[800,1536]{1,0:T(8,128)(2,1)} %get-tuple-element.97.act_ref, ...), custom_call_target="tpu_custom_call" | custom-call | flops 345000000 | bytes 100000 | tf_op jit(solution)/shard_map/hidden_layer/pallas_call | solution.py:469
  175.4 1.9 collective-permute-start.18
  177.4 1.3 collective-permute-start.16
  178.7 14.7 %block_output.1 = bf16[6,800,256]{2,1,0:T(8,128)(2,1)} custom-call(bf16[800,1664]{1,0:T(8,128)(2,1)} %collective-permute-done.8.wp_ref.refs_0_, bf16[800,1664]{1,0:T(8,128)(2,1)} %get-tuple-element.94.wp_ref.refs_1_, bf16[1536,768]{1,0:T(8,128)(2,1)} %get-tuple-element.99.refs_2_, bf16[1536,768]{1,0:T(8,128)(2,1)} %get-tuple-element.105.refs_3_, ...), custom_call_target="tpu_custom_call" | custom-call | flops 333500000 | bytes 100000 | tf_op jit(solution)/shard_map/block_output/pallas_call | solution.py:559
  193.4 6.4 %collective-permute-done.17 = bf16[200,768]{1,0:T(8,128)(2,1)} collective-permute-done((bf16[200,768]{1,0:T(8,128)(2,1)}, bf16[200,768]{1,0:T(8,128)(2,1)}, u32[]{:S(2)}, u32[]{:S(2)}) %collective-permute-start.17) | collective-permute-done | bytes 307232 | tf_op jit(solution)/shard_map/ppermute | solution.py:737
  199.8 2.1 add_convert_fusion.2
  202.0 1.3 convert_add_fusion
  204.1 1.3 convert_add_fusion.1
  206.2 1.6 collective-permute-start.21
  208.2 16.2 %activation_gradient.1 = (f32[6,800,256]{2,1,0:T(8,128)}, f32[32,16,128]{2,1,0:T(8,128)}) custom-call(bf16[800,1664]{1,0:T(8,128)(2,1)} %copy-done, bf16[800,1664]{1,0:T(8,128)(2,1)} %get-tuple-element.98.we_ref.refs_1_, bf16[1536,768]{1,0:T(8,128)(2,1)} %get-tuple-element.117.refs_2_, bf16[1536,768]{1,0:T(8,128)(2,1)} %get-tuple-element.118.refs_3_, ...), custom_call_target="tpu_custom_call" | custom-call | flops 368000000 | bytes 100000 | tf_op jit(solution)/shard_map/activation_gradient/pallas_call | solution.py:526
  224.5 3.1 all-to-all-start.2
  228.4 1.8 add_convert_fusion.1
  230.2 9.2 %all-to-all-done.2.all_ref = f32[32,16,128]{2,1,0:T(8,128)S(1)} async-done(((f32[32,16,128]{2,1,0:T(8,128)}), f32[32,16,128]{2,1,0:T(8,128)S(1)}, u32[]{:S(2)}, u32[]{:S(2)}) %all-to-all-start.2) | async-done | bytes 262176 | tf_op jit(solution)/shard_map/all_to_all | solution.py:894
  240.2 9.8 %conv_gradient.1 = (bf16[6,800,256]{2,1,0:T(8,128)(2,1)}, bf16[3,800,256]{2,1,0:T(8,128)(2,1)}, bf16[3,800,256]{2,1,0:T(8,128)(2,1)}, f32[16,128]{1,0:T(8,128)}) custom-call(f32[6,800,256]{2,1,0:T(8,128)} %get-tuple-element.133.da_ref, f32[6,800,256]{2,1,0:T(8,128)} %get-tuple-element.90.conv_ref.refs_6_, f32[6,16,256]{2,1,0:T(8,128)} %broadcast_in_dim.47.m_ref.refs_7_, ...), custom_call_target="tpu_custom_call" | custom-call | flops 218500000 | bytes 100000 | tf_op jit(solution)/shard_map/conv_gradient/pallas_call | solution.py:615
  250.0 1.4 collective-permute-start.22
  251.3 1.3 collective-permute-start.23
  252.9 17.7 %tap_gradient.1 = f32[4,49,200]{2,1,0:T(8,128)} custom-call(bf16[6,800,256]{2,1,0:T(8,128)(2,1)} %bitcast.40, bf16[3,800,256]{2,1,0:T(8,128)(2,1)} %copy-done.1, bf16[3,800,256]{2,1,0:T(8,128)(2,1)} %copy-done.2, bf16[6,800,256]{2,1,0:T(8,128)(2,1)} %get-tuple-element.138.g_ref), custom_call_target="tpu_custom_call" | custom-call | flops 402500000 | bytes 100000 | tf_op jit(solution)/shard_map/tap_gradient/pallas_call | solution.py:280
  271.5 8.9 %all_to_all.25 = f32[4,54,200]{2,1,0:T(8,128)S(1)} all-to-all(f32[4,54,200]{2,1,0:T(8,128)S(1)} %pad_maximum_fusion), channel_id=1, replica_groups=mesh['dp'=8,'fsdp'=4] {'fsdp'}, dimensions={0} | all-to-all | bytes 345600 | tf_op jit(solution)/shard_map/all_to_all | solution.py:914
  281.2 6.7 %all-to-all-start.4 = ((f32[8,54,200]{2,1,0:T(8,128)}), f32[8,54,200]{2,1,0:T(8,128)S(1)}, u32[]{:S(2)}, u32[]{:S(2)}) async-start(f32[8,54,200]{2,1,0:T(8,128)} %broadcast_in_dim.51), calls=%async_computation.4 | async-start | bytes 917504 | tf_op jit(solution)/shard_map/all_to_all | solution.py:732
  291.1 16.3 %input_gradient.1 = f32[6,800,256]{2,1,0:T(8,128)} custom-call(bf16[6,800,256]{2,1,0:T(8,128)(2,1)} %get-tuple-element.138.g_ref, bf16[3,800,256]{2,1,0:T(8,128)(2,1)} %copy-done.8, bf16[3,800,256]{2,1,0:T(8,128)(2,1)} %copy-done.9, f32[800,128]{1,0:T(8,128)} %get-tuple-element.143.par_ref.refs_8_, bf16[6,800,256]{2,1,0:T(8,128)(2,1)} %bitcast.42, ...), custom_call_target="tpu_custom_call" | custom-call | flops 368000000 | bytes 100000 | tf_op jit(solution)/shard_map/input_gradient/pallas_call | solution.py:216
  307.4 6.0 %all-reduce.10.cloned.1.call-done = (bf16[200,896]{1,0:T(8,128)(2,1)}, bf16[200,896]{1,0:T(8,128)(2,1)}) async-done(((bf16[200,896]{1,0:T(8,128)(2,1)}, bf16[200,896]{1,0:T(8,128)(2,1)}), (bf16[200,896]{1,0:T(8,128)(2,1)}, bf16[200,896]{1,0:T(8,128)(2,1)})) %all-reduce.10.cloned.1.call-update) | async-done | bytes 716816 | tf_op jit(solution)/shard_map/psum | solution.py:865
  318.1 4.3 %place_columns.1 = (f32[200,3200]{1,0:T(8,128)}, f32[200,3200]{1,0:T(8,128)}) custom-call(s32[1]{0:T(128)} %bitcast.22.core_ref, bf16[200,768]{1,0:T(8,128)(2,1)} %get-tuple-element.155.refs_0_, bf16[200,768]{1,0:T(8,128)(2,1)} %copy-done.17, bf16[200,896]{1,0:T(8,128)(2,1)} %get-tuple-element.151.refs_2_, bf16[200,896]{1,0:T(8,128)(2,1)} %copy-done.16, ...), custom_call_target="tpu_custom_call" | custom-call | flops 92000000 | bytes 100000 | tf_op jit(solution)/shard_map/place_columns/pallas_call | solution.py:703
  (141 shorter events, 28.8 us)
Async XLA Ops:
  10.8 12.0 %all-to-all-start = ((f32[4,56,200]{2,1,0:T(8,128)}), f32[4,56,200]{2,1,0:T(8,128)S(1)}, u32[]{:S(2)}, u32[]{:S(2)}) async-start(f32[4,56,200]{2,1,0:T(8,128)} %broadcast_in_dim.46), calls=%async_computation | async-start | bytes 458752 | tf_op jit(solution)/shard_map/all_to_all | solution.py:732
  16.0 4.9 %copy-start.6 = (bf16[200,3200]{1,0:T(8,128)(2,1)S(1)}, bf16[200,3200]{1,0:T(8,128)(2,1)}, u32[]{:S(2)}) copy-start(bf16[200,3200]{1,0:T(8,128)(2,1)} %param.20) | copy-start | bytes 3840004
  19.4 26.7 %collective-permute-start.4 = (bf16[3,800,256]{2,1,0:T(8,128)(2,1)}, bf16[3,800,256]{2,1,0:T(8,128)(2,1)S(1)}, u32[]{:S(2)}, u32[]{:S(2)}) collective-permute-start(bf16[3,800,256]{2,1,0:T(8,128)(2,1)} %get-tuple-element.160), channel_id=1, source_target_pairs={{0,4},{4,8},{8,12},{12,16},{16,20},{20,24},{24,28},{1,5},{5,9},{9,... | collective-permute-start | bytes 3686408 | tf_op jit(solution)/shard_map/ppermute | solution.py:721
  22.8 6.9 %copy-start.27 = (s32[4]{0:T(128)S(1)}, s32[4]{0:T(128)}, u32[]{:S(2)}) copy-start(s32[4]{0:T(128)} %param.14) | copy-start | bytes 52
  22.8 8.1 %copy-start.20 = (s32[6,256]{1,0:T(8,128)S(1)}, s32[6,256]{1,0:T(8,128)}, u32[]{:S(2)}) copy-start(s32[6,256]{1,0:T(8,128)} %param.13) | copy-start | bytes 18436
  22.8 14.3 %copy-start.14 = (f32[4,56,200]{2,1,0:T(8,128)}, f32[4,56,200]{2,1,0:T(8,128)S(1)}, u32[]{:S(2)}) copy-start(f32[4,56,200]{2,1,0:T(8,128)S(1)} %all-to-all-done.small_ref) | copy-start | bytes 537604
  24.1 20.0 %copy-start.3 = (bf16[200,1664]{1,0:T(8,128)(2,1)}, bf16[200,1664]{1,0:T(8,128)(2,1)S(1)}, u32[]{:S(2)}) copy-start(bf16[200,1664]{1,0:T(8,128)(2,1)S(1)} %constant_dynamic-slice_fusion.refs_4_) | copy-start | bytes 1996804
  24.1 16.6 %collective-permute-start.2 = (bf16[200,1664]{1,0:T(8,128)(2,1)S(1)}, bf16[200,1664]{1,0:T(8,128)(2,1)}, u32[]{:S(2)}, u32[]{:S(2)}) collective-permute-start(bf16[200,1664]{1,0:T(8,128)(2,1)S(1)} %constant_dynamic-slice_fusion.refs_4_), channel_id=1, source_target_pairs={{0,2},{1,3},{2,0},{3,1},{4,6},{5,7},{6,4},{7,5},{8,10},{9,11},{10,... | collective-permute-start | bytes 1996808 | tf_op jit(solution)/shard_map/ppermute | solution.py:737
  26.9 17.2 %collective-permute-start = (bf16[200,1664]{1,0:T(8,128)(2,1)}, bf16[200,1664]{1,0:T(8,128)(2,1)}, u32[]{:S(2)}, u32[]{:S(2)}) collective-permute-start(bf16[200,1664]{1,0:T(8,128)(2,1)} %constant_dynamic-slice_fusion.1.refs_0_), channel_id=1, source_target_pairs={{0,1},{1,0},{2,3},{3,2},{4,5},{5,4},{6,7},{7,6},{8,9},{9,8},{10,11... | collective-permute-start | bytes 1996808 | tf_op jit(solution)/shard_map/ppermute | solution.py:737
  28.4 19.2 %collective-permute-start.5 = (bf16[3,800,256]{2,1,0:T(8,128)(2,1)}, bf16[3,800,256]{2,1,0:T(8,128)(2,1)S(1)}, u32[]{:S(2)}, u32[]{:S(2)}) collective-permute-start(bf16[3,800,256]{2,1,0:T(8,128)(2,1)} %get-tuple-element.159), channel_id=1, source_target_pairs={{4,0},{8,4},{12,8},{16,12},{20,16},{24,20},{28,24},{5,1},{9,5},{13... | collective-permute-start | bytes 3686408 | tf_op jit(solution)/shard_map/ppermute | solution.py:722
  40.7 28.8 %collective-permute-start.3 = (bf16[200,1664]{1,0:T(8,128)(2,1)}, bf16[200,1664]{1,0:T(8,128)(2,1)}, u32[]{:S(2)}, u32[]{:S(2)}) collective-permute-start(bf16[200,1664]{1,0:T(8,128)(2,1)} %collective-permute-done.2.refs_6_), channel_id=1, source_target_pairs={{0,1},{1,0},{2,3},{3,2},{4,5},{5,4},{6,7},{7,6},{8,9},{9,8},{10,11... | collective-permute-start | bytes 1996808 | tf_op jit(solution)/shard_map/ppermute | solution.py:737
  44.1 25.4 %collective-permute-start.1 = (bf16[200,1664]{1,0:T(8,128)(2,1)}, bf16[200,1664]{1,0:T(8,128)(2,1)}, u32[]{:S(2)}, u32[]{:S(2)}) collective-permute-start(bf16[200,1664]{1,0:T(8,128)(2,1)} %collective-permute-done.refs_1_), channel_id=1, source_target_pairs={{0,2},{1,3},{2,0},{3,1},{4,6},{5,7},{6,4},{7,5},{8,10},{9,11},{10,... | collective-permute-start | bytes 1996808 | tf_op jit(solution)/shard_map/ppermute | solution.py:737
  44.1 29.0 %collective-permute-start.7 = (bf16[200,1664]{1,0:T(8,128)(2,1)S(1)}, bf16[200,1664]{1,0:T(8,128)(2,1)}, u32[]{:S(2)}, u32[]{:S(2)}) collective-permute-start(bf16[200,1664]{1,0:T(8,128)(2,1)S(1)} %constant_dynamic-slice_fusion.refs_4_), channel_id=1, source_target_pairs={{0,1},{1,0},{2,3},{3,2},{4,5},{5,4},{6,7},{7,6},{8,9},{9,8},{10,11... | collective-permute-start | bytes 1996808 | tf_op jit(solution)/shard_map/ppermute | solution.py:737
  46.1 29.9 %collective-permute-start.6 = (bf16[200,1664]{1,0:T(8,128)(2,1)}, bf16[200,1664]{1,0:T(8,128)(2,1)}, u32[]{:S(2)}, u32[]{:S(2)}) collective-permute-start(bf16[200,1664]{1,0:T(8,128)(2,1)} %constant_dynamic-slice_fusion.1.refs_0_), channel_id=1, source_target_pairs={{0,2},{1,3},{2,0},{3,1},{4,6},{5,7},{6,4},{7,5},{8,10},{9,11},{10,... | collective-permute-start | bytes 1996808 | tf_op jit(solution)/shard_map/ppermute | solution.py:737
  81.8 55.1 %collective-permute-start.8 = (bf16[800,1664]{1,0:T(8,128)(2,1)}, bf16[800,1664]{1,0:T(8,128)(2,1)}, u32[]{:S(2)}, u32[]{:S(2)}) collective-permute-start(bf16[800,1664]{1,0:T(8,128)(2,1)} %get-tuple-element.94.wp_ref.refs_1_), channel_id=1, source_target_pairs={{0,4},{4,0},{8,12},{12,8},{16,20},{20,16},{24,28},{28,24},{1,5},{5... | collective-permute-start | bytes 7987208 | tf_op jit(solution)/shard_map/ppermute | solution.py:737
  82.2 54.8 %collective-permute-start.9 = (bf16[800,1664]{1,0:T(8,128)(2,1)}, bf16[800,1664]{1,0:T(8,128)(2,1)S(1)}, u32[]{:S(2)}, u32[]{:S(2)}) collective-permute-start(bf16[800,1664]{1,0:T(8,128)(2,1)} %get-tuple-element.98.we_ref.refs_1_), channel_id=1, source_target_pairs={{0,4},{4,0},{8,12},{12,8},{16,20},{20,16},{24,28},{28,24},{1,5},{5... | collective-permute-start | bytes 7987208 | tf_op jit(solution)/shard_map/ppermute | solution.py:737
  82.3 15.7 %all-to-all-start.1 = ((f32[32,16,128]{2,1,0:T(8,128)}), f32[32,16,128]{2,1,0:T(8,128)S(1)}, u32[]{:S(2)}, u32[]{:S(2)}) async-start(f32[32,16,128]{2,1,0:T(8,128)} %get-tuple-element.95), calls=%async_computation.1 | async-start | bytes 524288 | tf_op jit(solution)/shard_map/all_to_all | solution.py:828
  87.1 201.4 %all-reduce.8.cloned.1.call-start = ((), (), s32[]{:S(2)}) async-start(), calls=%async_computation.5 | async-start | bytes 1228800 | tf_op jit(solution)/shard_map/psum | solution.py:865
  118.8 17.7 %collective-permute-start.10 = (bf16[800,768]{1,0:T(8,128)(2,1)}, bf16[800,768]{1,0:T(8,128)(2,1)}, u32[]{:S(2)}, u32[]{:S(2)}) collective-permute-start(bf16[800,768]{1,0:T(8,128)(2,1)} %get-tuple-element.103), channel_id=1, source_target_pairs={{0,4},{4,0},{8,12},{12,8},{16,20},{20,16},{24,28},{28,24},{1,5},{5... | collective-permute-start | bytes 3686408 | tf_op jit(solution)/shard_map/ppermute | solution.py:737
  118.8 18.1 %collective-permute-start.11 = (bf16[800,768]{1,0:T(8,128)(2,1)}, bf16[800,768]{1,0:T(8,128)(2,1)}, u32[]{:S(2)}, u32[]{:S(2)}) collective-permute-start(bf16[800,768]{1,0:T(8,128)(2,1)} %get-tuple-element.104), channel_id=1, source_target_pairs={{0,4},{4,0},{8,12},{12,8},{16,20},{20,16},{24,28},{28,24},{1,5},{5... | collective-permute-start | bytes 3686408 | tf_op jit(solution)/shard_map/ppermute | solution.py:737
  136.4 18.0 %collective-permute-start.12 = (bf16[800,896]{1,0:T(8,128)(2,1)}, bf16[800,896]{1,0:T(8,128)(2,1)}, u32[]{:S(2)}, u32[]{:S(2)}) collective-permute-start(bf16[800,896]{1,0:T(8,128)(2,1)} %get-tuple-element.107), channel_id=1, source_target_pairs={{0,4},{4,0},{8,12},{12,8},{16,20},{20,16},{24,28},{28,24},{1,5},{5... | collective-permute-start | bytes 4300808 | tf_op jit(solution)/shard_map/ppermute | solution.py:737
  136.5 17.8 %collective-permute-start.13 = (bf16[800,896]{1,0:T(8,128)(2,1)}, bf16[800,896]{1,0:T(8,128)(2,1)}, u32[]{:S(2)}, u32[]{:S(2)}) collective-permute-start(bf16[800,896]{1,0:T(8,128)(2,1)} %get-tuple-element.108), channel_id=1, source_target_pairs={{0,4},{4,0},{8,12},{12,8},{16,20},{20,16},{24,28},{28,24},{1,5},{5... | collective-permute-start | bytes 4300808 | tf_op jit(solution)/shard_map/ppermute | solution.py:737
  152.9 19.5 %collective-permute-start.14 = (bf16[400,768]{1,0:T(8,128)(2,1)}, bf16[400,768]{1,0:T(8,128)(2,1)S(1)}, u32[]{:S(2)}, u32[]{:S(2)}) collective-permute-start(bf16[400,768]{1,0:T(8,128)(2,1)} %get-tuple-element.111), channel_id=1, source_target_pairs={{0,2},{1,3},{2,0},{3,1},{4,6},{5,7},{6,4},{7,5},{8,10},{9,11},{10,... | collective-permute-start | bytes 1843208 | tf_op jit(solution)/shard_map/ppermute | solution.py:737
  153.1 19.3 %collective-permute-start.15 = (bf16[400,768]{1,0:T(8,128)(2,1)}, bf16[400,768]{1,0:T(8,128)(2,1)S(1)}, u32[]{:S(2)}, u32[]{:S(2)}) collective-permute-start(bf16[400,768]{1,0:T(8,128)(2,1)} %get-tuple-element.112), channel_id=1, source_target_pairs={{0,1},{1,0},{2,3},{3,2},{4,5},{5,4},{6,7},{7,6},{8,9},{9,8},{10,11... | collective-permute-start | bytes 1843208 | tf_op jit(solution)/shard_map/ppermute | solution.py:737
  154.3 18.0 %copy-start.11 = (f32[400,768]{1,0:T(8,128)S(1)}, f32[400,768]{1,0:T(8,128)}, u32[]{:S(2)}) copy-start(f32[400,768]{1,0:T(8,128)} %get-tuple-element.114) | copy-start | bytes 3686404
  174.6 27.3 %collective-permute-start.19 = (bf16[400,896]{1,0:T(8,128)(2,1)}, bf16[400,896]{1,0:T(8,128)(2,1)}, u32[]{:S(2)}, u32[]{:S(2)}) collective-permute-start(bf16[400,896]{1,0:T(8,128)(2,1)} %get-tuple-element.128), channel_id=1, source_target_pairs={{0,1},{1,0},{2,3},{3,2},{4,5},{5,4},{6,7},{7,6},{8,9},{9,8},{10,11... | collective-permute-start | bytes 2150408 | tf_op jit(solution)/shard_map/ppermute | solution.py:737
  175.4 26.5 %collective-permute-start.18 = (bf16[400,896]{1,0:T(8,128)(2,1)}, bf16[400,896]{1,0:T(8,128)(2,1)}, u32[]{:S(2)}, u32[]{:S(2)}) collective-permute-start(bf16[400,896]{1,0:T(8,128)(2,1)} %get-tuple-element.126), channel_id=1, source_target_pairs={{0,2},{1,3},{2,0},{3,1},{4,6},{5,7},{6,4},{7,5},{8,10},{9,11},{10,... | collective-permute-start | bytes 2150408 | tf_op jit(solution)/shard_map/ppermute | solution.py:737
  177.3 22.5 %collective-permute-start.17 = (bf16[200,768]{1,0:T(8,128)(2,1)}, bf16[200,768]{1,0:T(8,128)(2,1)}, u32[]{:S(2)}, u32[]{:S(2)}) collective-permute-start(bf16[200,768]{1,0:T(8,128)(2,1)} %select_convert_fusion.2), channel_id=1, source_target_pairs={{0,2},{1,3},{2,0},{3,1},{4,6},{5,7},{6,4},{7,5},{8,10},{9,11},{10,... | collective-permute-start | bytes 921608 | tf_op jit(solution)/shard_map/ppermute | solution.py:737
  177.4 22.4 %collective-permute-start.16 = (bf16[200,768]{1,0:T(8,128)(2,1)}, bf16[200,768]{1,0:T(8,128)(2,1)}, u32[]{:S(2)}, u32[]{:S(2)}) collective-permute-start(bf16[200,768]{1,0:T(8,128)(2,1)} %select_convert_fusion.3), channel_id=1, source_target_pairs={{0,1},{1,0},{2,3},{3,2},{4,5},{5,4},{6,7},{7,6},{8,9},{9,8},{10,11... | collective-permute-start | bytes 921608 | tf_op jit(solution)/shard_map/ppermute | solution.py:737
  193.4 8.5 %copy-start.5 = (f32[400,896]{1,0:T(8,128)S(1)}, f32[400,896]{1,0:T(8,128)}, u32[]{:S(2)}) copy-start(f32[400,896]{1,0:T(8,128)} %get-tuple-element.130) | copy-start | bytes 4300804
  204.1 4.0 %copy-start.26 = (f32[1,16,128]{2,1,0:T(8,128)S(1)}, f32[1,16,128]{2,1,0:T(8,128)}, u32[]{:S(2)}) copy-start(f32[1,16,128]{2,1,0:T(8,128)} %get-tuple-element.144) | copy-start | bytes 24580
  204.1 4.1 %copy-start.25 = (f32[1,768]{1,0:T(1,128)S(1)}, f32[1,768]{1,0:T(1,128)}, u32[]{:S(2)}) copy-start(f32[1,768]{1,0:T(1,128)} %get-tuple-element.147) | copy-start | bytes 9220
  204.1 4.1 %copy-start.23 = (f32[1,896]{1,0:T(1,128)S(1)}, f32[1,896]{1,0:T(1,128)}, u32[]{:S(2)}) copy-start(f32[1,896]{1,0:T(1,128)} %get-tuple-element.148) | copy-start | bytes 10756
  206.2 21.3 %collective-permute-start.21 = (bf16[200,896]{1,0:T(8,128)(2,1)}, bf16[200,896]{1,0:T(8,128)(2,1)S(1)}, u32[]{:S(2)}, u32[]{:S(2)}) collective-permute-start(bf16[200,896]{1,0:T(8,128)(2,1)} %select_convert_fusion), channel_id=1, source_target_pairs={{0,2},{1,3},{2,0},{3,1},{4,6},{5,7},{6,4},{7,5},{8,10},{9,11},{10,... | collective-permute-start | bytes 1075208 | tf_op jit(solution)/shard_map/ppermute | solution.py:737
  207.8 19.8 %collective-permute-start.20 = (bf16[200,896]{1,0:T(8,128)(2,1)}, bf16[200,896]{1,0:T(8,128)(2,1)}, u32[]{:S(2)}, u32[]{:S(2)}) collective-permute-start(bf16[200,896]{1,0:T(8,128)(2,1)} %select_convert_fusion.1), channel_id=1, source_target_pairs={{0,1},{1,0},{2,3},{3,2},{4,5},{5,4},{6,7},{7,6},{8,9},{9,8},{10,11... | collective-permute-start | bytes 1075208 | tf_op jit(solution)/shard_map/ppermute | solution.py:737
  224.5 15.0 %all-to-all-start.2 = ((f32[32,16,128]{2,1,0:T(8,128)}), f32[32,16,128]{2,1,0:T(8,128)S(1)}, u32[]{:S(2)}, u32[]{:S(2)}) async-start(f32[32,16,128]{2,1,0:T(8,128)} %get-tuple-element.134), calls=%async_computation.2 | async-start | bytes 524288 | tf_op jit(solution)/shard_map/all_to_all | solution.py:894
  227.5 85.8 %all-reduce.10.cloned.1.call-start = ((), (), s32[]{:S(2)}) async-start(), calls=%async_computation.6 | async-start | bytes 1433600 | tf_op jit(solution)/shard_map/psum | solution.py:865
  230.2 22.4 %copy-start.24 = (f32[1,768]{1,0:T(1,128)S(1)}, f32[1,768]{1,0:T(1,128)}, u32[]{:S(2)}) copy-start(f32[1,768]{1,0:T(1,128)} %get-tuple-element.145) | copy-start | bytes 9220
  230.2 22.4 %copy-start.22 = (f32[1,896]{1,0:T(1,128)S(1)}, f32[1,896]{1,0:T(1,128)}, u32[]{:S(2)}) copy-start(f32[1,896]{1,0:T(1,128)} %get-tuple-element.146) | copy-start | bytes 10756
  250.0 39.1 %collective-permute-start.22 = (bf16[3,800,256]{2,1,0:T(8,128)(2,1)}, bf16[3,800,256]{2,1,0:T(8,128)(2,1)S(1)}, u32[]{:S(2)}, u32[]{:S(2)}) collective-permute-start(bf16[3,800,256]{2,1,0:T(8,128)(2,1)} %get-tuple-element.139), channel_id=1, source_target_pairs={{0,4},{4,8},{8,12},{12,16},{16,20},{20,24},{24,28},{1,5},{5,9},{9,... | collective-permute-start | bytes 3686408 | tf_op jit(solution)/shard_map/ppermute | solution.py:721
  251.3 37.7 %collective-permute-start.23 = (bf16[3,800,256]{2,1,0:T(8,128)(2,1)}, bf16[3,800,256]{2,1,0:T(8,128)(2,1)S(1)}, u32[]{:S(2)}, u32[]{:S(2)}) collective-permute-start(bf16[3,800,256]{2,1,0:T(8,128)(2,1)} %get-tuple-element.140), channel_id=1, source_target_pairs={{4,0},{8,4},{12,8},{16,12},{20,16},{24,20},{28,24},{5,1},{9,5},{13... | collective-permute-start | bytes 3686408 | tf_op jit(solution)/shard_map/ppermute | solution.py:722
  270.5 17.3 %copy-start.19 = (f32[32,128]{1,0:T(8,128)S(1)}, f32[32,128]{1,0:T(8,128)}, u32[]{:S(2)}) copy-start(f32[32,128]{1,0:T(8,128)} %get-tuple-element.132.refs_7_.stat_ref) | copy-start | bytes 49156
  281.2 33.9 %all-to-all-start.4 = ((f32[8,54,200]{2,1,0:T(8,128)}), f32[8,54,200]{2,1,0:T(8,128)S(1)}, u32[]{:S(2)}, u32[]{:S(2)}) async-start(f32[8,54,200]{2,1,0:T(8,128)} %broadcast_in_dim.51), calls=%async_computation.4 | async-start | bytes 917504 | tf_op jit(solution)/shard_map/all_to_all | solution.py:732
  288.4 28.6 %collective-permute-start.24 = (bf16[200,768]{1,0:T(8,128)(2,1)}, bf16[200,768]{1,0:T(8,128)(2,1)S(1)}, u32[]{:S(2)}, u32[]{:S(2)}) collective-permute-start(bf16[200,768]{1,0:T(8,128)(2,1)} %get-tuple-element.155.refs_0_), channel_id=1, source_target_pairs={{0,4},{4,0},{8,12},{12,8},{16,20},{20,16},{24,28},{28,24},{1,5},{5... | collective-permute-start | bytes 921608 | tf_op jit(solution)/shard_map/ppermute | solution.py:737
  288.9 24.9 %copy-start.21 = (f32[16,128]{1,0:T(8,128)S(1)}, f32[16,128]{1,0:T(8,128)}, u32[]{:S(2)}) copy-start(f32[16,128]{1,0:T(8,128)} %get-tuple-element.150) | copy-start | bytes 24580
  289.0 28.1 %collective-permute-start.26 = (bf16[200,768]{1,0:T(8,128)(2,1)}, bf16[200,768]{1,0:T(8,128)(2,1)S(1)}, u32[]{:S(2)}, u32[]{:S(2)}) collective-permute-start(bf16[200,768]{1,0:T(8,128)(2,1)} %get-tuple-element.156.refs_4_), channel_id=1, source_target_pairs={{0,4},{4,0},{8,12},{12,8},{16,20},{20,16},{24,28},{28,24},{1,5},{5... | collective-permute-start | bytes 921608 | tf_op jit(solution)/shard_map/ppermute | solution.py:737
  313.3 3.7 %collective-permute-start.27 = (bf16[200,896]{1,0:T(8,128)(2,1)}, bf16[200,896]{1,0:T(8,128)(2,1)S(1)}, u32[]{:S(2)}, u32[]{:S(2)}) collective-permute-start(bf16[200,896]{1,0:T(8,128)(2,1)} %get-tuple-element.152.refs_6_), channel_id=1, source_target_pairs={{0,4},{4,0},{8,12},{12,8},{16,20},{20,16},{24,28},{28,24},{1,5},{5... | collective-permute-start | bytes 1075208 | tf_op jit(solution)/shard_map/ppermute | solution.py:737
  313.4 3.7 %collective-permute-start.25 = (bf16[200,896]{1,0:T(8,128)(2,1)}, bf16[200,896]{1,0:T(8,128)(2,1)S(1)}, u32[]{:S(2)}, u32[]{:S(2)}) collective-permute-start(bf16[200,896]{1,0:T(8,128)(2,1)} %get-tuple-element.151.refs_2_), channel_id=1, source_target_pairs={{0,4},{4,0},{8,12},{12,8},{16,20},{20,16},{24,28},{28,24},{1,5},{5... | collective-permute-start | bytes 1075208 | tf_op jit(solution)/shard_map/ppermute | solution.py:737
  (14 other events, 16.4 us)
Sparse Core Ops, SparseCore 0:
  208.4 39.5 all-reduce.7
  252.8 60.4 all-reduce.9

commit v4 on v3

--- a/solution.py
+++ b/solution.py
@@ -293,7 +293,7 @@
             pltpu.VMEM((padded, 128), F32),
         ],
         compiler_params=params(),
-        cost_estimate=cost(0.35),
+        cost_estimate=cost(6),
         name="tap_gradient",
     )(x, up, dn, grad)
 
@@ -478,6 +478,50 @@
     )(*operands)
 
 
+def split_kernel(bits_ref, *refs, pieces):
+    n = len(pieces)
+    for k, piece in enumerate(pieces):
+        total = refs[2 * k][...] + refs[2 * k + 1][...].astype(F32)
+        keep, send = halves(total, bits_ref[k], piece)
+        refs[2 * n + 2 * k][...] = keep
+        refs[2 * n + 2 * k + 1][...] = send.astype(BF16)
+
+
+def split_sums(bits, pairs, pieces):
+    rows, cols = pairs[0][0].shape
+    shape = lambda dtype: jax.ShapeDtypeStruct((rows // 2, cols), dtype)
+    spec = lambda height: pl.BlockSpec((height, cols), lambda: (0, 0))
+    out = pl.pallas_call(
+        functools.partial(split_kernel, pieces=pieces),
+        in_specs=[pl.BlockSpec(memory_space=pltpu.SMEM)] + [spec(rows)] * (2 * len(pairs)),
+        out_specs=[spec(rows // 2)] * (2 * len(pairs)),
+        out_shape=[shape(F32), shape(BF16)] * len(pairs),
+        compiler_params=params(),
+        cost_estimate=cost(3),
+        name="split_sums",
+    )(bits, *[v for pair in pairs for v in pair])
+    return [(out[2 * k], out[2 * k + 1]) for k in range(len(pairs))]
+
+
+def round_kernel(*refs):
+    n = len(refs) // 3
+    for k in range(n):
+        refs[2 * n + k][...] = (refs[2 * k][...] + refs[2 * k + 1][...].astype(F32)).astype(BF16)
+
+
+def round_sums(pairs):
+    spec = pl.BlockSpec(pairs[0][0].shape, lambda: (0, 0))
+    return pl.pallas_call(
+        round_kernel,
+        in_specs=[spec] * (2 * len(pairs)),
+        out_specs=[spec] * len(pairs),
+        out_shape=[jax.ShapeDtypeStruct(pairs[0][0].shape, BF16)] * len(pairs),
+        compiler_params=params(),
+        cost_estimate=cost(3),
+        name="round_sums",
+    )(*[v for pair in pairs for v in pair])
+
+
 def contract(weights, hiddens):
     total = None
     for (w_ref, first, units), h_ref in zip(weights, hiddens, strict=True):
@@ -637,7 +681,7 @@
         ],
         scratch_shapes=[pltpu.VMEM((4, channels, 128), F32)],
         compiler_params=params(),
-        cost_estimate=cost(0.19),
+        cost_estimate=cost(0.2),
         name="conv_gradient",
     )(da, conv, m16, sums, stat, par)
 
@@ -780,9 +824,10 @@
     block = 5 * GRP
 
     ratio = expand_bias.shape[0] // share
+    x_first, x_last = x[:REACH], x[-REACH:]
     small = jnp.concatenate(
         [
-            conv_weight.T,
+            after(conv_weight, x_first, x_last).T,
             norm_gain[None],
             norm_bias[None],
             project_bias.astype(F32)[None],
@@ -792,11 +837,12 @@
     )
     every = from_all(small, "fsdp")
     e_bias = jnp.pad(every[:, TAPS + 3 :].reshape(1, units), ((0, 0), (0, 2 * half - units)))
-    x_up, x_dn = halo(x[:REACH], x[-REACH:])
+    x_up, x_dn = halo(x_first, x_last)
 
     def columns(weight):
-        wide = jnp.pad(weight, ((0, 0), (0, 2 * half - units)))
-        return lax.dynamic_slice_in_dim(after(wide, every), (1 - core) * half, half, axis=1)
+        weight = after(weight, every)
+        high = jnp.pad(weight[:, half:], ((0, 0), (0, 2 * half - units)))
+        return jnp.where(core == 0, high, weight[:, :half])
 
     eb_own = lax.dynamic_slice_in_dim(e_bias, core * half, half, axis=1)
     eb_peer = lax.dynamic_slice_in_dim(e_bias, (1 - core) * half, half, axis=1)
@@ -809,28 +855,31 @@
 
     we_pieces = gather_pieces(columns(expand_weight), bits)
     wp_pieces = gather_pieces(columns(project_weight), bits[::-1])
-    bg, bg_sum = mask_gradient(og, after(m16, small))
+
+    copies = n_fs * n_dp
+    orders = (bits[::-1], bits)
+    flags = jnp.stack([bit_of("fsdp", bit) for bit in bits]).astype(jnp.int32)
+    lead = jnp.stack([flags[o[0]] for o in orders])
+    bg, bg_sum = mask_gradient(og, after(m16, we_pieces[0], wp_pieces[0]))
     early = [p[1 << b] for p, b in ((we_pieces, bits[0]), (wp_pieces, bits[-1]))]
     we_pieces = gather_others(we_pieces, bits, bg)
     wp_pieces = gather_others(wp_pieces, bits[::-1], bg)
-
-    copies = n_fs * n_dp
-    ready = after(m16, bg, *early)
+    ready, eb_own, eb_peer, lead, *_ = lax.optimization_barrier(
+        (m16, eb_own, eb_peer, lead, bg, *early)
+    )
     conv, stats, par = conv_forward(x, x_up, x_dn, every, ready, copies, block)
+    stats = lax.all_to_all(stats, devices, 0, 0)
     index = lax.axis_index("fsdp")
     far = n_fs - 1
     we_pieces[far], wp_pieces[far], index, _ = lax.optimization_barrier(
         (we_pieces[far], wp_pieces[far], index, conv)
     )
     we_peer, wp_peer = join_pieces(index, we_pieces, wp_pieces)
-    we_own = flip_bit(we_peer, "dp", 0)
-    wp_own = flip_bit(wp_peer, "dp", 0)
-    stats = lax.all_to_all(stats, devices, 0, 0)
-    act, stat = activate(conv, stats, par)
+    act, stat = activate(conv, after(stats, we_peer, wp_peer), par)
+    we_own = flip_bit(after(we_peer, act), "dp", 0)
+    wp_own = flip_bit(after(wp_peer, act), "dp", 0)
 
     groups = [[i for i in range(n_dp) if i % 2 == c] for c in range(2)]
-    orders = (bits[::-1], bits)
-    flags = jnp.stack([bit_of("fsdp", bit) for bit in bits]).astype(jnp.int32)
     first = half // (2 * TILE) * TILE
     second = half - first
 
@@ -848,23 +897,15 @@
         return [(keep, v) for (keep, _), v in zip(pairs, came)]
 
     def split(pairs, n):
-        out = []
-        for (kept, came), order in zip(pairs, orders, strict=True):
-            total = kept + came.astype(F32)
-            keep, send = halves(total, flags[order[n]], piece(order, n))
-            out.append((keep, send.astype(BF16)))
-        return out
+        taken = [flags[order[n]] for order in orders]
+        return split_sums(jnp.stack(taken), pairs, tuple(piece(order, n) for order in orders))
 
     def sends(pairs):
         return [send for _, send in pairs]
 
-    def rounded(pairs):
-        return [(keep + came.astype(F32)).astype(BF16) for keep, came in pairs]
-
     def over_bands(sums, groups):
         return [lax.psum(v, "dp", axis_index_groups=groups) for v in sums]
 
-    lead = jnp.stack([flags[o[0]] for o in orders])
     pieces = tuple(piece(o, 0) for o in orders)
     q1 = hidden_layer(act, bg, we_peer, wp_peer, eb_peer, 0, first, lead)
     c1 = other_core(q1[2:4])
@@ -877,26 +918,28 @@
         s1 = split(arrived(s1, o2[0]), n)
         last = sends(s1)
         s1 = exchanged(s1, n)
+
     s2 = exchanged([(o2[2], after(o2[3], *last)), (o2[4], after(o2[5], *last))], 0)
-
     cuts = ((1, 0, first), (0, 0, first), (1, first, second), (0, first, second))
     parts = (q1, o1, q2, o2)
     hidden = [p[0] for p in parts]
-    block_out = block_output((wp_own, wp_peer), hidden, cuts, x, m16, after(par, *last))
-    s1 = rounded(arrived(s1, block_out))
+    da, sums = activation_gradient(
+        (we_own, we_peer), [p[1] for p in parts], cuts, conv, after(stat, *last), copies
+    )
+    sums = lax.all_to_all(sums, devices, 0, 0)
+    s1 = round_sums(arrived(s1, da))
     b1 = over_bands(s1, groups)
     for n in range(1, len(bits)):
-        s2 = split(arrived(s2, block_out, *s1), n)
+        s2 = split(arrived(s2, da, *s1), n)
         last = sends(s2)
         s2 = exchanged(s2, n)
-    ready = after(stat, *s1, *last)
-    da, sums = activation_gradient((we_own, we_peer), [p[1] for p in parts], cuts, conv, ready, copies)
-    sums = lax.all_to_all(sums, devices, 0, 0)
-    s2 = rounded(arrived(s2, da))
-    conv_grad, g_first, g_last, totals = conv_gradient(da, conv, m16, sums, stat, after(par, *s2))
+    ready = after(sums, *last)
+    conv_grad, g_first, g_last, totals = conv_gradient(da, conv, m16, ready, stat, par)
     g_up, g_dn = halo(g_first, g_last)
-    b2 = over_bands(s2, groups[::-1])
-    tap_local = tap_gradient(x, x_up, x_dn, conv_grad, block, share)
+    s2 = round_sums(arrived(s2, conv_grad))
+    tap_local = tap_gradient(x, x_up, x_dn, after(conv_grad, *s2), block, share)
+    s2 = list(lax.optimization_barrier((*s2, *b1, tap_local))[:2])
+    b2 = over_bands(s2, groups)
 
     eb_o = jnp.concatenate([o1[-1], o2[-1]], axis=1)
     eb_q = jnp.concatenate([q1[-1], q2[-1]], axis=1)
@@ -912,14 +955,15 @@
         axis=1,
     )
     local = lax.all_to_all(local, "fsdp", 0, 0)
-    local = from_all(jnp.sum(local, axis=0), "dp")
     g_up, g_dn, ready, _ = lax.optimization_barrier((g_up, g_dn, par, tap_local))
     input_grad = input_gradient(conv_grad, g_up, g_dn, ready, og, m16, block)
     local = jnp.sum(after(local, input_grad), axis=0)
+    block_out = block_output((wp_own, wp_peer), hidden, cuts, x, m16, after(par, input_grad, local))
+    local = jnp.sum(after(from_all(local, "dp"), block_out), axis=0)
 
     pairs = []
     for one, two in zip(b1, b2, strict=True):
-        two = after(two, input_grad)
+        one, two = after(one, block_out), after(two, block_out)
         pairs.append([(one, flip_bit(one, "dp", 0)), (two, flip_bit(two, "dp", 0))])
     starts = ((0, half), (first, half + first))
     project_grad, expand_grad = place_columns(core, pairs, starts, units)

time: 331 us -> 311 us (0.940)
  Pallas kernels: 181 us -> 193 us
  other arithmetic: 13.1 us -> 3.46 us
  waiting for transfers between devices: 41.8 us -> 32.6 us
  blocking collectives: 8.85 us -> 0 us
  local copies, waits for them, and re-layouts: 25.5 us -> 19.8 us
    psum x2, waiting for transfers between devices: 5.97 us -> 18.9 us  [over_bands(): return [lax.psum(v, 'dp', axis_index_groups=groups) for v in sums]]
    pallas_call x0 -> x4, Pallas kernels: none -> 12.1 us  [the longest x2 7.2 us: split_sums(): pl.pallas_call(functools.partial(split_kernel, pieces=pieces), in_specs=[...]
    ppermute x24, waiting for transfers between devices: 17.9 us -> 7.28 us  [flip_bit(): return lax.ppermute(values, axis, [(i, i ^ 1 << bit) for i in range(size)])]
    all_to_all x1, waiting for transfers between devices: 9.23 us -> 0.01 us  [per_device(): sums = lax.all_to_all(sums, devices, 0, 0)]
    all_to_all x1 -> x0, blocking collectives: 8.85 us -> none  [per_device(): local = lax.all_to_all(local, 'fsdp', 0, 0)]
    convert_element_type x7 -> x0, other arithmetic: 7.89 us -> none  [the longest x3 4.73 us: rounded(): return [(keep + came.astype(F32)).astype(BF16) for keep, came in pairs]]
    all_to_all x1, waiting for transfers between devices: 8.62 us -> 4.9 us  [per_device(): stats = lax.all_to_all(stats, devices, 0, 0)]
    all_to_all x0 -> x1, starting transfers between devices: none -> 3.38 us  [per_device(): local = lax.all_to_all(local, 'fsdp', 0, 0)]
  transfers between devices with their start and end apart: 34 -> 35, of which waited for: 8 -> 8; matrix products, arithmetic and copies ran while one was open for 6% -> 3% of each run, Pallas kernels for 52% -> 59%
where the time goes in v4:
time: 311 us; the launch traced here: 310 us
  Pallas kernels  193 us (62%)
  starting transfers between devices  46.1 us (15%)
  waiting for transfers between devices  32.6 us (10%)
  local copies, waits for them, and re-layouts  19.8 us (6%)
  between operations  15.3 us (5%)
  other arithmetic  3.46 us (1%)
    pallas_call x4, Pallas kernels, hidden_layer(): pl.pallas_call(functools.partial(hidden_kernel, step=128, pieces=pieces),...  62.7 us
    pallas_call x1, Pallas kernels, conv_forward(): pl.pallas_call(functools.partial(conv_kernel, share=share), grid=(channel...  20.9 us
    psum x2, waiting for transfers between devices, over_bands(): return [lax.psum(v, 'dp', axis_index_groups=groups) for v in sums]  18.9 us
    pallas_call x1, Pallas kernels, tap_gradient(): pl.pallas_call(functools.partial(tap_grad_kernel, share=share), grid=(cha...  17.7 us
    ppermute x24, starting transfers between devices, flip_bit(): return lax.ppermute(values, axis, [(i, i ^ 1 << bit) for i in range(size)])  17.2 us
    pallas_call x1, Pallas kernels, input_gradient(): pl.pallas_call(input_grad_kernel, grid=(channels // block,), in_specs=[pl...  16.3 us
    pallas_call x1, Pallas kernels, activation_gradient(): pl.pallas_call(functools.partial(act_grad_kernel, cuts=cuts), grid=(rows,...  16.1 us
    pallas_call x1, Pallas kernels, block_output(): pl.pallas_call(functools.partial(block_out_kernel, cuts=cuts), grid=(rows...  14.8 us
  transfers between devices with their start and end apart: 35, of which 8 were waited for; matrix products, arithmetic and copies ran while one was open for 3% of the time, Pallas kernels for 59%

profile of v4, /device:TPU:0, one launch (start us, length us, event | category | flops | bytes accessed | tf_op | source)
XLA Modules:
  0.0 309.9 jit_solution(16827794204463432198)
XLA Ops:
  7.2 3.3 %fusion.1 = (bf16[3,800,256]{2,1,0:T(8,128)(2,1)}, bf16[3,800,256]{2,1,0:T(8,128)(2,1)}) fusion(bf16[6,800,256]{2,1,0:T(8,128)(2,1)} %bitcast.37), kind=kLoop, calls=%fused_computation.22 | loop fusion | bytes 4915200 | tf_op jit(solution)/shard_map/slice | solution.py:827
  11.4 5.2 %all-to-all-start = ((f32[4,56,200]{2,1,0:T(8,128)}), f32[4,56,200]{2,1,0:T(8,128)S(1)}, u32[]{:S(2)}, u32[]{:S(2)}) async-start(f32[4,56,200]{2,1,0:T(8,128)} %broadcast_in_dim.46), calls=%async_computation | async-start | bytes 458752 | tf_op jit(solution)/shard_map/all_to_all | solution.py:776
  16.6 2.5 collective-permute-start.4
  19.1 1.3 collective-permute-start.5
  20.4 1.5 all-to-all-done.small_ref
  22.1 1.2 collective-permute-start.2
  23.8 1.2 collective-permute-start
  27.0 0.9 collective-permute-start.7
  28.7 5.6 %mask_gradient.1 = (bf16[800,1536]{1,0:T(8,128)(2,1)}, f32[1,16,128]{2,1,0:T(8,128)}) custom-call(bf16[6,800,256]{2,1,0:T(8,128)(2,1)} %bitcast.41, f32[6,16,256]{2,1,0:T(8,128)} %broadcast_in_dim.47.m_ref.refs_7_), custom_call_target="tpu_custom_call" | custom-call | flops 126500000 | bytes 100000 | tf_op jit(solution)/shard_map/mask_gradient/pallas_call | solution.py:326
  34.2 5.3 %collective-permute-done.2.refs_6_ = bf16[200,1664]{1,0:T(8,128)(2,1)S(1)} collective-permute-done((bf16[200,1664]{1,0:T(8,128)(2,1)S(1)}, bf16[200,1664]{1,0:T(8,128)(2,1)S(1)}, u32[]{:S(2)}, u32[]{:S(2)}) %collective-permute-start.2) | collective-permute-done | bytes 665632 | tf_op jit(solution)/shard_map/ppermute | solution.py:781
  39.6 1.4 collective-permute-start.6
  41.6 1.1 collective-permute-start.3
  43.6 20.9 %conv_forward.1 = (f32[6,800,256]{2,1,0:T(8,128)}, f32[32,16,128]{2,1,0:T(8,128)}, f32[800,128]{1,0:T(8,128)}) custom-call(bf16[6,800,256]{2,1,0:T(8,128)(2,1)} %bitcast.38, bf16[3,800,256]{2,1,0:T(8,128)(2,1)} %collective-permute-done.4.up_ref, bf16[3,800,256]{2,1,0:T(8,128)(2,1)} %collective-permute-done.5.dn_ref, f32[4,56,200]{2,1,0:T(8,128)} %copy-done.10, ...), custom_call_target="tpu_custom_call" | custom-call | flops 460000000 | bytes 100000 | tf_op jit(solution)/shard_map/conv_forward/pallas_call | solution.py:158
  64.6 6.7 %all-to-all-start.1 = ((f32[32,16,128]{2,1,0:T(8,128)}), f32[32,16,128]{2,1,0:T(8,128)S(1)}, u32[]{:S(2)}, u32[]{:S(2)}) async-start(f32[32,16,128]{2,1,0:T(8,128)} %get-tuple-element.121), calls=%async_computation.1 | async-start | bytes 524288 | tf_op jit(solution)/shard_map/all_to_all | solution.py:871
  71.3 5.8 %join_pieces.1 = (bf16[800,1664]{1,0:T(8,128)(2,1)}, bf16[800,1664]{1,0:T(8,128)(2,1)}) custom-call(s32[1]{0:T(128)} %bitcast.12.index_ref, bf16[200,1664]{1,0:T(8,128)(2,1)} %copy-done.2, bf16[200,1664]{1,0:T(8,128)(2,1)} %copy-done.12, bf16[200,1664]{1,0:T(8,128)(2,1)} %collective-permute-done.6.refs_2_, bf16[200,1664]{1,0:T(8,128)(2,1)} %collective-permute-done.1.refs_3_, ...), custom_call_target="tpu_custom_call" | custom-call | flops 92000000 | bytes 100000 | tf_op jit(solution)/shard_map/join_pieces/pallas_call | solution.py:716
  77.2 4.9 %all-to-all-done.1.all_ref = f32[32,16,128]{2,1,0:T(8,128)S(1)} async-done(((f32[32,16,128]{2,1,0:T(8,128)}), f32[32,16,128]{2,1,0:T(8,128)S(1)}, u32[]{:S(2)}, u32[]{:S(2)}) %all-to-all-start.1) | async-done | bytes 262176 | tf_op jit(solution)/shard_map/all_to_all | solution.py:871
  82.8 6.8 %activate.1 = (bf16[800,1536]{1,0:T(8,128)(2,1)}, f32[32,128]{1,0:T(8,128)}) custom-call(f32[6,800,256]{2,1,0:T(8,128)} %get-tuple-element.116.conv_ref.refs_6_, f32[32,16,128]{2,1,0:T(8,128)} %copy-done.8, f32[800,128]{1,0:T(8,128)} %get-tuple-element.194.par_ref.refs_8_), custom_call_target="tpu_custom_call" | custom-call | flops 149500000 | bytes 100000 | tf_op jit(solution)/shard_map/activate/pallas_call | solution.py:377
  90.1 13.4 %hidden_layer.4 = (bf16[1536,768]{1,0:T(8,128)(2,1)}, bf16[1536,768]{1,0:T(8,128)(2,1)}, bf16[800,768]{1,0:T(8,128)(2,1)}, bf16[800,768]{1,0:T(8,128)(2,1)}, f32[1,768]{1,0:T(1,128)}) custom-call(s32[2]{0:T(128)} %pad_add_fusion.bits_ref, bf16[800,1536]{1,0:T(8,128)(2,1)} %get-tuple-element.125.act_ref, bf16[800,1536]{1,0:T(8,128)(2,1)} %get-tuple-element.112.bg_ref, ...), custom_call_target="tpu_custom_call" | custom-call | flops 345000000 | bytes 100000 | tf_op jit(solution)/shard_map/hidden_layer/pallas_call | solution.py:469
  104.0 17.0 %hidden_layer.5 = (bf16[1536,896]{1,0:T(8,128)(2,1)}, bf16[1536,896]{1,0:T(8,128)(2,1)}, bf16[800,896]{1,0:T(8,128)(2,1)}, bf16[800,896]{1,0:T(8,128)(2,1)}, f32[1,896]{1,0:T(1,128)}) custom-call(s32[2]{0:T(128)} %pad_add_fusion.bits_ref, bf16[800,1536]{1,0:T(8,128)(2,1)} %get-tuple-element.125.act_ref, bf16[800,1536]{1,0:T(8,128)(2,1)} %get-tuple-element.112.bg_ref, ...), custom_call_target="tpu_custom_call" | custom-call | flops 345000000 | bytes 100000 | tf_op jit(solution)/shard_map/hidden_layer/pallas_call | solution.py:469
  121.6 14.3 %hidden_layer.6 = (bf16[1536,768]{1,0:T(8,128)(2,1)}, bf16[1536,768]{1,0:T(8,128)(2,1)}, f32[400,768]{1,0:T(8,128)}, bf16[400,768]{1,0:T(8,128)(2,1)}, f32[400,7...) custom-call(s32[2]{0:T(128)} %pad_add_fusion.bits_ref, bf16[800,1536]{1,0:T(8,128)(2,1)} %get-tuple-element.125.act_ref, ...), custom_call_target="tpu_custom_call" | custom-call | flops 345000000 | bytes 100000 | tf_op jit(solution)/shard_map/hidden_layer/pallas_call | solution.py:469
  136.1 1.3 collective-permute-start.15
  138.1 1.1 copy-done.5
  139.2 18.0 %hidden_layer.7 = (bf16[1536,896]{1,0:T(8,128)(2,1)}, bf16[1536,896]{1,0:T(8,128)(2,1)}, f32[400,896]{1,0:T(8,128)}, bf16[400,896]{1,0:T(8,128)(2,1)}, f32[400,8...) custom-call(s32[2]{0:T(128)} %pad_add_fusion.bits_ref, bf16[800,1536]{1,0:T(8,128)(2,1)} %get-tuple-element.125.act_ref, ...), custom_call_target="tpu_custom_call" | custom-call | flops 345000000 | bytes 100000 | tf_op jit(solution)/shard_map/hidden_layer/pallas_call | solution.py:469
  158.2 3.5 %split_sums.2 = (f32[200,768]{1,0:T(8,128)}, bf16[200,768]{1,0:T(8,128)(2,1)}, f32[200,768]{1,0:T(8,128)}, bf16[200,768]{1,0:T(8,128)(2,1)}) custom-call(s32[2]{0:T(128)} %pad_add_fusion.1.bits_ref, f32[400,768]{1,0:T(8,128)} %get-tuple-element.147.refs_0_, bf16[400,768]{1,0:T(8,128)(2,1)} %copy-done.35, f32[400,768]{1,0:T(8,128)} %get-tuple-element.151.refs_2_, ...), custom_call_target="tpu_custom_call" | custom-call | flops 3449999872 | bytes 100000 | tf_op jit(solution)/shard_map/split_sums/pallas_call | solution.py:494
  162.4 1.9 collective-permute-start.16
  164.4 1.3 collective-permute-start.19
  165.9 16.1 %activation_gradient.1 = (f32[6,800,256]{2,1,0:T(8,128)}, f32[32,16,128]{2,1,0:T(8,128)}) custom-call(bf16[800,1664]{1,0:T(8,128)(2,1)} %collective-permute-done.9.we_ref.refs_0_, bf16[800,1664]{1,0:T(8,128)(2,1)} %get-tuple-element.130.we_ref.refs_1_, bf16[1536,768]{1,0:T(8,128)(2,1)} %get-tuple-element.142.refs_2_, ...), custom_call_target="tpu_custom_call" | custom-call | flops 368000000 | bytes 100000 | tf_op jit(solution)/shard_map/activation_gradient/pallas_call | solution.py:570
  182.0 3.4 %all-to-all-start.2 = ((f32[32,16,128]{2,1,0:T(8,128)}), f32[32,16,128]{2,1,0:T(8,128)S(1)}, u32[]{:S(2)}, u32[]{:S(2)}) async-start(f32[32,16,128]{2,1,0:T(8,128)} %get-tuple-element.157), calls=%async_computation.2 | async-start | bytes 524288 | tf_op jit(solution)/shard_map/all_to_all | solution.py:929
  185.8 0.9 collective-permute-done.19.refs_3_
  186.7 2.3 round_sums.2
  190.1 3.7 %split_sums.3 = (f32[200,896]{1,0:T(8,128)}, bf16[200,896]{1,0:T(8,128)(2,1)}, f32[200,896]{1,0:T(8,128)}, bf16[200,896]{1,0:T(8,128)(2,1)}) custom-call(s32[2]{0:T(128)} %pad_add_fusion.1.bits_ref, f32[400,896]{1,0:T(8,128)} %get-tuple-element.158.refs_0_, bf16[400,896]{1,0:T(8,128)(2,1)} %copy-done.34, f32[400,896]{1,0:T(8,128)} %get-tuple-element.170.refs_2_, ...), custom_call_target="tpu_custom_call" | custom-call | flops 3449999872 | bytes 100000 | tf_op jit(solution)/shard_map/split_sums/pallas_call | solution.py:494
  193.8 1.3 collective-permute-start.22
  195.1 1.5 collective-permute-start.23
  197.4 9.8 %conv_gradient.1 = (bf16[6,800,256]{2,1,0:T(8,128)(2,1)}, bf16[3,800,256]{2,1,0:T(8,128)(2,1)}, bf16[3,800,256]{2,1,0:T(8,128)(2,1)}, f32[16,128]{1,0:T(8,128)}) custom-call(f32[6,800,256]{2,1,0:T(8,128)} %get-tuple-element.156.da_ref, f32[6,800,256]{2,1,0:T(8,128)} %get-tuple-element.116.conv_ref.refs_6_, f32[6,16,256]{2,1,0:T(8,128)} %broadcast_in_dim.47.m_ref.refs_7_, ...), custom_call_target="tpu_custom_call" | custom-call | flops 230000000 | bytes 100000 | tf_op jit(solution)/shard_map/conv_gradient/pallas_call | solution.py:659
  207.2 1.6 collective-permute-start.20
  208.8 1.3 collective-permute-start.21
  210.9 2.5 round_sums.3
  213.5 17.7 %tap_gradient.1 = f32[4,49,200]{2,1,0:T(8,128)} custom-call(bf16[6,800,256]{2,1,0:T(8,128)(2,1)} %bitcast.39, bf16[3,800,256]{2,1,0:T(8,128)(2,1)} %collective-permute-done.4.up_ref, bf16[3,800,256]{2,1,0:T(8,128)(2,1)} %collective-permute-done.5.dn_ref, bf16[6,800,256]{2,1,0:T(8,128)(2,1)} %get-tuple-element.184.g_ref), custom_call_target="tpu_custom_call" | custom-call | flops 6899999744 | bytes 100000 | tf_op jit(solution)/shard_map/tap_gradient/pallas_call | solution.py:280
  231.1 8.7 %all-reduce.10.cloned.1.call-done = (bf16[200,768]{1,0:T(8,128)(2,1)}, bf16[200,768]{1,0:T(8,128)(2,1)}) async-done(((bf16[200,768]{1,0:T(8,128)(2,1)}, bf16[200,768]{1,0:T(8,128)(2,1)}), (bf16[200,768]{1,0:T(8,128)(2,1)}, bf16[200,768]{1,0:T(8,128)(2,1)})) %all-reduce.10.cloned.1.call-update) | async-done | bytes 614416 | tf_op jit(solution)/shard_map/psum | solution.py:907
  240.1 1.6 pad_maximum_fusion
  241.7 3.4 %all-to-all-start.3 = ((f32[4,54,200]{2,1,0:T(8,128)}), f32[4,54,200]{2,1,0:T(8,128)S(1)}, u32[]{:S(2)}, u32[]{:S(2)}) async-start(f32[4,54,200]{2,1,0:T(8,128)} %pad_maximum_fusion), calls=%async_computation.3 | async-start | bytes 458752 | tf_op jit(solution)/shard_map/all_to_all | solution.py:957
  245.1 1.0 copy-done.6
  246.1 1.0 copy-done.7
  247.2 16.3 %input_gradient.1 = f32[6,800,256]{2,1,0:T(8,128)} custom-call(bf16[6,800,256]{2,1,0:T(8,128)(2,1)} %get-tuple-element.184.g_ref, bf16[3,800,256]{2,1,0:T(8,128)(2,1)} %copy-done.6, bf16[3,800,256]{2,1,0:T(8,128)(2,1)} %copy-done.7, f32[800,128]{1,0:T(8,128)} %get-tuple-element.194.par_ref.refs_8_, bf16[6,800,256]{2,1,0:T(8,128)(2,1)} %bitcast.42, ...), custom_call_target="tpu_custom_call" | custom-call | flops 368000000 | bytes 100000 | tf_op jit(solution)/shard_map/input_gradient/pallas_call | solution.py:216
  264.3 3.5 %all-to-all-start.4 = ((f32[8,54,200]{2,1,0:T(8,128)}), f32[8,54,200]{2,1,0:T(8,128)S(1)}, u32[]{:S(2)}, u32[]{:S(2)}) async-start(f32[8,54,200]{2,1,0:T(8,128)} %broadcast_in_dim.51), calls=%async_computation.4 | async-start | bytes 917504 | tf_op jit(solution)/shard_map/all_to_all | solution.py:776
  267.9 14.8 %block_output.1 = bf16[6,800,256]{2,1,0:T(8,128)(2,1)} custom-call(bf16[800,1664]{1,0:T(8,128)(2,1)} %collective-permute-done.8.wp_ref.refs_0_, bf16[800,1664]{1,0:T(8,128)(2,1)} %get-tuple-element.126.wp_ref.refs_1_, bf16[1536,768]{1,0:T(8,128)(2,1)} %get-tuple-element.129.refs_2_, bf16[1536,768]{1,0:T(8,128)(2,1)} %get-tuple-element.137.refs_3_, ...), custom_call_target="tpu_custom_call" | custom-call | flops 333500000 | bytes 100000 | tf_op jit(solution)/shard_map/block_output/pallas_call | solution.py:603
  283.3 10.1 %all-reduce.8.cloned.1.call-done = (bf16[200,896]{1,0:T(8,128)(2,1)}, bf16[200,896]{1,0:T(8,128)(2,1)}) async-done(((bf16[200,896]{1,0:T(8,128)(2,1)}, bf16[200,896]{1,0:T(8,128)(2,1)}), (bf16[200,896]{1,0:T(8,128)(2,1)}, bf16[200,896]{1,0:T(8,128)(2,1)})) %all-reduce.8.cloned.1.call-update) | async-done | bytes 716816 | tf_op jit(solution)/shard_map/psum | solution.py:907
  296.9 4.3 %place_columns.1 = (f32[200,3200]{1,0:T(8,128)}, f32[200,3200]{1,0:T(8,128)}) custom-call(s32[1]{0:T(128)} %bitcast.22.core_ref, bf16[200,768]{1,0:T(8,128)(2,1)} %get-tuple-element.197.refs_0_, bf16[200,768]{1,0:T(8,128)(2,1)} %copy-done.18, bf16[200,896]{1,0:T(8,128)(2,1)} %get-tuple-element.199.refs_2_, bf16[200,896]{1,0:T(8,128)(2,1)} %copy-done.14, ...), custom_call_target="tpu_custom_call" | custom-call | flops 92000000 | bytes 100000 | tf_op jit(solution)/shard_map/place_columns/pallas_call | solution.py:747
  (166 shorter events, 20.3 us)
Async XLA Ops:
  10.5 11.3 %copy-start.4 = (bf16[200,3200]{1,0:T(8,128)(2,1)S(1)}, bf16[200,3200]{1,0:T(8,128)(2,1)}, u32[]{:S(2)}) copy-start(bf16[200,3200]{1,0:T(8,128)(2,1)} %param.20) | copy-start | bytes 3840004
  10.5 11.3 %slice-start.1 = ((bf16[200,3200]{1,0:T(8,128)(2,1)}), bf16[200,1536]{1,0:T(8,128)(2,1)S(1)}, s32[]{:S(2)}) async-start(bf16[200,3200]{1,0:T(8,128)(2,1)} %param.20), calls=%async_computation.8 | async-start | bytes 1228800 | tf_op jit(solution)/shard_map/slice | solution.py:844
  11.4 10.4 %all-to-all-start = ((f32[4,56,200]{2,1,0:T(8,128)}), f32[4,56,200]{2,1,0:T(8,128)S(1)}, u32[]{:S(2)}, u32[]{:S(2)}) async-start(f32[4,56,200]{2,1,0:T(8,128)} %broadcast_in_dim.46), calls=%async_computation | async-start | bytes 458752 | tf_op jit(solution)/shard_map/all_to_all | solution.py:776
  16.6 26.2 %collective-permute-start.4 = (bf16[3,800,256]{2,1,0:T(8,128)(2,1)}, bf16[3,800,256]{2,1,0:T(8,128)(2,1)}, u32[]{:S(2)}, u32[]{:S(2)}) collective-permute-start(bf16[3,800,256]{2,1,0:T(8,128)(2,1)} %get-tuple-element.209), channel_id=1, source_target_pairs={{0,4},{4,8},{8,12},{12,16},{16,20},{20,24},{24,28},{1,5},{5,9},{9,... | collective-permute-start | bytes 3686408 | tf_op jit(solution)/shard_map/ppermute | solution.py:765
  19.1 24.6 %collective-permute-start.5 = (bf16[3,800,256]{2,1,0:T(8,128)(2,1)}, bf16[3,800,256]{2,1,0:T(8,128)(2,1)}, u32[]{:S(2)}, u32[]{:S(2)}) collective-permute-start(bf16[3,800,256]{2,1,0:T(8,128)(2,1)} %get-tuple-element.210), channel_id=1, source_target_pairs={{4,0},{8,4},{12,8},{16,12},{20,16},{24,20},{28,24},{5,1},{9,5},{13... | collective-permute-start | bytes 3686408 | tf_op jit(solution)/shard_map/ppermute | solution.py:766
  21.8 6.7 %copy-start.10 = (f32[4,56,200]{2,1,0:T(8,128)}, f32[4,56,200]{2,1,0:T(8,128)S(1)}, u32[]{:S(2)}) copy-start(f32[4,56,200]{2,1,0:T(8,128)S(1)} %all-to-all-done.small_ref) | copy-start | bytes 537604
  22.1 17.5 %collective-permute-start.2 = (bf16[200,1664]{1,0:T(8,128)(2,1)S(1)}, bf16[200,1664]{1,0:T(8,128)(2,1)S(1)}, u32[]{:S(2)}, u32[]{:S(2)}) collective-permute-start(bf16[200,1664]{1,0:T(8,128)(2,1)S(1)} %slice_select_fusion.refs_4_), channel_id=1, source_target_pairs={{0,2},{1,3},{2,0},{3,1},{4,6},{5,7},{6,4},{7,5},{8,10},{9,11},{10,... | collective-permute-start | bytes 1996808 | tf_op jit(solution)/shard_map/ppermute | solution.py:781
  23.8 40.7 %copy-start.2 = (bf16[200,1664]{1,0:T(8,128)(2,1)}, bf16[200,1664]{1,0:T(8,128)(2,1)S(1)}, u32[]{:S(2)}) copy-start(bf16[200,1664]{1,0:T(8,128)(2,1)S(1)} %slice_select_fusion.1.refs_0_) | copy-start | bytes 1996804
  23.8 17.8 %collective-permute-start = (bf16[200,1664]{1,0:T(8,128)(2,1)S(1)}, bf16[200,1664]{1,0:T(8,128)(2,1)S(1)}, u32[]{:S(2)}, u32[]{:S(2)}) collective-permute-start(bf16[200,1664]{1,0:T(8,128)(2,1)S(1)} %slice_select_fusion.1.refs_0_), channel_id=1, source_target_pairs={{0,1},{1,0},{2,3},{3,2},{4,5},{5,4},{6,7},{7,6},{8,9},{9,8},{10,11... | collective-permute-start | bytes 1996808 | tf_op jit(solution)/shard_map/ppermute | solution.py:781
  27.0 44.3 %collective-permute-start.7 = (bf16[200,1664]{1,0:T(8,128)(2,1)S(1)}, bf16[200,1664]{1,0:T(8,128)(2,1)}, u32[]{:S(2)}, u32[]{:S(2)}) collective-permute-start(bf16[200,1664]{1,0:T(8,128)(2,1)S(1)} %slice_select_fusion.refs_4_), channel_id=1, source_target_pairs={{0,1},{1,0},{2,3},{3,2},{4,5},{5,4},{6,7},{7,6},{8,9},{9,8},{10,11... | collective-permute-start | bytes 1996808 | tf_op jit(solution)/shard_map/ppermute | solution.py:781
  39.6 25.0 %copy-start.11 = (bf16[200,1664]{1,0:T(8,128)(2,1)}, bf16[200,1664]{1,0:T(8,128)(2,1)S(1)}, u32[]{:S(2)}) copy-start(bf16[200,1664]{1,0:T(8,128)(2,1)S(1)} %collective-permute-done.2.refs_6_) | copy-start | bytes 1996804
  39.6 31.7 %collective-permute-start.6 = (bf16[200,1664]{1,0:T(8,128)(2,1)S(1)}, bf16[200,1664]{1,0:T(8,128)(2,1)}, u32[]{:S(2)}, u32[]{:S(2)}) collective-permute-start(bf16[200,1664]{1,0:T(8,128)(2,1)S(1)} %slice_select_fusion.1.refs_0_), channel_id=1, source_target_pairs={{0,2},{1,3},{2,0},{3,1},{4,6},{5,7},{6,4},{7,5},{8,10},{9,11},{10,... | collective-permute-start | bytes 1996808 | tf_op jit(solution)/shard_map/ppermute | solution.py:781
  41.6 22.9 %copy-start.12 = (bf16[200,1664]{1,0:T(8,128)(2,1)}, bf16[200,1664]{1,0:T(8,128)(2,1)S(1)}, u32[]{:S(2)}) copy-start(bf16[200,1664]{1,0:T(8,128)(2,1)S(1)} %collective-permute-done.refs_1_) | copy-start | bytes 1996804
  41.6 29.7 %collective-permute-start.3 = (bf16[200,1664]{1,0:T(8,128)(2,1)S(1)}, bf16[200,1664]{1,0:T(8,128)(2,1)}, u32[]{:S(2)}, u32[]{:S(2)}) collective-permute-start(bf16[200,1664]{1,0:T(8,128)(2,1)S(1)} %collective-permute-done.2.refs_6_), channel_id=1, source_target_pairs={{0,1},{1,0},{2,3},{3,2},{4,5},{5,4},{6,7},{7,6},{8,9},{9,8},{10,11... | collective-permute-start | bytes 1996808 | tf_op jit(solution)/shard_map/ppermute | solution.py:781
  42.8 28.6 %collective-permute-start.1 = (bf16[200,1664]{1,0:T(8,128)(2,1)S(1)}, bf16[200,1664]{1,0:T(8,128)(2,1)}, u32[]{:S(2)}, u32[]{:S(2)}) collective-permute-start(bf16[200,1664]{1,0:T(8,128)(2,1)S(1)} %collective-permute-done.refs_1_), channel_id=1, source_target_pairs={{0,2},{1,3},{2,0},{3,1},{4,6},{5,7},{6,4},{7,5},{8,10},{9,11},{10,... | collective-permute-start | bytes 1996808 | tf_op jit(solution)/shard_map/ppermute | solution.py:781
  64.6 17.5 %all-to-all-start.1 = ((f32[32,16,128]{2,1,0:T(8,128)}), f32[32,16,128]{2,1,0:T(8,128)S(1)}, u32[]{:S(2)}, u32[]{:S(2)}) async-start(f32[32,16,128]{2,1,0:T(8,128)} %get-tuple-element.121), calls=%async_computation.1 | async-start | bytes 524288 | tf_op jit(solution)/shard_map/all_to_all | solution.py:871
  82.8 6.8 %copy-start = (bf16[800,1664]{1,0:T(8,128)(2,1)S(1)}, bf16[800,1664]{1,0:T(8,128)(2,1)}, u32[]{:S(2)}) copy-start(bf16[800,1664]{1,0:T(8,128)(2,1)} %get-tuple-element.126.wp_ref.refs_1_) | copy-start | bytes 7987204
  89.6 32.0 %collective-permute-start.9 = (bf16[800,1664]{1,0:T(8,128)(2,1)}, bf16[800,1664]{1,0:T(8,128)(2,1)}, u32[]{:S(2)}, u32[]{:S(2)}) collective-permute-start(bf16[800,1664]{1,0:T(8,128)(2,1)} %get-tuple-element.130.we_ref.refs_1_), channel_id=1, source_target_pairs={{0,4},{4,0},{8,12},{12,8},{16,20},{20,16},{24,28},{28,24},{1,5},{5... | collective-permute-start | bytes 7987208 | tf_op jit(solution)/shard_map/ppermute | solution.py:781
  89.6 32.0 %collective-permute-start.8 = (bf16[800,1664]{1,0:T(8,128)(2,1)S(1)}, bf16[800,1664]{1,0:T(8,128)(2,1)}, u32[]{:S(2)}, u32[]{:S(2)}) collective-permute-start(bf16[800,1664]{1,0:T(8,128)(2,1)S(1)} %copy-done), channel_id=1, source_target_pairs={{0,4},{4,0},{8,12},{12,8},{16,20},{20,16},{24,28},{28,24},{1,5},{5... | collective-permute-start | bytes 7987208 | tf_op jit(solution)/shard_map/ppermute | solution.py:781
  103.5 17.7 %collective-permute-start.10 = (bf16[800,768]{1,0:T(8,128)(2,1)}, bf16[800,768]{1,0:T(8,128)(2,1)}, u32[]{:S(2)}, u32[]{:S(2)}) collective-permute-start(bf16[800,768]{1,0:T(8,128)(2,1)} %get-tuple-element.135), channel_id=1, source_target_pairs={{0,4},{4,0},{8,12},{12,8},{16,20},{20,16},{24,28},{28,24},{1,5},{5... | collective-permute-start | bytes 3686408 | tf_op jit(solution)/shard_map/ppermute | solution.py:781
  103.6 18.0 %collective-permute-start.11 = (bf16[800,768]{1,0:T(8,128)(2,1)}, bf16[800,768]{1,0:T(8,128)(2,1)}, u32[]{:S(2)}, u32[]{:S(2)}) collective-permute-start(bf16[800,768]{1,0:T(8,128)(2,1)} %get-tuple-element.136), channel_id=1, source_target_pairs={{0,4},{4,0},{8,12},{12,8},{16,20},{20,16},{24,28},{28,24},{1,5},{5... | collective-permute-start | bytes 3686408 | tf_op jit(solution)/shard_map/ppermute | solution.py:781
  121.0 17.0 %collective-permute-start.12 = (bf16[800,896]{1,0:T(8,128)(2,1)}, bf16[800,896]{1,0:T(8,128)(2,1)S(1)}, u32[]{:S(2)}, u32[]{:S(2)}) collective-permute-start(bf16[800,896]{1,0:T(8,128)(2,1)} %get-tuple-element.139), channel_id=1, source_target_pairs={{0,4},{4,0},{8,12},{12,8},{16,20},{20,16},{24,28},{28,24},{1,5},{5... | collective-permute-start | bytes 4300808 | tf_op jit(solution)/shard_map/ppermute | solution.py:781
  121.2 16.9 %collective-permute-start.13 = (bf16[800,896]{1,0:T(8,128)(2,1)}, bf16[800,896]{1,0:T(8,128)(2,1)}, u32[]{:S(2)}, u32[]{:S(2)}) collective-permute-start(bf16[800,896]{1,0:T(8,128)(2,1)} %get-tuple-element.140), channel_id=1, source_target_pairs={{0,4},{4,0},{8,12},{12,8},{16,20},{20,16},{24,28},{28,24},{1,5},{5... | collective-permute-start | bytes 4300808 | tf_op jit(solution)/shard_map/ppermute | solution.py:781
  135.9 21.2 %collective-permute-start.14 = (bf16[400,768]{1,0:T(8,128)(2,1)}, bf16[400,768]{1,0:T(8,128)(2,1)S(1)}, u32[]{:S(2)}, u32[]{:S(2)}) collective-permute-start(bf16[400,768]{1,0:T(8,128)(2,1)} %get-tuple-element.148), channel_id=1, source_target_pairs={{0,2},{1,3},{2,0},{3,1},{4,6},{5,7},{6,4},{7,5},{8,10},{9,11},{10,... | collective-permute-start | bytes 1843208 | tf_op jit(solution)/shard_map/ppermute | solution.py:781
  136.1 21.0 %collective-permute-start.15 = (bf16[400,768]{1,0:T(8,128)(2,1)}, bf16[400,768]{1,0:T(8,128)(2,1)S(1)}, u32[]{:S(2)}, u32[]{:S(2)}) collective-permute-start(bf16[400,768]{1,0:T(8,128)(2,1)} %get-tuple-element.149), channel_id=1, source_target_pairs={{0,1},{1,0},{2,3},{3,2},{4,5},{5,4},{6,7},{7,6},{8,9},{9,8},{10,11... | collective-permute-start | bytes 1843208 | tf_op jit(solution)/shard_map/ppermute | solution.py:781
  158.2 7.6 %copy-start.28 = (f32[1,16,128]{2,1,0:T(8,128)S(1)}, f32[1,16,128]{2,1,0:T(8,128)}, u32[]{:S(2)}) copy-start(f32[1,16,128]{2,1,0:T(8,128)} %get-tuple-element.188) | copy-start | bytes 24580
  158.2 7.6 %copy-start.26 = (f32[1,768]{1,0:T(1,128)S(1)}, f32[1,768]{1,0:T(1,128)}, u32[]{:S(2)}) copy-start(f32[1,768]{1,0:T(1,128)} %get-tuple-element.191) | copy-start | bytes 9220
  161.7 27.3 %collective-permute-start.17 = (bf16[400,896]{1,0:T(8,128)(2,1)S(1)}, bf16[400,896]{1,0:T(8,128)(2,1)S(1)}, u32[]{:S(2)}, u32[]{:S(2)}) collective-permute-start(bf16[400,896]{1,0:T(8,128)(2,1)S(1)} %copy-done.32), channel_id=1, source_target_pairs={{0,1},{1,0},{2,3},{3,2},{4,5},{5,4},{6,7},{7,6},{8,9},{9,8},{10,11... | collective-permute-start | bytes 2150408 | tf_op jit(solution)/shard_map/ppermute | solution.py:781
  162.4 26.6 %collective-permute-start.16 = (bf16[400,896]{1,0:T(8,128)(2,1)S(1)}, bf16[400,896]{1,0:T(8,128)(2,1)S(1)}, u32[]{:S(2)}, u32[]{:S(2)}) collective-permute-start(bf16[400,896]{1,0:T(8,128)(2,1)S(1)} %copy-done.31), channel_id=1, source_target_pairs={{0,2},{1,3},{2,0},{3,1},{4,6},{5,7},{6,4},{7,5},{8,10},{9,11},{10,... | collective-permute-start | bytes 2150408 | tf_op jit(solution)/shard_map/ppermute | solution.py:781
  164.4 21.4 %collective-permute-start.18 = (bf16[200,768]{1,0:T(8,128)(2,1)}, bf16[200,768]{1,0:T(8,128)(2,1)S(1)}, u32[]{:S(2)}, u32[]{:S(2)}) collective-permute-start(bf16[200,768]{1,0:T(8,128)(2,1)} %get-tuple-element.153), channel_id=1, source_target_pairs={{0,1},{1,0},{2,3},{3,2},{4,5},{5,4},{6,7},{7,6},{8,9},{9,8},{10,11... | collective-permute-start | bytes 921608 | tf_op jit(solution)/shard_map/ppermute | solution.py:781
  164.4 22.2 %collective-permute-start.19 = (bf16[200,768]{1,0:T(8,128)(2,1)}, bf16[200,768]{1,0:T(8,128)(2,1)}, u32[]{:S(2)}, u32[]{:S(2)}) collective-permute-start(bf16[200,768]{1,0:T(8,128)(2,1)} %get-tuple-element.154), channel_id=1, source_target_pairs={{0,2},{1,3},{2,0},{3,1},{4,6},{5,7},{6,4},{7,5},{8,10},{9,11},{10,... | collective-permute-start | bytes 921608 | tf_op jit(solution)/shard_map/ppermute | solution.py:781
  182.0 14.7 %all-to-all-start.2 = ((f32[32,16,128]{2,1,0:T(8,128)}), f32[32,16,128]{2,1,0:T(8,128)S(1)}, u32[]{:S(2)}, u32[]{:S(2)}) async-start(f32[32,16,128]{2,1,0:T(8,128)} %get-tuple-element.157), calls=%async_computation.2 | async-start | bytes 524288 | tf_op jit(solution)/shard_map/all_to_all | solution.py:929
  185.4 54.5 %all-reduce.10.cloned.1.call-start = ((), (), s32[]{:S(2)}) async-start(), calls=%async_computation.6 | async-start | bytes 1228800 | tf_op jit(solution)/shard_map/psum | solution.py:907
  193.8 16.2 %collective-permute-start.22 = (bf16[200,896]{1,0:T(8,128)(2,1)}, bf16[200,896]{1,0:T(8,128)(2,1)S(1)}, u32[]{:S(2)}, u32[]{:S(2)}) collective-permute-start(bf16[200,896]{1,0:T(8,128)(2,1)} %get-tuple-element.172), channel_id=1, source_target_pairs={{0,1},{1,0},{2,3},{3,2},{4,5},{5,4},{6,7},{7,6},{8,9},{9,8},{10,11... | collective-permute-start | bytes 1075208 | tf_op jit(solution)/shard_map/ppermute | solution.py:781
  195.1 15.0 %collective-permute-start.23 = (bf16[200,896]{1,0:T(8,128)(2,1)}, bf16[200,896]{1,0:T(8,128)(2,1)S(1)}, u32[]{:S(2)}, u32[]{:S(2)}) collective-permute-start(bf16[200,896]{1,0:T(8,128)(2,1)} %get-tuple-element.173), channel_id=1, source_target_pairs={{0,2},{1,3},{2,0},{3,1},{4,6},{5,7},{6,4},{7,5},{8,10},{9,11},{10,... | collective-permute-start | bytes 1075208 | tf_op jit(solution)/shard_map/ppermute | solution.py:781
  196.6 96.8 %all-reduce.8.cloned.1.call-start = ((), (), s32[]{:S(2)}) async-start(), calls=%async_computation.5 | async-start | bytes 1433600 | tf_op jit(solution)/shard_map/psum | solution.py:907
  207.2 37.9 %collective-permute-start.20 = (bf16[3,800,256]{2,1,0:T(8,128)(2,1)}, bf16[3,800,256]{2,1,0:T(8,128)(2,1)S(1)}, u32[]{:S(2)}, u32[]{:S(2)}) collective-permute-start(bf16[3,800,256]{2,1,0:T(8,128)(2,1)} %get-tuple-element.176), channel_id=1, source_target_pairs={{0,4},{4,8},{8,12},{12,16},{16,20},{20,24},{24,28},{1,5},{5,9},{9,... | collective-permute-start | bytes 3686408 | tf_op jit(solution)/shard_map/ppermute | solution.py:765
  208.8 36.4 %collective-permute-start.21 = (bf16[3,800,256]{2,1,0:T(8,128)(2,1)}, bf16[3,800,256]{2,1,0:T(8,128)(2,1)S(1)}, u32[]{:S(2)}, u32[]{:S(2)}) collective-permute-start(bf16[3,800,256]{2,1,0:T(8,128)(2,1)} %get-tuple-element.177), channel_id=1, source_target_pairs={{4,0},{8,4},{12,8},{16,12},{20,16},{24,20},{28,24},{5,1},{9,5},{13... | collective-permute-start | bytes 3686408 | tf_op jit(solution)/shard_map/ppermute | solution.py:766
  241.7 21.7 %all-to-all-start.3 = ((f32[4,54,200]{2,1,0:T(8,128)}), f32[4,54,200]{2,1,0:T(8,128)S(1)}, u32[]{:S(2)}, u32[]{:S(2)}) async-start(f32[4,54,200]{2,1,0:T(8,128)} %pad_maximum_fusion), calls=%async_computation.3 | async-start | bytes 458752 | tf_op jit(solution)/shard_map/all_to_all | solution.py:957
  264.3 36.9 %all-to-all-start.4 = ((f32[8,54,200]{2,1,0:T(8,128)}), f32[8,54,200]{2,1,0:T(8,128)S(1)}, u32[]{:S(2)}, u32[]{:S(2)}) async-start(f32[8,54,200]{2,1,0:T(8,128)} %broadcast_in_dim.51), calls=%async_computation.4 | async-start | bytes 917504 | tf_op jit(solution)/shard_map/all_to_all | solution.py:776
  267.8 14.8 %copy-start.16 = (bf16[200,768]{1,0:T(8,128)(2,1)S(1)}, bf16[200,768]{1,0:T(8,128)(2,1)}, u32[]{:S(2)}) copy-start(bf16[200,768]{1,0:T(8,128)(2,1)} %get-tuple-element.200.refs_4_) | copy-start | bytes 921604
  267.8 15.4 %copy-start.15 = (bf16[200,768]{1,0:T(8,128)(2,1)S(1)}, bf16[200,768]{1,0:T(8,128)(2,1)}, u32[]{:S(2)}) copy-start(bf16[200,768]{1,0:T(8,128)(2,1)} %get-tuple-element.197.refs_0_) | copy-start | bytes 921604
  267.8 26.1 %copy-start.19 = (f32[32,128]{1,0:T(8,128)S(1)}, f32[32,128]{1,0:T(8,128)}, u32[]{:S(2)}) copy-start(f32[32,128]{1,0:T(8,128)} %get-tuple-element.155.refs_7_.stat_ref) | copy-start | bytes 49156
  267.8 26.7 %copy-start.22 = (f32[16,128]{1,0:T(8,128)S(1)}, f32[16,128]{1,0:T(8,128)}, u32[]{:S(2)}) copy-start(f32[16,128]{1,0:T(8,128)} %get-tuple-element.196) | copy-start | bytes 24580
  282.6 13.2 %collective-permute-start.26 = (bf16[200,768]{1,0:T(8,128)(2,1)S(1)}, bf16[200,768]{1,0:T(8,128)(2,1)S(1)}, u32[]{:S(2)}, u32[]{:S(2)}) collective-permute-start(bf16[200,768]{1,0:T(8,128)(2,1)S(1)} %copy-done.16), channel_id=1, source_target_pairs={{0,4},{4,0},{8,12},{12,8},{16,20},{20,16},{24,28},{28,24},{1,5},{5... | collective-permute-start | bytes 921608 | tf_op jit(solution)/shard_map/ppermute | solution.py:781
  283.2 12.6 %collective-permute-start.24 = (bf16[200,768]{1,0:T(8,128)(2,1)S(1)}, bf16[200,768]{1,0:T(8,128)(2,1)S(1)}, u32[]{:S(2)}, u32[]{:S(2)}) collective-permute-start(bf16[200,768]{1,0:T(8,128)(2,1)S(1)} %copy-done.15), channel_id=1, source_target_pairs={{0,4},{4,0},{8,12},{12,8},{16,20},{20,16},{24,28},{28,24},{1,5},{5... | collective-permute-start | bytes 921608 | tf_op jit(solution)/shard_map/ppermute | solution.py:781
  293.4 2.4 collective-permute-start.27
  293.5 2.4 collective-permute-start.25
  (31 other events, 74.9 us)
Sparse Core Ops, SparseCore 0:
  196.7 43.0 all-reduce.9
  242.3 51.0 all-reduce.7

commit v5 on v4

--- a/solution.py
+++ b/solution.py
@@ -15,15 +15,15 @@
 F32, BF16 = jnp.float32, jnp.bfloat16
 GRP = 16
 TILE = 256
-MIB = 2**20
+VMEM = 639 * 2**20 // 10
 GELU_A = 0.7978845608028654
 GELU_B = 0.044715
 NT = (((1,), (1,)), ((), ()))
 TN = (((0,), (0,)), ((), ()))
 
 
-def params(limit=60):
-    return pltpu.CompilerParams(vmem_limit_bytes=limit * MIB)
+def params():
+    return pltpu.CompilerParams(vmem_limit_bytes=VMEM)
 
 
 def cost(us):
@@ -232,12 +232,14 @@
             pltpu.VMEM((KS, 128, 128), BF16),
         ],
         compiler_params=params(),
-        cost_estimate=cost(0.32),
+        cost_estimate=cost(5),
         name="input_gradient",
     )(grad, up, dn, par, og, m16)
 
 
-def tap_grad_kernel(x_ref, up_ref, dn_ref, g_ref, out_ref, field_ref, cols_ref, *, share):
+def tap_grad_kernel(
+    x_ref, up_ref, dn_ref, g_ref, bg_ref, eb_ref, out_ref, field_ref, cols_ref, *, share
+):
     rows, block, width = x_ref.shape
     field_ref[0:REACH] = up_ref[...]
     field_ref[REACH : REACH + rows] = x_ref[...]
@@ -270,13 +272,21 @@
         blocks = [cols_ref[k : k + 128, :].T for k in range(0, cols_ref.shape[0], 128)]
         wide = jnp.concatenate(blocks, axis=1)
         taps = jnp.concatenate([wide[GRP * i : GRP * i + KS] for i in range(KS)], axis=0)
+        band = jnp.concatenate([bg_ref[0, k : k + 1, :] for k in range(wide.shape[1] // 128)], axis=1)
+        units = eb_ref[...]
+        ratio = out_ref.shape[1] - TAPS - 1
         for f in range(out_ref.shape[0]):
-            out_ref[f] = taps[:, f * share : (f + 1) * share]
-
-
-def tap_gradient(x, up, dn, grad, block, share):
+            out_ref[f, 0:TAPS, :] = taps[:, f * share : (f + 1) * share]
+            out_ref[f, TAPS : TAPS + 1, :] = band[:, f * share : (f + 1) * share]
+            for q in range(ratio):
+                at = (f * ratio + q) * share
+                out_ref[f, TAPS + 1 + q : TAPS + 2 + q, :] = units[:, at : at + share]
+
+
+def tap_gradient(x, up, dn, grad, bg_sum, eb_sum, block, share):
     rows, channels, width = x.shape
     padded = pl.cdiv(channels, 128) * 128
+    height = TAPS + 1 + eb_sum.shape[1] // channels
     return pl.pallas_call(
         functools.partial(tap_grad_kernel, share=share),
         grid=(channels // block,),
@@ -285,17 +295,19 @@
             pl.BlockSpec((REACH, block, width), lambda g: (0, g, 0)),
             pl.BlockSpec((REACH, block, width), lambda g: (0, g, 0)),
             pl.BlockSpec((rows, block, width), lambda g: (0, g, 0)),
-        ],
-        out_specs=pl.BlockSpec((channels // share, TAPS, share), lambda g: (0, 0, 0)),
-        out_shape=jax.ShapeDtypeStruct((channels // share, TAPS, share), F32),
+            whole(bg_sum.shape),
+            whole(eb_sum.shape),
+        ],
+        out_specs=pl.BlockSpec((channels // share, height, share), lambda g: (0, 0, 0)),
+        out_shape=jax.ShapeDtypeStruct((channels // share, height, share), F32),
         scratch_shapes=[
             pltpu.VMEM((rows + 2 * REACH, block, width), BF16),
             pltpu.VMEM((padded, 128), F32),
         ],
         compiler_params=params(),
-        cost_estimate=cost(6),
+        cost_estimate=cost(15),
         name="tap_gradient",
-    )(x, up, dn, grad)
+    )(x, up, dn, grad, bg_sum, eb_sum)
 
 
 def mask_grad_kernel(og_ref, m_ref, out_ref, sum_ref, cols_ref):
@@ -340,61 +352,32 @@
         ],
         scratch_shapes=[pltpu.VMEM((padded, 128), F32)],
         compiler_params=params(),
-        cost_estimate=cost(0.11),
+        cost_estimate=cost(0.1),
         name="mask_gradient",
     )(og, m16)
 
 
-def activate_kernel(conv_ref, all_ref, par_ref, out_ref, stat_ref, cols_ref):
-    channels = conv_ref.shape[1]
-
-    @pl.when(pl.program_id(0) == 0)
-    def _():
-        means, squares = all_ref[:, 0:8, :], all_ref[:, 8:16, :]
-        counts = all_ref[:, 7:8, :]
-        count = jnp.sum(counts, axis=0)
-        mean = jnp.sum(counts * means, axis=0) / count
-        apart = means - mean[None]
-        variance = jnp.sum(squares + counts * apart * apart, axis=0) / count
-        inv_std = lax.rsqrt(variance + EPS)
-        stat_ref[0:8] = mean
-        stat_ref[8:16] = inv_std
-        stat_ref[16:24] = jnp.sqrt(variance + EPS)
-        stat_ref[24:32] = jnp.broadcast_to(count, (8, 128))
-        c, p = columns_of(mean[0:7], inv_std[0:7])[:channels], par_ref[...]
-        cols_ref[0] = wide(c[:, 0:1])
-        cols_ref[1] = wide(c[:, 1:2] * p[:, TAPS : TAPS + 1])
-        cols_ref[2] = wide(p[:, TAPS + 1 : TAPS + 2])
-
-    for k in range(0, out_ref.shape[1], 128):
-        v = (conv_ref[0, :, k : k + 128] - cols_ref[0]) * cols_ref[1] + cols_ref[2]
-        out_ref[:, k : k + 128] = v.astype(BF16)
-
-
-def activate(conv, stats, par):
-    rows, channels, width = conv.shape
-    pixels = rows * width
-    return pl.pallas_call(
-        activate_kernel,
-        grid=(rows,),
-        in_specs=[
-            pl.BlockSpec((1, channels, width), lambda r: (r, 0, 0)),
-            whole(stats.shape),
-            whole(par.shape),
-        ],
-        out_specs=[
-            pl.BlockSpec((channels, width), lambda r: (0, r)),
-            pl.BlockSpec((32, 128), lambda r: (0, 0)),
-        ],
-        out_shape=[
-            jax.ShapeDtypeStruct((channels, pixels), BF16),
-            jax.ShapeDtypeStruct((32, 128), F32),
-        ],
-        scratch_shapes=[pltpu.VMEM((3, channels, 128), F32)],
-        compiler_params=params(),
-        cost_estimate=cost(0.13),
-        name="activate",
-    )(conv, stats, par)
+def activate(conv_ref, all_ref, par_ref, act_ref, stat_ref):
+    rows, channels, width = conv_ref.shape
+    means, squares = all_ref[:, 0:8, :], all_ref[:, 8:16, :]
+    counts = all_ref[:, 7:8, :]
+    count = jnp.sum(counts, axis=0)
+    mean = jnp.sum(counts * means, axis=0) / count
+    apart = means - mean[None]
+    variance = jnp.sum(squares + counts * apart * apart, axis=0) / count
+    inv_std = lax.rsqrt(variance + EPS)
+    stat_ref[0:8] = mean
+    stat_ref[8:16] = inv_std
+    stat_ref[16:24] = jnp.sqrt(variance + EPS)
+    stat_ref[24:32] = jnp.broadcast_to(count, (8, 128))
+    c, p = columns_of(mean[0:7], inv_std[0:7])[:channels], par_ref[...]
+    centre = wide(c[:, 0:1])
+    scale = wide(c[:, 1:2] * p[:, TAPS : TAPS + 1])
+    shift = wide(p[:, TAPS + 1 : TAPS + 2])
+    for r in range(rows):
+        for k in range(0, width, 128):
+            v = (conv_ref[r, :, k : k + 128] - centre) * scale + shift
+            act_ref[:, r * width + k : r * width + k + 128] = v.astype(BF16)
 
 
 def gelu_parts(v):
@@ -414,8 +397,19 @@
     return jnp.concatenate(keep, axis=0), jnp.concatenate(send, axis=0)
 
 
-def hidden_kernel(bits_ref, act_ref, bg_ref, we_ref, wp_ref, eb_ref, *refs, step, pieces):
-    if pieces is None:
+def hidden_kernel(bits_ref, bg_ref, we_ref, wp_ref, eb_ref, *refs, step, pieces, leads):
+    if leads:
+        conv_ref, all_ref, par_ref, h_ref, g_ref, dwp_ref, dwe_ref, ebg_ref, act_ref, stat_ref = refs
+
+        @pl.when(pl.program_id(0) == 0)
+        def _():
+            activate(conv_ref, all_ref, par_ref, act_ref, stat_ref)
+
+    else:
+        act_ref, refs = refs[0], refs[1:]
+    if leads:
+        pass
+    elif pieces is None:
         h_ref, g_ref, dwp_ref, dwe_ref, ebg_ref = refs
     else:
         other_p, other_e, h_ref, g_ref, keep_p, send_p, keep_e, send_e, ebg_ref = refs
@@ -445,15 +439,17 @@
         send_e[...] = send.astype(BF16)
 
 
-def hidden_layer(act, bg, we, wp, eb, first, units, bits, others=None, pieces=None):
-    channels, pixels = act.shape
+def hidden_layer(act, bg, we, wp, eb, first, units, bits, others=None, pieces=None, front=None):
+    channels, pixels = bg.shape
     off = first // TILE
     column = lambda rows: pl.BlockSpec((rows, TILE), lambda g: (0, g))
     weight = pl.BlockSpec((channels, TILE), lambda g: (0, g + off))
     shape = lambda rows, dtype: jax.ShapeDtypeStruct((rows, units), dtype)
-    in_specs = [pl.BlockSpec(memory_space=pltpu.SMEM), whole(act.shape), whole(bg.shape), weight, weight]
+    in_specs = [pl.BlockSpec(memory_space=pltpu.SMEM), whole(bg.shape), weight, weight]
     in_specs.append(pl.BlockSpec((1, TILE), lambda g: (0, g + off)))
-    operands = [bits, act, bg, we, wp, eb]
+    made = [act] if front is None else list(front)
+    operands = [bits, bg, we, wp, eb] + made
+    in_specs += [whole(v.shape) for v in made]
     out_specs = [column(pixels), column(pixels)]
     out_shape = [shape(pixels, BF16), shape(pixels, BF16)]
     if others is None:
@@ -466,8 +462,11 @@
         out_shape += [shape(channels // 2, F32), shape(channels // 2, BF16)] * 2
     out_specs.append(column(1))
     out_shape.append(shape(1, F32))
-    return pl.pallas_call(
-        functools.partial(hidden_kernel, step=128, pieces=pieces),
+    if front is not None:
+        out_specs += [pl.BlockSpec((channels, pixels), lambda g: (0, 0)), pl.BlockSpec((32, 128), lambda g: (0, 0))]
+        out_shape += [jax.ShapeDtypeStruct((channels, pixels), BF16), jax.ShapeDtypeStruct((32, 128), F32)]
+    return pl.pallas_call(
+        functools.partial(hidden_kernel, step=128, pieces=pieces, leads=front is not None),
         grid=(pl.cdiv(units, TILE),),
         in_specs=in_specs,
         out_specs=out_specs,
@@ -501,6 +500,33 @@
         name="split_sums",
     )(bits, *[v for pair in pairs for v in pair])
     return [(out[2 * k], out[2 * k + 1]) for k in range(len(pairs))]
+
+
+def band_split_kernel(bit_ref, *refs):
+    keep_ref, send_ref = refs[-2:]
+    rows = keep_ref.shape[1]
+    for k in range(keep_ref.shape[0]):
+        total = refs[2 * k][...] + refs[2 * k + 1][...].astype(F32)
+        low, high = total[:rows], total[total.shape[0] - rows :]
+        keep_ref[k] = jnp.where(bit_ref[0] == 0, low, high)
+        send_ref[k] = jnp.where(bit_ref[0] == 0, high, low).astype(BF16)
+
+
+def band_split(bit, pairs):
+    share, cols = pairs[0][0].shape
+    rows = pl.cdiv(pl.cdiv(share, 2), 8) * 8
+    spec = pl.BlockSpec((share, cols), lambda: (0, 0))
+    out = pl.BlockSpec((len(pairs), rows, cols), lambda: (0, 0, 0))
+    shape = lambda dtype: jax.ShapeDtypeStruct((len(pairs), rows, cols), dtype)
+    return pl.pallas_call(
+        band_split_kernel,
+        in_specs=[pl.BlockSpec(memory_space=pltpu.SMEM)] + [spec] * (2 * len(pairs)),
+        out_specs=[out, out],
+        out_shape=[shape(F32), shape(BF16)],
+        compiler_params=params(),
+        cost_estimate=cost(3),
+        name="band_split",
+    )(bit[None], *[v for pair in pairs for v in pair])
 
 
 def round_kernel(*refs):
@@ -583,7 +609,7 @@
         ],
         scratch_shapes=[pltpu.VMEM((padded, 128), F32), pltpu.VMEM((2, padded, 128), F32)],
         compiler_params=params(),
-        cost_estimate=cost(0.32),
+        cost_estimate=cost(0.3),
         name="activation_gradient",
     )(*weights, *hiddens, conv, stat)
 
@@ -613,7 +639,7 @@
         out_specs=pl.BlockSpec((1, channels, width), lambda r: (r, 0, 0)),
         out_shape=jax.ShapeDtypeStruct((rows, channels, width), BF16),
         compiler_params=params(),
-        cost_estimate=cost(0.29),
+        cost_estimate=cost(5),
         name="block_output",
     )(*weights, *hiddens, x, m16, par)
 
@@ -720,41 +746,49 @@
         out_specs=[column(channels)] * 2,
         out_shape=[jax.ShapeDtypeStruct((channels, cols), BF16)] * 2,
         compiler_params=params(),
-        cost_estimate=cost(0.08),
+        cost_estimate=cost(0.1),
         name="join_pieces",
     )(index[None], *[first[k] for k in names], *[second[k] for k in names])
 
 
-def place_kernel(core_ref, *refs, starts):
-    n = len(starts)
-    for w in range(2):
-        out_ref = refs[4 * n + w]
-        for k, (low, high) in enumerate(starts):
-            mine, other = refs[2 * (w * n + k)][...], refs[2 * (w * n + k) + 1][...]
-            mine, other = mine.astype(F32), other.astype(F32)
-            for at, v in (
-                (low, jnp.where(core_ref[0] == 0, mine, other)),
-                (high, jnp.where(core_ref[0] == 0, other, mine)),
-            ):
-                wide = min(v.shape[1], out_ref.shape[1] - at)
-                out_ref[:, at : at + wide] = v[:, :wide]
-
-
-def place_columns(core, pairs, starts, units):
-    share = pairs[0][0][0].shape[0]
-    tile = share
-    operands = [v for parts in pairs for pair in parts for v in pair]
+def place_kernel(flags_ref, *refs, starts):
+    outs = refs[-2:]
+    core, band = flags_ref[0], flags_ref[1]
+    (low, high), (low_half, high_half) = starts
+
+    def put(out_ref, rows, at, v):
+        wide = min(v.shape[1], out_ref.shape[1] - at)
+        out_ref[rows, at : at + wide] = v[:, :wide]
+
+    for w, out_ref in enumerate(outs):
+        share = out_ref.shape[0]
+        mine, other = refs[2 * w][...].astype(F32), refs[2 * w + 1][...].astype(F32)
+        put(out_ref, slice(0, share), low, jnp.where(core == 0, mine, other))
+        put(out_ref, slice(0, share), high, jnp.where(core == 0, other, mine))
+        own, far, own_other, far_other = (ref[w].astype(F32) for ref in refs[4:8])
+        rows = own.shape[0]
+        both = []
+        for near, away in ((own, far), (own_other, far_other)):
+            first = jnp.where(band == 0, near, away)
+            last = jnp.where(band == 0, away, near)[2 * rows - share :]
+            both.append((first, last))
+        for part, at in ((slice(0, rows), 0), (slice(rows, share), 1)):
+            put(out_ref, part, low_half, jnp.where(core == 0, both[0][at], both[1][at]))
+            put(out_ref, part, high_half, jnp.where(core == 0, both[1][at], both[0][at]))
+
+
+def place_columns(flags, whole_parts, half_parts, starts, share, units):
+    operands = [v for pair in whole_parts for v in pair] + list(half_parts)
     return pl.pallas_call(
         functools.partial(place_kernel, starts=starts),
-        grid=(share // tile,),
         in_specs=[pl.BlockSpec(memory_space=pltpu.SMEM)]
-        + [pl.BlockSpec((tile, v.shape[1]), lambda g: (g, 0)) for v in operands],
-        out_specs=[pl.BlockSpec((tile, units), lambda g: (g, 0))] * 2,
+        + [pl.BlockSpec(v.shape, lambda n=v.ndim: (0,) * n) for v in operands],
+        out_specs=[pl.BlockSpec((share, units), lambda: (0, 0))] * 2,
         out_shape=[jax.ShapeDtypeStruct((share, units), F32)] * 2,
         compiler_params=params(),
-        cost_estimate=cost(0.08),
+        cost_estimate=cost(0.1),
         name="place_columns",
-    )(core[None], *operands)
+    )(flags, *operands)
 
 
 def halo(first, last):
@@ -875,10 +909,6 @@
         (we_pieces[far], wp_pieces[far], index, conv)
     )
     we_peer, wp_peer = join_pieces(index, we_pieces, wp_pieces)
-    act, stat = activate(conv, after(stats, we_peer, wp_peer), par)
-    we_own = flip_bit(after(we_peer, act), "dp", 0)
-    wp_own = flip_bit(after(wp_peer, act), "dp", 0)
-
     groups = [[i for i in range(n_dp) if i % 2 == c] for c in range(2)]
     first = half // (2 * TILE) * TILE
     second = half - first
@@ -907,7 +937,10 @@
         return [lax.psum(v, "dp", axis_index_groups=groups) for v in sums]
 
     pieces = tuple(piece(o, 0) for o in orders)
-    q1 = hidden_layer(act, bg, we_peer, wp_peer, eb_peer, 0, first, lead)
+    front = (conv, after(stats, we_peer, wp_peer), par)
+    *q1, act, stat = hidden_layer(None, bg, we_peer, wp_peer, eb_peer, 0, first, lead, front=front)
+    we_own = flip_bit(after(we_peer, act), "dp", 0)
+    wp_own = flip_bit(after(wp_peer, act), "dp", 0)
     c1 = other_core(q1[2:4])
     q2 = hidden_layer(act, bg, we_peer, wp_peer, after(eb_peer, q1[0]), first, second, lead)
     c2 = other_core(q2[2:4])
@@ -920,6 +953,11 @@
         s1 = exchanged(s1, n)
 
     s2 = exchanged([(o2[2], after(o2[3], *last)), (o2[4], after(o2[5], *last))], 0)
+    eb_o = jnp.concatenate([o1[-1], o2[-1]], axis=1)
+    eb_q = jnp.concatenate([q1[-1], q2[-1]], axis=1)
+    eb_sum = jnp.concatenate(
+        [jnp.where(core == 0, eb_o, eb_q), jnp.where(core == 0, eb_q, eb_o)], axis=1
+    )[:, :units]
     cuts = ((1, 0, first), (0, 0, first), (1, first, second), (0, first, second))
     parts = (q1, o1, q2, o2)
     hidden = [p[0] for p in parts]
@@ -927,46 +965,43 @@
         (we_own, we_peer), [p[1] for p in parts], cuts, conv, after(stat, *last), copies
     )
     sums = lax.all_to_all(sums, devices, 0, 0)
-    s1 = round_sums(arrived(s1, da))
-    b1 = over_bands(s1, groups)
+    band = bit_of("dp", 1)
+    z_keep, z_send = band_split(band, arrived(s1, da))
+    z_came = flip_bit(z_send, "dp", 1)
     for n in range(1, len(bits)):
-        s2 = split(arrived(s2, da, *s1), n)
+        s2 = split(arrived(s2, da, z_send), n)
         last = sends(s2)
         s2 = exchanged(s2, n)
     ready = after(sums, *last)
     conv_grad, g_first, g_last, totals = conv_gradient(da, conv, m16, ready, stat, par)
     g_up, g_dn = halo(g_first, g_last)
-    s2 = round_sums(arrived(s2, conv_grad))
-    tap_local = tap_gradient(x, x_up, x_dn, after(conv_grad, *s2), block, share)
-    s2 = list(lax.optimization_barrier((*s2, *b1, tap_local))[:2])
+    z_came, *came = lax.optimization_barrier((z_came, *[v for _, v in s2], conv_grad))
+    s2 = round_sums([(keep, v) for (keep, _), v in zip(s2, came)])
     b2 = over_bands(s2, groups)
-
-    eb_o = jnp.concatenate([o1[-1], o2[-1]], axis=1)
-    eb_q = jnp.concatenate([q1[-1], q2[-1]], axis=1)
-    eb_all = jnp.concatenate(
-        [jnp.where(core == 0, eb_o, eb_q), jnp.where(core == 0, eb_q, eb_o)], axis=1
-    )[0, :units]
-    local = jnp.concatenate(
-        [
-            tap_local,
-            bg_sum[0, :8].reshape(-1)[:channels].reshape(n_fs, 1, share),
-            eb_all.reshape(n_fs, ratio, share),
-        ],
-        axis=1,
-    )
-    local = lax.all_to_all(local, "fsdp", 0, 0)
-    g_up, g_dn, ready, _ = lax.optimization_barrier((g_up, g_dn, par, tap_local))
-    input_grad = input_gradient(conv_grad, g_up, g_dn, ready, og, m16, block)
+    half_sum = (z_keep + z_came.astype(F32)).astype(BF16)
+    ready = after(conv_grad, half_sum, *s2)
+    tap_local = tap_gradient(x, x_up, x_dn, ready, bg_sum, eb_sum, block, share)
+    g_up, g_dn, half_sum, _ = lax.optimization_barrier((g_up, g_dn, half_sum, tap_local))
+    half_came = flip_bit(half_sum, "dp", 2)
+    bands = n_dp.bit_length() - 1
+
+    local = lax.all_to_all(tap_local, "fsdp", 0, 0)
+    input_grad = input_gradient(conv_grad, g_up, g_dn, after(par, tap_local), og, m16, block)
+    half_came, _ = lax.optimization_barrier((half_came, input_grad))
+    half_sum = (half_sum.astype(F32) + half_came.astype(F32)).astype(BF16)
+    for bit in range(3, bands):
+        half_sum = (half_sum.astype(F32) + flip_bit(half_sum, "dp", bit).astype(F32)).astype(BF16)
+    half_far = flip_bit(half_sum, "dp", 1)
     local = jnp.sum(after(local, input_grad), axis=0)
-    block_out = block_output((wp_own, wp_peer), hidden, cuts, x, m16, after(par, input_grad, local))
+    block_out = block_output((wp_own, wp_peer), hidden, cuts, x, m16, after(par, input_grad, local, half_sum))
     local = jnp.sum(after(from_all(local, "dp"), block_out), axis=0)
 
-    pairs = []
-    for one, two in zip(b1, b2, strict=True):
-        one, two = after(one, block_out), after(two, block_out)
-        pairs.append([(one, flip_bit(one, "dp", 0)), (two, flip_bit(two, "dp", 0))])
-    starts = ((0, half), (first, half + first))
-    project_grad, expand_grad = place_columns(core, pairs, starts, units)
+    half_far, *b2 = lax.optimization_barrier((half_far, *b2, block_out))
+    whole_parts = [(v, flip_bit(v, "dp", 0)) for v in b2[:2]]
+    half_parts = (half_sum, half_far, flip_bit(half_sum, "dp", 0), flip_bit(half_far, "dp", 0))
+    starts = ((first, half + first), (0, half))
+    places = jnp.stack([core, band])
+    project_grad, expand_grad = place_columns(places, whole_parts, half_parts, starts, share, units)
 
     start = lax.axis_index("fsdp") * share
     totals = totals.reshape(2, -1)

time: 311 us -> 302 us (0.971)
  waiting for transfers between devices: 32.6 us -> 17.7 us
  starting transfers between devices: 46.1 us -> 57.6 us
  local copies, waits for them, and re-layouts: 19.8 us -> 11.4 us
  other arithmetic: 3.46 us -> 10.4 us
  Pallas kernels: 193 us -> 189 us
    psum x2 -> x1, waiting for transfers between devices: 18.9 us -> 0.01 us  [over_bands(): return [lax.psum(v, 'dp', axis_index_groups=groups) for v in sums]]
    ppermute x24 -> x27, starting transfers between devices: 17.2 us -> 26.4 us  [flip_bit(): return lax.ppermute(values, axis, [(i, i ^ 1 << bit) for i in range(size)])]
    unnamed x86 -> x34, local copies, waits for them, and re-layouts: 8.77 us -> 0.07 us
    ppermute x24 -> x27, waiting for transfers between devices: 7.28 us -> 11.3 us  [flip_bit(): return lax.ppermute(values, axis, [(i, i ^ 1 << bit) for i in range(size)])]
    convert_element_type x0 -> x2, other arithmetic: none -> 3.73 us  [the longest x1 1.94 us: per_device(): half_sum = (z_keep + z_came.astype(F32)).astype(BF16)]
  transfers between devices with their start and end apart: 35 -> 37, of which waited for: 8 -> 5; matrix products, arithmetic and copies ran while one was open for 3% -> 6% of each run, Pallas kernels for 59% -> 55%
where the time goes in v5:
time: 302 us; the launch traced here: 301 us
  Pallas kernels  189 us (63%)
  starting transfers between devices  57.6 us (19%)
  waiting for transfers between devices  17.7 us (6%)
  between operations  15.1 us (5%)
  local copies, waits for them, and re-layouts  11.4 us (4%)
  other arithmetic  10.4 us (3%)
    pallas_call x4, Pallas kernels, hidden_layer(): pl.pallas_call(functools.partial(hidden_kernel, step=128, pieces=pieces,...  65.3 us
    ppermute x27, starting transfers between devices, flip_bit(): return lax.ppermute(values, axis, [(i, i ^ 1 << bit) for i in range(size)])  26.4 us
    pallas_call x1, Pallas kernels, conv_forward(): pl.pallas_call(functools.partial(conv_kernel, share=share), grid=(channel...  20.9 us
    pallas_call x1, Pallas kernels, tap_gradient(): pl.pallas_call(functools.partial(tap_grad_kernel, share=share), grid=(cha...  17.8 us
    pallas_call x1, Pallas kernels, input_gradient(): pl.pallas_call(input_grad_kernel, grid=(channels // block,), in_specs=[pl...  16.3 us
    pallas_call x1, Pallas kernels, activation_gradient(): pl.pallas_call(functools.partial(act_grad_kernel, cuts=cuts), grid=(rows,...  16.1 us
    pallas_call x1, Pallas kernels, block_output(): pl.pallas_call(functools.partial(block_out_kernel, cuts=cuts), grid=(rows...  14.6 us
    ppermute x27, waiting for transfers between devices, flip_bit(): return lax.ppermute(values, axis, [(i, i ^ 1 << bit) for i in range(size)])  11.3 us
  transfers between devices with their start and end apart: 37, of which 5 were waited for; matrix products, arithmetic and copies ran while one was open for 6% of the time, Pallas kernels for 55%

profile of v5, /device:TPU:0, one launch (start us, length us, event | category | flops | bytes accessed | tf_op | source)
XLA Modules:
  0.0 300.7 jit_solution(762350327588631768)
XLA Ops:
  7.2 3.3 %fusion = (bf16[3,800,256]{2,1,0:T(8,128)(2,1)}, bf16[3,800,256]{2,1,0:T(8,128)(2,1)}) fusion(bf16[6,800,256]{2,1,0:T(8,128)(2,1)} %bitcast.35), kind=kLoop, calls=%fused_computation.22 | loop fusion | bytes 4915200 | tf_op jit(solution)/shard_map/slice | solution.py:861
  11.4 5.2 %all-to-all-start = ((f32[4,56,200]{2,1,0:T(8,128)}), f32[4,56,200]{2,1,0:T(8,128)S(1)}, u32[]{:S(2)}, u32[]{:S(2)}) async-start(f32[4,56,200]{2,1,0:T(8,128)} %broadcast_in_dim.46), calls=%async_computation | async-start | bytes 458752 | tf_op jit(solution)/shard_map/all_to_all | solution.py:810
  16.6 2.5 collective-permute-start.4
  19.0 1.3 collective-permute-start.5
  20.3 1.5 all-to-all-done.small_ref
  21.9 1.1 slice_select_fusion.refs_4_
  23.0 1.2 collective-permute-start.2
  27.7 1.4 collective-permute-start.7
  29.9 5.6 %mask_gradient.1 = (bf16[800,1536]{1,0:T(8,128)(2,1)}, f32[1,16,128]{2,1,0:T(8,128)}) custom-call(bf16[6,800,256]{2,1,0:T(8,128)(2,1)} %bitcast.39, f32[6,16,256]{2,1,0:T(8,128)} %broadcast_in_dim.47.m_ref.refs_7_), custom_call_target="tpu_custom_call" | custom-call | flops 115000000 | bytes 100000 | tf_op jit(solution)/shard_map/mask_gradient/pallas_call | solution.py:338
  35.4 5.3 %collective-permute-done.2.refs_6_ = bf16[200,1664]{1,0:T(8,128)(2,1)} collective-permute-done((bf16[200,1664]{1,0:T(8,128)(2,1)}, bf16[200,1664]{1,0:T(8,128)(2,1)}, u32[]{:S(2)}, u32[]{:S(2)}) %collective-permute-start.2) | collective-permute-done | bytes 665632 | tf_op jit(solution)/shard_map/ppermute | solution.py:815
  40.7 1.4 collective-permute-start.6
  42.1 1.2 collective-permute-done.refs_1_
  43.4 1.7 collective-permute-start.1
  45.7 20.9 %conv_forward.1 = (f32[6,800,256]{2,1,0:T(8,128)}, f32[32,16,128]{2,1,0:T(8,128)}, f32[800,128]{1,0:T(8,128)}) custom-call(bf16[6,800,256]{2,1,0:T(8,128)(2,1)} %bitcast.36, bf16[3,800,256]{2,1,0:T(8,128)(2,1)} %collective-permute-done.4.up_ref, bf16[3,800,256]{2,1,0:T(8,128)(2,1)} %collective-permute-done.5.dn_ref, f32[4,56,200]{2,1,0:T(8,128)} %copy-done.3, ...), custom_call_target="tpu_custom_call" | custom-call | flops 460000000 | bytes 100000 | tf_op jit(solution)/shard_map/conv_forward/pallas_call | solution.py:158
  66.6 6.7 %all-to-all-start.1 = ((f32[32,16,128]{2,1,0:T(8,128)}), f32[32,16,128]{2,1,0:T(8,128)}, u32[]{:S(2)}, u32[]{:S(2)}) async-start(f32[32,16,128]{2,1,0:T(8,128)} %get-tuple-element.124), calls=%async_computation.1 | async-start | bytes 524288 | tf_op jit(solution)/shard_map/all_to_all | solution.py:905
  73.3 5.8 %join_pieces.1 = (bf16[800,1664]{1,0:T(8,128)(2,1)}, bf16[800,1664]{1,0:T(8,128)(2,1)}) custom-call(s32[1]{0:T(128)} %bitcast.12.index_ref, bf16[200,1664]{1,0:T(8,128)(2,1)} %slice_select_fusion.1.refs_0_, bf16[200,1664]{1,0:T(8,128)(2,1)} %collective-permute-done.refs_1_, bf16[200,1664]{1,0:T(8,128)(2,1)} %collective-permute-done.6.refs_2_, ...), custom_call_target="tpu_custom_call" | custom-call | flops 115000000 | bytes 100000 | tf_op jit(solution)/shard_map/join_pieces/pallas_call | solution.py:742
  79.1 4.9 %all-to-all-done.1.refs_1_ = f32[32,16,128]{2,1,0:T(8,128)} async-done(((f32[32,16,128]{2,1,0:T(8,128)}), f32[32,16,128]{2,1,0:T(8,128)}, u32[]{:S(2)}, u32[]{:S(2)}) %all-to-all-start.1) | async-done | bytes 262176 | tf_op jit(solution)/shard_map/all_to_all | solution.py:905
  84.0 15.9 %hidden_layer.4 = (bf16[1536,768]{1,0:T(8,128)(2,1)}, bf16[1536,768]{1,0:T(8,128)(2,1)}, bf16[800,768]{1,0:T(8,128)(2,1)}, bf16[800,768]{1,0:T(8,128)(2,1)}, f32...) custom-call(s32[2]{0:T(128)} %pad_add_fusion.bits_ref, bf16[800,1536]{1,0:T(8,128)(2,1)} %get-tuple-element.112.bg_ref, ...), custom_call_target="tpu_custom_call" | custom-call | flops 345000000 | bytes 100000 | tf_op jit(solution)/shard_map/hidden_layer/pallas_call | solution.py:468
  101.0 17.0 %hidden_layer.5 = (bf16[1536,896]{1,0:T(8,128)(2,1)}, bf16[1536,896]{1,0:T(8,128)(2,1)}, bf16[800,896]{1,0:T(8,128)(2,1)}, bf16[800,896]{1,0:T(8,128)(2,1)}, f32[1,896]{1,0:T(1,128)}) custom-call(s32[2]{0:T(128)} %pad_add_fusion.bits_ref, bf16[800,1536]{1,0:T(8,128)(2,1)} %get-tuple-element.112.bg_ref, bf16[800,1664]{1,0:T(8,128)(2,1)} %get-tuple-element.130.we_ref.refs_1_, ...), custom_call_target="tpu_custom_call" | custom-call | flops 345000000 | bytes 100000 | tf_op jit(solution)/shard_map/hidden_layer/pallas_call | solution.py:468
  119.8 14.5 %hidden_layer.6 = (bf16[1536,768]{1,0:T(8,128)(2,1)}, bf16[1536,768]{1,0:T(8,128)(2,1)}, f32[400,768]{1,0:T(8,128)}, bf16[400,768]{1,0:T(8,128)(2,1)}, f32[400,7...) custom-call(s32[2]{0:T(128)} %pad_add_fusion.bits_ref, bf16[800,1536]{1,0:T(8,128)(2,1)} %get-tuple-element.112.bg_ref, ...), custom_call_target="tpu_custom_call" | custom-call | flops 345000000 | bytes 100000 | tf_op jit(solution)/shard_map/hidden_layer/pallas_call | solution.py:468
  134.5 1.3 collective-permute-start.15
  136.4 17.9 %hidden_layer.7 = (bf16[1536,896]{1,0:T(8,128)(2,1)}, bf16[1536,896]{1,0:T(8,128)(2,1)}, f32[400,896]{1,0:T(8,128)}, bf16[400,896]{1,0:T(8,128)(2,1)}, f32[400,8...) custom-call(s32[2]{0:T(128)} %pad_add_fusion.bits_ref, bf16[800,1536]{1,0:T(8,128)(2,1)} %get-tuple-element.112.bg_ref, ...), custom_call_target="tpu_custom_call" | custom-call | flops 345000000 | bytes 100000 | tf_op jit(solution)/shard_map/hidden_layer/pallas_call | solution.py:468
  155.0 3.3 %split_sums.2 = (f32[200,768]{1,0:T(8,128)}, bf16[200,768]{1,0:T(8,128)(2,1)}, f32[200,768]{1,0:T(8,128)}, bf16[200,768]{1,0:T(8,128)(2,1)}) custom-call(s32[2]{0:T(128)} %pad_add_fusion.1.bits_ref, f32[400,768]{1,0:T(8,128)} %get-tuple-element.147.refs_0_, bf16[400,768]{1,0:T(8,128)(2,1)} %collective-permute-done.14.refs_1_, ...), custom_call_target="tpu_custom_call" | custom-call | flops 3449999872 | bytes 100000 | tf_op jit(solution)/shard_map/split_sums/pallas_call | solution.py:493
  159.1 1.9 collective-permute-start.19
  161.0 1.4 collective-permute-start.16
  162.4 16.1 %activation_gradient.1 = (f32[6,800,256]{2,1,0:T(8,128)}, f32[32,16,128]{2,1,0:T(8,128)}) custom-call(bf16[800,1664]{1,0:T(8,128)(2,1)} %collective-permute-done.9.we_ref.refs_0_, bf16[800,1664]{1,0:T(8,128)(2,1)} %get-tuple-element.130.we_ref.refs_1_, bf16[1536,768]{1,0:T(8,128)(2,1)} %get-tuple-element.142.refs_2_, ...), custom_call_target="tpu_custom_call" | custom-call | flops 345000000 | bytes 100000 | tf_op jit(solution)/shard_map/activation_gradient/pallas_call | solution.py:596
  178.5 3.5 %all-to-all-start.2 = ((f32[32,16,128]{2,1,0:T(8,128)}), f32[32,16,128]{2,1,0:T(8,128)}, u32[]{:S(2)}, u32[]{:S(2)}) async-start(f32[32,16,128]{2,1,0:T(8,128)} %get-tuple-element.157), calls=%async_computation.2 | async-start | bytes 524288 | tf_op jit(solution)/shard_map/all_to_all | solution.py:967
  182.1 2.6 band_split.1
  184.7 1.7 collective-permute-start.22
  186.4 3.7 %split_sums.3 = (f32[200,896]{1,0:T(8,128)}, bf16[200,896]{1,0:T(8,128)(2,1)}, f32[200,896]{1,0:T(8,128)}, bf16[200,896]{1,0:T(8,128)(2,1)}) custom-call(s32[2]{0:T(128)} %pad_add_fusion.1.bits_ref, f32[400,896]{1,0:T(8,128)} %get-tuple-element.158.refs_0_, bf16[400,896]{1,0:T(8,128)(2,1)} %collective-permute-done.16.refs_1_, ...), custom_call_target="tpu_custom_call" | custom-call | flops 3449999872 | bytes 100000 | tf_op jit(solution)/shard_map/split_sums/pallas_call | solution.py:493
  190.1 1.5 collective-permute-start.23
  191.5 1.5 collective-permute-start.24
  193.6 9.8 %conv_gradient.1 = (bf16[6,800,256]{2,1,0:T(8,128)(2,1)}, bf16[3,800,256]{2,1,0:T(8,128)(2,1)}, bf16[3,800,256]{2,1,0:T(8,128)(2,1)}, f32[16,128]{1,0:T(8,128)}) custom-call(f32[6,800,256]{2,1,0:T(8,128)} %get-tuple-element.156.da_ref, f32[6,800,256]{2,1,0:T(8,128)} %get-tuple-element.116.refs_0_.refs_6_.conv_ref, ...), custom_call_target="tpu_custom_call" | custom-call | flops 230000000 | bytes 100000 | tf_op jit(solution)/shard_map/conv_gradient/pallas_call | solution.py:685
  203.4 2.4 collective-permute-start.20
  205.8 1.3 collective-permute-start.21
  207.1 1.9 add_convert_fusion.1
  209.0 2.5 round_sums.1
  211.5 17.8 %tap_gradient.1 = f32[4,54,200]{2,1,0:T(8,128)} custom-call(bf16[6,800,256]{2,1,0:T(8,128)(2,1)} %bitcast.37, bf16[3,800,256]{2,1,0:T(8,128)(2,1)} %collective-permute-done.4.up_ref, bf16[3,800,256]{2,1,0:T(8,128)(2,1)} %collective-permute-done.5.dn_ref, bf16[6,800,256]{2,1,0:T(8,128)(2,1)} %get-tuple-element.185.g_ref, ...), custom_call_target="tpu_custom_call" | custom-call | flops 17250000896 | bytes 100000 | tf_op jit(solution)/shard_map/tap_gradient/pallas_call | solution.py:290
  229.3 4.0 %all-to-all-start.3 = ((f32[4,54,200]{2,1,0:T(8,128)}), f32[4,54,200]{2,1,0:T(8,128)}, u32[]{:S(2)}, u32[]{:S(2)}) async-start(f32[4,54,200]{2,1,0:T(8,128)} %tap_gradient.1), calls=%async_computation.3 | async-start | bytes 458752 | tf_op jit(solution)/shard_map/all_to_all | solution.py:988
  233.3 4.4 %collective-permute-start.25 = (bf16[2,104,768]{2,1,0:T(8,128)(2,1)}, bf16[2,104,768]{2,1,0:T(8,128)(2,1)}, u32[]{:S(2)}, u32[]{:S(2)}) collective-permute-start(bf16[2,104,768]{2,1,0:T(8,128)(2,1)} %add_convert_fusion.1), channel_id=1, source_target_pairs={{0,16},{4,20},{8,24},{12,28},{16,0},{20,4},{24,8},{28,12},{1,17},{... | collective-permute-start | bytes 958472 | tf_op jit(solution)/shard_map/ppermute | solution.py:815
  237.8 16.3 %input_gradient.1 = f32[6,800,256]{2,1,0:T(8,128)} custom-call(bf16[6,800,256]{2,1,0:T(8,128)(2,1)} %get-tuple-element.185.g_ref, bf16[3,800,256]{2,1,0:T(8,128)(2,1)} %collective-permute-done.20.up_ref, bf16[3,800,256]{2,1,0:T(8,128)(2,1)} %collective-permute-done.21.dn_ref, f32[800,128]{1,0:T(8,128)} %get-tuple-element.197.refs_2_.par_ref.refs_8_, ...), custom_call_target="tpu_custom_call" | custom-call | flops 5750000128 | bytes 100000 | tf_op jit(solution)/shard_map/input_gradient/pallas_call | solution.py:216
  255.9 4.4 %all-to-all-start.4 = ((f32[8,54,200]{2,1,0:T(8,128)}), f32[8,54,200]{2,1,0:T(8,128)}, u32[]{:S(2)}, u32[]{:S(2)}) async-start(f32[8,54,200]{2,1,0:T(8,128)} %broadcast_in_dim.52), calls=%async_computation.4 | async-start | bytes 917504 | tf_op jit(solution)/shard_map/all_to_all | solution.py:810
  260.3 4.7 %collective-permute-done.25 = bf16[2,104,768]{2,1,0:T(8,128)(2,1)} collective-permute-done((bf16[2,104,768]{2,1,0:T(8,128)(2,1)}, bf16[2,104,768]{2,1,0:T(8,128)(2,1)}, u32[]{:S(2)}, u32[]{:S(2)}) %collective-permute-start.25) | collective-permute-done | bytes 319520 | tf_op jit(solution)/shard_map/ppermute | solution.py:815
  265.0 1.8 add_convert_fusion.refs_4_
  266.8 2.8 collective-permute-start.26
  269.6 14.6 %block_output.1 = bf16[6,800,256]{2,1,0:T(8,128)(2,1)} custom-call(bf16[800,1664]{1,0:T(8,128)(2,1)} %collective-permute-done.8.wp_ref.refs_0_, bf16[800,1664]{1,0:T(8,128)(2,1)} %get-tuple-element.128.wp_ref.refs_1_, bf16[1536,768]{1,0:T(8,128)(2,1)} %get-tuple-element.129.refs_2_, bf16[1536,768]{1,0:T(8,128)(2,1)} %get-tuple-element.137.refs_3_, ...), custom_call_target="tpu_custom_call" | custom-call | flops 5750000128 | bytes 100000 | tf_op jit(solution)/shard_map/block_output/pallas_call | solution.py:629
  286.5 1.1 reduce_sum.19
  289.5 4.4 %place_columns.1 = (f32[200,3200]{1,0:T(8,128)}, f32[200,3200]{1,0:T(8,128)}) custom-call(s32[2]{0:T(128)} %pad_add_fusion.2.flags_ref, bf16[200,896]{1,0:T(8,128)(2,1)} %get-tuple-element.200.refs_0_, bf16[200,896]{1,0:T(8,128)(2,1)} %collective-permute-done.27.refs_1_, bf16[200,896]{1,0:T(8,128)(2,1)} %get-tuple-element.201.refs_2_, ...), custom_call_target="tpu_custom_call" | custom-call | flops 115000000 | bytes 100000 | tf_op jit(solution)/shard_map/place_columns/pallas_call | solution.py:782
  (115 shorter events, 17.1 us)
Async XLA Ops:
  7.2 3.4 %copy-start.5 = (f32[200,49]{0,1:T(8,128)S(1)}, f32[200,49]{0,1:T(8,128)}, u32[]{:S(2)}) copy-start(f32[200,49]{0,1:T(8,128)} %param.15) | copy-start | bytes 117604
  10.5 11.3 %copy-start.1 = (bf16[200,3200]{1,0:T(8,128)(2,1)S(1)}, bf16[200,3200]{1,0:T(8,128)(2,1)}, u32[]{:S(2)}) copy-start(bf16[200,3200]{1,0:T(8,128)(2,1)} %param.20) | copy-start | bytes 3840004
  10.5 11.3 %slice-start.1 = ((bf16[200,3200]{1,0:T(8,128)(2,1)}), bf16[200,1536]{1,0:T(8,128)(2,1)S(1)}, s32[]{:S(2)}) async-start(bf16[200,3200]{1,0:T(8,128)(2,1)} %param.20), calls=%async_computation.7 | async-start | bytes 1228800 | tf_op jit(solution)/shard_map/slice | solution.py:878
  11.4 10.4 %all-to-all-start = ((f32[4,56,200]{2,1,0:T(8,128)}), f32[4,56,200]{2,1,0:T(8,128)S(1)}, u32[]{:S(2)}, u32[]{:S(2)}) async-start(f32[4,56,200]{2,1,0:T(8,128)} %broadcast_in_dim.46), calls=%async_computation | async-start | bytes 458752 | tf_op jit(solution)/shard_map/all_to_all | solution.py:810
  16.6 26.8 %collective-permute-start.4 = (bf16[3,800,256]{2,1,0:T(8,128)(2,1)}, bf16[3,800,256]{2,1,0:T(8,128)(2,1)}, u32[]{:S(2)}, u32[]{:S(2)}) collective-permute-start(bf16[3,800,256]{2,1,0:T(8,128)(2,1)} %get-tuple-element.207), channel_id=1, source_target_pairs={{0,4},{4,8},{8,12},{12,16},{16,20},{20,24},{24,28},{1,5},{5,9},{9,... | collective-permute-start | bytes 3686408 | tf_op jit(solution)/shard_map/ppermute | solution.py:799
  19.0 26.7 %collective-permute-start.5 = (bf16[3,800,256]{2,1,0:T(8,128)(2,1)}, bf16[3,800,256]{2,1,0:T(8,128)(2,1)}, u32[]{:S(2)}, u32[]{:S(2)}) collective-permute-start(bf16[3,800,256]{2,1,0:T(8,128)(2,1)} %get-tuple-element.208), channel_id=1, source_target_pairs={{4,0},{8,4},{12,8},{16,12},{20,16},{24,20},{28,24},{5,1},{9,5},{13... | collective-permute-start | bytes 3686408 | tf_op jit(solution)/shard_map/ppermute | solution.py:800
  21.8 7.9 %copy-start.3 = (f32[4,56,200]{2,1,0:T(8,128)}, f32[4,56,200]{2,1,0:T(8,128)S(1)}, u32[]{:S(2)}) copy-start(f32[4,56,200]{2,1,0:T(8,128)S(1)} %all-to-all-done.small_ref) | copy-start | bytes 537604
  23.0 4.8 %copy-start.6 = (s32[6,256]{1,0:T(8,128)S(1)}, s32[6,256]{1,0:T(8,128)}, u32[]{:S(2)}) copy-start(s32[6,256]{1,0:T(8,128)} %param.13) | copy-start | bytes 18436
  23.0 17.7 %collective-permute-start.2 = (bf16[200,1664]{1,0:T(8,128)(2,1)}, bf16[200,1664]{1,0:T(8,128)(2,1)}, u32[]{:S(2)}, u32[]{:S(2)}) collective-permute-start(bf16[200,1664]{1,0:T(8,128)(2,1)} %slice_select_fusion.refs_4_), channel_id=1, source_target_pairs={{0,2},{1,3},{2,0},{3,1},{4,6},{5,7},{6,4},{7,5},{8,10},{9,11},{10,... | collective-permute-start | bytes 1996808 | tf_op jit(solution)/shard_map/ppermute | solution.py:815
  25.2 18.1 %collective-permute-start = (bf16[200,1664]{1,0:T(8,128)(2,1)}, bf16[200,1664]{1,0:T(8,128)(2,1)}, u32[]{:S(2)}, u32[]{:S(2)}) collective-permute-start(bf16[200,1664]{1,0:T(8,128)(2,1)} %slice_select_fusion.1.refs_0_), channel_id=1, source_target_pairs={{0,1},{1,0},{2,3},{3,2},{4,5},{5,4},{6,7},{7,6},{8,9},{9,8},{10,11... | collective-permute-start | bytes 1996808 | tf_op jit(solution)/shard_map/ppermute | solution.py:815
  27.7 45.6 %collective-permute-start.7 = (bf16[200,1664]{1,0:T(8,128)(2,1)}, bf16[200,1664]{1,0:T(8,128)(2,1)}, u32[]{:S(2)}, u32[]{:S(2)}) collective-permute-start(bf16[200,1664]{1,0:T(8,128)(2,1)} %slice_select_fusion.refs_4_), channel_id=1, source_target_pairs={{0,1},{1,0},{2,3},{3,2},{4,5},{5,4},{6,7},{7,6},{8,9},{9,8},{10,11... | collective-permute-start | bytes 1996808 | tf_op jit(solution)/shard_map/ppermute | solution.py:815
  40.7 32.6 %collective-permute-start.6 = (bf16[200,1664]{1,0:T(8,128)(2,1)}, bf16[200,1664]{1,0:T(8,128)(2,1)}, u32[]{:S(2)}, u32[]{:S(2)}) collective-permute-start(bf16[200,1664]{1,0:T(8,128)(2,1)} %slice_select_fusion.1.refs_0_), channel_id=1, source_target_pairs={{0,2},{1,3},{2,0},{3,1},{4,6},{5,7},{6,4},{7,5},{8,10},{9,11},{10,... | collective-permute-start | bytes 1996808 | tf_op jit(solution)/shard_map/ppermute | solution.py:815
  43.3 30.0 %collective-permute-start.3 = (bf16[200,1664]{1,0:T(8,128)(2,1)}, bf16[200,1664]{1,0:T(8,128)(2,1)}, u32[]{:S(2)}, u32[]{:S(2)}) collective-permute-start(bf16[200,1664]{1,0:T(8,128)(2,1)} %collective-permute-done.2.refs_6_), channel_id=1, source_target_pairs={{0,1},{1,0},{2,3},{3,2},{4,5},{5,4},{6,7},{7,6},{8,9},{9,8},{10,11... | collective-permute-start | bytes 1996808 | tf_op jit(solution)/shard_map/ppermute | solution.py:815
  43.4 29.9 %collective-permute-start.1 = (bf16[200,1664]{1,0:T(8,128)(2,1)}, bf16[200,1664]{1,0:T(8,128)(2,1)}, u32[]{:S(2)}, u32[]{:S(2)}) collective-permute-start(bf16[200,1664]{1,0:T(8,128)(2,1)} %collective-permute-done.refs_1_), channel_id=1, source_target_pairs={{0,2},{1,3},{2,0},{3,1},{4,6},{5,7},{6,4},{7,5},{8,10},{9,11},{10,... | collective-permute-start | bytes 1996808 | tf_op jit(solution)/shard_map/ppermute | solution.py:815
  66.6 17.4 %all-to-all-start.1 = ((f32[32,16,128]{2,1,0:T(8,128)}), f32[32,16,128]{2,1,0:T(8,128)}, u32[]{:S(2)}, u32[]{:S(2)}) async-start(f32[32,16,128]{2,1,0:T(8,128)} %get-tuple-element.124), calls=%async_computation.1 | async-start | bytes 524288 | tf_op jit(solution)/shard_map/all_to_all | solution.py:905
  99.9 19.9 %collective-permute-start.9 = (bf16[800,1664]{1,0:T(8,128)(2,1)}, bf16[800,1664]{1,0:T(8,128)(2,1)}, u32[]{:S(2)}, u32[]{:S(2)}) collective-permute-start(bf16[800,1664]{1,0:T(8,128)(2,1)} %get-tuple-element.130.we_ref.refs_1_), channel_id=1, source_target_pairs={{0,4},{4,0},{8,12},{12,8},{16,20},{20,16},{24,28},{28,24},{1,5},{5... | collective-permute-start | bytes 7987208 | tf_op jit(solution)/shard_map/ppermute | solution.py:815
  100.0 19.8 %collective-permute-start.8 = (bf16[800,1664]{1,0:T(8,128)(2,1)}, bf16[800,1664]{1,0:T(8,128)(2,1)}, u32[]{:S(2)}, u32[]{:S(2)}) collective-permute-start(bf16[800,1664]{1,0:T(8,128)(2,1)} %get-tuple-element.128.wp_ref.refs_1_), channel_id=1, source_target_pairs={{0,4},{4,0},{8,12},{12,8},{16,20},{20,16},{24,28},{28,24},{1,5},{5... | collective-permute-start | bytes 7987208 | tf_op jit(solution)/shard_map/ppermute | solution.py:815
  100.5 17.6 %collective-permute-start.10 = (bf16[800,768]{1,0:T(8,128)(2,1)}, bf16[800,768]{1,0:T(8,128)(2,1)}, u32[]{:S(2)}, u32[]{:S(2)}) collective-permute-start(bf16[800,768]{1,0:T(8,128)(2,1)} %get-tuple-element.135), channel_id=1, source_target_pairs={{0,4},{4,0},{8,12},{12,8},{16,20},{20,16},{24,28},{28,24},{1,5},{5... | collective-permute-start | bytes 3686408 | tf_op jit(solution)/shard_map/ppermute | solution.py:815
  100.6 19.2 %collective-permute-start.11 = (bf16[800,768]{1,0:T(8,128)(2,1)}, bf16[800,768]{1,0:T(8,128)(2,1)}, u32[]{:S(2)}, u32[]{:S(2)}) collective-permute-start(bf16[800,768]{1,0:T(8,128)(2,1)} %get-tuple-element.136), channel_id=1, source_target_pairs={{0,4},{4,0},{8,12},{12,8},{16,20},{20,16},{24,28},{28,24},{1,5},{5... | collective-permute-start | bytes 3686408 | tf_op jit(solution)/shard_map/ppermute | solution.py:815
  118.0 18.4 %collective-permute-start.12 = (bf16[800,896]{1,0:T(8,128)(2,1)}, bf16[800,896]{1,0:T(8,128)(2,1)}, u32[]{:S(2)}, u32[]{:S(2)}) collective-permute-start(bf16[800,896]{1,0:T(8,128)(2,1)} %get-tuple-element.139), channel_id=1, source_target_pairs={{0,4},{4,0},{8,12},{12,8},{16,20},{20,16},{24,28},{28,24},{1,5},{5... | collective-permute-start | bytes 4300808 | tf_op jit(solution)/shard_map/ppermute | solution.py:815
  118.1 18.3 %collective-permute-start.13 = (bf16[800,896]{1,0:T(8,128)(2,1)}, bf16[800,896]{1,0:T(8,128)(2,1)}, u32[]{:S(2)}, u32[]{:S(2)}) collective-permute-start(bf16[800,896]{1,0:T(8,128)(2,1)} %get-tuple-element.140), channel_id=1, source_target_pairs={{0,4},{4,0},{8,12},{12,8},{16,20},{20,16},{24,28},{28,24},{1,5},{5... | collective-permute-start | bytes 4300808 | tf_op jit(solution)/shard_map/ppermute | solution.py:815
  119.8 16.0 %copy-start.9 = (f32[1,768]{1,0:T(1,128)S(1)}, f32[1,768]{1,0:T(1,128)}, u32[]{:S(2)}) copy-start(f32[1,768]{1,0:T(1,128)} %get-tuple-element.189) | copy-start | bytes 9220
  119.8 16.0 %copy-start.8 = (f32[1,896]{1,0:T(1,128)S(1)}, f32[1,896]{1,0:T(1,128)}, u32[]{:S(2)}) copy-start(f32[1,896]{1,0:T(1,128)} %get-tuple-element.190) | copy-start | bytes 10756
  119.8 16.0 %copy-start.4 = (f32[32,128]{1,0:T(8,128)S(1)}, f32[32,128]{1,0:T(8,128)}, u32[]{:S(2)}) copy-start(f32[32,128]{1,0:T(8,128)} %get-tuple-element.155.refs_7_.stat_ref) | copy-start | bytes 49156
  134.3 20.7 %collective-permute-start.14 = (bf16[400,768]{1,0:T(8,128)(2,1)}, bf16[400,768]{1,0:T(8,128)(2,1)}, u32[]{:S(2)}, u32[]{:S(2)}) collective-permute-start(bf16[400,768]{1,0:T(8,128)(2,1)} %get-tuple-element.148), channel_id=1, source_target_pairs={{0,2},{1,3},{2,0},{3,1},{4,6},{5,7},{6,4},{7,5},{8,10},{9,11},{10,... | collective-permute-start | bytes 1843208 | tf_op jit(solution)/shard_map/ppermute | solution.py:815
  134.5 20.5 %collective-permute-start.15 = (bf16[400,768]{1,0:T(8,128)(2,1)}, bf16[400,768]{1,0:T(8,128)(2,1)}, u32[]{:S(2)}, u32[]{:S(2)}) collective-permute-start(bf16[400,768]{1,0:T(8,128)(2,1)} %get-tuple-element.149), channel_id=1, source_target_pairs={{0,1},{1,0},{2,3},{3,2},{4,5},{5,4},{6,7},{7,6},{8,9},{9,8},{10,11... | collective-permute-start | bytes 1843208 | tf_op jit(solution)/shard_map/ppermute | solution.py:815
  136.4 17.9 %copy-start.10 = (f32[1,768]{1,0:T(1,128)S(1)}, f32[1,768]{1,0:T(1,128)}, u32[]{:S(2)}) copy-start(f32[1,768]{1,0:T(1,128)} %get-tuple-element.187) | copy-start | bytes 9220
  158.4 23.8 %collective-permute-start.18 = (bf16[200,768]{1,0:T(8,128)(2,1)}, bf16[200,768]{1,0:T(8,128)(2,1)}, u32[]{:S(2)}, u32[]{:S(2)}) collective-permute-start(bf16[200,768]{1,0:T(8,128)(2,1)} %get-tuple-element.153), channel_id=1, source_target_pairs={{0,1},{1,0},{2,3},{3,2},{4,5},{5,4},{6,7},{7,6},{8,9},{9,8},{10,11... | collective-permute-start | bytes 921608 | tf_op jit(solution)/shard_map/ppermute | solution.py:815
  159.1 23.0 %collective-permute-start.19 = (bf16[200,768]{1,0:T(8,128)(2,1)}, bf16[200,768]{1,0:T(8,128)(2,1)}, u32[]{:S(2)}, u32[]{:S(2)}) collective-permute-start(bf16[200,768]{1,0:T(8,128)(2,1)} %get-tuple-element.154), channel_id=1, source_target_pairs={{0,2},{1,3},{2,0},{3,1},{4,6},{5,7},{6,4},{7,5},{8,10},{9,11},{10,... | collective-permute-start | bytes 921608 | tf_op jit(solution)/shard_map/ppermute | solution.py:815
  161.0 25.4 %collective-permute-start.17 = (bf16[400,896]{1,0:T(8,128)(2,1)}, bf16[400,896]{1,0:T(8,128)(2,1)}, u32[]{:S(2)}, u32[]{:S(2)}) collective-permute-start(bf16[400,896]{1,0:T(8,128)(2,1)} %get-tuple-element.162), channel_id=1, source_target_pairs={{0,1},{1,0},{2,3},{3,2},{4,5},{5,4},{6,7},{7,6},{8,9},{9,8},{10,11... | collective-permute-start | bytes 2150408 | tf_op jit(solution)/shard_map/ppermute | solution.py:815
  161.0 25.4 %collective-permute-start.16 = (bf16[400,896]{1,0:T(8,128)(2,1)}, bf16[400,896]{1,0:T(8,128)(2,1)}, u32[]{:S(2)}, u32[]{:S(2)}) collective-permute-start(bf16[400,896]{1,0:T(8,128)(2,1)} %get-tuple-element.160), channel_id=1, source_target_pairs={{0,2},{1,3},{2,0},{3,1},{4,6},{5,7},{6,4},{7,5},{8,10},{9,11},{10,... | collective-permute-start | bytes 2150408 | tf_op jit(solution)/shard_map/ppermute | solution.py:815
  178.5 15.1 %all-to-all-start.2 = ((f32[32,16,128]{2,1,0:T(8,128)}), f32[32,16,128]{2,1,0:T(8,128)}, u32[]{:S(2)}, u32[]{:S(2)}) async-start(f32[32,16,128]{2,1,0:T(8,128)} %get-tuple-element.157), calls=%async_computation.2 | async-start | bytes 524288 | tf_op jit(solution)/shard_map/all_to_all | solution.py:967
  182.1 102.1 %all-reduce.6.cloned.1.call-start = ((), (), s32[]{:S(2)}) async-start(), calls=%async_computation.5 | async-start | bytes 1433600 | tf_op jit(solution)/shard_map/psum | solution.py:937
  184.7 22.4 %collective-permute-start.22 = (bf16[2,104,768]{2,1,0:T(8,128)(2,1)}, bf16[2,104,768]{2,1,0:T(8,128)(2,1)}, u32[]{:S(2)}, u32[]{:S(2)}) collective-permute-start(bf16[2,104,768]{2,1,0:T(8,128)(2,1)} %get-tuple-element.167), channel_id=1, source_target_pairs={{0,8},{4,12},{8,0},{12,4},{16,24},{20,28},{24,16},{28,20},{1,9},{5... | collective-permute-start | bytes 958472 | tf_op jit(solution)/shard_map/ppermute | solution.py:815
  190.1 17.0 %collective-permute-start.23 = (bf16[200,896]{1,0:T(8,128)(2,1)}, bf16[200,896]{1,0:T(8,128)(2,1)}, u32[]{:S(2)}, u32[]{:S(2)}) collective-permute-start(bf16[200,896]{1,0:T(8,128)(2,1)} %get-tuple-element.171), channel_id=1, source_target_pairs={{0,1},{1,0},{2,3},{3,2},{4,5},{5,4},{6,7},{7,6},{8,9},{9,8},{10,11... | collective-permute-start | bytes 1075208 | tf_op jit(solution)/shard_map/ppermute | solution.py:815
  191.5 15.5 %collective-permute-start.24 = (bf16[200,896]{1,0:T(8,128)(2,1)}, bf16[200,896]{1,0:T(8,128)(2,1)}, u32[]{:S(2)}, u32[]{:S(2)}) collective-permute-start(bf16[200,896]{1,0:T(8,128)(2,1)} %get-tuple-element.172), channel_id=1, source_target_pairs={{0,2},{1,3},{2,0},{3,1},{4,6},{5,7},{6,4},{7,5},{8,10},{9,11},{10,... | collective-permute-start | bytes 1075208 | tf_op jit(solution)/shard_map/ppermute | solution.py:815
  203.4 29.9 %collective-permute-start.20 = (bf16[3,800,256]{2,1,0:T(8,128)(2,1)}, bf16[3,800,256]{2,1,0:T(8,128)(2,1)}, u32[]{:S(2)}, u32[]{:S(2)}) collective-permute-start(bf16[3,800,256]{2,1,0:T(8,128)(2,1)} %get-tuple-element.175), channel_id=1, source_target_pairs={{0,4},{4,8},{8,12},{12,16},{16,20},{20,24},{24,28},{1,5},{5,9},{9,... | collective-permute-start | bytes 3686408 | tf_op jit(solution)/shard_map/ppermute | solution.py:799
  205.8 27.6 %collective-permute-start.21 = (bf16[3,800,256]{2,1,0:T(8,128)(2,1)}, bf16[3,800,256]{2,1,0:T(8,128)(2,1)}, u32[]{:S(2)}, u32[]{:S(2)}) collective-permute-start(bf16[3,800,256]{2,1,0:T(8,128)(2,1)} %get-tuple-element.176), channel_id=1, source_target_pairs={{4,0},{8,4},{12,8},{16,12},{20,16},{24,20},{28,24},{5,1},{9,5},{13... | collective-permute-start | bytes 3686408 | tf_op jit(solution)/shard_map/ppermute | solution.py:800
  229.3 24.8 %all-to-all-start.3 = ((f32[4,54,200]{2,1,0:T(8,128)}), f32[4,54,200]{2,1,0:T(8,128)}, u32[]{:S(2)}, u32[]{:S(2)}) async-start(f32[4,54,200]{2,1,0:T(8,128)} %tap_gradient.1), calls=%async_computation.3 | async-start | bytes 458752 | tf_op jit(solution)/shard_map/all_to_all | solution.py:988
  233.3 31.7 %collective-permute-start.25 = (bf16[2,104,768]{2,1,0:T(8,128)(2,1)}, bf16[2,104,768]{2,1,0:T(8,128)(2,1)}, u32[]{:S(2)}, u32[]{:S(2)}) collective-permute-start(bf16[2,104,768]{2,1,0:T(8,128)(2,1)} %add_convert_fusion.1), channel_id=1, source_target_pairs={{0,16},{4,20},{8,24},{12,28},{16,0},{20,4},{24,8},{28,12},{1,17},{... | collective-permute-start | bytes 958472 | tf_op jit(solution)/shard_map/ppermute | solution.py:815
  254.1 10.9 %copy-start.2 = (bf16[2,104,768]{2,1,0:T(8,128)(2,1)S(1)}, bf16[2,104,768]{2,1,0:T(8,128)(2,1)}, u32[]{:S(2)}) copy-start(bf16[2,104,768]{2,1,0:T(8,128)(2,1)} %add_convert_fusion.1) | copy-start | bytes 958468
  255.9 30.7 %all-to-all-start.4 = ((f32[8,54,200]{2,1,0:T(8,128)}), f32[8,54,200]{2,1,0:T(8,128)}, u32[]{:S(2)}, u32[]{:S(2)}) async-start(f32[8,54,200]{2,1,0:T(8,128)} %broadcast_in_dim.52), calls=%async_computation.4 | async-start | bytes 917504 | tf_op jit(solution)/shard_map/all_to_all | solution.py:810
  266.8 18.5 %copy-start.7 = (f32[16,128]{1,0:T(8,128)S(1)}, f32[16,128]{1,0:T(8,128)}, u32[]{:S(2)}) copy-start(f32[16,128]{1,0:T(8,128)} %get-tuple-element.199) | copy-start | bytes 24580
  266.8 17.4 %collective-permute-start.26 = (bf16[2,104,768]{2,1,0:T(8,128)(2,1)}, bf16[2,104,768]{2,1,0:T(8,128)(2,1)}, u32[]{:S(2)}, u32[]{:S(2)}) collective-permute-start(bf16[2,104,768]{2,1,0:T(8,128)(2,1)} %add_convert_fusion.refs_4_), channel_id=1, source_target_pairs={{0,8},{4,12},{8,0},{12,4},{16,24},{20,28},{24,16},{28,20},{1,9},{5... | collective-permute-start | bytes 958472 | tf_op jit(solution)/shard_map/ppermute | solution.py:815
  269.6 19.9 %collective-permute-start.29 = (bf16[2,104,768]{2,1,0:T(8,128)(2,1)}, bf16[2,104,768]{2,1,0:T(8,128)(2,1)}, u32[]{:S(2)}, u32[]{:S(2)}) collective-permute-start(bf16[2,104,768]{2,1,0:T(8,128)(2,1)} %add_convert_fusion.refs_4_), channel_id=1, source_target_pairs={{0,4},{4,0},{8,12},{12,8},{16,20},{20,16},{24,28},{28,24},{1,5},{5... | collective-permute-start | bytes 958472 | tf_op jit(solution)/shard_map/ppermute | solution.py:815
  284.2 5.3 %collective-permute-start.27 = (bf16[200,896]{1,0:T(8,128)(2,1)}, bf16[200,896]{1,0:T(8,128)(2,1)}, u32[]{:S(2)}, u32[]{:S(2)}) collective-permute-start(bf16[200,896]{1,0:T(8,128)(2,1)} %get-tuple-element.200.refs_0_), channel_id=1, source_target_pairs={{0,4},{4,0},{8,12},{12,8},{16,20},{20,16},{24,28},{28,24},{1,5},{5... | collective-permute-start | bytes 1075208 | tf_op jit(solution)/shard_map/ppermute | solution.py:815
  284.8 4.7 %collective-permute-start.28 = (bf16[200,896]{1,0:T(8,128)(2,1)}, bf16[200,896]{1,0:T(8,128)(2,1)}, u32[]{:S(2)}, u32[]{:S(2)}) collective-permute-start(bf16[200,896]{1,0:T(8,128)(2,1)} %get-tuple-element.201.refs_2_), channel_id=1, source_target_pairs={{0,4},{4,0},{8,12},{12,8},{16,20},{20,16},{24,28},{28,24},{1,5},{5... | collective-permute-start | bytes 1075208 | tf_op jit(solution)/shard_map/ppermute | solution.py:815
  284.8 4.7 %collective-permute-start.30 = (bf16[2,104,768]{2,1,0:T(8,128)(2,1)}, bf16[2,104,768]{2,1,0:T(8,128)(2,1)}, u32[]{:S(2)}, u32[]{:S(2)}) collective-permute-start(bf16[2,104,768]{2,1,0:T(8,128)(2,1)} %collective-permute-done.26.refs_5_), channel_id=1, source_target_pairs={{0,4},{4,0},{8,12},{12,8},{16,20},{20,16},{24,28},{28,24},{1,5},{5... | collective-permute-start | bytes 958472 | tf_op jit(solution)/shard_map/ppermute | solution.py:815
  (7 other events, 21.1 us)
Sparse Core Ops, SparseCore 0:
  211.6 53.3 all-reduce.5

commit v6 on v5

--- a/solution.py
+++ b/solution.py
@@ -238,8 +238,9 @@
 
 
 def tap_grad_kernel(
-    x_ref, up_ref, dn_ref, g_ref, bg_ref, eb_ref, out_ref, field_ref, cols_ref, *, share
+    bits_ref, x_ref, up_ref, dn_ref, g_ref, bg_ref, *refs, share
 ):
+    out_ref, field_ref, cols_ref = refs[-3:]
     rows, block, width = x_ref.shape
     field_ref[0:REACH] = up_ref[...]
     field_ref[REACH : REACH + rows] = x_ref[...]
@@ -273,7 +274,11 @@
         wide = jnp.concatenate(blocks, axis=1)
         taps = jnp.concatenate([wide[GRP * i : GRP * i + KS] for i in range(KS)], axis=0)
         band = jnp.concatenate([bg_ref[0, k : k + 1, :] for k in range(wide.shape[1] // 128)], axis=1)
-        units = eb_ref[...]
+        own, peer = (jnp.concatenate([refs[q][...], refs[q + 1][...]], axis=1) for q in (0, 2))
+        core = bits_ref[bits_ref.shape[0] - 2]
+        units = jnp.concatenate(
+            [jnp.where(core == 0, own, peer), jnp.where(core == 0, peer, own)], axis=1
+        )
         ratio = out_ref.shape[1] - TAPS - 1
         for f in range(out_ref.shape[0]):
             out_ref[f, 0:TAPS, :] = taps[:, f * share : (f + 1) * share]
@@ -283,21 +288,22 @@
                 out_ref[f, TAPS + 1 + q : TAPS + 2 + q, :] = units[:, at : at + share]
 
 
-def tap_gradient(x, up, dn, grad, bg_sum, eb_sum, block, share):
+def tap_gradient(bits, x, up, dn, grad, bg_sum, eb_sums, units, block, share):
     rows, channels, width = x.shape
     padded = pl.cdiv(channels, 128) * 128
-    height = TAPS + 1 + eb_sum.shape[1] // channels
+    height = TAPS + 1 + units // channels
     return pl.pallas_call(
         functools.partial(tap_grad_kernel, share=share),
         grid=(channels // block,),
         in_specs=[
+            pl.BlockSpec(memory_space=pltpu.SMEM),
             pl.BlockSpec((rows, block, width), lambda g: (0, g, 0)),
             pl.BlockSpec((REACH, block, width), lambda g: (0, g, 0)),
             pl.BlockSpec((REACH, block, width), lambda g: (0, g, 0)),
             pl.BlockSpec((rows, block, width), lambda g: (0, g, 0)),
             whole(bg_sum.shape),
-            whole(eb_sum.shape),
-        ],
+        ]
+        + [whole(v.shape) for v in eb_sums],
         out_specs=pl.BlockSpec((channels // share, height, share), lambda g: (0, 0, 0)),
         out_shape=jax.ShapeDtypeStruct((channels // share, height, share), F32),
         scratch_shapes=[
@@ -307,7 +313,7 @@
         compiler_params=params(),
         cost_estimate=cost(15),
         name="tap_gradient",
-    )(x, up, dn, grad, bg_sum, eb_sum)
+    )(bits, x, up, dn, grad, bg_sum, *eb_sums)
 
 
 def mask_grad_kernel(og_ref, m_ref, out_ref, sum_ref, cols_ref):
@@ -397,7 +403,7 @@
     return jnp.concatenate(keep, axis=0), jnp.concatenate(send, axis=0)
 
 
-def hidden_kernel(bits_ref, bg_ref, we_ref, wp_ref, eb_ref, *refs, step, pieces, leads):
+def hidden_kernel(bits_ref, bg_ref, we_ref, wp_ref, eb_ref, *refs, step, pieces, slots, leads):
     if leads:
         conv_ref, all_ref, par_ref, h_ref, g_ref, dwp_ref, dwe_ref, ebg_ref, act_ref, stat_ref = refs
 
@@ -431,15 +437,15 @@
         dwp_ref[...] = dwp.astype(BF16)
         dwe_ref[...] = dwe.astype(BF16)
     else:
-        keep, send = halves(dwp + other_p[...].astype(F32), bits_ref[0], pieces[0])
+        keep, send = halves(dwp + other_p[...].astype(F32), bits_ref[slots[0]], pieces[0])
         keep_p[...] = keep
         send_p[...] = send.astype(BF16)
-        keep, send = halves(dwe + other_e[...].astype(F32), bits_ref[1], pieces[1])
+        keep, send = halves(dwe + other_e[...].astype(F32), bits_ref[slots[1]], pieces[1])
         keep_e[...] = keep
         send_e[...] = send.astype(BF16)
 
 
-def hidden_layer(act, bg, we, wp, eb, first, units, bits, others=None, pieces=None, front=None):
+def hidden_layer(act, bg, we, wp, eb, first, units, bits, others=None, pieces=None, slots=None, front=None):
     channels, pixels = bg.shape
     off = first // TILE
     column = lambda rows: pl.BlockSpec((rows, TILE), lambda g: (0, g))
@@ -466,7 +472,7 @@
         out_specs += [pl.BlockSpec((channels, pixels), lambda g: (0, 0)), pl.BlockSpec((32, 128), lambda g: (0, 0))]
         out_shape += [jax.ShapeDtypeStruct((channels, pixels), BF16), jax.ShapeDtypeStruct((32, 128), F32)]
     return pl.pallas_call(
-        functools.partial(hidden_kernel, step=128, pieces=pieces, leads=front is not None),
+        functools.partial(hidden_kernel, step=128, pieces=pieces, slots=slots, leads=front is not None),
         grid=(pl.cdiv(units, TILE),),
         in_specs=in_specs,
         out_specs=out_specs,
@@ -477,21 +483,21 @@
     )(*operands)
 
 
-def split_kernel(bits_ref, *refs, pieces):
+def split_kernel(bits_ref, *refs, pieces, slots):
     n = len(pieces)
-    for k, piece in enumerate(pieces):
+    for k, (piece, slot) in enumerate(zip(pieces, slots, strict=True)):
         total = refs[2 * k][...] + refs[2 * k + 1][...].astype(F32)
-        keep, send = halves(total, bits_ref[k], piece)
+        keep, send = halves(total, bits_ref[slot], piece)
         refs[2 * n + 2 * k][...] = keep
         refs[2 * n + 2 * k + 1][...] = send.astype(BF16)
 
 
-def split_sums(bits, pairs, pieces):
+def split_sums(bits, pairs, pieces, slots):
     rows, cols = pairs[0][0].shape
     shape = lambda dtype: jax.ShapeDtypeStruct((rows // 2, cols), dtype)
     spec = lambda height: pl.BlockSpec((height, cols), lambda: (0, 0))
     out = pl.pallas_call(
-        functools.partial(split_kernel, pieces=pieces),
+        functools.partial(split_kernel, pieces=pieces, slots=slots),
         in_specs=[pl.BlockSpec(memory_space=pltpu.SMEM)] + [spec(rows)] * (2 * len(pairs)),
         out_specs=[spec(rows // 2)] * (2 * len(pairs)),
         out_shape=[shape(F32), shape(BF16)] * len(pairs),
@@ -502,17 +508,18 @@
     return [(out[2 * k], out[2 * k + 1]) for k in range(len(pairs))]
 
 
-def band_split_kernel(bit_ref, *refs):
+def band_split_kernel(bits_ref, *refs):
     keep_ref, send_ref = refs[-2:]
     rows = keep_ref.shape[1]
+    band = bits_ref[bits_ref.shape[0] - 1]
     for k in range(keep_ref.shape[0]):
         total = refs[2 * k][...] + refs[2 * k + 1][...].astype(F32)
         low, high = total[:rows], total[total.shape[0] - rows :]
-        keep_ref[k] = jnp.where(bit_ref[0] == 0, low, high)
-        send_ref[k] = jnp.where(bit_ref[0] == 0, high, low).astype(BF16)
-
-
-def band_split(bit, pairs):
+        keep_ref[k] = jnp.where(band == 0, low, high)
+        send_ref[k] = jnp.where(band == 0, high, low).astype(BF16)
+
+
+def band_split(bits, pairs):
     share, cols = pairs[0][0].shape
     rows = pl.cdiv(pl.cdiv(share, 2), 8) * 8
     spec = pl.BlockSpec((share, cols), lambda: (0, 0))
@@ -526,17 +533,19 @@
         compiler_params=params(),
         cost_estimate=cost(3),
         name="band_split",
-    )(bit[None], *[v for pair in pairs for v in pair])
+    )(bits, *[v for pair in pairs for v in pair])
 
 
 def round_kernel(*refs):
     n = len(refs) // 3
     for k in range(n):
-        refs[2 * n + k][...] = (refs[2 * k][...] + refs[2 * k + 1][...].astype(F32)).astype(BF16)
+        total = refs[2 * k][...].astype(F32) + refs[2 * k + 1][...].astype(F32)
+        refs[2 * n + k][...] = total.astype(BF16)
 
 
 def round_sums(pairs):
-    spec = pl.BlockSpec(pairs[0][0].shape, lambda: (0, 0))
+    shape = pairs[0][0].shape
+    spec = pl.BlockSpec(shape, lambda: (0,) * len(shape))
     return pl.pallas_call(
         round_kernel,
         in_specs=[spec] * (2 * len(pairs)),
@@ -753,7 +762,7 @@
 
 def place_kernel(flags_ref, *refs, starts):
     outs = refs[-2:]
-    core, band = flags_ref[0], flags_ref[1]
+    core, band = flags_ref[flags_ref.shape[0] - 2], flags_ref[flags_ref.shape[0] - 1]
     (low, high), (low_half, high_half) = starts
 
     def put(out_ref, rows, at, v):
@@ -892,14 +901,13 @@
 
     copies = n_fs * n_dp
     orders = (bits[::-1], bits)
-    flags = jnp.stack([bit_of("fsdp", bit) for bit in bits]).astype(jnp.int32)
-    lead = jnp.stack([flags[o[0]] for o in orders])
+    flags = jnp.stack([bit_of("fsdp", bit) for bit in bits] + [core, bit_of("dp", 1)]).astype(jnp.int32)
     bg, bg_sum = mask_gradient(og, after(m16, we_pieces[0], wp_pieces[0]))
     early = [p[1 << b] for p, b in ((we_pieces, bits[0]), (wp_pieces, bits[-1]))]
     we_pieces = gather_others(we_pieces, bits, bg)
     wp_pieces = gather_others(wp_pieces, bits[::-1], bg)
-    ready, eb_own, eb_peer, lead, *_ = lax.optimization_barrier(
-        (m16, eb_own, eb_peer, lead, bg, *early)
+    ready, eb_own, eb_peer, flags, *_ = lax.optimization_barrier(
+        (m16, eb_own, eb_peer, flags, bg, *early)
     )
     conv, stats, par = conv_forward(x, x_up, x_dn, every, ready, copies, block)
     stats = lax.all_to_all(stats, devices, 0, 0)
@@ -927,8 +935,8 @@
         return [(keep, v) for (keep, _), v in zip(pairs, came)]
 
     def split(pairs, n):
-        taken = [flags[order[n]] for order in orders]
-        return split_sums(jnp.stack(taken), pairs, tuple(piece(order, n) for order in orders))
+        slots = tuple(order[n] for order in orders)
+        return split_sums(flags, pairs, tuple(piece(order, n) for order in orders), slots)
 
     def sends(pairs):
         return [send for _, send in pairs]
@@ -937,27 +945,24 @@
         return [lax.psum(v, "dp", axis_index_groups=groups) for v in sums]
 
     pieces = tuple(piece(o, 0) for o in orders)
+    leads = tuple(o[0] for o in orders)
     front = (conv, after(stats, we_peer, wp_peer), par)
-    *q1, act, stat = hidden_layer(None, bg, we_peer, wp_peer, eb_peer, 0, first, lead, front=front)
+    *q1, act, stat = hidden_layer(None, bg, we_peer, wp_peer, eb_peer, 0, first, flags, front=front)
     we_own = flip_bit(after(we_peer, act), "dp", 0)
     wp_own = flip_bit(after(wp_peer, act), "dp", 0)
     c1 = other_core(q1[2:4])
-    q2 = hidden_layer(act, bg, we_peer, wp_peer, after(eb_peer, q1[0]), first, second, lead)
+    q2 = hidden_layer(act, bg, we_peer, wp_peer, after(eb_peer, q1[0]), first, second, flags)
     c2 = other_core(q2[2:4])
-    o1 = hidden_layer(act, bg, we_own, wp_own, after(eb_own, q2[0]), 0, first, lead, c1, pieces)
+    o1 = hidden_layer(act, bg, we_own, wp_own, after(eb_own, q2[0]), 0, first, flags, c1, pieces, leads)
     s1 = exchanged([(o1[2], o1[3]), (o1[4], o1[5])], 0)
-    o2 = hidden_layer(act, bg, we_own, wp_own, after(eb_own, o1[0]), first, second, lead, c2, pieces)
+    o2 = hidden_layer(act, bg, we_own, wp_own, after(eb_own, o1[0]), first, second, flags, c2, pieces, leads)
     for n in range(1, len(bits)):
         s1 = split(arrived(s1, o2[0]), n)
         last = sends(s1)
         s1 = exchanged(s1, n)
 
     s2 = exchanged([(o2[2], after(o2[3], *last)), (o2[4], after(o2[5], *last))], 0)
-    eb_o = jnp.concatenate([o1[-1], o2[-1]], axis=1)
-    eb_q = jnp.concatenate([q1[-1], q2[-1]], axis=1)
-    eb_sum = jnp.concatenate(
-        [jnp.where(core == 0, eb_o, eb_q), jnp.where(core == 0, eb_q, eb_o)], axis=1
-    )[:, :units]
+    eb_sums = (o1[-1], o2[-1], q1[-1], q2[-1])
     cuts = ((1, 0, first), (0, 0, first), (1, first, second), (0, first, second))
     parts = (q1, o1, q2, o2)
     hidden = [p[0] for p in parts]
@@ -965,8 +970,7 @@
         (we_own, we_peer), [p[1] for p in parts], cuts, conv, after(stat, *last), copies
     )
     sums = lax.all_to_all(sums, devices, 0, 0)
-    band = bit_of("dp", 1)
-    z_keep, z_send = band_split(band, arrived(s1, da))
+    z_keep, z_send = band_split(flags, arrived(s1, da))
     z_came = flip_bit(z_send, "dp", 1)
     for n in range(1, len(bits)):
         s2 = split(arrived(s2, da, z_send), n)
@@ -978,9 +982,9 @@
     z_came, *came = lax.optimization_barrier((z_came, *[v for _, v in s2], conv_grad))
     s2 = round_sums([(keep, v) for (keep, _), v in zip(s2, came)])
     b2 = over_bands(s2, groups)
-    half_sum = (z_keep + z_came.astype(F32)).astype(BF16)
+    half_sum = round_sums([(z_keep, z_came)])[0]
     ready = after(conv_grad, half_sum, *s2)
-    tap_local = tap_gradient(x, x_up, x_dn, ready, bg_sum, eb_sum, block, share)
+    tap_local = tap_gradient(flags, x, x_up, x_dn, ready, bg_sum, eb_sums, units, block, share)
     g_up, g_dn, half_sum, _ = lax.optimization_barrier((g_up, g_dn, half_sum, tap_local))
     half_came = flip_bit(half_sum, "dp", 2)
     bands = n_dp.bit_length() - 1
@@ -988,7 +992,7 @@
     local = lax.all_to_all(tap_local, "fsdp", 0, 0)
     input_grad = input_gradient(conv_grad, g_up, g_dn, after(par, tap_local), og, m16, block)
     half_came, _ = lax.optimization_barrier((half_came, input_grad))
-    half_sum = (half_sum.astype(F32) + half_came.astype(F32)).astype(BF16)
+    half_sum = round_sums([(half_sum, half_came)])[0]
     for bit in range(3, bands):
         half_sum = (half_sum.astype(F32) + flip_bit(half_sum, "dp", bit).astype(F32)).astype(BF16)
     half_far = flip_bit(half_sum, "dp", 1)
@@ -1000,8 +1004,7 @@
     whole_parts = [(v, flip_bit(v, "dp", 0)) for v in b2[:2]]
     half_parts = (half_sum, half_far, flip_bit(half_sum, "dp", 0), flip_bit(half_far, "dp", 0))
     starts = ((first, half + first), (0, half))
-    places = jnp.stack([core, band])
-    project_grad, expand_grad = place_columns(places, whole_parts, half_parts, starts, share, units)
+    project_grad, expand_grad = place_columns(flags, whole_parts, half_parts, starts, share, units)
 
     start = lax.axis_index("fsdp") * share
     totals = totals.reshape(2, -1)

time: 302 us -> 299 us (0.990)
  other arithmetic: 10.4 us -> 4.74 us
  Pallas kernels: 189 us -> 193 us
  starting transfers between devices: 57.6 us -> 53.8 us
    ppermute x27, starting transfers between devices: 26.4 us -> 22.6 us  [flip_bit(): return lax.ppermute(values, axis, [(i, i ^ 1 << bit) for i in range(size)])]
    pallas_call x1 -> x3, Pallas kernels: 2.47 us -> 6.31 us  [round_sums(): pl.pallas_call(round_kernel, in_specs=[spec] * (2 * len(pairs)), out_spec...]
    convert_element_type x2 -> x0, other arithmetic: 3.73 us -> none  [the longest x1 1.94 us: per_device(): half_sum = (z_keep + z_came.astype(F32)).astype(BF16)]
  transfers between devices with their start and end apart: 37 -> 37, of which waited for: 5 -> 7; matrix products, arithmetic and copies ran while one was open for 6% -> 4% of each run, Pallas kernels for 55% -> 57%
where the time goes in v6:
time: 299 us; the launch traced here: 297 us
  Pallas kernels  193 us (65%)
  starting transfers between devices  53.8 us (18%)
  waiting for transfers between devices  20.1 us (7%)
  between operations  15 us (5%)
  local copies, waits for them, and re-layouts  10.7 us (4%)
  other arithmetic  4.74 us (2%)
    pallas_call x4, Pallas kernels, hidden_layer(): pl.pallas_call(functools.partial(hidden_kernel, step=128, pieces=pieces,...  65.4 us
    ppermute x27, starting transfers between devices, flip_bit(): return lax.ppermute(values, axis, [(i, i ^ 1 << bit) for i in range(size)])  22.6 us
    pallas_call x1, Pallas kernels, conv_forward(): pl.pallas_call(functools.partial(conv_kernel, share=share), grid=(channel...  20.9 us
    pallas_call x1, Pallas kernels, tap_gradient(): pl.pallas_call(functools.partial(tap_grad_kernel, share=share), grid=(cha...  18.2 us
    pallas_call x1, Pallas kernels, input_gradient(): pl.pallas_call(input_grad_kernel, grid=(channels // block,), in_specs=[pl...  16.3 us
    pallas_call x1, Pallas kernels, activation_gradient(): pl.pallas_call(functools.partial(act_grad_kernel, cuts=cuts), grid=(rows,...  16.1 us
    pallas_call x1, Pallas kernels, block_output(): pl.pallas_call(functools.partial(block_out_kernel, cuts=cuts), grid=(rows...  14.6 us
    ppermute x27, waiting for transfers between devices, flip_bit(): return lax.ppermute(values, axis, [(i, i ^ 1 << bit) for i in range(size)])  13.7 us
  transfers between devices with their start and end apart: 37, of which 7 were waited for; matrix products, arithmetic and copies ran while one was open for 4% of the time, Pallas kernels for 57%

profile of v6, /device:TPU:0, one launch (start us, length us, event | category | flops | bytes accessed | tf_op | source)
XLA Modules:
  0.0 297.1 jit_solution(1111359736261254352)
XLA Ops:
  7.2 3.3 %fusion = (bf16[3,800,256]{2,1,0:T(8,128)(2,1)}, bf16[3,800,256]{2,1,0:T(8,128)(2,1)}) fusion(bf16[6,800,256]{2,1,0:T(8,128)(2,1)} %bitcast.35), kind=kLoop, calls=%fused_computation.11 | loop fusion | bytes 4915200 | tf_op jit(solution)/shard_map/slice | solution.py:870
  11.4 5.2 %all-to-all-start = ((f32[4,56,200]{2,1,0:T(8,128)}), f32[4,56,200]{2,1,0:T(8,128)S(1)}, u32[]{:S(2)}, u32[]{:S(2)}) async-start(f32[4,56,200]{2,1,0:T(8,128)} %broadcast_in_dim.43), calls=%async_computation | async-start | bytes 458752 | tf_op jit(solution)/shard_map/all_to_all | solution.py:819
  16.6 2.5 collective-permute-start.4
  19.0 1.3 collective-permute-start.5
  20.3 1.5 all-to-all-done.small_ref
  21.9 1.0 slice_select_fusion.refs_4_
  22.9 1.2 collective-permute-start.2
  24.1 1.0 slice_select_fusion.1.refs_0_
  27.7 1.3 collective-permute-start.7
  29.8 5.6 %mask_gradient.1 = (bf16[800,1536]{1,0:T(8,128)(2,1)}, f32[1,16,128]{2,1,0:T(8,128)}) custom-call(bf16[6,800,256]{2,1,0:T(8,128)(2,1)} %bitcast.39, f32[6,16,256]{2,1,0:T(8,128)} %broadcast_in_dim.44.m_ref.refs_7_), custom_call_target="tpu_custom_call" | custom-call | flops 115000000 | bytes 100000 | tf_op jit(solution)/shard_map/mask_gradient/pallas_call | solution.py:344
  35.4 5.3 %collective-permute-done.2.refs_6_ = bf16[200,1664]{1,0:T(8,128)(2,1)} collective-permute-done((bf16[200,1664]{1,0:T(8,128)(2,1)}, bf16[200,1664]{1,0:T(8,128)(2,1)}, u32[]{:S(2)}, u32[]{:S(2)}) %collective-permute-start.2) | collective-permute-done | bytes 665632 | tf_op jit(solution)/shard_map/ppermute | solution.py:824
  40.7 1.4 collective-permute-start.6
  42.1 1.2 collective-permute-done.refs_1_
  43.4 1.6 collective-permute-start.1
  45.6 20.9 %conv_forward.1 = (f32[6,800,256]{2,1,0:T(8,128)}, f32[32,16,128]{2,1,0:T(8,128)}, f32[800,128]{1,0:T(8,128)}) custom-call(bf16[6,800,256]{2,1,0:T(8,128)(2,1)} %bitcast.36, bf16[3,800,256]{2,1,0:T(8,128)(2,1)} %collective-permute-done.4.up_ref, bf16[3,800,256]{2,1,0:T(8,128)(2,1)} %collective-permute-done.5.dn_ref, f32[4,56,200]{2,1,0:T(8,128)} %copy-done.2, ...), custom_call_target="tpu_custom_call" | custom-call | flops 460000000 | bytes 100000 | tf_op jit(solution)/shard_map/conv_forward/pallas_call | solution.py:158
  66.5 6.7 %all-to-all-start.1 = ((f32[32,16,128]{2,1,0:T(8,128)}), f32[32,16,128]{2,1,0:T(8,128)}, u32[]{:S(2)}, u32[]{:S(2)}) async-start(f32[32,16,128]{2,1,0:T(8,128)} %get-tuple-element.124), calls=%async_computation.1 | async-start | bytes 524288 | tf_op jit(solution)/shard_map/all_to_all | solution.py:913
  73.3 5.8 %join_pieces.1 = (bf16[800,1664]{1,0:T(8,128)(2,1)}, bf16[800,1664]{1,0:T(8,128)(2,1)}) custom-call(s32[1]{0:T(128)} %bitcast.14.index_ref, bf16[200,1664]{1,0:T(8,128)(2,1)} %slice_select_fusion.1.refs_0_, bf16[200,1664]{1,0:T(8,128)(2,1)} %collective-permute-done.refs_1_, bf16[200,1664]{1,0:T(8,128)(2,1)} %collective-permute-done.6.refs_2_, ...), custom_call_target="tpu_custom_call" | custom-call | flops 115000000 | bytes 100000 | tf_op jit(solution)/shard_map/join_pieces/pallas_call | solution.py:751
  79.1 4.9 %all-to-all-done.1.refs_1_ = f32[32,16,128]{2,1,0:T(8,128)} async-done(((f32[32,16,128]{2,1,0:T(8,128)}), f32[32,16,128]{2,1,0:T(8,128)}, u32[]{:S(2)}, u32[]{:S(2)}) %all-to-all-start.1) | async-done | bytes 262176 | tf_op jit(solution)/shard_map/all_to_all | solution.py:913
  84.0 15.9 %hidden_layer.4 = (bf16[1536,768]{1,0:T(8,128)(2,1)}, bf16[1536,768]{1,0:T(8,128)(2,1)}, bf16[800,768]{1,0:T(8,128)(2,1)}, bf16[800,768]{1,0:T(8,128)(2,1)}, f32...) custom-call(s32[4]{0:T(128)} %pad_add_fusion.bits_ref.flags_ref, ...), custom_call_target="tpu_custom_call" | custom-call | flops 345000000 | bytes 100000 | tf_op jit(solution)/shard_map/hidden_layer/pallas_call | solution.py:474
  101.0 17.0 %hidden_layer.5 = (bf16[1536,896]{1,0:T(8,128)(2,1)}, bf16[1536,896]{1,0:T(8,128)(2,1)}, bf16[800,896]{1,0:T(8,128)(2,1)}, bf16[800,896]{1,0:T(8,128)(2,1)}, f32[1,896]{1,0:T(1,128)}) custom-call(s32[4]{0:T(128)} %pad_add_fusion.bits_ref.flags_ref, bf16[800,1536]{1,0:T(8,128)(2,1)} %get-tuple-element.112.bg_ref, ...), custom_call_target="tpu_custom_call" | custom-call | flops 345000000 | bytes 100000 | tf_op jit(solution)/shard_map/hidden_layer/pallas_call | solution.py:474
  118.5 14.5 %hidden_layer.6 = (bf16[1536,768]{1,0:T(8,128)(2,1)}, bf16[1536,768]{1,0:T(8,128)(2,1)}, f32[400,768]{1,0:T(8,128)}, bf16[400,768]{1,0:T(8,128)(2,1)}, f32[400,7...) custom-call(s32[4]{0:T(128)} %pad_add_fusion.bits_ref.flags_ref, ...), custom_call_target="tpu_custom_call" | custom-call | flops 345000000 | bytes 100000 | tf_op jit(solution)/shard_map/hidden_layer/pallas_call | solution.py:474
  133.2 1.3 collective-permute-start.15
  134.5 18.0 %hidden_layer.7 = (bf16[1536,896]{1,0:T(8,128)(2,1)}, bf16[1536,896]{1,0:T(8,128)(2,1)}, f32[400,896]{1,0:T(8,128)}, bf16[400,896]{1,0:T(8,128)(2,1)}, f32[400,8...) custom-call(s32[4]{0:T(128)} %pad_add_fusion.bits_ref.flags_ref, ...), custom_call_target="tpu_custom_call" | custom-call | flops 345000000 | bytes 100000 | tf_op jit(solution)/shard_map/hidden_layer/pallas_call | solution.py:474
  152.5 3.4 %split_sums.2 = (f32[200,768]{1,0:T(8,128)}, bf16[200,768]{1,0:T(8,128)(2,1)}, f32[200,768]{1,0:T(8,128)}, bf16[200,768]{1,0:T(8,128)(2,1)}) custom-call(s32[4]{0:T(128)} %pad_add_fusion.bits_ref.flags_ref, f32[400,768]{1,0:T(8,128)} %get-tuple-element.147.refs_0_, bf16[400,768]{1,0:T(8,128)(2,1)} %collective-permute-done.14.refs_1_, ...), custom_call_target="tpu_custom_call" | custom-call | flops 3449999872 | bytes 100000 | tf_op jit(solution)/shard_map/split_sums/pallas_call | solution.py:499
  156.6 1.9 collective-permute-start.16
  158.5 1.4 collective-permute-start.19
  159.9 16.1 %activation_gradient.1 = (f32[6,800,256]{2,1,0:T(8,128)}, f32[32,16,128]{2,1,0:T(8,128)}) custom-call(bf16[800,1664]{1,0:T(8,128)(2,1)} %collective-permute-done.9.we_ref.refs_0_, bf16[800,1664]{1,0:T(8,128)(2,1)} %get-tuple-element.130.we_ref.refs_1_, bf16[1536,768]{1,0:T(8,128)(2,1)} %get-tuple-element.142.refs_2_, ...), custom_call_target="tpu_custom_call" | custom-call | flops 345000000 | bytes 100000 | tf_op jit(solution)/shard_map/activation_gradient/pallas_call | solution.py:605
  176.0 3.5 %all-to-all-start.2 = ((f32[32,16,128]{2,1,0:T(8,128)}), f32[32,16,128]{2,1,0:T(8,128)}, u32[]{:S(2)}, u32[]{:S(2)}) async-start(f32[32,16,128]{2,1,0:T(8,128)} %get-tuple-element.157), calls=%async_computation.2 | async-start | bytes 524288 | tf_op jit(solution)/shard_map/all_to_all | solution.py:972
  181.1 2.5 band_split.1
  183.6 3.7 %split_sums.3 = (f32[200,896]{1,0:T(8,128)}, bf16[200,896]{1,0:T(8,128)(2,1)}, f32[200,896]{1,0:T(8,128)}, bf16[200,896]{1,0:T(8,128)(2,1)}) custom-call(s32[4]{0:T(128)} %pad_add_fusion.bits_ref.flags_ref, f32[400,896]{1,0:T(8,128)} %get-tuple-element.158.refs_0_, bf16[400,896]{1,0:T(8,128)(2,1)} %collective-permute-done.16.refs_1_, ...), custom_call_target="tpu_custom_call" | custom-call | flops 3449999872 | bytes 100000 | tf_op jit(solution)/shard_map/split_sums/pallas_call | solution.py:499
  188.2 0.9 collective-permute-start.24
  189.1 1.3 collective-permute-start.22
  191.0 9.8 %conv_gradient.1 = (bf16[6,800,256]{2,1,0:T(8,128)(2,1)}, bf16[3,800,256]{2,1,0:T(8,128)(2,1)}, bf16[3,800,256]{2,1,0:T(8,128)(2,1)}, f32[16,128]{1,0:T(8,128)}) custom-call(f32[6,800,256]{2,1,0:T(8,128)} %get-tuple-element.156.da_ref, f32[6,800,256]{2,1,0:T(8,128)} %get-tuple-element.116.refs_0_.refs_6_.conv_ref, ...), custom_call_target="tpu_custom_call" | custom-call | flops 230000000 | bytes 100000 | tf_op jit(solution)/shard_map/conv_gradient/pallas_call | solution.py:694
  200.8 2.3 collective-permute-start.20
  203.2 1.3 collective-permute-start.21
  204.5 1.9 round_sums.3.refs_0_
  206.4 2.5 round_sums.4
  208.9 18.2 %tap_gradient.1 = f32[4,54,200]{2,1,0:T(8,128)} custom-call(s32[4]{0:T(128)} %pad_add_fusion.bits_ref.flags_ref, bf16[6,800,256]{2,1,0:T(8,128)(2,1)} %bitcast.37, bf16[3,800,256]{2,1,0:T(8,128)(2,1)} %collective-permute-done.4.up_ref, bf16[3,800,256]{2,1,0:T(8,128)(2,1)} %collective-permute-done.5.dn_ref, bf16[6,800,256]{2,1,0:T(8,128)(2,1)} %get-tuple-element.185.g_ref, ...), custom_call_target="tpu_custom_call" | custom-call | flops 17250000896 | bytes 100000 | tf_op jit(solution)/shard_map/tap_gradient/pallas_call | solution.py:295
  227.1 4.0 %all-to-all-start.3 = ((f32[4,54,200]{2,1,0:T(8,128)}), f32[4,54,200]{2,1,0:T(8,128)}, u32[]{:S(2)}, u32[]{:S(2)}) async-start(f32[4,54,200]{2,1,0:T(8,128)} %tap_gradient.1), calls=%async_computation.3 | async-start | bytes 458752 | tf_op jit(solution)/shard_map/all_to_all | solution.py:992
  231.2 4.4 %collective-permute-start.25 = (bf16[2,104,768]{2,1,0:T(8,128)(2,1)}, bf16[2,104,768]{2,1,0:T(8,128)(2,1)}, u32[]{:S(2)}, u32[]{:S(2)}) collective-permute-start(bf16[2,104,768]{2,1,0:T(8,128)(2,1)} %round_sums.3.refs_0_), channel_id=1, source_target_pairs={{0,16},{4,20},{8,24},{12,28},{16,0},{20,4},{24,8},{28,12},{1,17},{... | collective-permute-start | bytes 958472 | tf_op jit(solution)/shard_map/ppermute | solution.py:824
  235.6 16.3 %input_gradient.1 = f32[6,800,256]{2,1,0:T(8,128)} custom-call(bf16[6,800,256]{2,1,0:T(8,128)(2,1)} %get-tuple-element.185.g_ref, bf16[3,800,256]{2,1,0:T(8,128)(2,1)} %collective-permute-done.20.up_ref, bf16[3,800,256]{2,1,0:T(8,128)(2,1)} %collective-permute-done.21.dn_ref, f32[800,128]{1,0:T(8,128)} %get-tuple-element.197.refs_2_.par_ref.refs_8_, ...), custom_call_target="tpu_custom_call" | custom-call | flops 5750000128 | bytes 100000 | tf_op jit(solution)/shard_map/input_gradient/pallas_call | solution.py:216
  251.8 1.0 reduce_sum.18
  253.6 4.4 %all-to-all-start.4 = ((f32[8,54,200]{2,1,0:T(8,128)}), f32[8,54,200]{2,1,0:T(8,128)}, u32[]{:S(2)}, u32[]{:S(2)}) async-start(f32[8,54,200]{2,1,0:T(8,128)} %broadcast_in_dim.48), calls=%async_computation.4 | async-start | bytes 917504 | tf_op jit(solution)/shard_map/all_to_all | solution.py:819
  258.0 5.6 %collective-permute-done.25.refs_1_ = bf16[2,104,768]{2,1,0:T(8,128)(2,1)} collective-permute-done((bf16[2,104,768]{2,1,0:T(8,128)(2,1)}, bf16[2,104,768]{2,1,0:T(8,128)(2,1)}, u32[]{:S(2)}, u32[]{:S(2)}) %collective-permute-start.25) | collective-permute-done | bytes 319520 | tf_op jit(solution)/shard_map/ppermute | solution.py:824
  263.6 1.9 round_sums.5.refs_4_
  266.0 14.6 %block_output.1 = bf16[6,800,256]{2,1,0:T(8,128)(2,1)} custom-call(bf16[800,1664]{1,0:T(8,128)(2,1)} %collective-permute-done.8.wp_ref.refs_0_, bf16[800,1664]{1,0:T(8,128)(2,1)} %get-tuple-element.128.wp_ref.refs_1_, bf16[1536,768]{1,0:T(8,128)(2,1)} %get-tuple-element.129.refs_2_, bf16[1536,768]{1,0:T(8,128)(2,1)} %get-tuple-element.137.refs_3_, ...), custom_call_target="tpu_custom_call" | custom-call | flops 5750000128 | bytes 100000 | tf_op jit(solution)/shard_map/block_output/pallas_call | solution.py:638
  282.9 1.1 reduce_sum.19
  285.9 4.4 %place_columns.1 = (f32[200,3200]{1,0:T(8,128)}, f32[200,3200]{1,0:T(8,128)}) custom-call(s32[4]{0:T(128)} %pad_add_fusion.bits_ref.flags_ref, bf16[200,896]{1,0:T(8,128)(2,1)} %get-tuple-element.200.refs_0_, bf16[200,896]{1,0:T(8,128)(2,1)} %collective-permute-done.27.refs_1_, bf16[200,896]{1,0:T(8,128)(2,1)} %get-tuple-element.201.refs_2_, ...), custom_call_target="tpu_custom_call" | custom-call | flops 115000000 | bytes 100000 | tf_op jit(solution)/shard_map/place_columns/pallas_call | solution.py:791
  (99 shorter events, 15.5 us)
Async XLA Ops:
  7.2 3.3 %copy-start.7 = (bf16[800]{0:T(1024)(128)(2,1)S(1)}, bf16[800]{0:T(1024)(128)(2,1)}, u32[]{:S(2)}) copy-start(bf16[800]{0:T(1024)(128)(2,1)} %param.19) | copy-start | bytes 4804
  7.2 3.4 %copy-start.10 = (bf16[200]{0:T(256)(128)(2,1)S(1)}, bf16[200]{0:T(256)(128)(2,1)}, u32[]{:S(2)}) copy-start(bf16[200]{0:T(256)(128)(2,1)} %param.21) | copy-start | bytes 1204
  7.2 3.4 %copy-start.4 = (f32[200,49]{0,1:T(8,128)S(1)}, f32[200,49]{0,1:T(8,128)}, u32[]{:S(2)}) copy-start(f32[200,49]{0,1:T(8,128)} %param.15) | copy-start | bytes 117604
  7.2 3.4 %copy-start.8 = (f32[200]{0:T(256)S(1)}, f32[200]{0:T(256)}, u32[]{:S(2)}) copy-start(f32[200]{0:T(256)} %param.16) | copy-start | bytes 2404
  7.2 3.4 %copy-start.9 = (f32[200]{0:T(256)S(1)}, f32[200]{0:T(256)}, u32[]{:S(2)}) copy-start(f32[200]{0:T(256)} %param.17) | copy-start | bytes 2404
  10.5 11.3 %copy-start.1 = (bf16[200,3200]{1,0:T(8,128)(2,1)S(1)}, bf16[200,3200]{1,0:T(8,128)(2,1)}, u32[]{:S(2)}) copy-start(bf16[200,3200]{1,0:T(8,128)(2,1)} %param.20) | copy-start | bytes 3840004
  10.5 11.3 %slice-start.1 = ((bf16[200,3200]{1,0:T(8,128)(2,1)}), bf16[200,1536]{1,0:T(8,128)(2,1)S(1)}, s32[]{:S(2)}) async-start(bf16[200,3200]{1,0:T(8,128)(2,1)} %param.20), calls=%async_computation.7 | async-start | bytes 1228800 | tf_op jit(solution)/shard_map/slice | solution.py:887
  11.4 10.4 %all-to-all-start = ((f32[4,56,200]{2,1,0:T(8,128)}), f32[4,56,200]{2,1,0:T(8,128)S(1)}, u32[]{:S(2)}, u32[]{:S(2)}) async-start(f32[4,56,200]{2,1,0:T(8,128)} %broadcast_in_dim.43), calls=%async_computation | async-start | bytes 458752 | tf_op jit(solution)/shard_map/all_to_all | solution.py:819
  16.6 26.8 %collective-permute-start.4 = (bf16[3,800,256]{2,1,0:T(8,128)(2,1)}, bf16[3,800,256]{2,1,0:T(8,128)(2,1)}, u32[]{:S(2)}, u32[]{:S(2)}) collective-permute-start(bf16[3,800,256]{2,1,0:T(8,128)(2,1)} %get-tuple-element.207), channel_id=1, source_target_pairs={{0,4},{4,8},{8,12},{12,16},{16,20},{20,24},{24,28},{1,5},{5,9},{9,... | collective-permute-start | bytes 3686408 | tf_op jit(solution)/shard_map/ppermute | solution.py:808
  19.0 26.6 %collective-permute-start.5 = (bf16[3,800,256]{2,1,0:T(8,128)(2,1)}, bf16[3,800,256]{2,1,0:T(8,128)(2,1)}, u32[]{:S(2)}, u32[]{:S(2)}) collective-permute-start(bf16[3,800,256]{2,1,0:T(8,128)(2,1)} %get-tuple-element.208), channel_id=1, source_target_pairs={{4,0},{8,4},{12,8},{16,12},{20,16},{24,20},{28,24},{5,1},{9,5},{13... | collective-permute-start | bytes 3686408 | tf_op jit(solution)/shard_map/ppermute | solution.py:809
  21.8 7.9 %copy-start.2 = (f32[4,56,200]{2,1,0:T(8,128)}, f32[4,56,200]{2,1,0:T(8,128)S(1)}, u32[]{:S(2)}) copy-start(f32[4,56,200]{2,1,0:T(8,128)S(1)} %all-to-all-done.small_ref) | copy-start | bytes 537604
  22.9 4.8 %copy-start.5 = (s32[6,256]{1,0:T(8,128)S(1)}, s32[6,256]{1,0:T(8,128)}, u32[]{:S(2)}) copy-start(s32[6,256]{1,0:T(8,128)} %param.13) | copy-start | bytes 18436
  22.9 17.7 %collective-permute-start.2 = (bf16[200,1664]{1,0:T(8,128)(2,1)}, bf16[200,1664]{1,0:T(8,128)(2,1)}, u32[]{:S(2)}, u32[]{:S(2)}) collective-permute-start(bf16[200,1664]{1,0:T(8,128)(2,1)} %slice_select_fusion.refs_4_), channel_id=1, source_target_pairs={{0,2},{1,3},{2,0},{3,1},{4,6},{5,7},{6,4},{7,5},{8,10},{9,11},{10,... | collective-permute-start | bytes 1996808 | tf_op jit(solution)/shard_map/ppermute | solution.py:824
  25.1 18.1 %collective-permute-start = (bf16[200,1664]{1,0:T(8,128)(2,1)}, bf16[200,1664]{1,0:T(8,128)(2,1)}, u32[]{:S(2)}, u32[]{:S(2)}) collective-permute-start(bf16[200,1664]{1,0:T(8,128)(2,1)} %slice_select_fusion.1.refs_0_), channel_id=1, source_target_pairs={{0,1},{1,0},{2,3},{3,2},{4,5},{5,4},{6,7},{7,6},{8,9},{9,8},{10,11... | collective-permute-start | bytes 1996808 | tf_op jit(solution)/shard_map/ppermute | solution.py:824
  27.7 45.5 %collective-permute-start.7 = (bf16[200,1664]{1,0:T(8,128)(2,1)}, bf16[200,1664]{1,0:T(8,128)(2,1)}, u32[]{:S(2)}, u32[]{:S(2)}) collective-permute-start(bf16[200,1664]{1,0:T(8,128)(2,1)} %slice_select_fusion.refs_4_), channel_id=1, source_target_pairs={{0,1},{1,0},{2,3},{3,2},{4,5},{5,4},{6,7},{7,6},{8,9},{9,8},{10,11... | collective-permute-start | bytes 1996808 | tf_op jit(solution)/shard_map/ppermute | solution.py:824
  40.7 32.6 %collective-permute-start.6 = (bf16[200,1664]{1,0:T(8,128)(2,1)}, bf16[200,1664]{1,0:T(8,128)(2,1)}, u32[]{:S(2)}, u32[]{:S(2)}) collective-permute-start(bf16[200,1664]{1,0:T(8,128)(2,1)} %slice_select_fusion.1.refs_0_), channel_id=1, source_target_pairs={{0,2},{1,3},{2,0},{3,1},{4,6},{5,7},{6,4},{7,5},{8,10},{9,11},{10,... | collective-permute-start | bytes 1996808 | tf_op jit(solution)/shard_map/ppermute | solution.py:824
  43.3 30.0 %collective-permute-start.3 = (bf16[200,1664]{1,0:T(8,128)(2,1)}, bf16[200,1664]{1,0:T(8,128)(2,1)}, u32[]{:S(2)}, u32[]{:S(2)}) collective-permute-start(bf16[200,1664]{1,0:T(8,128)(2,1)} %collective-permute-done.2.refs_6_), channel_id=1, source_target_pairs={{0,1},{1,0},{2,3},{3,2},{4,5},{5,4},{6,7},{7,6},{8,9},{9,8},{10,11... | collective-permute-start | bytes 1996808 | tf_op jit(solution)/shard_map/ppermute | solution.py:824
  43.4 29.8 %collective-permute-start.1 = (bf16[200,1664]{1,0:T(8,128)(2,1)}, bf16[200,1664]{1,0:T(8,128)(2,1)}, u32[]{:S(2)}, u32[]{:S(2)}) collective-permute-start(bf16[200,1664]{1,0:T(8,128)(2,1)} %collective-permute-done.refs_1_), channel_id=1, source_target_pairs={{0,2},{1,3},{2,0},{3,1},{4,6},{5,7},{6,4},{7,5},{8,10},{9,11},{10,... | collective-permute-start | bytes 1996808 | tf_op jit(solution)/shard_map/ppermute | solution.py:824
  66.5 17.5 %all-to-all-start.1 = ((f32[32,16,128]{2,1,0:T(8,128)}), f32[32,16,128]{2,1,0:T(8,128)}, u32[]{:S(2)}, u32[]{:S(2)}) async-start(f32[32,16,128]{2,1,0:T(8,128)} %get-tuple-element.124), calls=%async_computation.1 | async-start | bytes 524288 | tf_op jit(solution)/shard_map/all_to_all | solution.py:913
  99.9 18.6 %collective-permute-start.9 = (bf16[800,1664]{1,0:T(8,128)(2,1)}, bf16[800,1664]{1,0:T(8,128)(2,1)}, u32[]{:S(2)}, u32[]{:S(2)}) collective-permute-start(bf16[800,1664]{1,0:T(8,128)(2,1)} %get-tuple-element.130.we_ref.refs_1_), channel_id=1, source_target_pairs={{0,4},{4,0},{8,12},{12,8},{16,20},{20,16},{24,28},{28,24},{1,5},{5... | collective-permute-start | bytes 7987208 | tf_op jit(solution)/shard_map/ppermute | solution.py:824
  100.0 18.5 %collective-permute-start.8 = (bf16[800,1664]{1,0:T(8,128)(2,1)}, bf16[800,1664]{1,0:T(8,128)(2,1)}, u32[]{:S(2)}, u32[]{:S(2)}) collective-permute-start(bf16[800,1664]{1,0:T(8,128)(2,1)} %get-tuple-element.128.wp_ref.refs_1_), channel_id=1, source_target_pairs={{0,4},{4,0},{8,12},{12,8},{16,20},{20,16},{24,28},{28,24},{1,5},{5... | collective-permute-start | bytes 7987208 | tf_op jit(solution)/shard_map/ppermute | solution.py:824
  100.5 17.6 %collective-permute-start.10 = (bf16[800,768]{1,0:T(8,128)(2,1)}, bf16[800,768]{1,0:T(8,128)(2,1)}, u32[]{:S(2)}, u32[]{:S(2)}) collective-permute-start(bf16[800,768]{1,0:T(8,128)(2,1)} %get-tuple-element.135), channel_id=1, source_target_pairs={{0,4},{4,0},{8,12},{12,8},{16,20},{20,16},{24,28},{28,24},{1,5},{5... | collective-permute-start | bytes 3686408 | tf_op jit(solution)/shard_map/ppermute | solution.py:824
  100.6 18.0 %collective-permute-start.11 = (bf16[800,768]{1,0:T(8,128)(2,1)}, bf16[800,768]{1,0:T(8,128)(2,1)}, u32[]{:S(2)}, u32[]{:S(2)}) collective-permute-start(bf16[800,768]{1,0:T(8,128)(2,1)} %get-tuple-element.136), channel_id=1, source_target_pairs={{0,4},{4,0},{8,12},{12,8},{16,20},{20,16},{24,28},{28,24},{1,5},{5... | collective-permute-start | bytes 3686408 | tf_op jit(solution)/shard_map/ppermute | solution.py:824
  118.0 16.5 %collective-permute-start.12 = (bf16[800,896]{1,0:T(8,128)(2,1)}, bf16[800,896]{1,0:T(8,128)(2,1)}, u32[]{:S(2)}, u32[]{:S(2)}) collective-permute-start(bf16[800,896]{1,0:T(8,128)(2,1)} %get-tuple-element.139), channel_id=1, source_target_pairs={{0,4},{4,0},{8,12},{12,8},{16,20},{20,16},{24,28},{28,24},{1,5},{5... | collective-permute-start | bytes 4300808 | tf_op jit(solution)/shard_map/ppermute | solution.py:824
  118.1 16.4 %collective-permute-start.13 = (bf16[800,896]{1,0:T(8,128)(2,1)}, bf16[800,896]{1,0:T(8,128)(2,1)}, u32[]{:S(2)}, u32[]{:S(2)}) collective-permute-start(bf16[800,896]{1,0:T(8,128)(2,1)} %get-tuple-element.140), channel_id=1, source_target_pairs={{0,4},{4,0},{8,12},{12,8},{16,20},{20,16},{24,28},{28,24},{1,5},{5... | collective-permute-start | bytes 4300808 | tf_op jit(solution)/shard_map/ppermute | solution.py:824
  133.0 19.5 %collective-permute-start.14 = (bf16[400,768]{1,0:T(8,128)(2,1)}, bf16[400,768]{1,0:T(8,128)(2,1)}, u32[]{:S(2)}, u32[]{:S(2)}) collective-permute-start(bf16[400,768]{1,0:T(8,128)(2,1)} %get-tuple-element.148), channel_id=1, source_target_pairs={{0,2},{1,3},{2,0},{3,1},{4,6},{5,7},{6,4},{7,5},{8,10},{9,11},{10,... | collective-permute-start | bytes 1843208 | tf_op jit(solution)/shard_map/ppermute | solution.py:824
  133.2 19.3 %collective-permute-start.15 = (bf16[400,768]{1,0:T(8,128)(2,1)}, bf16[400,768]{1,0:T(8,128)(2,1)}, u32[]{:S(2)}, u32[]{:S(2)}) collective-permute-start(bf16[400,768]{1,0:T(8,128)(2,1)} %get-tuple-element.149), channel_id=1, source_target_pairs={{0,1},{1,0},{2,3},{3,2},{4,5},{5,4},{6,7},{7,6},{8,9},{9,8},{10,11... | collective-permute-start | bytes 1843208 | tf_op jit(solution)/shard_map/ppermute | solution.py:824
  155.8 27.7 %collective-permute-start.17 = (bf16[400,896]{1,0:T(8,128)(2,1)}, bf16[400,896]{1,0:T(8,128)(2,1)}, u32[]{:S(2)}, u32[]{:S(2)}) collective-permute-start(bf16[400,896]{1,0:T(8,128)(2,1)} %get-tuple-element.162), channel_id=1, source_target_pairs={{0,1},{1,0},{2,3},{3,2},{4,5},{5,4},{6,7},{7,6},{8,9},{9,8},{10,11... | collective-permute-start | bytes 2150408 | tf_op jit(solution)/shard_map/ppermute | solution.py:824
  156.6 27.0 %collective-permute-start.16 = (bf16[400,896]{1,0:T(8,128)(2,1)}, bf16[400,896]{1,0:T(8,128)(2,1)}, u32[]{:S(2)}, u32[]{:S(2)}) collective-permute-start(bf16[400,896]{1,0:T(8,128)(2,1)} %get-tuple-element.160), channel_id=1, source_target_pairs={{0,2},{1,3},{2,0},{3,1},{4,6},{5,7},{6,4},{7,5},{8,10},{9,11},{10,... | collective-permute-start | bytes 2150408 | tf_op jit(solution)/shard_map/ppermute | solution.py:824
  158.5 21.7 %collective-permute-start.18 = (bf16[200,768]{1,0:T(8,128)(2,1)}, bf16[200,768]{1,0:T(8,128)(2,1)}, u32[]{:S(2)}, u32[]{:S(2)}) collective-permute-start(bf16[200,768]{1,0:T(8,128)(2,1)} %get-tuple-element.153), channel_id=1, source_target_pairs={{0,1},{1,0},{2,3},{3,2},{4,5},{5,4},{6,7},{7,6},{8,9},{9,8},{10,11... | collective-permute-start | bytes 921608 | tf_op jit(solution)/shard_map/ppermute | solution.py:824
  158.5 22.5 %collective-permute-start.19 = (bf16[200,768]{1,0:T(8,128)(2,1)}, bf16[200,768]{1,0:T(8,128)(2,1)}, u32[]{:S(2)}, u32[]{:S(2)}) collective-permute-start(bf16[200,768]{1,0:T(8,128)(2,1)} %get-tuple-element.154), channel_id=1, source_target_pairs={{0,2},{1,3},{2,0},{3,1},{4,6},{5,7},{6,4},{7,5},{8,10},{9,11},{10,... | collective-permute-start | bytes 921608 | tf_op jit(solution)/shard_map/ppermute | solution.py:824
  176.0 15.0 %all-to-all-start.2 = ((f32[32,16,128]{2,1,0:T(8,128)}), f32[32,16,128]{2,1,0:T(8,128)}, u32[]{:S(2)}, u32[]{:S(2)}) async-start(f32[32,16,128]{2,1,0:T(8,128)} %get-tuple-element.157), calls=%async_computation.2 | async-start | bytes 524288 | tf_op jit(solution)/shard_map/all_to_all | solution.py:972
  179.5 101.1 %all-reduce.6.cloned.1.call-start = ((), (), s32[]{:S(2)}) async-start(), calls=%async_computation.5 | async-start | bytes 1433600 | tf_op jit(solution)/shard_map/psum | solution.py:945
  183.6 6.9 %copy-start.3 = (f32[32,128]{1,0:T(8,128)S(1)}, f32[32,128]{1,0:T(8,128)}, u32[]{:S(2)}) copy-start(f32[32,128]{1,0:T(8,128)} %get-tuple-element.155.refs_7_.stat_ref) | copy-start | bytes 49156
  187.3 17.2 %collective-permute-start.23 = (bf16[200,896]{1,0:T(8,128)(2,1)}, bf16[200,896]{1,0:T(8,128)(2,1)}, u32[]{:S(2)}, u32[]{:S(2)}) collective-permute-start(bf16[200,896]{1,0:T(8,128)(2,1)} %get-tuple-element.171), channel_id=1, source_target_pairs={{0,1},{1,0},{2,3},{3,2},{4,5},{5,4},{6,7},{7,6},{8,9},{9,8},{10,11... | collective-permute-start | bytes 1075208 | tf_op jit(solution)/shard_map/ppermute | solution.py:824
  188.2 16.3 %collective-permute-start.24 = (bf16[200,896]{1,0:T(8,128)(2,1)}, bf16[200,896]{1,0:T(8,128)(2,1)}, u32[]{:S(2)}, u32[]{:S(2)}) collective-permute-start(bf16[200,896]{1,0:T(8,128)(2,1)} %get-tuple-element.172), channel_id=1, source_target_pairs={{0,2},{1,3},{2,0},{3,1},{4,6},{5,7},{6,4},{7,5},{8,10},{9,11},{10,... | collective-permute-start | bytes 1075208 | tf_op jit(solution)/shard_map/ppermute | solution.py:824
  189.1 15.3 %collective-permute-start.22 = (bf16[2,104,768]{2,1,0:T(8,128)(2,1)}, bf16[2,104,768]{2,1,0:T(8,128)(2,1)}, u32[]{:S(2)}, u32[]{:S(2)}) collective-permute-start(bf16[2,104,768]{2,1,0:T(8,128)(2,1)} %get-tuple-element.167), channel_id=1, source_target_pairs={{0,8},{4,12},{8,0},{12,4},{16,24},{20,28},{24,16},{28,20},{1,9},{5... | collective-permute-start | bytes 958472 | tf_op jit(solution)/shard_map/ppermute | solution.py:824
  200.8 30.3 %collective-permute-start.20 = (bf16[3,800,256]{2,1,0:T(8,128)(2,1)}, bf16[3,800,256]{2,1,0:T(8,128)(2,1)}, u32[]{:S(2)}, u32[]{:S(2)}) collective-permute-start(bf16[3,800,256]{2,1,0:T(8,128)(2,1)} %get-tuple-element.175), channel_id=1, source_target_pairs={{0,4},{4,8},{8,12},{12,16},{16,20},{20,24},{24,28},{1,5},{5,9},{9,... | collective-permute-start | bytes 3686408 | tf_op jit(solution)/shard_map/ppermute | solution.py:808
  203.2 28.0 %collective-permute-start.21 = (bf16[3,800,256]{2,1,0:T(8,128)(2,1)}, bf16[3,800,256]{2,1,0:T(8,128)(2,1)}, u32[]{:S(2)}, u32[]{:S(2)}) collective-permute-start(bf16[3,800,256]{2,1,0:T(8,128)(2,1)} %get-tuple-element.176), channel_id=1, source_target_pairs={{4,0},{8,4},{12,8},{16,12},{20,16},{24,20},{28,24},{5,1},{9,5},{13... | collective-permute-start | bytes 3686408 | tf_op jit(solution)/shard_map/ppermute | solution.py:809
  227.1 24.7 %all-to-all-start.3 = ((f32[4,54,200]{2,1,0:T(8,128)}), f32[4,54,200]{2,1,0:T(8,128)}, u32[]{:S(2)}, u32[]{:S(2)}) async-start(f32[4,54,200]{2,1,0:T(8,128)} %tap_gradient.1), calls=%async_computation.3 | async-start | bytes 458752 | tf_op jit(solution)/shard_map/all_to_all | solution.py:992
  231.2 32.5 %collective-permute-start.25 = (bf16[2,104,768]{2,1,0:T(8,128)(2,1)}, bf16[2,104,768]{2,1,0:T(8,128)(2,1)}, u32[]{:S(2)}, u32[]{:S(2)}) collective-permute-start(bf16[2,104,768]{2,1,0:T(8,128)(2,1)} %round_sums.3.refs_0_), channel_id=1, source_target_pairs={{0,16},{4,20},{8,24},{12,28},{16,0},{20,4},{24,8},{28,12},{1,17},{... | collective-permute-start | bytes 958472 | tf_op jit(solution)/shard_map/ppermute | solution.py:824
  253.6 29.4 %all-to-all-start.4 = ((f32[8,54,200]{2,1,0:T(8,128)}), f32[8,54,200]{2,1,0:T(8,128)}, u32[]{:S(2)}, u32[]{:S(2)}) async-start(f32[8,54,200]{2,1,0:T(8,128)} %broadcast_in_dim.48), calls=%async_computation.4 | async-start | bytes 917504 | tf_op jit(solution)/shard_map/all_to_all | solution.py:819
  265.5 16.1 %copy-start.6 = (f32[16,128]{1,0:T(8,128)S(1)}, f32[16,128]{1,0:T(8,128)}, u32[]{:S(2)}) copy-start(f32[16,128]{1,0:T(8,128)} %get-tuple-element.199) | copy-start | bytes 24580
  265.5 15.1 %collective-permute-start.26 = (bf16[2,104,768]{2,1,0:T(8,128)(2,1)}, bf16[2,104,768]{2,1,0:T(8,128)(2,1)}, u32[]{:S(2)}, u32[]{:S(2)}) collective-permute-start(bf16[2,104,768]{2,1,0:T(8,128)(2,1)} %round_sums.5.refs_4_), channel_id=1, source_target_pairs={{0,8},{4,12},{8,0},{12,4},{16,24},{20,28},{24,16},{28,20},{1,9},{5... | collective-permute-start | bytes 958472 | tf_op jit(solution)/shard_map/ppermute | solution.py:824
  266.0 19.9 %collective-permute-start.29 = (bf16[2,104,768]{2,1,0:T(8,128)(2,1)}, bf16[2,104,768]{2,1,0:T(8,128)(2,1)}, u32[]{:S(2)}, u32[]{:S(2)}) collective-permute-start(bf16[2,104,768]{2,1,0:T(8,128)(2,1)} %round_sums.5.refs_4_), channel_id=1, source_target_pairs={{0,4},{4,0},{8,12},{12,8},{16,20},{20,16},{24,28},{28,24},{1,5},{5... | collective-permute-start | bytes 958472 | tf_op jit(solution)/shard_map/ppermute | solution.py:824
  280.6 5.3 %collective-permute-start.27 = (bf16[200,896]{1,0:T(8,128)(2,1)}, bf16[200,896]{1,0:T(8,128)(2,1)}, u32[]{:S(2)}, u32[]{:S(2)}) collective-permute-start(bf16[200,896]{1,0:T(8,128)(2,1)} %get-tuple-element.200.refs_0_), channel_id=1, source_target_pairs={{0,4},{4,0},{8,12},{12,8},{16,20},{20,16},{24,28},{28,24},{1,5},{5... | collective-permute-start | bytes 1075208 | tf_op jit(solution)/shard_map/ppermute | solution.py:824
  281.2 4.7 %collective-permute-start.28 = (bf16[200,896]{1,0:T(8,128)(2,1)}, bf16[200,896]{1,0:T(8,128)(2,1)}, u32[]{:S(2)}, u32[]{:S(2)}) collective-permute-start(bf16[200,896]{1,0:T(8,128)(2,1)} %get-tuple-element.201.refs_2_), channel_id=1, source_target_pairs={{0,4},{4,0},{8,12},{12,8},{16,20},{20,16},{24,28},{28,24},{1,5},{5... | collective-permute-start | bytes 1075208 | tf_op jit(solution)/shard_map/ppermute | solution.py:824
  281.2 4.7 %collective-permute-start.30 = (bf16[2,104,768]{2,1,0:T(8,128)(2,1)}, bf16[2,104,768]{2,1,0:T(8,128)(2,1)}, u32[]{:S(2)}, u32[]{:S(2)}) collective-permute-start(bf16[2,104,768]{2,1,0:T(8,128)(2,1)} %collective-permute-done.26.refs_5_), channel_id=1, source_target_pairs={{0,4},{4,0},{8,12},{12,8},{16,20},{20,16},{24,28},{28,24},{1,5},{5... | collective-permute-start | bytes 958472 | tf_op jit(solution)/shard_map/ppermute | solution.py:824
  (3 other events, 7.4 us)
Sparse Core Ops, SparseCore 0:
  209.0 54.0 all-reduce.5

commit v7 on v6

--- a/solution.py
+++ b/solution.py
@@ -673,39 +673,39 @@
         cols_ref[2] = wide(factor * c[:, 2:3])
         cols_ref[3] = wide(factor * c[:, 1:2] * c[:, 3:4])
 
-    for k in range(0, out_ref.shape[2], 128):
-        s = slice(k, k + 128)
-        apart = conv_ref[0, :, s] - cols_ref[0]
-        correction = m_ref[0, 0:1, s] * (cols_ref[2] + apart * cols_ref[3])
-        out_ref[0, :, s] = (cols_ref[1] * da_ref[0, :, s] - correction).astype(BF16)
-    grad = out_ref[0]
-
-    @pl.when(row < REACH)
+    for r in range(out_ref.shape[0]):
+        for k in range(0, out_ref.shape[2], 128):
+            s = slice(k, k + 128)
+            apart = conv_ref[r, :, s] - cols_ref[0]
+            correction = m_ref[r, 0:1, s] * (cols_ref[2] + apart * cols_ref[3])
+            out_ref[r, :, s] = (cols_ref[1] * da_ref[r, :, s] - correction).astype(BF16)
+
+    @pl.when(row == 0)
     def _():
-        top_ref[0] = grad
-
-    @pl.when(row >= pl.num_programs(0) - REACH)
+        top_ref[...] = out_ref[...]
+
+    @pl.when(row == pl.num_programs(0) - 1)
     def _():
-        end_ref[0] = grad
+        end_ref[...] = out_ref[...]
 
 
 def conv_gradient(da, conv, m16, sums, stat, par):
     rows, channels, width = conv.shape
     return pl.pallas_call(
         conv_grad_kernel,
-        grid=(rows,),
+        grid=(rows // REACH,),
         in_specs=[
-            pl.BlockSpec((1, channels, width), lambda r: (r, 0, 0)),
-            pl.BlockSpec((1, channels, width), lambda r: (r, 0, 0)),
-            pl.BlockSpec((1, GRP, width), lambda r: (r, 0, 0)),
+            pl.BlockSpec((REACH, channels, width), lambda r: (r, 0, 0)),
+            pl.BlockSpec((REACH, channels, width), lambda r: (r, 0, 0)),
+            pl.BlockSpec((REACH, GRP, width), lambda r: (r, 0, 0)),
             whole(sums.shape),
             whole(stat.shape),
             whole(par.shape),
         ],
         out_specs=[
-            pl.BlockSpec((1, channels, width), lambda r: (r, 0, 0)),
-            pl.BlockSpec((1, channels, width), lambda r: (jnp.minimum(r, REACH - 1), 0, 0)),
-            pl.BlockSpec((1, channels, width), lambda r: (jnp.maximum(r - rows + REACH, 0), 0, 0)),
+            pl.BlockSpec((REACH, channels, width), lambda r: (r, 0, 0)),
+            pl.BlockSpec((REACH, channels, width), lambda r: (0, 0, 0)),
+            pl.BlockSpec((REACH, channels, width), lambda r: (0, 0, 0)),
             pl.BlockSpec((16, 128), lambda r: (0, 0)),
         ],
         out_shape=[

time: 299 us -> 297 us (level)
  no operation moved by 1% of the time
where the time goes in v7:
time: 297 us; the launch traced here: 296 us
  Pallas kernels  191 us (64%)
  starting transfers between devices  54 us (18%)
  waiting for transfers between devices  19.9 us (7%)
  between operations  15 us (5%)
  local copies, waits for them, and re-layouts  10.7 us (4%)
  other arithmetic  4.74 us (2%)
    pallas_call x4, Pallas kernels, hidden_layer(): pl.pallas_call(functools.partial(hidden_kernel, step=128, pieces=pieces,...  65.4 us
    ppermute x27, starting transfers between devices, flip_bit(): return lax.ppermute(values, axis, [(i, i ^ 1 << bit) for i in range(size)])  22.7 us
    pallas_call x1, Pallas kernels, conv_forward(): pl.pallas_call(functools.partial(conv_kernel, share=share), grid=(channel...  20.9 us
    pallas_call x1, Pallas kernels, tap_gradient(): pl.pallas_call(functools.partial(tap_grad_kernel, share=share), grid=(cha...  18.1 us
    pallas_call x1, Pallas kernels, input_gradient(): pl.pallas_call(input_grad_kernel, grid=(channels // block,), in_specs=[pl...  16.3 us
    pallas_call x1, Pallas kernels, activation_gradient(): pl.pallas_call(functools.partial(act_grad_kernel, cuts=cuts), grid=(rows,...  16.1 us
    pallas_call x1, Pallas kernels, block_output(): pl.pallas_call(functools.partial(block_out_kernel, cuts=cuts), grid=(rows...  14.6 us
    ppermute x27, waiting for transfers between devices, flip_bit(): return lax.ppermute(values, axis, [(i, i ^ 1 << bit) for i in range(size)])  13.5 us
  transfers between devices with their start and end apart: 37, of which 7 were waited for; matrix products, arithmetic and copies ran while one was open for 4% of the time, Pallas kernels for 57%

profile of v7, /device:TPU:0, one launch (start us, length us, event | category | flops | bytes accessed | tf_op | source)
XLA Modules:
  0.0 295.7 jit_solution(7146907707255151458)
XLA Ops:
  7.2 3.3 %fusion = (bf16[3,800,256]{2,1,0:T(8,128)(2,1)}, bf16[3,800,256]{2,1,0:T(8,128)(2,1)}) fusion(bf16[6,800,256]{2,1,0:T(8,128)(2,1)} %bitcast.35), kind=kLoop, calls=%fused_computation.11 | loop fusion | bytes 4915200 | tf_op jit(solution)/shard_map/slice | solution.py:870
  11.4 5.2 %all-to-all-start = ((f32[4,56,200]{2,1,0:T(8,128)}), f32[4,56,200]{2,1,0:T(8,128)S(1)}, u32[]{:S(2)}, u32[]{:S(2)}) async-start(f32[4,56,200]{2,1,0:T(8,128)} %broadcast_in_dim.43), calls=%async_computation | async-start | bytes 458752 | tf_op jit(solution)/shard_map/all_to_all | solution.py:819
  16.6 2.5 collective-permute-start.4
  19.0 1.3 collective-permute-start.5
  20.3 1.5 all-to-all-done.small_ref
  21.9 1.0 slice_select_fusion.refs_4_
  22.9 1.2 collective-permute-start.2
  24.1 1.0 slice_select_fusion.1.refs_0_
  27.7 1.3 collective-permute-start.7
  29.8 5.6 %mask_gradient.1 = (bf16[800,1536]{1,0:T(8,128)(2,1)}, f32[1,16,128]{2,1,0:T(8,128)}) custom-call(bf16[6,800,256]{2,1,0:T(8,128)(2,1)} %bitcast.39, f32[6,16,256]{2,1,0:T(8,128)} %broadcast_in_dim.44.m_ref.refs_7_), custom_call_target="tpu_custom_call" | custom-call | flops 115000000 | bytes 100000 | tf_op jit(solution)/shard_map/mask_gradient/pallas_call | solution.py:344
  35.4 5.3 %collective-permute-done.2.refs_6_ = bf16[200,1664]{1,0:T(8,128)(2,1)} collective-permute-done((bf16[200,1664]{1,0:T(8,128)(2,1)}, bf16[200,1664]{1,0:T(8,128)(2,1)}, u32[]{:S(2)}, u32[]{:S(2)}) %collective-permute-start.2) | collective-permute-done | bytes 665632 | tf_op jit(solution)/shard_map/ppermute | solution.py:824
  40.7 1.4 collective-permute-start.6
  42.1 1.2 collective-permute-done.refs_1_
  43.4 1.6 collective-permute-start.1
  45.6 20.9 %conv_forward.1 = (f32[6,800,256]{2,1,0:T(8,128)}, f32[32,16,128]{2,1,0:T(8,128)}, f32[800,128]{1,0:T(8,128)}) custom-call(bf16[6,800,256]{2,1,0:T(8,128)(2,1)} %bitcast.36, bf16[3,800,256]{2,1,0:T(8,128)(2,1)} %collective-permute-done.4.up_ref, bf16[3,800,256]{2,1,0:T(8,128)(2,1)} %collective-permute-done.5.dn_ref, f32[4,56,200]{2,1,0:T(8,128)} %copy-done.2, ...), custom_call_target="tpu_custom_call" | custom-call | flops 460000000 | bytes 100000 | tf_op jit(solution)/shard_map/conv_forward/pallas_call | solution.py:158
  66.5 6.7 %all-to-all-start.1 = ((f32[32,16,128]{2,1,0:T(8,128)}), f32[32,16,128]{2,1,0:T(8,128)}, u32[]{:S(2)}, u32[]{:S(2)}) async-start(f32[32,16,128]{2,1,0:T(8,128)} %get-tuple-element.124), calls=%async_computation.1 | async-start | bytes 524288 | tf_op jit(solution)/shard_map/all_to_all | solution.py:913
  73.3 5.8 %join_pieces.1 = (bf16[800,1664]{1,0:T(8,128)(2,1)}, bf16[800,1664]{1,0:T(8,128)(2,1)}) custom-call(s32[1]{0:T(128)} %bitcast.14.index_ref, bf16[200,1664]{1,0:T(8,128)(2,1)} %slice_select_fusion.1.refs_0_, bf16[200,1664]{1,0:T(8,128)(2,1)} %collective-permute-done.refs_1_, bf16[200,1664]{1,0:T(8,128)(2,1)} %collective-permute-done.6.refs_2_, ...), custom_call_target="tpu_custom_call" | custom-call | flops 115000000 | bytes 100000 | tf_op jit(solution)/shard_map/join_pieces/pallas_call | solution.py:751
  79.1 4.9 %all-to-all-done.1.refs_1_ = f32[32,16,128]{2,1,0:T(8,128)} async-done(((f32[32,16,128]{2,1,0:T(8,128)}), f32[32,16,128]{2,1,0:T(8,128)}, u32[]{:S(2)}, u32[]{:S(2)}) %all-to-all-start.1) | async-done | bytes 262176 | tf_op jit(solution)/shard_map/all_to_all | solution.py:913
  84.0 15.9 %hidden_layer.4 = (bf16[1536,768]{1,0:T(8,128)(2,1)}, bf16[1536,768]{1,0:T(8,128)(2,1)}, bf16[800,768]{1,0:T(8,128)(2,1)}, bf16[800,768]{1,0:T(8,128)(2,1)}, f32...) custom-call(s32[4]{0:T(128)} %pad_add_fusion.bits_ref.flags_ref, ...), custom_call_target="tpu_custom_call" | custom-call | flops 345000000 | bytes 100000 | tf_op jit(solution)/shard_map/hidden_layer/pallas_call | solution.py:474
  101.0 17.0 %hidden_layer.5 = (bf16[1536,896]{1,0:T(8,128)(2,1)}, bf16[1536,896]{1,0:T(8,128)(2,1)}, bf16[800,896]{1,0:T(8,128)(2,1)}, bf16[800,896]{1,0:T(8,128)(2,1)}, f32[1,896]{1,0:T(1,128)}) custom-call(s32[4]{0:T(128)} %pad_add_fusion.bits_ref.flags_ref, bf16[800,1536]{1,0:T(8,128)(2,1)} %get-tuple-element.112.bg_ref, ...), custom_call_target="tpu_custom_call" | custom-call | flops 345000000 | bytes 100000 | tf_op jit(solution)/shard_map/hidden_layer/pallas_call | solution.py:474
  118.5 14.5 %hidden_layer.6 = (bf16[1536,768]{1,0:T(8,128)(2,1)}, bf16[1536,768]{1,0:T(8,128)(2,1)}, f32[400,768]{1,0:T(8,128)}, bf16[400,768]{1,0:T(8,128)(2,1)}, f32[400,7...) custom-call(s32[4]{0:T(128)} %pad_add_fusion.bits_ref.flags_ref, ...), custom_call_target="tpu_custom_call" | custom-call | flops 345000000 | bytes 100000 | tf_op jit(solution)/shard_map/hidden_layer/pallas_call | solution.py:474
  133.2 1.3 collective-permute-start.15
  134.5 18.0 %hidden_layer.7 = (bf16[1536,896]{1,0:T(8,128)(2,1)}, bf16[1536,896]{1,0:T(8,128)(2,1)}, f32[400,896]{1,0:T(8,128)}, bf16[400,896]{1,0:T(8,128)(2,1)}, f32[400,8...) custom-call(s32[4]{0:T(128)} %pad_add_fusion.bits_ref.flags_ref, ...), custom_call_target="tpu_custom_call" | custom-call | flops 345000000 | bytes 100000 | tf_op jit(solution)/shard_map/hidden_layer/pallas_call | solution.py:474
  152.5 3.4 %split_sums.2 = (f32[200,768]{1,0:T(8,128)}, bf16[200,768]{1,0:T(8,128)(2,1)}, f32[200,768]{1,0:T(8,128)}, bf16[200,768]{1,0:T(8,128)(2,1)}) custom-call(s32[4]{0:T(128)} %pad_add_fusion.bits_ref.flags_ref, f32[400,768]{1,0:T(8,128)} %get-tuple-element.147.refs_0_, bf16[400,768]{1,0:T(8,128)(2,1)} %collective-permute-done.14.refs_1_, ...), custom_call_target="tpu_custom_call" | custom-call | flops 3449999872 | bytes 100000 | tf_op jit(solution)/shard_map/split_sums/pallas_call | solution.py:499
  156.6 1.9 collective-permute-start.16
  158.5 1.4 collective-permute-start.19
  159.9 16.1 %activation_gradient.1 = (f32[6,800,256]{2,1,0:T(8,128)}, f32[32,16,128]{2,1,0:T(8,128)}) custom-call(bf16[800,1664]{1,0:T(8,128)(2,1)} %collective-permute-done.9.we_ref.refs_0_, bf16[800,1664]{1,0:T(8,128)(2,1)} %get-tuple-element.130.we_ref.refs_1_, bf16[1536,768]{1,0:T(8,128)(2,1)} %get-tuple-element.142.refs_2_, ...), custom_call_target="tpu_custom_call" | custom-call | flops 345000000 | bytes 100000 | tf_op jit(solution)/shard_map/activation_gradient/pallas_call | solution.py:605
  176.0 3.5 %all-to-all-start.2 = ((f32[32,16,128]{2,1,0:T(8,128)}), f32[32,16,128]{2,1,0:T(8,128)}, u32[]{:S(2)}, u32[]{:S(2)}) async-start(f32[32,16,128]{2,1,0:T(8,128)} %get-tuple-element.157), calls=%async_computation.2 | async-start | bytes 524288 | tf_op jit(solution)/shard_map/all_to_all | solution.py:972
  181.1 2.5 band_split.1
  183.6 3.7 %split_sums.3 = (f32[200,896]{1,0:T(8,128)}, bf16[200,896]{1,0:T(8,128)(2,1)}, f32[200,896]{1,0:T(8,128)}, bf16[200,896]{1,0:T(8,128)(2,1)}) custom-call(s32[4]{0:T(128)} %pad_add_fusion.bits_ref.flags_ref, f32[400,896]{1,0:T(8,128)} %get-tuple-element.158.refs_0_, bf16[400,896]{1,0:T(8,128)(2,1)} %collective-permute-done.16.refs_1_, ...), custom_call_target="tpu_custom_call" | custom-call | flops 3449999872 | bytes 100000 | tf_op jit(solution)/shard_map/split_sums/pallas_call | solution.py:499
  188.2 0.9 collective-permute-start.24
  189.1 1.3 collective-permute-start.22
  191.0 8.3 %conv_gradient.1 = (bf16[6,800,256]{2,1,0:T(8,128)(2,1)}, bf16[3,800,256]{2,1,0:T(8,128)(2,1)}, bf16[3,800,256]{2,1,0:T(8,128)(2,1)}, f32[16,128]{1,0:T(8,128)}) custom-call(f32[6,800,256]{2,1,0:T(8,128)} %get-tuple-element.156.da_ref, f32[6,800,256]{2,1,0:T(8,128)} %get-tuple-element.116.refs_0_.refs_6_.conv_ref, ...), custom_call_target="tpu_custom_call" | custom-call | flops 230000000 | bytes 100000 | tf_op jit(solution)/shard_map/conv_gradient/pallas_call | solution.py:694
  199.4 2.3 collective-permute-start.20
  201.7 1.3 collective-permute-start.21
  203.1 1.9 round_sums.3.refs_0_
  205.0 2.5 round_sums.4
  207.5 18.1 %tap_gradient.1 = f32[4,54,200]{2,1,0:T(8,128)} custom-call(s32[4]{0:T(128)} %pad_add_fusion.bits_ref.flags_ref, bf16[6,800,256]{2,1,0:T(8,128)(2,1)} %bitcast.37, bf16[3,800,256]{2,1,0:T(8,128)(2,1)} %collective-permute-done.4.up_ref, bf16[3,800,256]{2,1,0:T(8,128)(2,1)} %collective-permute-done.5.dn_ref, bf16[6,800,256]{2,1,0:T(8,128)(2,1)} %get-tuple-element.185.g_ref, ...), custom_call_target="tpu_custom_call" | custom-call | flops 17250000896 | bytes 100000 | tf_op jit(solution)/shard_map/tap_gradient/pallas_call | solution.py:295
  225.6 4.0 %all-to-all-start.3 = ((f32[4,54,200]{2,1,0:T(8,128)}), f32[4,54,200]{2,1,0:T(8,128)}, u32[]{:S(2)}, u32[]{:S(2)}) async-start(f32[4,54,200]{2,1,0:T(8,128)} %tap_gradient.1), calls=%async_computation.3 | async-start | bytes 458752 | tf_op jit(solution)/shard_map/all_to_all | solution.py:992
  229.7 4.5 %collective-permute-start.25 = (bf16[2,104,768]{2,1,0:T(8,128)(2,1)}, bf16[2,104,768]{2,1,0:T(8,128)(2,1)}, u32[]{:S(2)}, u32[]{:S(2)}) collective-permute-start(bf16[2,104,768]{2,1,0:T(8,128)(2,1)} %round_sums.3.refs_0_), channel_id=1, source_target_pairs={{0,16},{4,20},{8,24},{12,28},{16,0},{20,4},{24,8},{28,12},{1,17},{... | collective-permute-start | bytes 958472 | tf_op jit(solution)/shard_map/ppermute | solution.py:824
  234.1 16.3 %input_gradient.1 = f32[6,800,256]{2,1,0:T(8,128)} custom-call(bf16[6,800,256]{2,1,0:T(8,128)(2,1)} %get-tuple-element.185.g_ref, bf16[3,800,256]{2,1,0:T(8,128)(2,1)} %collective-permute-done.20.up_ref, bf16[3,800,256]{2,1,0:T(8,128)(2,1)} %collective-permute-done.21.dn_ref, f32[800,128]{1,0:T(8,128)} %get-tuple-element.197.refs_2_.par_ref.refs_8_, ...), custom_call_target="tpu_custom_call" | custom-call | flops 5750000128 | bytes 100000 | tf_op jit(solution)/shard_map/input_gradient/pallas_call | solution.py:216
  250.4 1.0 reduce_sum.18
  252.2 4.4 %all-to-all-start.4 = ((f32[8,54,200]{2,1,0:T(8,128)}), f32[8,54,200]{2,1,0:T(8,128)}, u32[]{:S(2)}, u32[]{:S(2)}) async-start(f32[8,54,200]{2,1,0:T(8,128)} %broadcast_in_dim.48), calls=%async_computation.4 | async-start | bytes 917504 | tf_op jit(solution)/shard_map/all_to_all | solution.py:819
  256.6 5.5 %collective-permute-done.25.refs_1_ = bf16[2,104,768]{2,1,0:T(8,128)(2,1)} collective-permute-done((bf16[2,104,768]{2,1,0:T(8,128)(2,1)}, bf16[2,104,768]{2,1,0:T(8,128)(2,1)}, u32[]{:S(2)}, u32[]{:S(2)}) %collective-permute-start.25) | collective-permute-done | bytes 319520 | tf_op jit(solution)/shard_map/ppermute | solution.py:824
  262.1 1.9 round_sums.5.refs_4_
  264.5 14.6 %block_output.1 = bf16[6,800,256]{2,1,0:T(8,128)(2,1)} custom-call(bf16[800,1664]{1,0:T(8,128)(2,1)} %collective-permute-done.8.wp_ref.refs_0_, bf16[800,1664]{1,0:T(8,128)(2,1)} %get-tuple-element.128.wp_ref.refs_1_, bf16[1536,768]{1,0:T(8,128)(2,1)} %get-tuple-element.129.refs_2_, bf16[1536,768]{1,0:T(8,128)(2,1)} %get-tuple-element.137.refs_3_, ...), custom_call_target="tpu_custom_call" | custom-call | flops 5750000128 | bytes 100000 | tf_op jit(solution)/shard_map/block_output/pallas_call | solution.py:638
  281.5 1.1 reduce_sum.19
  284.5 4.4 %place_columns.1 = (f32[200,3200]{1,0:T(8,128)}, f32[200,3200]{1,0:T(8,128)}) custom-call(s32[4]{0:T(128)} %pad_add_fusion.bits_ref.flags_ref, bf16[200,896]{1,0:T(8,128)(2,1)} %get-tuple-element.200.refs_0_, bf16[200,896]{1,0:T(8,128)(2,1)} %collective-permute-done.27.refs_1_, bf16[200,896]{1,0:T(8,128)(2,1)} %get-tuple-element.201.refs_2_, ...), custom_call_target="tpu_custom_call" | custom-call | flops 115000000 | bytes 100000 | tf_op jit(solution)/shard_map/place_columns/pallas_call | solution.py:791
  (99 shorter events, 15.6 us)
Async XLA Ops:
  7.2 3.3 %copy-start.7 = (bf16[800]{0:T(1024)(128)(2,1)S(1)}, bf16[800]{0:T(1024)(128)(2,1)}, u32[]{:S(2)}) copy-start(bf16[800]{0:T(1024)(128)(2,1)} %param.19) | copy-start | bytes 4804
  7.2 3.4 %copy-start.10 = (bf16[200]{0:T(256)(128)(2,1)S(1)}, bf16[200]{0:T(256)(128)(2,1)}, u32[]{:S(2)}) copy-start(bf16[200]{0:T(256)(128)(2,1)} %param.21) | copy-start | bytes 1204
  7.2 3.4 %copy-start.4 = (f32[200,49]{0,1:T(8,128)S(1)}, f32[200,49]{0,1:T(8,128)}, u32[]{:S(2)}) copy-start(f32[200,49]{0,1:T(8,128)} %param.15) | copy-start | bytes 117604
  7.2 3.4 %copy-start.8 = (f32[200]{0:T(256)S(1)}, f32[200]{0:T(256)}, u32[]{:S(2)}) copy-start(f32[200]{0:T(256)} %param.16) | copy-start | bytes 2404
  7.2 3.4 %copy-start.9 = (f32[200]{0:T(256)S(1)}, f32[200]{0:T(256)}, u32[]{:S(2)}) copy-start(f32[200]{0:T(256)} %param.17) | copy-start | bytes 2404
  10.5 11.3 %copy-start.1 = (bf16[200,3200]{1,0:T(8,128)(2,1)S(1)}, bf16[200,3200]{1,0:T(8,128)(2,1)}, u32[]{:S(2)}) copy-start(bf16[200,3200]{1,0:T(8,128)(2,1)} %param.20) | copy-start | bytes 3840004
  10.5 11.3 %slice-start.1 = ((bf16[200,3200]{1,0:T(8,128)(2,1)}), bf16[200,1536]{1,0:T(8,128)(2,1)S(1)}, s32[]{:S(2)}) async-start(bf16[200,3200]{1,0:T(8,128)(2,1)} %param.20), calls=%async_computation.7 | async-start | bytes 1228800 | tf_op jit(solution)/shard_map/slice | solution.py:887
  11.4 10.4 %all-to-all-start = ((f32[4,56,200]{2,1,0:T(8,128)}), f32[4,56,200]{2,1,0:T(8,128)S(1)}, u32[]{:S(2)}, u32[]{:S(2)}) async-start(f32[4,56,200]{2,1,0:T(8,128)} %broadcast_in_dim.43), calls=%async_computation | async-start | bytes 458752 | tf_op jit(solution)/shard_map/all_to_all | solution.py:819
  16.6 26.8 %collective-permute-start.4 = (bf16[3,800,256]{2,1,0:T(8,128)(2,1)}, bf16[3,800,256]{2,1,0:T(8,128)(2,1)}, u32[]{:S(2)}, u32[]{:S(2)}) collective-permute-start(bf16[3,800,256]{2,1,0:T(8,128)(2,1)} %get-tuple-element.207), channel_id=1, source_target_pairs={{0,4},{4,8},{8,12},{12,16},{16,20},{20,24},{24,28},{1,5},{5,9},{9,... | collective-permute-start | bytes 3686408 | tf_op jit(solution)/shard_map/ppermute | solution.py:808
  19.0 26.6 %collective-permute-start.5 = (bf16[3,800,256]{2,1,0:T(8,128)(2,1)}, bf16[3,800,256]{2,1,0:T(8,128)(2,1)}, u32[]{:S(2)}, u32[]{:S(2)}) collective-permute-start(bf16[3,800,256]{2,1,0:T(8,128)(2,1)} %get-tuple-element.208), channel_id=1, source_target_pairs={{4,0},{8,4},{12,8},{16,12},{20,16},{24,20},{28,24},{5,1},{9,5},{13... | collective-permute-start | bytes 3686408 | tf_op jit(solution)/shard_map/ppermute | solution.py:809
  21.8 7.9 %copy-start.2 = (f32[4,56,200]{2,1,0:T(8,128)}, f32[4,56,200]{2,1,0:T(8,128)S(1)}, u32[]{:S(2)}) copy-start(f32[4,56,200]{2,1,0:T(8,128)S(1)} %all-to-all-done.small_ref) | copy-start | bytes 537604
  22.9 4.8 %copy-start.5 = (s32[6,256]{1,0:T(8,128)S(1)}, s32[6,256]{1,0:T(8,128)}, u32[]{:S(2)}) copy-start(s32[6,256]{1,0:T(8,128)} %param.13) | copy-start | bytes 18436
  22.9 17.7 %collective-permute-start.2 = (bf16[200,1664]{1,0:T(8,128)(2,1)}, bf16[200,1664]{1,0:T(8,128)(2,1)}, u32[]{:S(2)}, u32[]{:S(2)}) collective-permute-start(bf16[200,1664]{1,0:T(8,128)(2,1)} %slice_select_fusion.refs_4_), channel_id=1, source_target_pairs={{0,2},{1,3},{2,0},{3,1},{4,6},{5,7},{6,4},{7,5},{8,10},{9,11},{10,... | collective-permute-start | bytes 1996808 | tf_op jit(solution)/shard_map/ppermute | solution.py:824
  25.1 18.1 %collective-permute-start = (bf16[200,1664]{1,0:T(8,128)(2,1)}, bf16[200,1664]{1,0:T(8,128)(2,1)}, u32[]{:S(2)}, u32[]{:S(2)}) collective-permute-start(bf16[200,1664]{1,0:T(8,128)(2,1)} %slice_select_fusion.1.refs_0_), channel_id=1, source_target_pairs={{0,1},{1,0},{2,3},{3,2},{4,5},{5,4},{6,7},{7,6},{8,9},{9,8},{10,11... | collective-permute-start | bytes 1996808 | tf_op jit(solution)/shard_map/ppermute | solution.py:824
  27.7 45.5 %collective-permute-start.7 = (bf16[200,1664]{1,0:T(8,128)(2,1)}, bf16[200,1664]{1,0:T(8,128)(2,1)}, u32[]{:S(2)}, u32[]{:S(2)}) collective-permute-start(bf16[200,1664]{1,0:T(8,128)(2,1)} %slice_select_fusion.refs_4_), channel_id=1, source_target_pairs={{0,1},{1,0},{2,3},{3,2},{4,5},{5,4},{6,7},{7,6},{8,9},{9,8},{10,11... | collective-permute-start | bytes 1996808 | tf_op jit(solution)/shard_map/ppermute | solution.py:824
  40.7 32.6 %collective-permute-start.6 = (bf16[200,1664]{1,0:T(8,128)(2,1)}, bf16[200,1664]{1,0:T(8,128)(2,1)}, u32[]{:S(2)}, u32[]{:S(2)}) collective-permute-start(bf16[200,1664]{1,0:T(8,128)(2,1)} %slice_select_fusion.1.refs_0_), channel_id=1, source_target_pairs={{0,2},{1,3},{2,0},{3,1},{4,6},{5,7},{6,4},{7,5},{8,10},{9,11},{10,... | collective-permute-start | bytes 1996808 | tf_op jit(solution)/shard_map/ppermute | solution.py:824
  43.3 30.0 %collective-permute-start.3 = (bf16[200,1664]{1,0:T(8,128)(2,1)}, bf16[200,1664]{1,0:T(8,128)(2,1)}, u32[]{:S(2)}, u32[]{:S(2)}) collective-permute-start(bf16[200,1664]{1,0:T(8,128)(2,1)} %collective-permute-done.2.refs_6_), channel_id=1, source_target_pairs={{0,1},{1,0},{2,3},{3,2},{4,5},{5,4},{6,7},{7,6},{8,9},{9,8},{10,11... | collective-permute-start | bytes 1996808 | tf_op jit(solution)/shard_map/ppermute | solution.py:824
  43.4 29.8 %collective-permute-start.1 = (bf16[200,1664]{1,0:T(8,128)(2,1)}, bf16[200,1664]{1,0:T(8,128)(2,1)}, u32[]{:S(2)}, u32[]{:S(2)}) collective-permute-start(bf16[200,1664]{1,0:T(8,128)(2,1)} %collective-permute-done.refs_1_), channel_id=1, source_target_pairs={{0,2},{1,3},{2,0},{3,1},{4,6},{5,7},{6,4},{7,5},{8,10},{9,11},{10,... | collective-permute-start | bytes 1996808 | tf_op jit(solution)/shard_map/ppermute | solution.py:824
  66.5 17.5 %all-to-all-start.1 = ((f32[32,16,128]{2,1,0:T(8,128)}), f32[32,16,128]{2,1,0:T(8,128)}, u32[]{:S(2)}, u32[]{:S(2)}) async-start(f32[32,16,128]{2,1,0:T(8,128)} %get-tuple-element.124), calls=%async_computation.1 | async-start | bytes 524288 | tf_op jit(solution)/shard_map/all_to_all | solution.py:913
  99.9 18.6 %collective-permute-start.9 = (bf16[800,1664]{1,0:T(8,128)(2,1)}, bf16[800,1664]{1,0:T(8,128)(2,1)}, u32[]{:S(2)}, u32[]{:S(2)}) collective-permute-start(bf16[800,1664]{1,0:T(8,128)(2,1)} %get-tuple-element.130.we_ref.refs_1_), channel_id=1, source_target_pairs={{0,4},{4,0},{8,12},{12,8},{16,20},{20,16},{24,28},{28,24},{1,5},{5... | collective-permute-start | bytes 7987208 | tf_op jit(solution)/shard_map/ppermute | solution.py:824
  100.0 18.5 %collective-permute-start.8 = (bf16[800,1664]{1,0:T(8,128)(2,1)}, bf16[800,1664]{1,0:T(8,128)(2,1)}, u32[]{:S(2)}, u32[]{:S(2)}) collective-permute-start(bf16[800,1664]{1,0:T(8,128)(2,1)} %get-tuple-element.128.wp_ref.refs_1_), channel_id=1, source_target_pairs={{0,4},{4,0},{8,12},{12,8},{16,20},{20,16},{24,28},{28,24},{1,5},{5... | collective-permute-start | bytes 7987208 | tf_op jit(solution)/shard_map/ppermute | solution.py:824
  100.5 17.6 %collective-permute-start.10 = (bf16[800,768]{1,0:T(8,128)(2,1)}, bf16[800,768]{1,0:T(8,128)(2,1)}, u32[]{:S(2)}, u32[]{:S(2)}) collective-permute-start(bf16[800,768]{1,0:T(8,128)(2,1)} %get-tuple-element.135), channel_id=1, source_target_pairs={{0,4},{4,0},{8,12},{12,8},{16,20},{20,16},{24,28},{28,24},{1,5},{5... | collective-permute-start | bytes 3686408 | tf_op jit(solution)/shard_map/ppermute | solution.py:824
  100.6 18.0 %collective-permute-start.11 = (bf16[800,768]{1,0:T(8,128)(2,1)}, bf16[800,768]{1,0:T(8,128)(2,1)}, u32[]{:S(2)}, u32[]{:S(2)}) collective-permute-start(bf16[800,768]{1,0:T(8,128)(2,1)} %get-tuple-element.136), channel_id=1, source_target_pairs={{0,4},{4,0},{8,12},{12,8},{16,20},{20,16},{24,28},{28,24},{1,5},{5... | collective-permute-start | bytes 3686408 | tf_op jit(solution)/shard_map/ppermute | solution.py:824
  118.0 16.5 %collective-permute-start.12 = (bf16[800,896]{1,0:T(8,128)(2,1)}, bf16[800,896]{1,0:T(8,128)(2,1)}, u32[]{:S(2)}, u32[]{:S(2)}) collective-permute-start(bf16[800,896]{1,0:T(8,128)(2,1)} %get-tuple-element.139), channel_id=1, source_target_pairs={{0,4},{4,0},{8,12},{12,8},{16,20},{20,16},{24,28},{28,24},{1,5},{5... | collective-permute-start | bytes 4300808 | tf_op jit(solution)/shard_map/ppermute | solution.py:824
  118.1 16.4 %collective-permute-start.13 = (bf16[800,896]{1,0:T(8,128)(2,1)}, bf16[800,896]{1,0:T(8,128)(2,1)}, u32[]{:S(2)}, u32[]{:S(2)}) collective-permute-start(bf16[800,896]{1,0:T(8,128)(2,1)} %get-tuple-element.140), channel_id=1, source_target_pairs={{0,4},{4,0},{8,12},{12,8},{16,20},{20,16},{24,28},{28,24},{1,5},{5... | collective-permute-start | bytes 4300808 | tf_op jit(solution)/shard_map/ppermute | solution.py:824
  133.0 19.5 %collective-permute-start.14 = (bf16[400,768]{1,0:T(8,128)(2,1)}, bf16[400,768]{1,0:T(8,128)(2,1)}, u32[]{:S(2)}, u32[]{:S(2)}) collective-permute-start(bf16[400,768]{1,0:T(8,128)(2,1)} %get-tuple-element.148), channel_id=1, source_target_pairs={{0,2},{1,3},{2,0},{3,1},{4,6},{5,7},{6,4},{7,5},{8,10},{9,11},{10,... | collective-permute-start | bytes 1843208 | tf_op jit(solution)/shard_map/ppermute | solution.py:824
  133.2 19.3 %collective-permute-start.15 = (bf16[400,768]{1,0:T(8,128)(2,1)}, bf16[400,768]{1,0:T(8,128)(2,1)}, u32[]{:S(2)}, u32[]{:S(2)}) collective-permute-start(bf16[400,768]{1,0:T(8,128)(2,1)} %get-tuple-element.149), channel_id=1, source_target_pairs={{0,1},{1,0},{2,3},{3,2},{4,5},{5,4},{6,7},{7,6},{8,9},{9,8},{10,11... | collective-permute-start | bytes 1843208 | tf_op jit(solution)/shard_map/ppermute | solution.py:824
  155.8 27.7 %collective-permute-start.17 = (bf16[400,896]{1,0:T(8,128)(2,1)}, bf16[400,896]{1,0:T(8,128)(2,1)}, u32[]{:S(2)}, u32[]{:S(2)}) collective-permute-start(bf16[400,896]{1,0:T(8,128)(2,1)} %get-tuple-element.162), channel_id=1, source_target_pairs={{0,1},{1,0},{2,3},{3,2},{4,5},{5,4},{6,7},{7,6},{8,9},{9,8},{10,11... | collective-permute-start | bytes 2150408 | tf_op jit(solution)/shard_map/ppermute | solution.py:824
  156.6 27.0 %collective-permute-start.16 = (bf16[400,896]{1,0:T(8,128)(2,1)}, bf16[400,896]{1,0:T(8,128)(2,1)}, u32[]{:S(2)}, u32[]{:S(2)}) collective-permute-start(bf16[400,896]{1,0:T(8,128)(2,1)} %get-tuple-element.160), channel_id=1, source_target_pairs={{0,2},{1,3},{2,0},{3,1},{4,6},{5,7},{6,4},{7,5},{8,10},{9,11},{10,... | collective-permute-start | bytes 2150408 | tf_op jit(solution)/shard_map/ppermute | solution.py:824
  158.5 21.7 %collective-permute-start.18 = (bf16[200,768]{1,0:T(8,128)(2,1)}, bf16[200,768]{1,0:T(8,128)(2,1)}, u32[]{:S(2)}, u32[]{:S(2)}) collective-permute-start(bf16[200,768]{1,0:T(8,128)(2,1)} %get-tuple-element.153), channel_id=1, source_target_pairs={{0,1},{1,0},{2,3},{3,2},{4,5},{5,4},{6,7},{7,6},{8,9},{9,8},{10,11... | collective-permute-start | bytes 921608 | tf_op jit(solution)/shard_map/ppermute | solution.py:824
  158.5 22.5 %collective-permute-start.19 = (bf16[200,768]{1,0:T(8,128)(2,1)}, bf16[200,768]{1,0:T(8,128)(2,1)}, u32[]{:S(2)}, u32[]{:S(2)}) collective-permute-start(bf16[200,768]{1,0:T(8,128)(2,1)} %get-tuple-element.154), channel_id=1, source_target_pairs={{0,2},{1,3},{2,0},{3,1},{4,6},{5,7},{6,4},{7,5},{8,10},{9,11},{10,... | collective-permute-start | bytes 921608 | tf_op jit(solution)/shard_map/ppermute | solution.py:824
  176.0 15.0 %all-to-all-start.2 = ((f32[32,16,128]{2,1,0:T(8,128)}), f32[32,16,128]{2,1,0:T(8,128)}, u32[]{:S(2)}, u32[]{:S(2)}) async-start(f32[32,16,128]{2,1,0:T(8,128)} %get-tuple-element.157), calls=%async_computation.2 | async-start | bytes 524288 | tf_op jit(solution)/shard_map/all_to_all | solution.py:972
  179.5 99.6 %all-reduce.6.cloned.1.call-start = ((), (), s32[]{:S(2)}) async-start(), calls=%async_computation.5 | async-start | bytes 1433600 | tf_op jit(solution)/shard_map/psum | solution.py:945
  183.6 6.9 %copy-start.3 = (f32[32,128]{1,0:T(8,128)S(1)}, f32[32,128]{1,0:T(8,128)}, u32[]{:S(2)}) copy-start(f32[32,128]{1,0:T(8,128)} %get-tuple-element.155.refs_7_.stat_ref) | copy-start | bytes 49156
  187.3 15.8 %collective-permute-start.23 = (bf16[200,896]{1,0:T(8,128)(2,1)}, bf16[200,896]{1,0:T(8,128)(2,1)}, u32[]{:S(2)}, u32[]{:S(2)}) collective-permute-start(bf16[200,896]{1,0:T(8,128)(2,1)} %get-tuple-element.171), channel_id=1, source_target_pairs={{0,1},{1,0},{2,3},{3,2},{4,5},{5,4},{6,7},{7,6},{8,9},{9,8},{10,11... | collective-permute-start | bytes 1075208 | tf_op jit(solution)/shard_map/ppermute | solution.py:824
  188.2 14.9 %collective-permute-start.24 = (bf16[200,896]{1,0:T(8,128)(2,1)}, bf16[200,896]{1,0:T(8,128)(2,1)}, u32[]{:S(2)}, u32[]{:S(2)}) collective-permute-start(bf16[200,896]{1,0:T(8,128)(2,1)} %get-tuple-element.172), channel_id=1, source_target_pairs={{0,2},{1,3},{2,0},{3,1},{4,6},{5,7},{6,4},{7,5},{8,10},{9,11},{10,... | collective-permute-start | bytes 1075208 | tf_op jit(solution)/shard_map/ppermute | solution.py:824
  189.1 13.9 %collective-permute-start.22 = (bf16[2,104,768]{2,1,0:T(8,128)(2,1)}, bf16[2,104,768]{2,1,0:T(8,128)(2,1)}, u32[]{:S(2)}, u32[]{:S(2)}) collective-permute-start(bf16[2,104,768]{2,1,0:T(8,128)(2,1)} %get-tuple-element.167), channel_id=1, source_target_pairs={{0,8},{4,12},{8,0},{12,4},{16,24},{20,28},{24,16},{28,20},{1,9},{5... | collective-permute-start | bytes 958472 | tf_op jit(solution)/shard_map/ppermute | solution.py:824
  199.4 30.3 %collective-permute-start.20 = (bf16[3,800,256]{2,1,0:T(8,128)(2,1)}, bf16[3,800,256]{2,1,0:T(8,128)(2,1)}, u32[]{:S(2)}, u32[]{:S(2)}) collective-permute-start(bf16[3,800,256]{2,1,0:T(8,128)(2,1)} %get-tuple-element.175), channel_id=1, source_target_pairs={{0,4},{4,8},{8,12},{12,16},{16,20},{20,24},{24,28},{1,5},{5,9},{9,... | collective-permute-start | bytes 3686408 | tf_op jit(solution)/shard_map/ppermute | solution.py:808
  201.7 27.9 %collective-permute-start.21 = (bf16[3,800,256]{2,1,0:T(8,128)(2,1)}, bf16[3,800,256]{2,1,0:T(8,128)(2,1)}, u32[]{:S(2)}, u32[]{:S(2)}) collective-permute-start(bf16[3,800,256]{2,1,0:T(8,128)(2,1)} %get-tuple-element.176), channel_id=1, source_target_pairs={{4,0},{8,4},{12,8},{16,12},{20,16},{24,20},{28,24},{5,1},{9,5},{13... | collective-permute-start | bytes 3686408 | tf_op jit(solution)/shard_map/ppermute | solution.py:809
  225.6 24.8 %all-to-all-start.3 = ((f32[4,54,200]{2,1,0:T(8,128)}), f32[4,54,200]{2,1,0:T(8,128)}, u32[]{:S(2)}, u32[]{:S(2)}) async-start(f32[4,54,200]{2,1,0:T(8,128)} %tap_gradient.1), calls=%async_computation.3 | async-start | bytes 458752 | tf_op jit(solution)/shard_map/all_to_all | solution.py:992
  229.7 32.4 %collective-permute-start.25 = (bf16[2,104,768]{2,1,0:T(8,128)(2,1)}, bf16[2,104,768]{2,1,0:T(8,128)(2,1)}, u32[]{:S(2)}, u32[]{:S(2)}) collective-permute-start(bf16[2,104,768]{2,1,0:T(8,128)(2,1)} %round_sums.3.refs_0_), channel_id=1, source_target_pairs={{0,16},{4,20},{8,24},{12,28},{16,0},{20,4},{24,8},{28,12},{1,17},{... | collective-permute-start | bytes 958472 | tf_op jit(solution)/shard_map/ppermute | solution.py:824
  252.2 29.3 %all-to-all-start.4 = ((f32[8,54,200]{2,1,0:T(8,128)}), f32[8,54,200]{2,1,0:T(8,128)}, u32[]{:S(2)}, u32[]{:S(2)}) async-start(f32[8,54,200]{2,1,0:T(8,128)} %broadcast_in_dim.48), calls=%async_computation.4 | async-start | bytes 917504 | tf_op jit(solution)/shard_map/all_to_all | solution.py:819
  264.0 16.2 %copy-start.6 = (f32[16,128]{1,0:T(8,128)S(1)}, f32[16,128]{1,0:T(8,128)}, u32[]{:S(2)}) copy-start(f32[16,128]{1,0:T(8,128)} %get-tuple-element.199) | copy-start | bytes 24580
  264.0 15.2 %collective-permute-start.26 = (bf16[2,104,768]{2,1,0:T(8,128)(2,1)}, bf16[2,104,768]{2,1,0:T(8,128)(2,1)}, u32[]{:S(2)}, u32[]{:S(2)}) collective-permute-start(bf16[2,104,768]{2,1,0:T(8,128)(2,1)} %round_sums.5.refs_4_), channel_id=1, source_target_pairs={{0,8},{4,12},{8,0},{12,4},{16,24},{20,28},{24,16},{28,20},{1,9},{5... | collective-permute-start | bytes 958472 | tf_op jit(solution)/shard_map/ppermute | solution.py:824
  264.5 19.9 %collective-permute-start.29 = (bf16[2,104,768]{2,1,0:T(8,128)(2,1)}, bf16[2,104,768]{2,1,0:T(8,128)(2,1)}, u32[]{:S(2)}, u32[]{:S(2)}) collective-permute-start(bf16[2,104,768]{2,1,0:T(8,128)(2,1)} %round_sums.5.refs_4_), channel_id=1, source_target_pairs={{0,4},{4,0},{8,12},{12,8},{16,20},{20,16},{24,28},{28,24},{1,5},{5... | collective-permute-start | bytes 958472 | tf_op jit(solution)/shard_map/ppermute | solution.py:824
  279.2 5.3 %collective-permute-start.27 = (bf16[200,896]{1,0:T(8,128)(2,1)}, bf16[200,896]{1,0:T(8,128)(2,1)}, u32[]{:S(2)}, u32[]{:S(2)}) collective-permute-start(bf16[200,896]{1,0:T(8,128)(2,1)} %get-tuple-element.200.refs_0_), channel_id=1, source_target_pairs={{0,4},{4,0},{8,12},{12,8},{16,20},{20,16},{24,28},{28,24},{1,5},{5... | collective-permute-start | bytes 1075208 | tf_op jit(solution)/shard_map/ppermute | solution.py:824
  279.7 4.7 %collective-permute-start.28 = (bf16[200,896]{1,0:T(8,128)(2,1)}, bf16[200,896]{1,0:T(8,128)(2,1)}, u32[]{:S(2)}, u32[]{:S(2)}) collective-permute-start(bf16[200,896]{1,0:T(8,128)(2,1)} %get-tuple-element.201.refs_2_), channel_id=1, source_target_pairs={{0,4},{4,0},{8,12},{12,8},{16,20},{20,16},{24,28},{28,24},{1,5},{5... | collective-permute-start | bytes 1075208 | tf_op jit(solution)/shard_map/ppermute | solution.py:824
  279.8 4.7 %collective-permute-start.30 = (bf16[2,104,768]{2,1,0:T(8,128)(2,1)}, bf16[2,104,768]{2,1,0:T(8,128)(2,1)}, u32[]{:S(2)}, u32[]{:S(2)}) collective-permute-start(bf16[2,104,768]{2,1,0:T(8,128)(2,1)} %collective-permute-done.26.refs_5_), channel_id=1, source_target_pairs={{0,4},{4,0},{8,12},{12,8},{16,20},{20,16},{24,28},{28,24},{1,5},{5... | collective-permute-start | bytes 958472 | tf_op jit(solution)/shard_map/ppermute | solution.py:824
  (3 other events, 7.4 us)
Sparse Core Ops, SparseCore 0:
  207.6 54.0 all-reduce.5

commit v8 on v7

--- a/solution.py
+++ b/solution.py
@@ -319,11 +319,14 @@
 def mask_grad_kernel(og_ref, m_ref, out_ref, sum_ref, cols_ref):
     row = pl.program_id(0)
     channels = og_ref.shape[1]
-    v = og_ref[0].astype(F32) * m_ref[0, 0:1]
-    out_ref[...] = v.astype(BF16)
-    part = v[:, 0:128]
-    for k in range(128, v.shape[1], 128):
-        part = part + v[:, k : k + 128]
+    width = og_ref.shape[2]
+    part = None
+    for r in range(og_ref.shape[0]):
+        v = og_ref[r].astype(F32) * m_ref[r, 0:1]
+        out_ref[:, r * width : (r + 1) * width] = v.astype(BF16)
+        for k in range(0, width, 128):
+            piece = v[:, k : k + 128]
+            part = piece if part is None else part + piece
 
     @pl.when(row == 0)
     def _():
@@ -343,13 +346,13 @@
     pixels = rows * width
     return pl.pallas_call(
         mask_grad_kernel,
-        grid=(rows,),
+        grid=(rows // REACH,),
         in_specs=[
-            pl.BlockSpec((1, channels, width), lambda r: (r, 0, 0)),
-            pl.BlockSpec((1, GRP, width), lambda r: (r, 0, 0)),
+            pl.BlockSpec((REACH, channels, width), lambda r: (r, 0, 0)),
+            pl.BlockSpec((REACH, GRP, width), lambda r: (r, 0, 0)),
         ],
         out_specs=[
-            pl.BlockSpec((channels, width), lambda r: (0, r)),
+            pl.BlockSpec((channels, REACH * width), lambda r: (0, r)),
             pl.BlockSpec((1, 16, 128), lambda r: (0, 0, 0)),
         ],
         out_shape=[

time: 297 us -> 297 us (level)
  transfers between devices with their start and end apart: 37 -> 37, of which waited for: 7 -> 7; matrix products, arithmetic and copies ran while one was open for 4% -> 4% of each run, Pallas kernels for 57% -> 56%
where the time goes in v8:
time: 297 us; the launch traced here: 296 us
  Pallas kernels  189 us (64%)
  starting transfers between devices  54 us (18%)
  waiting for transfers between devices  22.2 us (7%)
  between operations  15 us (5%)
  local copies, waits for them, and re-layouts  10.7 us (4%)
  other arithmetic  4.74 us (2%)
    pallas_call x4, Pallas kernels, hidden_layer(): pl.pallas_call(functools.partial(hidden_kernel, step=128, pieces=pieces,...  65.4 us
    ppermute x27, starting transfers between devices, flip_bit(): return lax.ppermute(values, axis, [(i, i ^ 1 << bit) for i in range(size)])  22.7 us
    pallas_call x1, Pallas kernels, conv_forward(): pl.pallas_call(functools.partial(conv_kernel, share=share), grid=(channel...  20.9 us
    pallas_call x1, Pallas kernels, tap_gradient(): pl.pallas_call(functools.partial(tap_grad_kernel, share=share), grid=(cha...  18.1 us
    pallas_call x1, Pallas kernels, input_gradient(): pl.pallas_call(input_grad_kernel, grid=(channels // block,), in_specs=[pl...  16.3 us
    pallas_call x1, Pallas kernels, activation_gradient(): pl.pallas_call(functools.partial(act_grad_kernel, cuts=cuts), grid=(rows,...  16.1 us
    ppermute x27, waiting for transfers between devices, flip_bit(): return lax.ppermute(values, axis, [(i, i ^ 1 << bit) for i in range(size)])  15.8 us
    pallas_call x1, Pallas kernels, block_output(): pl.pallas_call(functools.partial(block_out_kernel, cuts=cuts), grid=(rows...  14.6 us
  transfers between devices with their start and end apart: 37, of which 7 were waited for; matrix products, arithmetic and copies ran while one was open for 4% of the time, Pallas kernels for 56%

profile of v8, /device:TPU:0, one launch (start us, length us, event | category | flops | bytes accessed | tf_op | source)
XLA Modules:
  0.0 295.7 jit_solution(16686564180308005493)
XLA Ops:
  7.2 3.3 %fusion = (bf16[3,800,256]{2,1,0:T(8,128)(2,1)}, bf16[3,800,256]{2,1,0:T(8,128)(2,1)}) fusion(bf16[6,800,256]{2,1,0:T(8,128)(2,1)} %bitcast.35), kind=kLoop, calls=%fused_computation.11 | loop fusion | bytes 4915200 | tf_op jit(solution)/shard_map/slice | solution.py:873
  11.4 5.2 %all-to-all-start = ((f32[4,56,200]{2,1,0:T(8,128)}), f32[4,56,200]{2,1,0:T(8,128)S(1)}, u32[]{:S(2)}, u32[]{:S(2)}) async-start(f32[4,56,200]{2,1,0:T(8,128)} %broadcast_in_dim.43), calls=%async_computation | async-start | bytes 458752 | tf_op jit(solution)/shard_map/all_to_all | solution.py:822
  16.6 2.5 collective-permute-start.4
  19.0 1.3 collective-permute-start.5
  20.3 1.5 all-to-all-done.small_ref
  21.9 1.0 slice_select_fusion.refs_4_
  22.9 1.2 collective-permute-start.2
  24.1 1.0 slice_select_fusion.1.refs_0_
  27.7 1.3 collective-permute-start.7
  29.8 3.3 %mask_gradient.1 = (bf16[800,1536]{1,0:T(8,128)(2,1)}, f32[1,16,128]{2,1,0:T(8,128)}) custom-call(bf16[6,800,256]{2,1,0:T(8,128)(2,1)} %bitcast.39, f32[6,16,256]{2,1,0:T(8,128)} %broadcast_in_dim.44.m_ref.refs_7_), custom_call_target="tpu_custom_call" | custom-call | flops 115000000 | bytes 100000 | tf_op jit(solution)/shard_map/mask_gradient/pallas_call | solution.py:347
  33.2 7.5 %collective-permute-done.2.refs_6_ = bf16[200,1664]{1,0:T(8,128)(2,1)} collective-permute-done((bf16[200,1664]{1,0:T(8,128)(2,1)}, bf16[200,1664]{1,0:T(8,128)(2,1)}, u32[]{:S(2)}, u32[]{:S(2)}) %collective-permute-start.2) | collective-permute-done | bytes 665632 | tf_op jit(solution)/shard_map/ppermute | solution.py:827
  40.7 1.4 collective-permute-start.6
  42.1 1.2 collective-permute-done.refs_1_
  43.4 1.6 collective-permute-start.1
  45.6 20.9 %conv_forward.1 = (f32[6,800,256]{2,1,0:T(8,128)}, f32[32,16,128]{2,1,0:T(8,128)}, f32[800,128]{1,0:T(8,128)}) custom-call(bf16[6,800,256]{2,1,0:T(8,128)(2,1)} %bitcast.36, bf16[3,800,256]{2,1,0:T(8,128)(2,1)} %collective-permute-done.4.up_ref, bf16[3,800,256]{2,1,0:T(8,128)(2,1)} %collective-permute-done.5.dn_ref, f32[4,56,200]{2,1,0:T(8,128)} %copy-done.2, ...), custom_call_target="tpu_custom_call" | custom-call | flops 460000000 | bytes 100000 | tf_op jit(solution)/shard_map/conv_forward/pallas_call | solution.py:158
  66.5 6.7 %all-to-all-start.1 = ((f32[32,16,128]{2,1,0:T(8,128)}), f32[32,16,128]{2,1,0:T(8,128)}, u32[]{:S(2)}, u32[]{:S(2)}) async-start(f32[32,16,128]{2,1,0:T(8,128)} %get-tuple-element.124), calls=%async_computation.1 | async-start | bytes 524288 | tf_op jit(solution)/shard_map/all_to_all | solution.py:916
  73.3 5.8 %join_pieces.1 = (bf16[800,1664]{1,0:T(8,128)(2,1)}, bf16[800,1664]{1,0:T(8,128)(2,1)}) custom-call(s32[1]{0:T(128)} %bitcast.14.index_ref, bf16[200,1664]{1,0:T(8,128)(2,1)} %slice_select_fusion.1.refs_0_, bf16[200,1664]{1,0:T(8,128)(2,1)} %collective-permute-done.refs_1_, bf16[200,1664]{1,0:T(8,128)(2,1)} %collective-permute-done.6.refs_2_, ...), custom_call_target="tpu_custom_call" | custom-call | flops 115000000 | bytes 100000 | tf_op jit(solution)/shard_map/join_pieces/pallas_call | solution.py:754
  79.1 4.9 %all-to-all-done.1.refs_1_ = f32[32,16,128]{2,1,0:T(8,128)} async-done(((f32[32,16,128]{2,1,0:T(8,128)}), f32[32,16,128]{2,1,0:T(8,128)}, u32[]{:S(2)}, u32[]{:S(2)}) %all-to-all-start.1) | async-done | bytes 262176 | tf_op jit(solution)/shard_map/all_to_all | solution.py:916
  84.0 15.9 %hidden_layer.4 = (bf16[1536,768]{1,0:T(8,128)(2,1)}, bf16[1536,768]{1,0:T(8,128)(2,1)}, bf16[800,768]{1,0:T(8,128)(2,1)}, bf16[800,768]{1,0:T(8,128)(2,1)}, f32...) custom-call(s32[4]{0:T(128)} %pad_add_fusion.bits_ref.flags_ref, ...), custom_call_target="tpu_custom_call" | custom-call | flops 345000000 | bytes 100000 | tf_op jit(solution)/shard_map/hidden_layer/pallas_call | solution.py:477
  101.0 17.0 %hidden_layer.5 = (bf16[1536,896]{1,0:T(8,128)(2,1)}, bf16[1536,896]{1,0:T(8,128)(2,1)}, bf16[800,896]{1,0:T(8,128)(2,1)}, bf16[800,896]{1,0:T(8,128)(2,1)}, f32[1,896]{1,0:T(1,128)}) custom-call(s32[4]{0:T(128)} %pad_add_fusion.bits_ref.flags_ref, bf16[800,1536]{1,0:T(8,128)(2,1)} %get-tuple-element.112.bg_ref, ...), custom_call_target="tpu_custom_call" | custom-call | flops 345000000 | bytes 100000 | tf_op jit(solution)/shard_map/hidden_layer/pallas_call | solution.py:477
  118.5 14.5 %hidden_layer.6 = (bf16[1536,768]{1,0:T(8,128)(2,1)}, bf16[1536,768]{1,0:T(8,128)(2,1)}, f32[400,768]{1,0:T(8,128)}, bf16[400,768]{1,0:T(8,128)(2,1)}, f32[400,7...) custom-call(s32[4]{0:T(128)} %pad_add_fusion.bits_ref.flags_ref, ...), custom_call_target="tpu_custom_call" | custom-call | flops 345000000 | bytes 100000 | tf_op jit(solution)/shard_map/hidden_layer/pallas_call | solution.py:477
  133.2 1.3 collective-permute-start.15
  134.5 18.0 %hidden_layer.7 = (bf16[1536,896]{1,0:T(8,128)(2,1)}, bf16[1536,896]{1,0:T(8,128)(2,1)}, f32[400,896]{1,0:T(8,128)}, bf16[400,896]{1,0:T(8,128)(2,1)}, f32[400,8...) custom-call(s32[4]{0:T(128)} %pad_add_fusion.bits_ref.flags_ref, ...), custom_call_target="tpu_custom_call" | custom-call | flops 345000000 | bytes 100000 | tf_op jit(solution)/shard_map/hidden_layer/pallas_call | solution.py:477
  152.5 3.4 %split_sums.2 = (f32[200,768]{1,0:T(8,128)}, bf16[200,768]{1,0:T(8,128)(2,1)}, f32[200,768]{1,0:T(8,128)}, bf16[200,768]{1,0:T(8,128)(2,1)}) custom-call(s32[4]{0:T(128)} %pad_add_fusion.bits_ref.flags_ref, f32[400,768]{1,0:T(8,128)} %get-tuple-element.147.refs_0_, bf16[400,768]{1,0:T(8,128)(2,1)} %collective-permute-done.14.refs_1_, ...), custom_call_target="tpu_custom_call" | custom-call | flops 3449999872 | bytes 100000 | tf_op jit(solution)/shard_map/split_sums/pallas_call | solution.py:502
  156.6 1.9 collective-permute-start.16
  158.5 1.4 collective-permute-start.19
  159.9 16.1 %activation_gradient.1 = (f32[6,800,256]{2,1,0:T(8,128)}, f32[32,16,128]{2,1,0:T(8,128)}) custom-call(bf16[800,1664]{1,0:T(8,128)(2,1)} %collective-permute-done.9.we_ref.refs_0_, bf16[800,1664]{1,0:T(8,128)(2,1)} %get-tuple-element.130.we_ref.refs_1_, bf16[1536,768]{1,0:T(8,128)(2,1)} %get-tuple-element.142.refs_2_, ...), custom_call_target="tpu_custom_call" | custom-call | flops 345000000 | bytes 100000 | tf_op jit(solution)/shard_map/activation_gradient/pallas_call | solution.py:608
  176.0 3.5 %all-to-all-start.2 = ((f32[32,16,128]{2,1,0:T(8,128)}), f32[32,16,128]{2,1,0:T(8,128)}, u32[]{:S(2)}, u32[]{:S(2)}) async-start(f32[32,16,128]{2,1,0:T(8,128)} %get-tuple-element.157), calls=%async_computation.2 | async-start | bytes 524288 | tf_op jit(solution)/shard_map/all_to_all | solution.py:975
  181.1 2.5 band_split.1
  183.6 3.7 %split_sums.3 = (f32[200,896]{1,0:T(8,128)}, bf16[200,896]{1,0:T(8,128)(2,1)}, f32[200,896]{1,0:T(8,128)}, bf16[200,896]{1,0:T(8,128)(2,1)}) custom-call(s32[4]{0:T(128)} %pad_add_fusion.bits_ref.flags_ref, f32[400,896]{1,0:T(8,128)} %get-tuple-element.158.refs_0_, bf16[400,896]{1,0:T(8,128)(2,1)} %collective-permute-done.16.refs_1_, ...), custom_call_target="tpu_custom_call" | custom-call | flops 3449999872 | bytes 100000 | tf_op jit(solution)/shard_map/split_sums/pallas_call | solution.py:502
  188.2 0.9 collective-permute-start.24
  189.1 1.3 collective-permute-start.22
  191.0 8.3 %conv_gradient.1 = (bf16[6,800,256]{2,1,0:T(8,128)(2,1)}, bf16[3,800,256]{2,1,0:T(8,128)(2,1)}, bf16[3,800,256]{2,1,0:T(8,128)(2,1)}, f32[16,128]{1,0:T(8,128)}) custom-call(f32[6,800,256]{2,1,0:T(8,128)} %get-tuple-element.156.da_ref, f32[6,800,256]{2,1,0:T(8,128)} %get-tuple-element.116.refs_0_.refs_6_.conv_ref, ...), custom_call_target="tpu_custom_call" | custom-call | flops 230000000 | bytes 100000 | tf_op jit(solution)/shard_map/conv_gradient/pallas_call | solution.py:697
  199.4 2.3 collective-permute-start.20
  201.7 1.3 collective-permute-start.21
  203.1 1.9 round_sums.3.refs_0_
  205.0 2.5 round_sums.4
  207.5 18.1 %tap_gradient.1 = f32[4,54,200]{2,1,0:T(8,128)} custom-call(s32[4]{0:T(128)} %pad_add_fusion.bits_ref.flags_ref, bf16[6,800,256]{2,1,0:T(8,128)(2,1)} %bitcast.37, bf16[3,800,256]{2,1,0:T(8,128)(2,1)} %collective-permute-done.4.up_ref, bf16[3,800,256]{2,1,0:T(8,128)(2,1)} %collective-permute-done.5.dn_ref, bf16[6,800,256]{2,1,0:T(8,128)(2,1)} %get-tuple-element.185.g_ref, ...), custom_call_target="tpu_custom_call" | custom-call | flops 17250000896 | bytes 100000 | tf_op jit(solution)/shard_map/tap_gradient/pallas_call | solution.py:295
  225.6 4.0 %all-to-all-start.3 = ((f32[4,54,200]{2,1,0:T(8,128)}), f32[4,54,200]{2,1,0:T(8,128)}, u32[]{:S(2)}, u32[]{:S(2)}) async-start(f32[4,54,200]{2,1,0:T(8,128)} %tap_gradient.1), calls=%async_computation.3 | async-start | bytes 458752 | tf_op jit(solution)/shard_map/all_to_all | solution.py:995
  229.7 4.5 %collective-permute-start.25 = (bf16[2,104,768]{2,1,0:T(8,128)(2,1)}, bf16[2,104,768]{2,1,0:T(8,128)(2,1)}, u32[]{:S(2)}, u32[]{:S(2)}) collective-permute-start(bf16[2,104,768]{2,1,0:T(8,128)(2,1)} %round_sums.3.refs_0_), channel_id=1, source_target_pairs={{0,16},{4,20},{8,24},{12,28},{16,0},{20,4},{24,8},{28,12},{1,17},{... | collective-permute-start | bytes 958472 | tf_op jit(solution)/shard_map/ppermute | solution.py:827
  234.1 16.3 %input_gradient.1 = f32[6,800,256]{2,1,0:T(8,128)} custom-call(bf16[6,800,256]{2,1,0:T(8,128)(2,1)} %get-tuple-element.185.g_ref, bf16[3,800,256]{2,1,0:T(8,128)(2,1)} %collective-permute-done.20.up_ref, bf16[3,800,256]{2,1,0:T(8,128)(2,1)} %collective-permute-done.21.dn_ref, f32[800,128]{1,0:T(8,128)} %get-tuple-element.197.refs_2_.par_ref.refs_8_, ...), custom_call_target="tpu_custom_call" | custom-call | flops 5750000128 | bytes 100000 | tf_op jit(solution)/shard_map/input_gradient/pallas_call | solution.py:216
  250.4 1.0 reduce_sum.18
  252.2 4.4 %all-to-all-start.4 = ((f32[8,54,200]{2,1,0:T(8,128)}), f32[8,54,200]{2,1,0:T(8,128)}, u32[]{:S(2)}, u32[]{:S(2)}) async-start(f32[8,54,200]{2,1,0:T(8,128)} %broadcast_in_dim.48), calls=%async_computation.4 | async-start | bytes 917504 | tf_op jit(solution)/shard_map/all_to_all | solution.py:822
  256.6 5.5 %collective-permute-done.25.refs_1_ = bf16[2,104,768]{2,1,0:T(8,128)(2,1)} collective-permute-done((bf16[2,104,768]{2,1,0:T(8,128)(2,1)}, bf16[2,104,768]{2,1,0:T(8,128)(2,1)}, u32[]{:S(2)}, u32[]{:S(2)}) %collective-permute-start.25) | collective-permute-done | bytes 319520 | tf_op jit(solution)/shard_map/ppermute | solution.py:827
  262.1 1.9 round_sums.5.refs_4_
  264.5 14.6 %block_output.1 = bf16[6,800,256]{2,1,0:T(8,128)(2,1)} custom-call(bf16[800,1664]{1,0:T(8,128)(2,1)} %collective-permute-done.8.wp_ref.refs_0_, bf16[800,1664]{1,0:T(8,128)(2,1)} %get-tuple-element.128.wp_ref.refs_1_, bf16[1536,768]{1,0:T(8,128)(2,1)} %get-tuple-element.129.refs_2_, bf16[1536,768]{1,0:T(8,128)(2,1)} %get-tuple-element.137.refs_3_, ...), custom_call_target="tpu_custom_call" | custom-call | flops 5750000128 | bytes 100000 | tf_op jit(solution)/shard_map/block_output/pallas_call | solution.py:641
  281.5 1.1 reduce_sum.19
  284.5 4.4 %place_columns.1 = (f32[200,3200]{1,0:T(8,128)}, f32[200,3200]{1,0:T(8,128)}) custom-call(s32[4]{0:T(128)} %pad_add_fusion.bits_ref.flags_ref, bf16[200,896]{1,0:T(8,128)(2,1)} %get-tuple-element.200.refs_0_, bf16[200,896]{1,0:T(8,128)(2,1)} %collective-permute-done.27.refs_1_, bf16[200,896]{1,0:T(8,128)(2,1)} %get-tuple-element.201.refs_2_, ...), custom_call_target="tpu_custom_call" | custom-call | flops 115000000 | bytes 100000 | tf_op jit(solution)/shard_map/place_columns/pallas_call | solution.py:794
  (99 shorter events, 15.6 us)
Async XLA Ops:
  7.2 3.3 %copy-start.7 = (bf16[800]{0:T(1024)(128)(2,1)S(1)}, bf16[800]{0:T(1024)(128)(2,1)}, u32[]{:S(2)}) copy-start(bf16[800]{0:T(1024)(128)(2,1)} %param.19) | copy-start | bytes 4804
  7.2 3.4 %copy-start.10 = (bf16[200]{0:T(256)(128)(2,1)S(1)}, bf16[200]{0:T(256)(128)(2,1)}, u32[]{:S(2)}) copy-start(bf16[200]{0:T(256)(128)(2,1)} %param.21) | copy-start | bytes 1204
  7.2 3.4 %copy-start.4 = (f32[200,49]{0,1:T(8,128)S(1)}, f32[200,49]{0,1:T(8,128)}, u32[]{:S(2)}) copy-start(f32[200,49]{0,1:T(8,128)} %param.15) | copy-start | bytes 117604
  7.2 3.4 %copy-start.8 = (f32[200]{0:T(256)S(1)}, f32[200]{0:T(256)}, u32[]{:S(2)}) copy-start(f32[200]{0:T(256)} %param.16) | copy-start | bytes 2404
  7.2 3.4 %copy-start.9 = (f32[200]{0:T(256)S(1)}, f32[200]{0:T(256)}, u32[]{:S(2)}) copy-start(f32[200]{0:T(256)} %param.17) | copy-start | bytes 2404
  10.5 11.3 %copy-start.1 = (bf16[200,3200]{1,0:T(8,128)(2,1)S(1)}, bf16[200,3200]{1,0:T(8,128)(2,1)}, u32[]{:S(2)}) copy-start(bf16[200,3200]{1,0:T(8,128)(2,1)} %param.20) | copy-start | bytes 3840004
  10.5 11.3 %slice-start.1 = ((bf16[200,3200]{1,0:T(8,128)(2,1)}), bf16[200,1536]{1,0:T(8,128)(2,1)S(1)}, s32[]{:S(2)}) async-start(bf16[200,3200]{1,0:T(8,128)(2,1)} %param.20), calls=%async_computation.7 | async-start | bytes 1228800 | tf_op jit(solution)/shard_map/slice | solution.py:890
  11.4 10.4 %all-to-all-start = ((f32[4,56,200]{2,1,0:T(8,128)}), f32[4,56,200]{2,1,0:T(8,128)S(1)}, u32[]{:S(2)}, u32[]{:S(2)}) async-start(f32[4,56,200]{2,1,0:T(8,128)} %broadcast_in_dim.43), calls=%async_computation | async-start | bytes 458752 | tf_op jit(solution)/shard_map/all_to_all | solution.py:822
  16.6 26.8 %collective-permute-start.4 = (bf16[3,800,256]{2,1,0:T(8,128)(2,1)}, bf16[3,800,256]{2,1,0:T(8,128)(2,1)}, u32[]{:S(2)}, u32[]{:S(2)}) collective-permute-start(bf16[3,800,256]{2,1,0:T(8,128)(2,1)} %get-tuple-element.207), channel_id=1, source_target_pairs={{0,4},{4,8},{8,12},{12,16},{16,20},{20,24},{24,28},{1,5},{5,9},{9,... | collective-permute-start | bytes 3686408 | tf_op jit(solution)/shard_map/ppermute | solution.py:811
  19.0 26.6 %collective-permute-start.5 = (bf16[3,800,256]{2,1,0:T(8,128)(2,1)}, bf16[3,800,256]{2,1,0:T(8,128)(2,1)}, u32[]{:S(2)}, u32[]{:S(2)}) collective-permute-start(bf16[3,800,256]{2,1,0:T(8,128)(2,1)} %get-tuple-element.208), channel_id=1, source_target_pairs={{4,0},{8,4},{12,8},{16,12},{20,16},{24,20},{28,24},{5,1},{9,5},{13... | collective-permute-start | bytes 3686408 | tf_op jit(solution)/shard_map/ppermute | solution.py:812
  21.8 7.9 %copy-start.2 = (f32[4,56,200]{2,1,0:T(8,128)}, f32[4,56,200]{2,1,0:T(8,128)S(1)}, u32[]{:S(2)}) copy-start(f32[4,56,200]{2,1,0:T(8,128)S(1)} %all-to-all-done.small_ref) | copy-start | bytes 537604
  22.9 4.8 %copy-start.5 = (s32[6,256]{1,0:T(8,128)S(1)}, s32[6,256]{1,0:T(8,128)}, u32[]{:S(2)}) copy-start(s32[6,256]{1,0:T(8,128)} %param.13) | copy-start | bytes 18436
  22.9 17.7 %collective-permute-start.2 = (bf16[200,1664]{1,0:T(8,128)(2,1)}, bf16[200,1664]{1,0:T(8,128)(2,1)}, u32[]{:S(2)}, u32[]{:S(2)}) collective-permute-start(bf16[200,1664]{1,0:T(8,128)(2,1)} %slice_select_fusion.refs_4_), channel_id=1, source_target_pairs={{0,2},{1,3},{2,0},{3,1},{4,6},{5,7},{6,4},{7,5},{8,10},{9,11},{10,... | collective-permute-start | bytes 1996808 | tf_op jit(solution)/shard_map/ppermute | solution.py:827
  25.1 18.1 %collective-permute-start = (bf16[200,1664]{1,0:T(8,128)(2,1)}, bf16[200,1664]{1,0:T(8,128)(2,1)}, u32[]{:S(2)}, u32[]{:S(2)}) collective-permute-start(bf16[200,1664]{1,0:T(8,128)(2,1)} %slice_select_fusion.1.refs_0_), channel_id=1, source_target_pairs={{0,1},{1,0},{2,3},{3,2},{4,5},{5,4},{6,7},{7,6},{8,9},{9,8},{10,11... | collective-permute-start | bytes 1996808 | tf_op jit(solution)/shard_map/ppermute | solution.py:827
  27.7 45.5 %collective-permute-start.7 = (bf16[200,1664]{1,0:T(8,128)(2,1)}, bf16[200,1664]{1,0:T(8,128)(2,1)}, u32[]{:S(2)}, u32[]{:S(2)}) collective-permute-start(bf16[200,1664]{1,0:T(8,128)(2,1)} %slice_select_fusion.refs_4_), channel_id=1, source_target_pairs={{0,1},{1,0},{2,3},{3,2},{4,5},{5,4},{6,7},{7,6},{8,9},{9,8},{10,11... | collective-permute-start | bytes 1996808 | tf_op jit(solution)/shard_map/ppermute | solution.py:827
  40.7 32.6 %collective-permute-start.6 = (bf16[200,1664]{1,0:T(8,128)(2,1)}, bf16[200,1664]{1,0:T(8,128)(2,1)}, u32[]{:S(2)}, u32[]{:S(2)}) collective-permute-start(bf16[200,1664]{1,0:T(8,128)(2,1)} %slice_select_fusion.1.refs_0_), channel_id=1, source_target_pairs={{0,2},{1,3},{2,0},{3,1},{4,6},{5,7},{6,4},{7,5},{8,10},{9,11},{10,... | collective-permute-start | bytes 1996808 | tf_op jit(solution)/shard_map/ppermute | solution.py:827
  43.3 30.0 %collective-permute-start.3 = (bf16[200,1664]{1,0:T(8,128)(2,1)}, bf16[200,1664]{1,0:T(8,128)(2,1)}, u32[]{:S(2)}, u32[]{:S(2)}) collective-permute-start(bf16[200,1664]{1,0:T(8,128)(2,1)} %collective-permute-done.2.refs_6_), channel_id=1, source_target_pairs={{0,1},{1,0},{2,3},{3,2},{4,5},{5,4},{6,7},{7,6},{8,9},{9,8},{10,11... | collective-permute-start | bytes 1996808 | tf_op jit(solution)/shard_map/ppermute | solution.py:827
  43.4 29.8 %collective-permute-start.1 = (bf16[200,1664]{1,0:T(8,128)(2,1)}, bf16[200,1664]{1,0:T(8,128)(2,1)}, u32[]{:S(2)}, u32[]{:S(2)}) collective-permute-start(bf16[200,1664]{1,0:T(8,128)(2,1)} %collective-permute-done.refs_1_), channel_id=1, source_target_pairs={{0,2},{1,3},{2,0},{3,1},{4,6},{5,7},{6,4},{7,5},{8,10},{9,11},{10,... | collective-permute-start | bytes 1996808 | tf_op jit(solution)/shard_map/ppermute | solution.py:827
  66.5 17.5 %all-to-all-start.1 = ((f32[32,16,128]{2,1,0:T(8,128)}), f32[32,16,128]{2,1,0:T(8,128)}, u32[]{:S(2)}, u32[]{:S(2)}) async-start(f32[32,16,128]{2,1,0:T(8,128)} %get-tuple-element.124), calls=%async_computation.1 | async-start | bytes 524288 | tf_op jit(solution)/shard_map/all_to_all | solution.py:916
  99.9 18.6 %collective-permute-start.9 = (bf16[800,1664]{1,0:T(8,128)(2,1)}, bf16[800,1664]{1,0:T(8,128)(2,1)}, u32[]{:S(2)}, u32[]{:S(2)}) collective-permute-start(bf16[800,1664]{1,0:T(8,128)(2,1)} %get-tuple-element.130.we_ref.refs_1_), channel_id=1, source_target_pairs={{0,4},{4,0},{8,12},{12,8},{16,20},{20,16},{24,28},{28,24},{1,5},{5... | collective-permute-start | bytes 7987208 | tf_op jit(solution)/shard_map/ppermute | solution.py:827
  100.0 18.5 %collective-permute-start.8 = (bf16[800,1664]{1,0:T(8,128)(2,1)}, bf16[800,1664]{1,0:T(8,128)(2,1)}, u32[]{:S(2)}, u32[]{:S(2)}) collective-permute-start(bf16[800,1664]{1,0:T(8,128)(2,1)} %get-tuple-element.128.wp_ref.refs_1_), channel_id=1, source_target_pairs={{0,4},{4,0},{8,12},{12,8},{16,20},{20,16},{24,28},{28,24},{1,5},{5... | collective-permute-start | bytes 7987208 | tf_op jit(solution)/shard_map/ppermute | solution.py:827
  100.5 17.6 %collective-permute-start.10 = (bf16[800,768]{1,0:T(8,128)(2,1)}, bf16[800,768]{1,0:T(8,128)(2,1)}, u32[]{:S(2)}, u32[]{:S(2)}) collective-permute-start(bf16[800,768]{1,0:T(8,128)(2,1)} %get-tuple-element.135), channel_id=1, source_target_pairs={{0,4},{4,0},{8,12},{12,8},{16,20},{20,16},{24,28},{28,24},{1,5},{5... | collective-permute-start | bytes 3686408 | tf_op jit(solution)/shard_map/ppermute | solution.py:827
  100.6 18.0 %collective-permute-start.11 = (bf16[800,768]{1,0:T(8,128)(2,1)}, bf16[800,768]{1,0:T(8,128)(2,1)}, u32[]{:S(2)}, u32[]{:S(2)}) collective-permute-start(bf16[800,768]{1,0:T(8,128)(2,1)} %get-tuple-element.136), channel_id=1, source_target_pairs={{0,4},{4,0},{8,12},{12,8},{16,20},{20,16},{24,28},{28,24},{1,5},{5... | collective-permute-start | bytes 3686408 | tf_op jit(solution)/shard_map/ppermute | solution.py:827
  118.0 16.5 %collective-permute-start.12 = (bf16[800,896]{1,0:T(8,128)(2,1)}, bf16[800,896]{1,0:T(8,128)(2,1)}, u32[]{:S(2)}, u32[]{:S(2)}) collective-permute-start(bf16[800,896]{1,0:T(8,128)(2,1)} %get-tuple-element.139), channel_id=1, source_target_pairs={{0,4},{4,0},{8,12},{12,8},{16,20},{20,16},{24,28},{28,24},{1,5},{5... | collective-permute-start | bytes 4300808 | tf_op jit(solution)/shard_map/ppermute | solution.py:827
  118.1 16.4 %collective-permute-start.13 = (bf16[800,896]{1,0:T(8,128)(2,1)}, bf16[800,896]{1,0:T(8,128)(2,1)}, u32[]{:S(2)}, u32[]{:S(2)}) collective-permute-start(bf16[800,896]{1,0:T(8,128)(2,1)} %get-tuple-element.140), channel_id=1, source_target_pairs={{0,4},{4,0},{8,12},{12,8},{16,20},{20,16},{24,28},{28,24},{1,5},{5... | collective-permute-start | bytes 4300808 | tf_op jit(solution)/shard_map/ppermute | solution.py:827
  133.0 19.5 %collective-permute-start.14 = (bf16[400,768]{1,0:T(8,128)(2,1)}, bf16[400,768]{1,0:T(8,128)(2,1)}, u32[]{:S(2)}, u32[]{:S(2)}) collective-permute-start(bf16[400,768]{1,0:T(8,128)(2,1)} %get-tuple-element.148), channel_id=1, source_target_pairs={{0,2},{1,3},{2,0},{3,1},{4,6},{5,7},{6,4},{7,5},{8,10},{9,11},{10,... | collective-permute-start | bytes 1843208 | tf_op jit(solution)/shard_map/ppermute | solution.py:827
  133.2 19.3 %collective-permute-start.15 = (bf16[400,768]{1,0:T(8,128)(2,1)}, bf16[400,768]{1,0:T(8,128)(2,1)}, u32[]{:S(2)}, u32[]{:S(2)}) collective-permute-start(bf16[400,768]{1,0:T(8,128)(2,1)} %get-tuple-element.149), channel_id=1, source_target_pairs={{0,1},{1,0},{2,3},{3,2},{4,5},{5,4},{6,7},{7,6},{8,9},{9,8},{10,11... | collective-permute-start | bytes 1843208 | tf_op jit(solution)/shard_map/ppermute | solution.py:827
  155.8 27.7 %collective-permute-start.17 = (bf16[400,896]{1,0:T(8,128)(2,1)}, bf16[400,896]{1,0:T(8,128)(2,1)}, u32[]{:S(2)}, u32[]{:S(2)}) collective-permute-start(bf16[400,896]{1,0:T(8,128)(2,1)} %get-tuple-element.162), channel_id=1, source_target_pairs={{0,1},{1,0},{2,3},{3,2},{4,5},{5,4},{6,7},{7,6},{8,9},{9,8},{10,11... | collective-permute-start | bytes 2150408 | tf_op jit(solution)/shard_map/ppermute | solution.py:827
  156.6 27.0 %collective-permute-start.16 = (bf16[400,896]{1,0:T(8,128)(2,1)}, bf16[400,896]{1,0:T(8,128)(2,1)}, u32[]{:S(2)}, u32[]{:S(2)}) collective-permute-start(bf16[400,896]{1,0:T(8,128)(2,1)} %get-tuple-element.160), channel_id=1, source_target_pairs={{0,2},{1,3},{2,0},{3,1},{4,6},{5,7},{6,4},{7,5},{8,10},{9,11},{10,... | collective-permute-start | bytes 2150408 | tf_op jit(solution)/shard_map/ppermute | solution.py:827
  158.5 21.7 %collective-permute-start.18 = (bf16[200,768]{1,0:T(8,128)(2,1)}, bf16[200,768]{1,0:T(8,128)(2,1)}, u32[]{:S(2)}, u32[]{:S(2)}) collective-permute-start(bf16[200,768]{1,0:T(8,128)(2,1)} %get-tuple-element.153), channel_id=1, source_target_pairs={{0,1},{1,0},{2,3},{3,2},{4,5},{5,4},{6,7},{7,6},{8,9},{9,8},{10,11... | collective-permute-start | bytes 921608 | tf_op jit(solution)/shard_map/ppermute | solution.py:827
  158.5 22.5 %collective-permute-start.19 = (bf16[200,768]{1,0:T(8,128)(2,1)}, bf16[200,768]{1,0:T(8,128)(2,1)}, u32[]{:S(2)}, u32[]{:S(2)}) collective-permute-start(bf16[200,768]{1,0:T(8,128)(2,1)} %get-tuple-element.154), channel_id=1, source_target_pairs={{0,2},{1,3},{2,0},{3,1},{4,6},{5,7},{6,4},{7,5},{8,10},{9,11},{10,... | collective-permute-start | bytes 921608 | tf_op jit(solution)/shard_map/ppermute | solution.py:827
  176.0 15.0 %all-to-all-start.2 = ((f32[32,16,128]{2,1,0:T(8,128)}), f32[32,16,128]{2,1,0:T(8,128)}, u32[]{:S(2)}, u32[]{:S(2)}) async-start(f32[32,16,128]{2,1,0:T(8,128)} %get-tuple-element.157), calls=%async_computation.2 | async-start | bytes 524288 | tf_op jit(solution)/shard_map/all_to_all | solution.py:975
  179.5 99.6 %all-reduce.6.cloned.1.call-start = ((), (), s32[]{:S(2)}) async-start(), calls=%async_computation.5 | async-start | bytes 1433600 | tf_op jit(solution)/shard_map/psum | solution.py:948
  183.6 6.9 %copy-start.3 = (f32[32,128]{1,0:T(8,128)S(1)}, f32[32,128]{1,0:T(8,128)}, u32[]{:S(2)}) copy-start(f32[32,128]{1,0:T(8,128)} %get-tuple-element.155.refs_7_.stat_ref) | copy-start | bytes 49156
  187.3 15.8 %collective-permute-start.23 = (bf16[200,896]{1,0:T(8,128)(2,1)}, bf16[200,896]{1,0:T(8,128)(2,1)}, u32[]{:S(2)}, u32[]{:S(2)}) collective-permute-start(bf16[200,896]{1,0:T(8,128)(2,1)} %get-tuple-element.171), channel_id=1, source_target_pairs={{0,1},{1,0},{2,3},{3,2},{4,5},{5,4},{6,7},{7,6},{8,9},{9,8},{10,11... | collective-permute-start | bytes 1075208 | tf_op jit(solution)/shard_map/ppermute | solution.py:827
  188.2 14.9 %collective-permute-start.24 = (bf16[200,896]{1,0:T(8,128)(2,1)}, bf16[200,896]{1,0:T(8,128)(2,1)}, u32[]{:S(2)}, u32[]{:S(2)}) collective-permute-start(bf16[200,896]{1,0:T(8,128)(2,1)} %get-tuple-element.172), channel_id=1, source_target_pairs={{0,2},{1,3},{2,0},{3,1},{4,6},{5,7},{6,4},{7,5},{8,10},{9,11},{10,... | collective-permute-start | bytes 1075208 | tf_op jit(solution)/shard_map/ppermute | solution.py:827
  189.1 13.9 %collective-permute-start.22 = (bf16[2,104,768]{2,1,0:T(8,128)(2,1)}, bf16[2,104,768]{2,1,0:T(8,128)(2,1)}, u32[]{:S(2)}, u32[]{:S(2)}) collective-permute-start(bf16[2,104,768]{2,1,0:T(8,128)(2,1)} %get-tuple-element.167), channel_id=1, source_target_pairs={{0,8},{4,12},{8,0},{12,4},{16,24},{20,28},{24,16},{28,20},{1,9},{5... | collective-permute-start | bytes 958472 | tf_op jit(solution)/shard_map/ppermute | solution.py:827
  199.4 30.3 %collective-permute-start.20 = (bf16[3,800,256]{2,1,0:T(8,128)(2,1)}, bf16[3,800,256]{2,1,0:T(8,128)(2,1)}, u32[]{:S(2)}, u32[]{:S(2)}) collective-permute-start(bf16[3,800,256]{2,1,0:T(8,128)(2,1)} %get-tuple-element.175), channel_id=1, source_target_pairs={{0,4},{4,8},{8,12},{12,16},{16,20},{20,24},{24,28},{1,5},{5,9},{9,... | collective-permute-start | bytes 3686408 | tf_op jit(solution)/shard_map/ppermute | solution.py:811
  201.7 27.9 %collective-permute-start.21 = (bf16[3,800,256]{2,1,0:T(8,128)(2,1)}, bf16[3,800,256]{2,1,0:T(8,128)(2,1)}, u32[]{:S(2)}, u32[]{:S(2)}) collective-permute-start(bf16[3,800,256]{2,1,0:T(8,128)(2,1)} %get-tuple-element.176), channel_id=1, source_target_pairs={{4,0},{8,4},{12,8},{16,12},{20,16},{24,20},{28,24},{5,1},{9,5},{13... | collective-permute-start | bytes 3686408 | tf_op jit(solution)/shard_map/ppermute | solution.py:812
  225.6 24.8 %all-to-all-start.3 = ((f32[4,54,200]{2,1,0:T(8,128)}), f32[4,54,200]{2,1,0:T(8,128)}, u32[]{:S(2)}, u32[]{:S(2)}) async-start(f32[4,54,200]{2,1,0:T(8,128)} %tap_gradient.1), calls=%async_computation.3 | async-start | bytes 458752 | tf_op jit(solution)/shard_map/all_to_all | solution.py:995
  229.7 32.4 %collective-permute-start.25 = (bf16[2,104,768]{2,1,0:T(8,128)(2,1)}, bf16[2,104,768]{2,1,0:T(8,128)(2,1)}, u32[]{:S(2)}, u32[]{:S(2)}) collective-permute-start(bf16[2,104,768]{2,1,0:T(8,128)(2,1)} %round_sums.3.refs_0_), channel_id=1, source_target_pairs={{0,16},{4,20},{8,24},{12,28},{16,0},{20,4},{24,8},{28,12},{1,17},{... | collective-permute-start | bytes 958472 | tf_op jit(solution)/shard_map/ppermute | solution.py:827
  252.2 29.3 %all-to-all-start.4 = ((f32[8,54,200]{2,1,0:T(8,128)}), f32[8,54,200]{2,1,0:T(8,128)}, u32[]{:S(2)}, u32[]{:S(2)}) async-start(f32[8,54,200]{2,1,0:T(8,128)} %broadcast_in_dim.48), calls=%async_computation.4 | async-start | bytes 917504 | tf_op jit(solution)/shard_map/all_to_all | solution.py:822
  264.0 16.2 %copy-start.6 = (f32[16,128]{1,0:T(8,128)S(1)}, f32[16,128]{1,0:T(8,128)}, u32[]{:S(2)}) copy-start(f32[16,128]{1,0:T(8,128)} %get-tuple-element.199) | copy-start | bytes 24580
  264.0 15.2 %collective-permute-start.26 = (bf16[2,104,768]{2,1,0:T(8,128)(2,1)}, bf16[2,104,768]{2,1,0:T(8,128)(2,1)}, u32[]{:S(2)}, u32[]{:S(2)}) collective-permute-start(bf16[2,104,768]{2,1,0:T(8,128)(2,1)} %round_sums.5.refs_4_), channel_id=1, source_target_pairs={{0,8},{4,12},{8,0},{12,4},{16,24},{20,28},{24,16},{28,20},{1,9},{5... | collective-permute-start | bytes 958472 | tf_op jit(solution)/shard_map/ppermute | solution.py:827
  264.5 19.9 %collective-permute-start.29 = (bf16[2,104,768]{2,1,0:T(8,128)(2,1)}, bf16[2,104,768]{2,1,0:T(8,128)(2,1)}, u32[]{:S(2)}, u32[]{:S(2)}) collective-permute-start(bf16[2,104,768]{2,1,0:T(8,128)(2,1)} %round_sums.5.refs_4_), channel_id=1, source_target_pairs={{0,4},{4,0},{8,12},{12,8},{16,20},{20,16},{24,28},{28,24},{1,5},{5... | collective-permute-start | bytes 958472 | tf_op jit(solution)/shard_map/ppermute | solution.py:827
  279.2 5.3 %collective-permute-start.27 = (bf16[200,896]{1,0:T(8,128)(2,1)}, bf16[200,896]{1,0:T(8,128)(2,1)}, u32[]{:S(2)}, u32[]{:S(2)}) collective-permute-start(bf16[200,896]{1,0:T(8,128)(2,1)} %get-tuple-element.200.refs_0_), channel_id=1, source_target_pairs={{0,4},{4,0},{8,12},{12,8},{16,20},{20,16},{24,28},{28,24},{1,5},{5... | collective-permute-start | bytes 1075208 | tf_op jit(solution)/shard_map/ppermute | solution.py:827
  279.7 4.7 %collective-permute-start.28 = (bf16[200,896]{1,0:T(8,128)(2,1)}, bf16[200,896]{1,0:T(8,128)(2,1)}, u32[]{:S(2)}, u32[]{:S(2)}) collective-permute-start(bf16[200,896]{1,0:T(8,128)(2,1)} %get-tuple-element.201.refs_2_), channel_id=1, source_target_pairs={{0,4},{4,0},{8,12},{12,8},{16,20},{20,16},{24,28},{28,24},{1,5},{5... | collective-permute-start | bytes 1075208 | tf_op jit(solution)/shard_map/ppermute | solution.py:827
  279.8 4.7 %collective-permute-start.30 = (bf16[2,104,768]{2,1,0:T(8,128)(2,1)}, bf16[2,104,768]{2,1,0:T(8,128)(2,1)}, u32[]{:S(2)}, u32[]{:S(2)}) collective-permute-start(bf16[2,104,768]{2,1,0:T(8,128)(2,1)} %collective-permute-done.26.refs_5_), channel_id=1, source_target_pairs={{0,4},{4,0},{8,12},{12,8},{16,20},{20,16},{24,28},{28,24},{1,5},{5... | collective-permute-start | bytes 958472 | tf_op jit(solution)/shard_map/ppermute | solution.py:827
  (3 other events, 7.4 us)
Sparse Core Ops, SparseCore 0:
  207.6 54.0 all-reduce.5
